TPU v7x, 256 devices: a whole 4x4x8 slice. The times are simulated.
256 devices in a mesh: il: 16 (over y, x), xl: 16 (over z, core).
Axes of the slice: x: 4, y: 4, z: 8, core: 2. Of those that a mesh axis runs over, the one named last changes fastest.
Arguments:
- patches: bfloat16 [16, 192, 128, 768], P('il', 'xl'), may hold values from -9 to 9
- out_cot: bfloat16 [16, 192, 128, 768], P('il', 'xl'), may hold values from -6 to 6
- vis_count: int32 [16, 192], P('il', 'xl'), may hold values from 0 to 128, as said below
- w_qkv: bfloat16 [768, 1152], P(('il', 'xl')), may hold values from -1.5 to 1.5
- w_out: bfloat16 [768, 384], P(('il', 'xl')), may hold values from -0.3125 to 0.3125
- ln_gain: float32 [768], replicated, may hold values from 0.1 to 1.9
Outputs:
- enc_out: bfloat16 [16, 192, 128, 768], P('il', 'xl')
- grad_in: bfloat16 [16, 192, 128, 768], P('il', 'xl')
- grad_wqkv: float32 [768, 1152], P(('il', 'xl'))
- grad_wout: float32 [768, 384], P(('il', 'xl'))
Inputs may be any that keep to these rules, and one draw needn't show every extreme that they name: `vis_count`: A block with count 0 holds no data. On each inline row of tiles exactly 96 blocks have data; one device holds 0 to 12 of them, and some device of each row holds 12.
All inputs are finite; a program needn't handle non-finite values.
Results may differ from a plain program's by a relative error of at most 0.0096.
Values may be sent and summed in bfloat16 or wider, within the bound.
No kernel may reach another device: no remote copies, remote signals or barrier semaphores. Data moves between devices by JAX's collectives and lax.ppermute only.
A program may use at most 128 MiB of HBM per device.

v0:
```python
import jax
import jax.numpy as jnp
from jax import lax
from jax.sharding import PartitionSpec as P

HEAD_DIM = 64
HEADS = 6


def block_pass(tiles, cotan, counts, weights_qkv, weights_out, ln_gain):
    nblock, vrows, width = tiles.shape
    inner = HEADS * HEAD_DIM
    factor = HEAD_DIM ** (-0.5)
    positions = jnp.arange(vrows)
    row_mask = (positions[None, :] < counts[:, None]).astype(jnp.float32)
    tiles_f = tiles.astype(jnp.float32)
    centred = tiles_f - jnp.mean(tiles_f, axis=-1, keepdims=True)
    inv_std = lax.rsqrt(jnp.mean(centred * centred, axis=-1, keepdims=True) + 1e-06)
    normed = centred * inv_std
    normed_b = (normed * ln_gain).astype(jnp.bfloat16).reshape(nblock * vrows, width)
    project = jnp.dot(normed_b, weights_qkv, preferred_element_type=jnp.float32).astype(
        jnp.bfloat16
    )
    project = project.reshape(nblock, vrows, 3, HEADS, HEAD_DIM)
    queries = project[:, :, 0]
    keys_b = project[:, :, 1]
    values_b = project[:, :, 2]
    scores = (
        jnp.einsum("nqhe,nkhe->nhqk", queries, keys_b, preferred_element_type=jnp.float32) * factor
    )
    key_mask = (positions[None, :] < counts[:, None])[:, None, None, :]
    scores = jnp.where(key_mask, scores, jnp.float32(-1e30))
    probs_f = jnp.exp(scores - jnp.max(scores, axis=-1, keepdims=True))
    probs_f = probs_f / jnp.sum(probs_f, axis=-1, keepdims=True)
    probs_b = probs_f.astype(jnp.bfloat16)
    attended = jnp.einsum("nhqk,nkhe->nqhe", probs_b, values_b, preferred_element_type=jnp.float32)
    attended = attended.astype(jnp.bfloat16).reshape(nblock * vrows, inner)
    mixed = lax.dot_general(
        attended, weights_out, (((1,), (1,)), ((), ())), preferred_element_type=jnp.float32
    )
    mixed = mixed.reshape(nblock, vrows, width)
    encoded = ((tiles_f + mixed) * row_mask[..., None]).astype(jnp.bfloat16)
    grad_out = (cotan * row_mask[..., None].astype(jnp.bfloat16)).reshape(nblock * vrows, width)
    grad_wout = lax.dot_general(
        grad_out, attended, (((0,), (0,)), ((), ())), preferred_element_type=jnp.float32
    )
    grad_att = jnp.dot(grad_out, weights_out, preferred_element_type=jnp.float32).astype(
        jnp.bfloat16
    )
    grad_att = grad_att.reshape(nblock, vrows, HEADS, HEAD_DIM)
    grad_prob = jnp.einsum(
        "nqhe,nkhe->nhqk", grad_att, values_b, preferred_element_type=jnp.float32
    )
    grad_val = jnp.einsum("nhqk,nqhe->nkhe", probs_b, grad_att, preferred_element_type=jnp.float32)
    grad_score = (
        probs_f * (grad_prob - jnp.sum(probs_f * grad_prob, axis=-1, keepdims=True)) * factor
    )
    grad_score = grad_score.astype(jnp.bfloat16)
    grad_query = jnp.einsum(
        "nhqk,nkhe->nqhe", grad_score, keys_b, preferred_element_type=jnp.float32
    )
    grad_key = jnp.einsum(
        "nhqk,nqhe->nkhe", grad_score, queries, preferred_element_type=jnp.float32
    )
    grad_proj = (
        jnp.stack([grad_query, grad_key, grad_val], axis=2)
        .astype(jnp.bfloat16)
        .reshape(nblock * vrows, 3 * inner)
    )
    grad_wqkv = lax.dot_general(
        normed_b, grad_proj, (((0,), (0,)), ((), ())), preferred_element_type=jnp.float32
    )
    grad_norm = lax.dot_general(
        grad_proj, weights_qkv, (((1,), (1,)), ((), ())), preferred_element_type=jnp.float32
    )
    grad_norm = grad_norm.reshape(nblock, vrows, width) * ln_gain
    grad_ln = inv_std * (
        grad_norm
        - jnp.mean(grad_norm, axis=-1, keepdims=True)
        - normed * jnp.mean(grad_norm * normed, axis=-1, keepdims=True)
    )
    grad_rows = grad_out.reshape(nblock, vrows, width).astype(jnp.float32)
    grad_input = ((grad_rows + grad_ln) * row_mask[..., None]).astype(jnp.bfloat16)
    return (encoded, grad_input, grad_wqkv, grad_wout)


def shards(patches, out_cot, vis_count, w_qkv, w_out, ln_gain):
    full_qkv, full_out = (
        lax.all_gather(w_qkv, ("il", "xl"), axis=0, tiled=True),
        lax.all_gather(w_out, ("il", "xl"), axis=0, tiled=True),
    )
    tiles = patches[0]
    cotan = out_cot[0]
    counts = vis_count[0]
    encoded, grad_input, grad_qkv, grad_proj_out = block_pass(
        tiles, cotan, counts, full_qkv, full_out, ln_gain
    )
    grad_terms = jnp.concatenate([grad_qkv, grad_proj_out], axis=1)
    summed = lax.psum_scatter(grad_terms, ("il", "xl"), scatter_dimension=0, tiled=True)
    qkv_width = grad_qkv.shape[1]
    return (encoded[None], grad_input[None], summed[:, :qkv_width], summed[:, qkv_width:])


def solution(mesh):
    return jax.shard_map(
        shards,
        mesh=mesh,
        in_specs=(
            P("il", "xl", None, None),
            P("il", "xl", None, None),
            P("il", "xl"),
            P(("il", "xl"), None),
            P(("il", "xl"), None),
            P(),
        ),
        out_specs=(
            P("il", "xl", None, None),
            P("il", "xl", None, None),
            P(("il", "xl"), None),
            P(("il", "xl"), None),
        ),
        check_vma=False,
    )
```

profile of v0, /device:TPU:1, one launch (start us, length us, event | category | flops | bytes accessed | tf_op | source)
XLA Modules:
  0.0 488.1 jit_solution(13470428343686679741)
XLA Ops:
  7.9 79.1 %all-gather.1 = bf16[256,3,384]{2,1,0:T(4,128)(2,1)S(1)} all-gather(bf16[1,3,384]{2,1,0:T(4,128)(2,1)} %bitcast.129), channel_id=1, replica_groups=mesh['il'=16,'xl'=16] {'il','xl'}, dimensions={0}, use_global_device_ids=true | all-gather | bytes 592128 | tf_op jit(solution)/shard_map/all_gather | solution.py:90
  89.0 1.9 bitcast_multiply_fusion
  91.0 2.4 convolution_convert_fusion.1
  93.4 4.8 reshape.191
  98.2 4.3 copy.45
  105.9 1.9 fusion.18
  107.8 2.0 fusion.4
  109.8 10.4 %all-gather.4.cloned.1.call-done = bf16[256,3,1152]{2,1,0:T(4,128)(2,1)} async-done(((bf16[1,3,1152]{2,1,0:T(4,128)(2,1)}), bf16[256,3,1152]{2,1,0:T(4,128)(2,1)}) %all-gather.4.cloned.1.call-update) | async-done | bytes 1769488 | tf_op jit(solution)/shard_map/all_gather | solution.py:89
  120.1 5.2 %reshape.183 = bf16[768,1152]{1,0:T(8,128)(2,1)} reshape(bf16[256,3,1152]{2,1,0:T(4,128)(2,1)} %all-gather.4.cloned.1.call-done) | data formatting | bytes 3538944
  125.3 7.2 %convolution_convert_fusion = bf16[1536,1152]{1,0:T(8,128)(2,1)} fusion(bf16[1536,768]{1,0:T(8,128)(2,1)} %fusion.4, bf16[768,1152]{1,0:T(8,128)(2,1)} %reshape.183), kind=kOutput, calls=%fused_computation.2 | convolution fusion | flops 2719678464 | bytes 7667712 | tf_op jit(solution)/shard_map/dot_general | solution.py:21
  132.5 11.5 %reshape.190 = bf16[12,128,3,6,64]{4,3,2,1,0:T(8,128)(2,1)} reshape(bf16[1536,1152]{1,0:T(8,128)(2,1)} %convolution_convert_fusion) | data formatting | bytes 7077888 | tf_op jit(solution)/shard_map/reshape | solution.py:24
  144.0 6.5 %fusion.70 = (bf16[12,128,1,6,64]{4,3,2,1,0:T(8,128)(2,1)}, bf16[12,128,1,6,64]{4,3,2,1,0:T(8,128)(2,1)}, bf16[12,128,1,6,64]{4,3,2,1,0:T(8,128)(2,1)}) fusion(bf16[12,128,3,6,64]{4,3,2,1,0:T(8,128)(2,1)} %reshape.190), kind=kLoop, calls=%fused_computation.87 | loop fusion | bytes 7077888 | tf_op jit(solution)/shard_map/slice | solution.py:25
  150.5 4.2 copy.66
  154.7 4.2 copy.68
  159.0 4.2 copy.67
  163.2 2.5 fusion.51
  165.7 2.7 fusion.71
  168.5 1.8 convolution_convert_fusion.2
  170.9 2.8 convolution_bitcast_fusion
  173.7 3.0 fusion.55
  176.7 9.3 %fusion.44 = bf16[12,128,1,6,64]{1,4,3,0,2:T(8,128)(2,1)} fusion(f32[12,6,128,128]{2,3,1,0:T(8,128)} %fusion.55, bf16[12,128,1,6,64]{1,4,3,0,2:T(8,128)(2,1)} %copy.67, f32[12,6,128,128]{2,3,1,0:T(8,128)} %copy-done.14, f32[12,6,128]{2,1,0:T(8,128)S(1)} %get-tuple-element.17), kind=kOutput, calls=%fused_computation.53 | convolution fusion | flops 159261824 | bytes 11833344 | tf_op jit(solution)/shard_map/nhqk,nqhe->nkhe/dot_general | solution.py:62
  186.0 9.4 %fusion.41 = bf16[12,128,1,6,64]{1,4,3,0,2:T(8,128)(2,1)} fusion(f32[12,6,128,128]{2,3,1,0:T(8,128)} %fusion.55, bf16[12,128,1,6,64]{1,4,3,0,2:T(8,128)(2,1)} %copy.68, f32[12,6,128,128]{2,3,1,0:T(8,128)} %copy-done.14, f32[12,6,128]{2,1,0:T(8,128)S(1)} %get-tuple-element.17), kind=kOutput, calls=%fused_computation.52 | convolution fusion | flops 159261824 | bytes 11833344 | tf_op jit(solution)/shard_map/nhqk,nkhe->nqhe/dot_general | solution.py:59
  195.4 2.2 copy.53
  199.3 3.1 copy.52
  204.1 3.3 fusion.23
  207.4 2.8 pad_maximum_fusion
  211.5 5.1 %copy.50 = bf16[12,128,3,6,64]{1,4,3,2,0:T(8,128)(2,1)} copy(bf16[12,128,3,6,64]{1,4,3,0,2:T(8,128)(2,1)} %copy-done.1) | data formatting | bytes 7077888 | tf_op jit(solution)/shard_map/convert_element_type | solution.py:67
  216.5 5.2 %reshape.187 = bf16[768,1152,1]{1,0,2:T(8,128)(2,1)} reshape(bf16[256,3,1152]{2,1,0:T(4,128)(2,1)} %all-gather.4.cloned.1.call-done) | data formatting | bytes 3538944
  221.7 6.9 %multiply_reduce_fusion.1 = (f32[12,128]{1,0:T(8,128)S(1)}, f32[12,128]{1,0:T(8,128)S(1)}, f32[12,128,768]{2,1,0:T(8,128)S(1)}) fusion(f32[768]{0:T(1024)S(1)} %copy-done.13, f32[12,128]{1,0:T(8,128)S(1)} %get-tuple-element.9, f32[12,128]{1,0:T(8,128)S(1)} %get-tuple-element.12, bf16[1,12,128,768]{3,2,1,0:T(8,128)(2,1)S(1)} %copy-done, ...), kind=kOutput, calls=%fused_computation.34 | convolution fusion | flops 2726163456 | bytes 12413952 | tf_op jit(solution)/shard_map/dot_general | solution.py:73
  228.7 3.0 fusion.34
  231.7 3.4 fusion.39
  235.1 243.3 %all-reduce.3.cloned.1.call-done = f32[768,1536]{1,0:T(8,128)} async-done(((f32[768,1536]{1,0:T(8,128)}), f32[768,1536]{1,0:T(8,128)}) %all-reduce.3.cloned.1.call-update) | async-done | bytes 4718608
  (47 shorter events, 14.3 us)
Async XLA Ops:
  7.2 112.9 %all-gather.4.cloned.1.call-start = ((), (), s32[]{:S(2)}) async-start(), calls=%async_computation | async-start | bytes 2368512 | tf_op jit(solution)/shard_map/all_gather | solution.py:89
  7.9 470.4 %all-reduce.3.cloned.1.call-start = ((), (), s32[]{:S(2)}) async-start(), calls=%async_computation.1 | async-start | bytes 9437184
  88.2 2.7 copy-start.12
  93.4 9.1 %copy-start = (bf16[1,12,128,768]{3,2,1,0:T(8,128)(2,1)S(1)}, bf16[1,12,128,768]{3,2,1,0:T(8,128)(2,1)}, u32[]{:S(2)}) copy-start(bf16[1,12,128,768]{3,2,1,0:T(8,128)(2,1)} %param.6) | copy-start | bytes 7077892
  102.5 1.7 copy-start.2
  102.9 3.0 copy-start.13
  165.7 2.8 copy-start.5
  168.4 2.5 copy-start.14
  168.5 2.5 copy-start.4
  195.3 2.2 copy-start.8
  195.4 2.3 copy-start.9
  199.3 3.1 copy-start.1
  199.3 3.1 copy-start.7
  202.5 1.7 copy-start.6
  221.7 7.0 %copy-start.10 = (bf16[12,6,64,128]{3,2,1,0:T(8,128)(2,1)S(1)}, bf16[12,6,64,128]{3,2,1,0:T(8,128)(2,1)}, u32[]{:S(2)}) copy-start(bf16[12,6,64,128]{3,2,1,0:T(8,128)(2,1)} %convolution_convert_fusion.2) | copy-start | bytes 3538948
  221.7 7.0 %copy-start.11 = (bf16[768,384,1]{1,0,2:T(8,128)(2,1)S(1)}, bf16[768,384,1]{1,0,2:T(8,128)(2,1)}, u32[]{:S(2)}) copy-start(bf16[768,384,1]{1,0,2:T(8,128)(2,1)} %reshape.186) | copy-start | bytes 1769476
  228.7 3.0 copy-start.3
Sparse Core Ops, SparseCore 0:
  11.6 108.5 all-gather.3
  210.3 267.9 all-reduce.2
where the time goes:
time: 490 us; the launch traced here: 488 us
  waiting for transfers between devices  254 us (52%)
  blocking collectives  79.1 us (16%)
  local copies, waits for them, and re-layouts  67.3 us (14%)
  matrix products  52.9 us (11%)
  other arithmetic  20.1 us (4%)
  between operations  14.3 us (3%)
    unnamed x3, waiting for transfers between devices  244 us
    all_gather x1, blocking collectives, shards(): lax.all_gather(w_out, ('il', 'xl'), axis=0, tiled=True)  79.1 us
    unnamed x37, local copies, waits for them, and re-layouts  26.9 us
    reshape x1, local copies, waits for them, and re-layouts, block_pass(): project = project.reshape(nblock, vrows, 3, HEADS, HEAD_DIM)  11.5 us
    all_gather x1, waiting for transfers between devices, shards(): lax.all_gather(w_qkv, ('il', 'xl'), axis=0, tiled=True)  10.4 us
  transfers between devices with their start and end apart: 2, of which 2 were waited for; matrix products, arithmetic and copies ran while one was open for 10% of the time, Pallas kernels for 0%

commit v1 on v0

v1 whole, which is shorter than its diff:
```python
import jax
import jax.numpy as jnp
from jax import lax
from jax.experimental import pallas as pl
from jax.experimental.pallas import tpu as pltpu
from jax.sharding import PartitionSpec as P

HEAD_DIM = 64
HEADS = 6
D = 768
HD = 384
VMAX = 128
GROUP = 2
ROWS = GROUP * VMAX
BF16 = jnp.bfloat16
F32 = jnp.float32


def hop_x(v, k):
    return lax.ppermute(v, "il", [(i, (i // 4) * 4 + (i + k) % 4) for i in range(16)])


def hop_y(v, k):
    return lax.ppermute(v, "il", [(i, (i + 4 * k) % 16) for i in range(16)])


def hop_z(v, k):
    return lax.ppermute(v, "xl", [(i, (i + 2 * k) % 16) for i in range(16)])


def hop_core(v):
    return lax.ppermute(v, "xl", [(i, i ^ 1) for i in range(16)])


def coords():
    il = lax.axis_index("il")
    xl = lax.axis_index("xl")
    return il // 4, il % 4, xl // 2, xl % 2


def gather4(v, hop, direct):
    r1 = hop(v, -1)
    r3 = hop(v, 1)
    if direct:
        r2 = hop(v, 2)
    else:
        h = v.shape[0] // 2
        r2 = jnp.concatenate([hop(r1[:h], -1), hop(r3[h:], 1)], axis=0)
    return [v, r1, r2, r3]


def gather_weights(w):
    y, x, z, c = coords()
    n = w.shape[1] // 2
    mine = lax.dynamic_slice(w, (0, c * n), (3, n))
    other = lax.dynamic_slice(w, (0, (1 - c) * n), (3, n))
    block = jnp.concatenate([mine, hop_core(other), jnp.zeros((2, n), w.dtype)], axis=0)
    stack = jnp.concatenate([block] + [hop_z(block, -k) for k in range(1, 8)], axis=0)
    r = jnp.arange(48)[:, None]
    s = jnp.arange(64)[None, :]
    j = s % 8
    row = ((z + s // 8) % 8) * 6 + (c ^ (j // 3)) * 3 + j % 3
    order = ((row == r) & (j < 6)).astype(w.dtype)
    v = jnp.dot(order, stack, preferred_element_type=F32).astype(w.dtype)
    v = jnp.concatenate(gather4(v, hop_x, True), axis=0)
    mine = gather4(v, hop_y, False)
    return mine + [hop_core(u) for u in mine]


def scatter4(parts, hop, direct, dt):
    if direct:
        got = [hop(parts[k].astype(dt), k) for k in (1, 2, 3)]
        return parts[0] + got[0].astype(F32) + got[1].astype(F32) + got[2].astype(F32)
    h = parts[2].shape[0] // 2
    far = parts[2].astype(dt)
    a = hop(far[:h], 1)
    b = hop(far[h:], -1)
    s1 = jnp.concatenate([parts[1][:h] + a.astype(F32), parts[1][h:]], axis=0).astype(dt)
    s3 = jnp.concatenate([parts[3][:h], parts[3][h:] + b.astype(F32)], axis=0).astype(dt)
    return parts[0] + hop(s1, 1).astype(F32) + hop(s3, -1).astype(F32)


def scatter_grads(keep, send):
    y, x, z, c = coords()
    n = keep.shape[1]
    total = keep + hop_core(send).astype(F32)
    rows = total.shape[0] // 4
    v = scatter4(
        [lax.dynamic_slice(total, (((y + k) % 4) * rows, 0), (rows, n)) for k in range(4)], hop_y, False, BF16
    )
    rows = rows // 4
    v = scatter4([lax.dynamic_slice(v, (((x + k) % 4) * rows, 0), (rows, n)) for k in range(4)], hop_x, True, F32)
    v = v.reshape(8, 6, n)
    v = lax.dynamic_slice(jnp.concatenate([v, v], axis=0), (z, 0, 0), (8, 6, n))
    acc = v[0]
    for k in range(1, 8):
        acc = acc + hop_z(v[k], k)
    mine = lax.dynamic_slice(acc, (3 * c, 0), (3, n))
    got = hop_core(lax.dynamic_slice(acc, (3 * (1 - c), 0), (3, n)))
    return jnp.concatenate([jnp.where(c == 0, mine, got), jnp.where(c == 0, got, mine)], axis=1)


def mm(a, b):
    return jnp.dot(a, b, preferred_element_type=F32)


def mm_t(a, b):
    return lax.dot_general(a, b, (((1,), (1,)), ((), ())), preferred_element_type=F32)


def tmm(a, b):
    return lax.dot_general(a, b, (((0,), (0,)), ((), ())), preferred_element_type=F32)


def layer_kernel(*refs):
    at_ref, counts_ref = refs[:2]
    pieces = refs[2:10]
    x_ref, cot_ref, gain_ref = refs[10:13]
    enc_ref, gin_ref, keep_ref, send_ref = refs[13:17]
    w_ref, nb_ref, go_ref, att_ref, gp_ref = refs[17:22]
    step = pl.program_id(0)
    factor = HEAD_DIM**-0.5
    core = at_ref[2]

    @pl.when(step == 0)
    def _():
        y, x = at_ref[0], at_ref[1]
        for rel in range(2):
            half = core ^ rel
            for ky in range(4):
                for kx in range(4):
                    row = ((y + ky) & 3) * 192 + ((x + kx) & 3) * 48
                    w_ref[half, pl.ds(pl.multiple_of(row, 16), 48), :] = pieces[rel * 4 + ky][kx * 48 : kx * 48 + 48, :]

    xf = x_ref[...].reshape(ROWS, D).astype(F32)
    gain = gain_ref[...]
    centred = xf - jnp.mean(xf, axis=-1, keepdims=True)
    inv = lax.rsqrt(jnp.mean(centred * centred, axis=-1, keepdims=True) + 1e-6)
    normed = centred * inv
    nb = (normed * gain).astype(BF16)
    row_id = lax.broadcasted_iota(jnp.int32, (VMAX, D), 0)
    masks = [row_id < counts_ref[step * GROUP + b] for b in range(GROUP)]
    mask = jnp.concatenate(masks, axis=0)
    cot = cot_ref[...].reshape(ROWS, D)
    go_f = jnp.where(mask, cot.astype(F32), 0.0)
    go = go_f.astype(BF16)
    at = pl.ds(pl.multiple_of(step * ROWS, ROWS), ROWS)
    nb_ref[at, :] = nb
    go_ref[at, :] = go

    w0 = w_ref[0]
    wv = w_ref[1, :, :HD]
    wo = w_ref[1, :, HD:]
    qk = mm(nb, w0).astype(BF16)
    vv = mm(nb, wv).astype(BF16)
    ga = mm(go, wo).astype(BF16)
    key_id = lax.broadcasted_iota(jnp.int32, (VMAX, VMAX), 1)
    for b in range(GROUP):
        live = key_id < counts_ref[step * GROUP + b]
        rs = slice(b * VMAX, (b + 1) * VMAX)
        atts, gqs, gks, gvs = [], [], [], []
        for h in range(HEADS):
            lo = h * HEAD_DIM
            q = qk[rs, lo : lo + HEAD_DIM]
            k = qk[rs, HD + lo : HD + lo + HEAD_DIM]
            v = vv[rs, lo : lo + HEAD_DIM]
            g = ga[rs, lo : lo + HEAD_DIM]
            s = jnp.where(live, mm_t(q, k) * factor, -1e30)
            e = jnp.exp(s - jnp.max(s, axis=-1, keepdims=True))
            p = e / jnp.sum(e, axis=-1, keepdims=True)
            pb = p.astype(BF16)
            atts.append(mm(pb, v).astype(BF16))
            dp = mm_t(g, v)
            gvs.append(tmm(pb, g).astype(BF16))
            ds = (p * (dp - jnp.sum(p * dp, axis=-1, keepdims=True)) * factor).astype(BF16)
            gqs.append(mm(ds, k).astype(BF16))
            gks.append(tmm(ds, q).astype(BF16))
        at_b = pl.ds(pl.multiple_of(step * ROWS + b * VMAX, VMAX), VMAX)
        att_ref[at_b, :] = jnp.concatenate(atts, axis=1)
        gp_ref[at_b, :] = jnp.concatenate(gqs + gks + gvs, axis=1)

    mixed = mm_t(att_ref[at, :], wo)
    enc_ref[...] = jnp.where(mask, xf + mixed, 0.0).astype(BF16).reshape(GROUP, VMAX, D)
    gp = gp_ref[at, :]
    gn = (mm_t(gp[:, :D], w0) + mm_t(gp[:, D:], wv)) * gain
    gl = inv * (
        gn - jnp.mean(gn, axis=-1, keepdims=True) - normed * jnp.mean(gn * normed, axis=-1, keepdims=True)
    )
    gin_ref[...] = jnp.where(mask, go_f + gl, 0.0).astype(BF16).reshape(GROUP, VMAX, D)

    @pl.when(step == pl.num_programs(0) - 1)
    def _():
        for r in range(0, D, 256):
            rr = slice(r, r + 256)
            nbt = nb_ref[:, rr]
            got = go_ref[:, rr]
            for half, cols, val in (
                (0, slice(0, D), tmm(nbt, gp_ref[:, :D])),
                (1, slice(0, HD), tmm(nbt, gp_ref[:, D:])),
                (1, slice(HD, D), tmm(got, att_ref[...])),
            ):

                @pl.when(core == half)
                def _():
                    keep_ref[rr, cols] = val

                @pl.when(core != half)
                def _():
                    send_ref[rr, cols] = val.astype(send_ref.dtype)


def layer(at, counts, pieces, tiles, cotan, gain):
    nblock = tiles.shape[0]
    whole = lambda shape: pl.BlockSpec(shape, lambda i, *_: (0,) * len(shape), pipeline_mode=pl.Buffered(1))
    tile = pl.BlockSpec((GROUP, VMAX, D), lambda i, *_: (i, 0, 0))
    rows = nblock * VMAX
    return pl.pallas_call(
        layer_kernel,
        grid_spec=pltpu.PrefetchScalarGridSpec(
            num_scalar_prefetch=2,
            grid=(nblock // GROUP,),
            in_specs=[whole((192, D))] * 8 + [tile, tile, whole((1, D))],
            out_specs=[tile, tile, whole((D, D)), whole((D, D))],
            scratch_shapes=[
                pltpu.VMEM((2, D, D), BF16),
                pltpu.VMEM((rows, D), BF16),
                pltpu.VMEM((rows, D), BF16),
                pltpu.VMEM((rows, HD), BF16),
                pltpu.VMEM((rows, 3 * HD), BF16),
            ],
        ),
        out_shape=[
            jax.ShapeDtypeStruct(tiles.shape, BF16),
            jax.ShapeDtypeStruct(tiles.shape, BF16),
            jax.ShapeDtypeStruct((D, D), F32),
            jax.ShapeDtypeStruct((D, D), F32),
        ],
        compiler_params=pltpu.CompilerParams(
            dimension_semantics=("arbitrary",), vmem_limit_bytes=48 * 1024 * 1024
        ),
        cost_estimate=pl.CostEstimate(flops=14_000_000_000, bytes_accessed=20_000_000, transcendentals=1_200_000),
    )(at, counts, *pieces, tiles, cotan, gain)


def shards(patches, out_cot, vis_count, w_qkv, w_out, ln_gain):
    y, x, z, c = coords()
    pieces = gather_weights(jnp.concatenate([w_qkv, w_out], axis=1))
    at = jnp.stack([y, x, c]).astype(jnp.int32)
    enc, gin, keep, send = layer(at, vis_count[0], pieces, patches[0], out_cot[0], ln_gain[None])
    grads = scatter_grads(keep, send)
    n = w_qkv.shape[1]
    return enc[None], gin[None], grads[:, :n], grads[:, n:]


def solution(mesh):
    return jax.shard_map(
        shards,
        mesh=mesh,
        in_specs=(
            P("il", "xl", None, None),
            P("il", "xl", None, None),
            P("il", "xl"),
            P(("il", "xl"), None),
            P(("il", "xl"), None),
            P(),
        ),
        out_specs=(
            P("il", "xl", None, None),
            P("il", "xl", None, None),
            P(("il", "xl"), None),
            P(("il", "xl"), None),
        ),
        check_vma=False,
    )
```

time: 490 us -> 189 us (0.39)
  waiting for transfers between devices: 254 us -> 35 us
  blocking collectives: 79.1 us -> 0 us
  starting transfers between devices: 0.08 us -> 69.8 us
  Pallas kernels: 0 us -> 64.7 us
  local copies, waits for them, and re-layouts: 67.3 us -> 12.8 us
  matrix products: 52.9 us -> 0.15 us
  other arithmetic: 20.1 us -> 5.11 us
  between operations: 14.3 us -> 0.96 us
    unnamed x3 -> x0, waiting for transfers between devices: 244 us -> none
    all_gather x1 -> x0, blocking collectives: 79.1 us -> none  [shards(): lax.all_gather(w_out, ('il', 'xl'), axis=0, tiled=True)]
    ppermute x0 -> x35, starting transfers between devices: none -> 69.8 us  [the longest x14 26.3 us: hop_z(): return lax.ppermute(v, 'xl', [(i, (i + 2 * k) % 16) for i in range(16)])]
    pallas_call x0 -> x1, Pallas kernels: none -> 64.7 us  [layer(): pl.pallas_call(layer_kernel, grid_spec=pltpu.PrefetchScalarGridSpec(num_s...]
    dot_general x12 -> x1, matrix products: 52.9 us -> 0.15 us  [gather_weights(): v = jnp.dot(order, stack, preferred_element_type=F32).astype(w.dtype)]
    ppermute x0 -> x35, waiting for transfers between devices: none -> 35 us  [the longest x8 14.5 us: hop_y(): return lax.ppermute(v, 'il', [(i, (i + 4 * k) % 16) for i in range(16)])]
    reshape x3 -> x1, local copies, waits for them, and re-layouts: 20.6 us -> 0.02 us  [scatter_grads(): v = v.reshape(8, 6, n)]
    unnamed x37 -> x22, local copies, waits for them, and re-layouts: 26.9 us -> 9.48 us
  transfers between devices with their start and end apart: 2 -> 35, of which waited for: 2 -> 17; matrix products, arithmetic and copies ran while one was open for 10% -> 1% of each run, Pallas kernels for 0% -> 0%
where the time goes in v1:
time: 189 us; the launch traced here: 188 us
  starting transfers between devices  69.8 us (37%)
  Pallas kernels  64.7 us (34%)
  waiting for transfers between devices  35 us (19%)
  local copies, waits for them, and re-layouts  12.8 us (7%)
  other arithmetic  5.11 us (3%)
    pallas_call x1, Pallas kernels, layer(): pl.pallas_call(layer_kernel, grid_spec=pltpu.PrefetchScalarGridSpec(num_s...  64.7 us
    ppermute x14, starting transfers between devices, hop_z(): return lax.ppermute(v, 'xl', [(i, (i + 2 * k) % 16) for i in range(16)])  26.3 us
    ppermute x7, starting transfers between devices, hop_core(): return lax.ppermute(v, 'xl', [(i, i ^ 1) for i in range(16)])  23.9 us
    ppermute x8, waiting for transfers between devices, hop_y(): return lax.ppermute(v, 'il', [(i, (i + 4 * k) % 16) for i in range(16)])  14.5 us
    ppermute x8, starting transfers between devices, hop_y(): return lax.ppermute(v, 'il', [(i, (i + 4 * k) % 16) for i in range(16)])  11.6 us
    unnamed x22, local copies, waits for them, and re-layouts  9.48 us
    ppermute x6, waiting for transfers between devices, hop_x(): lax.ppermute(v, 'il', [(i, i // 4 * 4 + (i + k) % 4) for i in range(16)])  8.16 us
    ppermute x6, starting transfers between devices, hop_x(): lax.ppermute(v, 'il', [(i, i // 4 * 4 + (i + k) % 4) for i in range(16)])  8.01 us
  transfers between devices with their start and end apart: 35, of which 17 were waited for; matrix products, arithmetic and copies ran while one was open for 1% of the time, Pallas kernels for 0%

profile of v1, /device:TPU:1, one launch (start us, length us, event | category | flops | bytes accessed | tf_op | source)
XLA Modules:
  0.0 188.4 jit_solution(17229103417438694673)
XLA Ops:
  2.1 3.3 %collective-permute-start = (bf16[3,768]{1,0:T(4,128)(2,1)S(1)}, bf16[3,768]{1,0:T(4,128)(2,1)S(1)}, u32[]{:S(2)}, u32[]{:S(2)}) collective-permute-start(bf16[3,768]{1,0:T(4,128)(2,1)S(1)} %get-tuple-element.30), channel_id=1, source_target_pairs={{0,1},{1,0},{2,3},{3,2},{4,5},{5,4},{6,7},{7,6},{8,9},{9,8},{10,11... | collective-permute-start | bytes 13832 | tf_op jit(solution)/shard_map/ppermute | solution.py:32
  6.2 3.9 %collective-permute-start.1 = (bf16[8,768]{1,0:T(8,128)(2,1)S(1)}, bf16[8,768]{1,0:T(8,128)(2,1)S(1)}, u32[]{:S(2)}, u32[]{:S(2)}) collective-permute-start(bf16[8,768]{1,0:T(8,128)(2,1)S(1)} %pad_maximum_fusion.4), channel_id=1, source_target_pairs={{0,14},{1,15},{2,0},{3,1},{4,2},{5,3},{6,4},{7,5},{8,6},{9,7},{10,... | collective-permute-start | bytes 36872 | tf_op jit(solution)/shard_map/ppermute | solution.py:28
  11.9 4.4 %collective-permute-start.4 = (bf16[8,768]{1,0:T(8,128)(2,1)S(1)}, bf16[8,768]{1,0:T(8,128)(2,1)S(1)}, u32[]{:S(2)}, u32[]{:S(2)}) collective-permute-start(bf16[8,768]{1,0:T(8,128)(2,1)S(1)} %pad_maximum_fusion.4), channel_id=1, source_target_pairs={{0,8},{1,9},{2,10},{3,11},{4,12},{5,13},{6,14},{7,15},{8,0},{9,1},... | collective-permute-start | bytes 36872 | tf_op jit(solution)/shard_map/ppermute | solution.py:28
  16.3 2.2 %collective-permute-start.6 = (bf16[8,768]{1,0:T(8,128)(2,1)S(1)}, bf16[8,768]{1,0:T(8,128)(2,1)S(1)}, u32[]{:S(2)}, u32[]{:S(2)}) collective-permute-start(bf16[8,768]{1,0:T(8,128)(2,1)S(1)} %pad_maximum_fusion.4), channel_id=1, source_target_pairs={{0,4},{1,5},{2,6},{3,7},{4,8},{5,9},{6,10},{7,11},{8,12},{9,13},{1... | collective-permute-start | bytes 36872 | tf_op jit(solution)/shard_map/ppermute | solution.py:28
  18.4 1.4 collective-permute-start.7
  19.8 2.0 %collective-permute-done.5 = bf16[8,768]{1,0:T(8,128)(2,1)S(1)} collective-permute-done((bf16[8,768]{1,0:T(8,128)(2,1)S(1)}, bf16[8,768]{1,0:T(8,128)(2,1)S(1)}, u32[]{:S(2)}, u32[]{:S(2)}) %collective-permute-start.5) | collective-permute-done | bytes 12320 | tf_op jit(solution)/shard_map/ppermute | solution.py:28
  22.4 1.3 collective-permute-start.10
  23.7 2.5 %collective-permute-start.9 = (bf16[48,768]{1,0:T(8,128)(2,1)S(1)}, bf16[48,768]{1,0:T(8,128)(2,1)S(1)}, u32[]{:S(2)}, u32[]{:S(2)}) collective-permute-start(bf16[48,768]{1,0:T(8,128)(2,1)S(1)} %convolution_convert_fusion), channel_id=1, source_target_pairs={{0,32},{16,48},{32,0},{48,16},{64,96},{80,112},{96,64},{112,80},{1... | collective-permute-start | bytes 221192 | tf_op jit(solution)/shard_map/ppermute | solution.py:20
  27.3 1.4 collective-permute-done.9
  29.3 2.8 %collective-permute-start.11 = (bf16[192,768]{1,0:T(8,128)(2,1)S(1)}, bf16[192,768]{1,0:T(8,128)(2,1)S(1)}, u32[]{:S(2)}, u32[]{:S(2)}) collective-permute-start(bf16[192,768]{1,0:T(8,128)(2,1)S(1)} %pad_maximum_fusion.refs_2_), channel_id=1, source_target_pairs={{0,192},{16,208},{32,224},{48,240},{64,0},{80,16},{96,32},{112,48}... | collective-permute-start | bytes 884744 | tf_op jit(solution)/shard_map/ppermute | solution.py:24
  32.2 3.7 %collective-permute-done.11.refs_3_ = bf16[192,768]{1,0:T(8,128)(2,1)S(1)} collective-permute-done((bf16[192,768]{1,0:T(8,128)(2,1)S(1)}, bf16[192,768]{1,0:T(8,128)(2,1)S(1)}, u32[]{:S(2)}, u32[]{:S(2)}) %collective-permute-start.11) | collective-permute-done | bytes 294944 | tf_op jit(solution)/shard_map/ppermute | solution.py:24
  35.8 3.2 %collective-permute-start.12 = (bf16[96,768]{1,0:T(8,128)(2,1)S(1)}, bf16[96,768]{1,0:T(8,128)(2,1)S(1)}, u32[]{:S(2)}, u32[]{:S(2)}) collective-permute-start(bf16[96,768]{1,0:T(8,128)(2,1)S(1)} %slice.74), channel_id=1, source_target_pairs={{0,192},{16,208},{32,224},{48,240},{64,0},{80,16},{96,32},{112,48}... | collective-permute-start | bytes 442376 | tf_op jit(solution)/shard_map/ppermute | solution.py:24
  39.1 7.5 %collective-permute-start.15 = (bf16[192,768]{1,0:T(8,128)(2,1)S(1)}, bf16[192,768]{1,0:T(8,128)(2,1)S(1)}, u32[]{:S(2)}, u32[]{:S(2)}) collective-permute-start(bf16[192,768]{1,0:T(8,128)(2,1)S(1)} %pad_maximum_fusion.refs_2_), channel_id=1, source_target_pairs={{0,1},{1,0},{2,3},{3,2},{4,5},{5,4},{6,7},{7,6},{8,9},{9,8},{10,11... | collective-permute-start | bytes 884744 | tf_op jit(solution)/shard_map/ppermute | solution.py:32
  47.2 5.8 %collective-permute-start.17 = (bf16[192,768]{1,0:T(8,128)(2,1)S(1)}, bf16[192,768]{1,0:T(8,128)(2,1)S(1)}, u32[]{:S(2)}, u32[]{:S(2)}) collective-permute-start(bf16[192,768]{1,0:T(8,128)(2,1)S(1)} %constant_dynamic-update-slice_fusion.2.refs_4_), channel_id=1, source_target_pairs={{0,1},{1,0},{2,3},{3,2},{4,5},{5,4},{6,7},{7,6},{8,9},{9,8},{10,11... | collective-permute-start | bytes 884744 | tf_op jit(solution)/shard_map/ppermute | solution.py:32
  61.2 64.7 %shard_map.93 = (bf16[12,128,768]{2,1,0:T(8,128)(2,1)}, bf16[12,128,768]{2,1,0:T(8,128)(2,1)}, f32[768,768]{1,0:T(8,128)S(1)}, f32[768,768]{1,0:T(8,128)}) custom-call(s32[3]{0:T(128)S(1)} %pad_add_fusion.refs_0_, s32[12]{0:T(128)S(1)} %bitcast.39, bf16[192,768]{1,0:T(8,128)(2,1)S(1)} %pad_maximum_fusion.refs_2_, ...), custom_call_target="tpu_custom_call" | custom-call | flops 14000000000 | bytes 20000000 | tf_op jit(solution)/shard_map/pallas_call | solution.py:217
  126.0 4.8 %collective-permute-done.19 = f32[768,768]{1,0:T(8,128)} collective-permute-done((f32[768,768]{1,0:T(8,128)}, f32[768,768]{1,0:T(8,128)}, u32[]{:S(2)}, u32[]{:S(2)}) %collective-permute-start.19) | collective-permute-done | bytes 2359328 | tf_op jit(solution)/shard_map/ppermute | solution.py:32
  130.8 2.0 %add.224 = f32[768,768]{1,0:T(8,128)S(1)} add(f32[768,768]{1,0:T(8,128)S(1)} %get-tuple-element.10, f32[768,768]{1,0:T(8,128)} %collective-permute-done.19) | non-fusion elementwise | flops 589824 | bytes 7077888 | tf_op jit(solution)/shard_map/add | solution.py:86
  132.8 1.4 copy-done.9
  134.6 2.7 %collective-permute-start.22 = (bf16[96,768]{1,0:T(8,128)(2,1)S(1)}, bf16[96,768]{1,0:T(8,128)(2,1)S(1)}, u32[]{:S(2)}, u32[]{:S(2)}) collective-permute-start(bf16[96,768]{1,0:T(8,128)(2,1)S(1)} %get-tuple-element.20), channel_id=1, source_target_pairs={{0,192},{16,208},{32,224},{48,240},{64,0},{80,16},{96,32},{112,48}... | collective-permute-start | bytes 442376 | tf_op jit(solution)/shard_map/ppermute | solution.py:24
  138.3 2.8 %collective-permute-done.20 = bf16[96,768]{1,0:T(8,128)(2,1)S(1)} collective-permute-done((bf16[96,768]{1,0:T(8,128)(2,1)S(1)}, bf16[96,768]{1,0:T(8,128)(2,1)S(1)}, u32[]{:S(2)}, u32[]{:S(2)}) %collective-permute-start.20) | collective-permute-done | bytes 147488 | tf_op jit(solution)/shard_map/ppermute | solution.py:24
  142.2 2.4 %collective-permute-start.23 = (bf16[192,768]{1,0:T(8,128)(2,1)S(1)}, bf16[192,768]{1,0:T(8,128)(2,1)S(1)}, u32[]{:S(2)}, u32[]{:S(2)}) collective-permute-start(bf16[192,768]{1,0:T(8,128)(2,1)S(1)} %pad_maximum_fusion.2), channel_id=1, source_target_pairs={{0,192},{16,208},{32,224},{48,240},{64,0},{80,16},{96,32},{112,48}... | collective-permute-start | bytes 884744 | tf_op jit(solution)/shard_map/ppermute | solution.py:24
  144.9 5.0 %collective-permute-done.23 = bf16[192,768]{1,0:T(8,128)(2,1)S(1)} collective-permute-done((bf16[192,768]{1,0:T(8,128)(2,1)S(1)}, bf16[192,768]{1,0:T(8,128)(2,1)S(1)}, u32[]{:S(2)}, u32[]{:S(2)}) %collective-permute-start.23) | collective-permute-done | bytes 294944 | tf_op jit(solution)/shard_map/ppermute | solution.py:24
  149.9 3.1 %collective-permute-done.21 = bf16[192,768]{1,0:T(8,128)(2,1)S(1)} collective-permute-done((bf16[192,768]{1,0:T(8,128)(2,1)S(1)}, bf16[192,768]{1,0:T(8,128)(2,1)S(1)}, u32[]{:S(2)}, u32[]{:S(2)}) %collective-permute-start.21) | collective-permute-done | bytes 294944 | tf_op jit(solution)/shard_map/ppermute | solution.py:24
  154.1 2.4 %collective-permute-start.26 = (f32[48,768]{1,0:T(8,128)S(1)}, f32[48,768]{1,0:T(8,128)S(1)}, u32[]{:S(2)}, u32[]{:S(2)}) collective-permute-start(f32[48,768]{1,0:T(8,128)S(1)} %get-tuple-element.17), channel_id=1, source_target_pairs={{0,48},{16,0},{32,16},{48,32},{64,112},{80,64},{96,80},{112,96},{1... | collective-permute-start | bytes 442376 | tf_op jit(solution)/shard_map/ppermute | solution.py:20
  157.2 3.0 %collective-permute-done.26 = f32[48,768]{1,0:T(8,128)S(1)} collective-permute-done((f32[48,768]{1,0:T(8,128)S(1)}, f32[48,768]{1,0:T(8,128)S(1)}, u32[]{:S(2)}, u32[]{:S(2)}) %collective-permute-start.26) | collective-permute-done | bytes 147488 | tf_op jit(solution)/shard_map/ppermute | solution.py:20
  160.2 1.9 %collective-permute-done.25 = f32[48,768]{1,0:T(8,128)S(1)} collective-permute-done((f32[48,768]{1,0:T(8,128)S(1)}, f32[48,768]{1,0:T(8,128)S(1)}, u32[]{:S(2)}, u32[]{:S(2)}) %collective-permute-start.25) | collective-permute-done | bytes 147488 | tf_op jit(solution)/shard_map/ppermute | solution.py:20
  163.6 3.4 %collective-permute-start.32 = (f32[6,768]{1,0:T(8,128)S(1)}, f32[6,768]{1,0:T(8,128)S(1)}, u32[]{:S(2)}, u32[]{:S(2)}) collective-permute-start(f32[6,768]{1,0:T(8,128)S(1)} %get-tuple-element.22), channel_id=1, source_target_pairs={{0,12},{1,13},{2,14},{3,15},{4,0},{5,1},{6,2},{7,3},{8,4},{9,5},{1... | collective-permute-start | bytes 55304 | tf_op jit(solution)/shard_map/ppermute | solution.py:28
  167.0 1.7 collective-permute-start.31
  168.8 2.0 %collective-permute-start.30 = (f32[6,768]{1,0:T(8,128)S(1)}, f32[6,768]{1,0:T(8,128)S(1)}, u32[]{:S(2)}, u32[]{:S(2)}) collective-permute-start(f32[6,768]{1,0:T(8,128)S(1)} %get-tuple-element.24), channel_id=1, source_target_pairs={{0,8},{1,9},{2,10},{3,11},{4,12},{5,13},{6,14},{7,15},{8,0},{9,1},... | collective-permute-start | bytes 55304 | tf_op jit(solution)/shard_map/ppermute | solution.py:28
  172.0 3.6 %collective-permute-start.28 = (f32[6,768]{1,0:T(8,128)S(1)}, f32[6,768]{1,0:T(8,128)S(1)}, u32[]{:S(2)}, u32[]{:S(2)}) collective-permute-start(f32[6,768]{1,0:T(8,128)S(1)} %get-tuple-element.26), channel_id=1, source_target_pairs={{0,4},{1,5},{2,6},{3,7},{4,8},{5,9},{6,10},{7,11},{8,12},{9,13},{1... | collective-permute-start | bytes 55304 | tf_op jit(solution)/shard_map/ppermute | solution.py:28
  177.1 2.6 %collective-permute-done.27 = f32[6,768]{1,0:T(8,128)S(1)} collective-permute-done((f32[6,768]{1,0:T(8,128)S(1)}, f32[6,768]{1,0:T(8,128)S(1)}, u32[]{:S(2)}, u32[]{:S(2)}) %collective-permute-start.27) | collective-permute-done | bytes 18464 | tf_op jit(solution)/shard_map/ppermute | solution.py:28
  179.8 6.6 %collective-permute-start.34 = (f32[3,768]{1,0:T(4,128)S(1)}, f32[3,768]{1,0:T(4,128)S(1)}, u32[]{:S(2)}, u32[]{:S(2)}) collective-permute-start(f32[3,768]{1,0:T(4,128)S(1)} %constant_dynamic-slice_fusion), channel_id=1, source_target_pairs={{0,1},{1,0},{2,3},{3,2},{4,5},{5,4},{6,7},{7,6},{8,9},{9,8},{10,11... | collective-permute-start | bytes 27656 | tf_op jit(solution)/shard_map/ppermute | solution.py:32
  (93 shorter events, 26.1 us)
Async XLA Ops:
  6.2 10.0 %collective-permute-start.1 = (bf16[8,768]{1,0:T(8,128)(2,1)S(1)}, bf16[8,768]{1,0:T(8,128)(2,1)S(1)}, u32[]{:S(2)}, u32[]{:S(2)}) collective-permute-start(bf16[8,768]{1,0:T(8,128)(2,1)S(1)} %pad_maximum_fusion.4), channel_id=1, source_target_pairs={{0,14},{1,15},{2,0},{3,1},{4,2},{5,3},{6,4},{7,5},{8,6},{9,7},{10,... | collective-permute-start | bytes 36872 | tf_op jit(solution)/shard_map/ppermute | solution.py:28
  10.2 8.3 %collective-permute-start.2 = (bf16[8,768]{1,0:T(8,128)(2,1)S(1)}, bf16[8,768]{1,0:T(8,128)(2,1)S(1)}, u32[]{:S(2)}, u32[]{:S(2)}) collective-permute-start(bf16[8,768]{1,0:T(8,128)(2,1)S(1)} %pad_maximum_fusion.4), channel_id=1, source_target_pairs={{0,12},{1,13},{2,14},{3,15},{4,0},{5,1},{6,2},{7,3},{8,4},{9,5},{1... | collective-permute-start | bytes 36872 | tf_op jit(solution)/shard_map/ppermute | solution.py:28
  11.3 8.5 %collective-permute-start.3 = (bf16[8,768]{1,0:T(8,128)(2,1)S(1)}, bf16[8,768]{1,0:T(8,128)(2,1)S(1)}, u32[]{:S(2)}, u32[]{:S(2)}) collective-permute-start(bf16[8,768]{1,0:T(8,128)(2,1)S(1)} %pad_maximum_fusion.4), channel_id=1, source_target_pairs={{0,10},{1,11},{2,12},{3,13},{4,14},{5,15},{6,0},{7,1},{8,2},{9,3},... | collective-permute-start | bytes 36872 | tf_op jit(solution)/shard_map/ppermute | solution.py:28
  11.9 8.0 %collective-permute-start.4 = (bf16[8,768]{1,0:T(8,128)(2,1)S(1)}, bf16[8,768]{1,0:T(8,128)(2,1)S(1)}, u32[]{:S(2)}, u32[]{:S(2)}) collective-permute-start(bf16[8,768]{1,0:T(8,128)(2,1)S(1)} %pad_maximum_fusion.4), channel_id=1, source_target_pairs={{0,8},{1,9},{2,10},{3,11},{4,12},{5,13},{6,14},{7,15},{8,0},{9,1},... | collective-permute-start | bytes 36872 | tf_op jit(solution)/shard_map/ppermute | solution.py:28
  16.3 5.6 %collective-permute-start.5 = (bf16[8,768]{1,0:T(8,128)(2,1)S(1)}, bf16[8,768]{1,0:T(8,128)(2,1)S(1)}, u32[]{:S(2)}, u32[]{:S(2)}) collective-permute-start(bf16[8,768]{1,0:T(8,128)(2,1)S(1)} %pad_maximum_fusion.4), channel_id=1, source_target_pairs={{0,6},{1,7},{2,8},{3,9},{4,10},{5,11},{6,12},{7,13},{8,14},{9,15},... | collective-permute-start | bytes 36872 | tf_op jit(solution)/shard_map/ppermute | solution.py:28
  16.3 5.6 %collective-permute-start.6 = (bf16[8,768]{1,0:T(8,128)(2,1)S(1)}, bf16[8,768]{1,0:T(8,128)(2,1)S(1)}, u32[]{:S(2)}, u32[]{:S(2)}) collective-permute-start(bf16[8,768]{1,0:T(8,128)(2,1)S(1)} %pad_maximum_fusion.4), channel_id=1, source_target_pairs={{0,4},{1,5},{2,6},{3,7},{4,8},{5,9},{6,10},{7,11},{8,12},{9,13},{1... | collective-permute-start | bytes 36872 | tf_op jit(solution)/shard_map/ppermute | solution.py:28
  22.4 4.9 %collective-permute-start.10 = (bf16[48,768]{1,0:T(8,128)(2,1)S(1)}, bf16[48,768]{1,0:T(8,128)(2,1)S(1)}, u32[]{:S(2)}, u32[]{:S(2)}) collective-permute-start(bf16[48,768]{1,0:T(8,128)(2,1)S(1)} %convolution_convert_fusion), channel_id=1, source_target_pairs={{0,16},{16,32},{32,48},{48,0},{64,80},{80,96},{96,112},{112,64},{1... | collective-permute-start | bytes 221192 | tf_op jit(solution)/shard_map/ppermute | solution.py:20
  23.7 5.0 %collective-permute-start.9 = (bf16[48,768]{1,0:T(8,128)(2,1)S(1)}, bf16[48,768]{1,0:T(8,128)(2,1)S(1)}, u32[]{:S(2)}, u32[]{:S(2)}) collective-permute-start(bf16[48,768]{1,0:T(8,128)(2,1)S(1)} %convolution_convert_fusion), channel_id=1, source_target_pairs={{0,32},{16,48},{32,0},{48,16},{64,96},{80,112},{96,64},{112,80},{1... | collective-permute-start | bytes 221192 | tf_op jit(solution)/shard_map/ppermute | solution.py:20
  29.3 6.5 %collective-permute-start.11 = (bf16[192,768]{1,0:T(8,128)(2,1)S(1)}, bf16[192,768]{1,0:T(8,128)(2,1)S(1)}, u32[]{:S(2)}, u32[]{:S(2)}) collective-permute-start(bf16[192,768]{1,0:T(8,128)(2,1)S(1)} %pad_maximum_fusion.refs_2_), channel_id=1, source_target_pairs={{0,192},{16,208},{32,224},{48,240},{64,0},{80,16},{96,32},{112,48}... | collective-permute-start | bytes 884744 | tf_op jit(solution)/shard_map/ppermute | solution.py:24
  32.1 6.9 %collective-permute-start.13 = (bf16[192,768]{1,0:T(8,128)(2,1)S(1)}, bf16[192,768]{1,0:T(8,128)(2,1)S(1)}, u32[]{:S(2)}, u32[]{:S(2)}) collective-permute-start(bf16[192,768]{1,0:T(8,128)(2,1)S(1)} %pad_maximum_fusion.refs_2_), channel_id=1, source_target_pairs={{0,64},{16,80},{32,96},{48,112},{64,128},{80,144},{96,160},{112,17... | collective-permute-start | bytes 884744 | tf_op jit(solution)/shard_map/ppermute | solution.py:24
  35.8 11.3 %collective-permute-start.12 = (bf16[96,768]{1,0:T(8,128)(2,1)S(1)}, bf16[96,768]{1,0:T(8,128)(2,1)S(1)}, u32[]{:S(2)}, u32[]{:S(2)}) collective-permute-start(bf16[96,768]{1,0:T(8,128)(2,1)S(1)} %slice.74), channel_id=1, source_target_pairs={{0,192},{16,208},{32,224},{48,240},{64,0},{80,16},{96,32},{112,48}... | collective-permute-start | bytes 442376 | tf_op jit(solution)/shard_map/ppermute | solution.py:24
  39.0 8.1 %collective-permute-start.14 = (bf16[96,768]{1,0:T(8,128)(2,1)S(1)}, bf16[96,768]{1,0:T(8,128)(2,1)S(1)}, u32[]{:S(2)}, u32[]{:S(2)}) collective-permute-start(bf16[96,768]{1,0:T(8,128)(2,1)S(1)} %slice.75), channel_id=1, source_target_pairs={{0,64},{16,80},{32,96},{48,112},{64,128},{80,144},{96,160},{112,17... | collective-permute-start | bytes 442376 | tf_op jit(solution)/shard_map/ppermute | solution.py:24
  39.1 14.6 %collective-permute-start.15 = (bf16[192,768]{1,0:T(8,128)(2,1)S(1)}, bf16[192,768]{1,0:T(8,128)(2,1)S(1)}, u32[]{:S(2)}, u32[]{:S(2)}) collective-permute-start(bf16[192,768]{1,0:T(8,128)(2,1)S(1)} %pad_maximum_fusion.refs_2_), channel_id=1, source_target_pairs={{0,1},{1,0},{2,3},{3,2},{4,5},{5,4},{6,7},{7,6},{8,9},{9,8},{10,11... | collective-permute-start | bytes 884744 | tf_op jit(solution)/shard_map/ppermute | solution.py:32
  46.6 7.8 %collective-permute-start.16 = (bf16[192,768]{1,0:T(8,128)(2,1)S(1)}, bf16[192,768]{1,0:T(8,128)(2,1)S(1)}, u32[]{:S(2)}, u32[]{:S(2)}) collective-permute-start(bf16[192,768]{1,0:T(8,128)(2,1)S(1)} %collective-permute-done.11.refs_3_), channel_id=1, source_target_pairs={{0,1},{1,0},{2,3},{3,2},{4,5},{5,4},{6,7},{7,6},{8,9},{9,8},{10,11... | collective-permute-start | bytes 884744 | tf_op jit(solution)/shard_map/ppermute | solution.py:32
  46.8 8.5 %collective-permute-start.18 = (bf16[192,768]{1,0:T(8,128)(2,1)S(1)}, bf16[192,768]{1,0:T(8,128)(2,1)S(1)}, u32[]{:S(2)}, u32[]{:S(2)}) collective-permute-start(bf16[192,768]{1,0:T(8,128)(2,1)S(1)} %collective-permute-done.13.refs_5_), channel_id=1, source_target_pairs={{0,1},{1,0},{2,3},{3,2},{4,5},{5,4},{6,7},{7,6},{8,9},{9,8},{10,11... | collective-permute-start | bytes 884744 | tf_op jit(solution)/shard_map/ppermute | solution.py:32
  47.2 8.7 %collective-permute-start.17 = (bf16[192,768]{1,0:T(8,128)(2,1)S(1)}, bf16[192,768]{1,0:T(8,128)(2,1)S(1)}, u32[]{:S(2)}, u32[]{:S(2)}) collective-permute-start(bf16[192,768]{1,0:T(8,128)(2,1)S(1)} %constant_dynamic-update-slice_fusion.2.refs_4_), channel_id=1, source_target_pairs={{0,1},{1,0},{2,3},{3,2},{4,5},{5,4},{6,7},{7,6},{8,9},{9,8},{10,11... | collective-permute-start | bytes 884744 | tf_op jit(solution)/shard_map/ppermute | solution.py:32
  125.9 5.0 %collective-permute-start.19 = (f32[768,768]{1,0:T(8,128)}, f32[768,768]{1,0:T(8,128)}, u32[]{:S(2)}, u32[]{:S(2)}) collective-permute-start(f32[768,768]{1,0:T(8,128)} %get-tuple-element.11), channel_id=1, source_target_pairs={{0,1},{1,0},{2,3},{3,2},{4,5},{5,4},{6,7},{7,6},{8,9},{9,8},{10,11... | collective-permute-start | bytes 7077896 | tf_op jit(solution)/shard_map/ppermute | solution.py:32
  134.3 6.8 %collective-permute-start.20 = (bf16[96,768]{1,0:T(8,128)(2,1)S(1)}, bf16[96,768]{1,0:T(8,128)(2,1)S(1)}, u32[]{:S(2)}, u32[]{:S(2)}) collective-permute-start(bf16[96,768]{1,0:T(8,128)(2,1)S(1)} %get-tuple-element.19), channel_id=1, source_target_pairs={{0,64},{16,80},{32,96},{48,112},{64,128},{80,144},{96,160},{112,17... | collective-permute-start | bytes 442376 | tf_op jit(solution)/shard_map/ppermute | solution.py:24
  134.6 6.5 %collective-permute-start.22 = (bf16[96,768]{1,0:T(8,128)(2,1)S(1)}, bf16[96,768]{1,0:T(8,128)(2,1)S(1)}, u32[]{:S(2)}, u32[]{:S(2)}) collective-permute-start(bf16[96,768]{1,0:T(8,128)(2,1)S(1)} %get-tuple-element.20), channel_id=1, source_target_pairs={{0,192},{16,208},{32,224},{48,240},{64,0},{80,16},{96,32},{112,48}... | collective-permute-start | bytes 442376 | tf_op jit(solution)/shard_map/ppermute | solution.py:24
  142.2 7.6 %collective-permute-start.23 = (bf16[192,768]{1,0:T(8,128)(2,1)S(1)}, bf16[192,768]{1,0:T(8,128)(2,1)S(1)}, u32[]{:S(2)}, u32[]{:S(2)}) collective-permute-start(bf16[192,768]{1,0:T(8,128)(2,1)S(1)} %pad_maximum_fusion.2), channel_id=1, source_target_pairs={{0,192},{16,208},{32,224},{48,240},{64,0},{80,16},{96,32},{112,48}... | collective-permute-start | bytes 884744 | tf_op jit(solution)/shard_map/ppermute | solution.py:24
  144.7 8.2 %collective-permute-start.21 = (bf16[192,768]{1,0:T(8,128)(2,1)S(1)}, bf16[192,768]{1,0:T(8,128)(2,1)S(1)}, u32[]{:S(2)}, u32[]{:S(2)}) collective-permute-start(bf16[192,768]{1,0:T(8,128)(2,1)S(1)} %pad_maximum_fusion.1), channel_id=1, source_target_pairs={{0,64},{16,80},{32,96},{48,112},{64,128},{80,144},{96,160},{112,17... | collective-permute-start | bytes 884744 | tf_op jit(solution)/shard_map/ppermute | solution.py:24
  154.1 6.1 %collective-permute-start.26 = (f32[48,768]{1,0:T(8,128)S(1)}, f32[48,768]{1,0:T(8,128)S(1)}, u32[]{:S(2)}, u32[]{:S(2)}) collective-permute-start(f32[48,768]{1,0:T(8,128)S(1)} %get-tuple-element.17), channel_id=1, source_target_pairs={{0,48},{16,0},{32,16},{48,32},{64,112},{80,64},{96,80},{112,96},{1... | collective-permute-start | bytes 442376 | tf_op jit(solution)/shard_map/ppermute | solution.py:20
  156.6 5.6 %collective-permute-start.25 = (f32[48,768]{1,0:T(8,128)S(1)}, f32[48,768]{1,0:T(8,128)S(1)}, u32[]{:S(2)}, u32[]{:S(2)}) collective-permute-start(f32[48,768]{1,0:T(8,128)S(1)} %get-tuple-element.18), channel_id=1, source_target_pairs={{0,32},{16,48},{32,0},{48,16},{64,96},{80,112},{96,64},{112,80},{1... | collective-permute-start | bytes 442376 | tf_op jit(solution)/shard_map/ppermute | solution.py:20
  156.6 6.8 %collective-permute-start.24 = (f32[48,768]{1,0:T(8,128)S(1)}, f32[48,768]{1,0:T(8,128)S(1)}, u32[]{:S(2)}, u32[]{:S(2)}) collective-permute-start(f32[48,768]{1,0:T(8,128)S(1)} %get-tuple-element.16), channel_id=1, source_target_pairs={{0,16},{16,32},{32,48},{48,0},{64,80},{80,96},{96,112},{112,64},{1... | collective-permute-start | bytes 442376 | tf_op jit(solution)/shard_map/ppermute | solution.py:20
  163.5 8.5 %collective-permute-start.33 = (f32[6,768]{1,0:T(8,128)S(1)}, f32[6,768]{1,0:T(8,128)S(1)}, u32[]{:S(2)}, u32[]{:S(2)}) collective-permute-start(f32[6,768]{1,0:T(8,128)S(1)} %get-tuple-element.27), channel_id=1, source_target_pairs={{0,14},{1,15},{2,0},{3,1},{4,2},{5,3},{6,4},{7,5},{8,6},{9,7},{10,... | collective-permute-start | bytes 55304 | tf_op jit(solution)/shard_map/ppermute | solution.py:28
  163.6 11.9 %collective-permute-start.32 = (f32[6,768]{1,0:T(8,128)S(1)}, f32[6,768]{1,0:T(8,128)S(1)}, u32[]{:S(2)}, u32[]{:S(2)}) collective-permute-start(f32[6,768]{1,0:T(8,128)S(1)} %get-tuple-element.22), channel_id=1, source_target_pairs={{0,12},{1,13},{2,14},{3,15},{4,0},{5,1},{6,2},{7,3},{8,4},{9,5},{1... | collective-permute-start | bytes 55304 | tf_op jit(solution)/shard_map/ppermute | solution.py:28
  167.0 9.2 %collective-permute-start.31 = (f32[6,768]{1,0:T(8,128)S(1)}, f32[6,768]{1,0:T(8,128)S(1)}, u32[]{:S(2)}, u32[]{:S(2)}) collective-permute-start(f32[6,768]{1,0:T(8,128)S(1)} %get-tuple-element.23), channel_id=1, source_target_pairs={{0,10},{1,11},{2,12},{3,13},{4,14},{5,15},{6,0},{7,1},{8,2},{9,3},... | collective-permute-start | bytes 55304 | tf_op jit(solution)/shard_map/ppermute | solution.py:28
  168.8 7.5 %collective-permute-start.30 = (f32[6,768]{1,0:T(8,128)S(1)}, f32[6,768]{1,0:T(8,128)S(1)}, u32[]{:S(2)}, u32[]{:S(2)}) collective-permute-start(f32[6,768]{1,0:T(8,128)S(1)} %get-tuple-element.24), channel_id=1, source_target_pairs={{0,8},{1,9},{2,10},{3,11},{4,12},{5,13},{6,14},{7,15},{8,0},{9,1},... | collective-permute-start | bytes 55304 | tf_op jit(solution)/shard_map/ppermute | solution.py:28
  170.8 5.7 %collective-permute-start.29 = (f32[6,768]{1,0:T(8,128)S(1)}, f32[6,768]{1,0:T(8,128)S(1)}, u32[]{:S(2)}, u32[]{:S(2)}) collective-permute-start(f32[6,768]{1,0:T(8,128)S(1)} %get-tuple-element.25), channel_id=1, source_target_pairs={{0,6},{1,7},{2,8},{3,9},{4,10},{5,11},{6,12},{7,13},{8,14},{9,15},... | collective-permute-start | bytes 55304 | tf_op jit(solution)/shard_map/ppermute | solution.py:28
  172.0 5.2 %collective-permute-start.28 = (f32[6,768]{1,0:T(8,128)S(1)}, f32[6,768]{1,0:T(8,128)S(1)}, u32[]{:S(2)}, u32[]{:S(2)}) collective-permute-start(f32[6,768]{1,0:T(8,128)S(1)} %get-tuple-element.26), channel_id=1, source_target_pairs={{0,4},{1,5},{2,6},{3,7},{4,8},{5,9},{6,10},{7,11},{8,12},{9,13},{1... | collective-permute-start | bytes 55304 | tf_op jit(solution)/shard_map/ppermute | solution.py:28
  175.5 4.2 %collective-permute-start.27 = (f32[6,768]{1,0:T(8,128)S(1)}, f32[6,768]{1,0:T(8,128)S(1)}, u32[]{:S(2)}, u32[]{:S(2)}) collective-permute-start(f32[6,768]{1,0:T(8,128)S(1)} %get-tuple-element.21), channel_id=1, source_target_pairs={{0,2},{1,3},{2,4},{3,5},{4,6},{5,7},{6,8},{7,9},{8,10},{9,11},{10,... | collective-permute-start | bytes 55304 | tf_op jit(solution)/shard_map/ppermute | solution.py:28
  179.8 7.4 %collective-permute-start.34 = (f32[3,768]{1,0:T(4,128)S(1)}, f32[3,768]{1,0:T(4,128)S(1)}, u32[]{:S(2)}, u32[]{:S(2)}) collective-permute-start(f32[3,768]{1,0:T(4,128)S(1)} %constant_dynamic-slice_fusion), channel_id=1, source_target_pairs={{0,1},{1,0},{2,3},{3,2},{4,5},{5,4},{6,7},{7,6},{8,9},{9,8},{10,11... | collective-permute-start | bytes 27656 | tf_op jit(solution)/shard_map/ppermute | solution.py:32
  (13 other events, 19.9 us)

commit v2 on v1

--- a/solution.py
+++ b/solution.py
@@ -10,7 +10,7 @@
 D = 768
 HD = 384
 VMAX = 128
-GROUP = 2
+GROUP = 4
 ROWS = GROUP * VMAX
 BF16 = jnp.bfloat16
 F32 = jnp.float32
@@ -55,15 +55,18 @@
     mine = lax.dynamic_slice(w, (0, c * n), (3, n))
     other = lax.dynamic_slice(w, (0, (1 - c) * n), (3, n))
     block = jnp.concatenate([mine, hop_core(other), jnp.zeros((2, n), w.dtype)], axis=0)
-    stack = jnp.concatenate([block] + [hop_z(block, -k) for k in range(1, 8)], axis=0)
+    block = jnp.concatenate([block, lax.ppermute(block, "xl", [(i, i ^ 2) for i in range(16)])], axis=0)
+    stack = jnp.concatenate([block, hop_z(block, 2), hop_z(block, -2), hop_z(block, 4)], axis=0)
     r = jnp.arange(48)[:, None]
     s = jnp.arange(64)[None, :]
+    slot = s // 16
     j = s % 8
-    row = ((z + s // 8) % 8) * 6 + (c ^ (j // 3)) * 3 + j % 3
+    origin = (z + jnp.where(slot == 3, 4, jnp.where(slot == 2, 2, jnp.where(slot == 1, 6, 0)))) % 8
+    row = (origin ^ ((s // 8) % 2)) * 6 + (c ^ (j // 3)) * 3 + j % 3
     order = ((row == r) & (j < 6)).astype(w.dtype)
     v = jnp.dot(order, stack, preferred_element_type=F32).astype(w.dtype)
     v = jnp.concatenate(gather4(v, hop_x, True), axis=0)
-    mine = gather4(v, hop_y, False)
+    mine = gather4(v, hop_y, True)
     return mine + [hop_core(u) for u in mine]
 
 
@@ -90,14 +93,9 @@
     )
     rows = rows // 4
     v = scatter4([lax.dynamic_slice(v, (((x + k) % 4) * rows, 0), (rows, n)) for k in range(4)], hop_x, True, F32)
-    v = v.reshape(8, 6, n)
-    v = lax.dynamic_slice(jnp.concatenate([v, v], axis=0), (z, 0, 0), (8, 6, n))
-    acc = v[0]
-    for k in range(1, 8):
-        acc = acc + hop_z(v[k], k)
-    mine = lax.dynamic_slice(acc, (3 * c, 0), (3, n))
-    got = hop_core(lax.dynamic_slice(acc, (3 * (1 - c), 0), (3, n)))
-    return jnp.concatenate([jnp.where(c == 0, mine, got), jnp.where(c == 0, got, mine)], axis=1)
+    got = lax.all_to_all(v.reshape(16, 3, n), "xl", split_axis=0, concat_axis=0, tiled=True)
+    acc = jnp.sum(got.reshape(8, 2, 3, n), axis=0)
+    return jnp.concatenate([acc[0], acc[1]], axis=1)
 
 
 def mm(a, b):
@@ -117,7 +115,7 @@
     pieces = refs[2:10]
     x_ref, cot_ref, gain_ref = refs[10:13]
     enc_ref, gin_ref, keep_ref, send_ref = refs[13:17]
-    w_ref, nb_ref, go_ref, att_ref, gp_ref = refs[17:22]
+    w_ref, nb_ref, go_ref, att_ref, gp_ref, sems = refs[17:23]
     step = pl.program_id(0)
     factor = HEAD_DIM**-0.5
     core = at_ref[2]
@@ -125,12 +123,23 @@
     @pl.when(step == 0)
     def _():
         y, x = at_ref[0], at_ref[1]
+        copies = []
         for rel in range(2):
             half = core ^ rel
             for ky in range(4):
                 for kx in range(4):
-                    row = ((y + ky) & 3) * 192 + ((x + kx) & 3) * 48
-                    w_ref[half, pl.ds(pl.multiple_of(row, 16), 48), :] = pieces[rel * 4 + ky][kx * 48 : kx * 48 + 48, :]
+                    row = pl.multiple_of(((y + ky) & 3) * 192 + ((x + kx) & 3) * 48, 16)
+                    copies.append(
+                        pltpu.make_async_copy(
+                            pieces[rel * 4 + ky].at[pl.ds(kx * 48, 48), :],
+                            w_ref.at[half, pl.ds(row, 48), :],
+                            sems.at[len(copies)],
+                        )
+                    )
+        for copy in copies:
+            copy.start()
+        for copy in copies:
+            copy.wait()
 
     xf = x_ref[...].reshape(ROWS, D).astype(F32)
     gain = gain_ref[...]
@@ -154,30 +163,33 @@
     qk = mm(nb, w0).astype(BF16)
     vv = mm(nb, wv).astype(BF16)
     ga = mm(go, wo).astype(BF16)
-    key_id = lax.broadcasted_iota(jnp.int32, (VMAX, VMAX), 1)
+    key_id = lax.broadcasted_iota(jnp.int32, (VMAX, 2 * VMAX), 0)
+    lane = lax.broadcasted_iota(jnp.int32, (1, 2 * HEAD_DIM), 1)
+    first = jnp.where(lane < HEAD_DIM, 1.0, 0.0)
+    m0, m1 = first.astype(BF16), (1.0 - first).astype(BF16)
+    f0, f1 = (first * factor).astype(BF16), ((1.0 - first) * factor).astype(BF16)
+    pair = lambda a, u, w: jnp.concatenate([a * u, a * w], axis=0)
     for b in range(GROUP):
         live = key_id < counts_ref[step * GROUP + b]
         rs = slice(b * VMAX, (b + 1) * VMAX)
-        atts, gqs, gks, gvs = [], [], [], []
-        for h in range(HEADS):
-            lo = h * HEAD_DIM
-            q = qk[rs, lo : lo + HEAD_DIM]
-            k = qk[rs, HD + lo : HD + lo + HEAD_DIM]
-            v = vv[rs, lo : lo + HEAD_DIM]
-            g = ga[rs, lo : lo + HEAD_DIM]
-            s = jnp.where(live, mm_t(q, k) * factor, -1e30)
-            e = jnp.exp(s - jnp.max(s, axis=-1, keepdims=True))
-            p = e / jnp.sum(e, axis=-1, keepdims=True)
+        at_b = pl.ds(pl.multiple_of(step * ROWS + b * VMAX, VMAX), VMAX)
+        for lo in range(0, HD, 2 * HEAD_DIM):
+            hi = lo + 2 * HEAD_DIM
+            k = qk[rs, HD + lo : HD + hi]
+            v = vv[rs, lo:hi]
+            q2 = pair(qk[rs, lo:hi], f0, f1)
+            g2 = pair(ga[rs, lo:hi], m0, m1)
+            s = jnp.where(live, mm_t(k, q2), -1e30)
+            e = jnp.exp(s - jnp.max(s, axis=0, keepdims=True))
+            p = e * (1.0 / jnp.sum(e, axis=0, keepdims=True))
             pb = p.astype(BF16)
-            atts.append(mm(pb, v).astype(BF16))
-            dp = mm_t(g, v)
-            gvs.append(tmm(pb, g).astype(BF16))
-            ds = (p * (dp - jnp.sum(p * dp, axis=-1, keepdims=True)) * factor).astype(BF16)
-            gqs.append(mm(ds, k).astype(BF16))
-            gks.append(tmm(ds, q).astype(BF16))
-        at_b = pl.ds(pl.multiple_of(step * ROWS + b * VMAX, VMAX), VMAX)
-        att_ref[at_b, :] = jnp.concatenate(atts, axis=1)
-        gp_ref[at_b, :] = jnp.concatenate(gqs + gks + gvs, axis=1)
+            dp = mm_t(v, g2)
+            ds = (p * (dp - jnp.sum(p * dp, axis=0, keepdims=True))).astype(BF16)
+            stack = lambda a: jnp.concatenate([a[:, :VMAX], a[:, VMAX:]], axis=0)
+            att_ref[at_b, lo:hi] = tmm(stack(pb), pair(v, m0, m1)).astype(BF16)
+            gp_ref[at_b, lo:hi] = tmm(stack(ds), pair(k, f0, f1)).astype(BF16)
+            gp_ref[at_b, HD + lo : HD + hi] = mm(ds, q2).astype(BF16)
+            gp_ref[at_b, D + lo : D + hi] = mm(pb, g2).astype(BF16)
 
     mixed = mm_t(att_ref[at, :], wo)
     enc_ref[...] = jnp.where(mask, xf + mixed, 0.0).astype(BF16).reshape(GROUP, VMAX, D)
@@ -192,11 +204,11 @@
     def _():
         for r in range(0, D, 256):
             rr = slice(r, r + 256)
-            nbt = nb_ref[:, rr]
+            gw = tmm(nb_ref[:, rr], gp_ref[...])
             got = go_ref[:, rr]
             for half, cols, val in (
-                (0, slice(0, D), tmm(nbt, gp_ref[:, :D])),
-                (1, slice(0, HD), tmm(nbt, gp_ref[:, D:])),
+                (0, slice(0, D), gw[:, :D]),
+                (1, slice(0, HD), gw[:, D:]),
                 (1, slice(HD, D), tmm(got, att_ref[...])),
             ):
 
@@ -219,7 +231,7 @@
         grid_spec=pltpu.PrefetchScalarGridSpec(
             num_scalar_prefetch=2,
             grid=(nblock // GROUP,),
-            in_specs=[whole((192, D))] * 8 + [tile, tile, whole((1, D))],
+            in_specs=[pl.BlockSpec(memory_space=pl.ANY)] * 8 + [tile, tile, whole((1, D))],
             out_specs=[tile, tile, whole((D, D)), whole((D, D))],
             scratch_shapes=[
                 pltpu.VMEM((2, D, D), BF16),
@@ -227,6 +239,7 @@
                 pltpu.VMEM((rows, D), BF16),
                 pltpu.VMEM((rows, HD), BF16),
                 pltpu.VMEM((rows, 3 * HD), BF16),
+                pltpu.SemaphoreType.DMA((32,)),
             ],
         ),
         out_shape=[

time: 189 us -> 151 us (0.80)
  Pallas kernels: 64.7 us -> 36 us
  starting transfers between devices: 69.8 us -> 44.9 us
  blocking collectives: 0 us -> 19.9 us
  waiting for transfers between devices: 35 us -> 30.4 us
    pallas_call x1, Pallas kernels: 64.7 us -> 36 us  [layer(): pl.pallas_call(layer_kernel, grid_spec=pltpu.PrefetchScalarGridSpec(num_s...]
    all_to_all x0 -> x1, blocking collectives: none -> 19.9 us  [scatter_grads(): lax.all_to_all(v.reshape(16, 3, n), 'xl', split_axis=0, concat_axis=0, ti...]
    ppermute x14 -> x3, starting transfers between devices: 26.3 us -> 8.83 us  [hop_z(): return lax.ppermute(v, 'xl', [(i, (i + 2 * k) % 16) for i in range(16)])]
    ppermute x7 -> x6, starting transfers between devices: 23.9 us -> 18.9 us  [hop_core(): return lax.ppermute(v, 'xl', [(i, i ^ 1) for i in range(16)])]
    ppermute x14 -> x3, waiting for transfers between devices: 5.79 us -> 2.19 us  [hop_z(): return lax.ppermute(v, 'xl', [(i, (i + 2 * k) % 16) for i in range(16)])]
    ppermute x8 -> x7, waiting for transfers between devices: 14.5 us -> 11.8 us  [hop_y(): return lax.ppermute(v, 'il', [(i, (i + 4 * k) % 16) for i in range(16)])]
    ppermute x0 -> x1, waiting for transfers between devices: none -> 2.5 us  [gather_weights(): lax.ppermute(block, 'xl', [(i, i ^ 2) for i in range(16)])]
    ppermute x8 -> x7, starting transfers between devices: 11.6 us -> 9.11 us  [hop_y(): return lax.ppermute(v, 'il', [(i, (i + 4 * k) % 16) for i in range(16)])]
  transfers between devices with their start and end apart: 35 -> 23, of which waited for: 17 -> 14; matrix products, arithmetic and copies ran while one was open for 1% -> 1% of each run, Pallas kernels for 0% -> 0%
where the time goes in v2:
time: 151 us; the launch traced here: 150 us
  starting transfers between devices  44.9 us (30%)
  Pallas kernels  36 us (24%)
  waiting for transfers between devices  30.4 us (20%)
  blocking collectives  19.9 us (13%)
  local copies, waits for them, and re-layouts  12.7 us (8%)
  other arithmetic  5.09 us (3%)
    pallas_call x1, Pallas kernels, layer(): pl.pallas_call(layer_kernel, grid_spec=pltpu.PrefetchScalarGridSpec(num_s...  36 us
    all_to_all x1, blocking collectives, scatter_grads(): lax.all_to_all(v.reshape(16, 3, n), 'xl', split_axis=0, concat_axis=0, ti...  19.9 us
    ppermute x6, starting transfers between devices, hop_core(): return lax.ppermute(v, 'xl', [(i, i ^ 1) for i in range(16)])  18.9 us
    ppermute x7, waiting for transfers between devices, hop_y(): return lax.ppermute(v, 'il', [(i, (i + 4 * k) % 16) for i in range(16)])  11.8 us
    unnamed x21, local copies, waits for them, and re-layouts  9.45 us
    ppermute x7, starting transfers between devices, hop_y(): return lax.ppermute(v, 'il', [(i, (i + 4 * k) % 16) for i in range(16)])  9.11 us
    ppermute x3, starting transfers between devices, hop_z(): return lax.ppermute(v, 'xl', [(i, (i + 2 * k) % 16) for i in range(16)])  8.83 us
    ppermute x6, waiting for transfers between devices, hop_x(): lax.ppermute(v, 'il', [(i, i // 4 * 4 + (i + k) % 4) for i in range(16)])  8.26 us
  transfers between devices with their start and end apart: 23, of which 14 were waited for; matrix products, arithmetic and copies ran while one was open for 1% of the time, Pallas kernels for 0%

profile of v2, /device:TPU:1, one launch (start us, length us, event | category | flops | bytes accessed | tf_op | source)
XLA Modules:
  0.0 150.1 jit_solution(991242290849294218)
XLA Ops:
  2.1 3.3 %collective-permute-start = (bf16[3,768]{1,0:T(4,128)(2,1)S(1)}, bf16[3,768]{1,0:T(4,128)(2,1)S(1)}, u32[]{:S(2)}, u32[]{:S(2)}) collective-permute-start(bf16[3,768]{1,0:T(4,128)(2,1)S(1)} %get-tuple-element.23), channel_id=1, source_target_pairs={{0,1},{1,0},{2,3},{3,2},{4,5},{5,4},{6,7},{7,6},{8,9},{9,8},{10,11... | collective-permute-start | bytes 13832 | tf_op jit(solution)/shard_map/ppermute | solution.py:32
  6.4 2.5 %collective-permute-done.1 = bf16[8,768]{1,0:T(8,128)(2,1)S(1)} collective-permute-done((bf16[8,768]{1,0:T(8,128)(2,1)S(1)}, bf16[8,768]{1,0:T(8,128)(2,1)S(1)}, u32[]{:S(2)}, u32[]{:S(2)}) %collective-permute-start.1) | collective-permute-done | bytes 12320 | tf_op jit(solution)/shard_map/ppermute | solution.py:58
  8.9 1.5 %collective-permute-start.2 = (bf16[16,768]{1,0:T(8,128)(2,1)S(1)}, bf16[16,768]{1,0:T(8,128)(2,1)S(1)}, u32[]{:S(2)}, u32[]{:S(2)}) collective-permute-start(bf16[16,768]{1,0:T(8,128)(2,1)S(1)} %pad_maximum_fusion.3), channel_id=1, source_target_pairs={{0,4},{1,5},{2,6},{3,7},{4,8},{5,9},{6,10},{7,11},{8,12},{9,13},{1... | collective-permute-start | bytes 73736 | tf_op jit(solution)/shard_map/ppermute | solution.py:28
  10.4 2.9 %collective-permute-start.3 = (bf16[16,768]{1,0:T(8,128)(2,1)S(1)}, bf16[16,768]{1,0:T(8,128)(2,1)S(1)}, u32[]{:S(2)}, u32[]{:S(2)}) collective-permute-start(bf16[16,768]{1,0:T(8,128)(2,1)S(1)} %pad_maximum_fusion.3), channel_id=1, source_target_pairs={{0,12},{1,13},{2,14},{3,15},{4,0},{5,1},{6,2},{7,3},{8,4},{9,5},{1... | collective-permute-start | bytes 73736 | tf_op jit(solution)/shard_map/ppermute | solution.py:28
  13.3 4.4 %collective-permute-start.4 = (bf16[16,768]{1,0:T(8,128)(2,1)S(1)}, bf16[16,768]{1,0:T(8,128)(2,1)S(1)}, u32[]{:S(2)}, u32[]{:S(2)}) collective-permute-start(bf16[16,768]{1,0:T(8,128)(2,1)S(1)} %pad_maximum_fusion.3), channel_id=1, source_target_pairs={{0,8},{1,9},{2,10},{3,11},{4,12},{5,13},{6,14},{7,15},{8,0},{9,1},... | collective-permute-start | bytes 73736 | tf_op jit(solution)/shard_map/ppermute | solution.py:28
  17.8 2.2 %collective-permute-done.4 = bf16[16,768]{1,0:T(8,128)(2,1)S(1)} collective-permute-done((bf16[16,768]{1,0:T(8,128)(2,1)S(1)}, bf16[16,768]{1,0:T(8,128)(2,1)S(1)}, u32[]{:S(2)}, u32[]{:S(2)}) %collective-permute-start.4) | collective-permute-done | bytes 24608 | tf_op jit(solution)/shard_map/ppermute | solution.py:28
  20.1 1.3 collective-permute-start.7
  21.4 2.5 %collective-permute-start.6 = (bf16[48,768]{1,0:T(8,128)(2,1)S(1)}, bf16[48,768]{1,0:T(8,128)(2,1)S(1)}, u32[]{:S(2)}, u32[]{:S(2)}) collective-permute-start(bf16[48,768]{1,0:T(8,128)(2,1)S(1)} %convolution_convert_fusion), channel_id=1, source_target_pairs={{0,32},{16,48},{32,0},{48,16},{64,96},{80,112},{96,64},{112,80},{1... | collective-permute-start | bytes 221192 | tf_op jit(solution)/shard_map/ppermute | solution.py:20
  23.9 1.2 collective-permute-start.5
  25.0 1.4 collective-permute-done.6
  27.1 2.8 %collective-permute-start.8 = (bf16[192,768]{1,0:T(8,128)(2,1)S(1)}, bf16[192,768]{1,0:T(8,128)(2,1)S(1)}, u32[]{:S(2)}, u32[]{:S(2)}) collective-permute-start(bf16[192,768]{1,0:T(8,128)(2,1)S(1)} %pad_maximum_fusion.refs_2_), channel_id=1, source_target_pairs={{0,192},{16,208},{32,224},{48,240},{64,0},{80,16},{96,32},{112,48}... | collective-permute-start | bytes 884744 | tf_op jit(solution)/shard_map/ppermute | solution.py:24
  30.9 5.5 %collective-permute-start.11 = (bf16[192,768]{1,0:T(8,128)(2,1)S(1)}, bf16[192,768]{1,0:T(8,128)(2,1)S(1)}, u32[]{:S(2)}, u32[]{:S(2)}) collective-permute-start(bf16[192,768]{1,0:T(8,128)(2,1)S(1)} %pad_maximum_fusion.refs_2_), channel_id=1, source_target_pairs={{0,1},{1,0},{2,3},{3,2},{4,5},{5,4},{6,7},{7,6},{8,9},{9,8},{10,11... | collective-permute-start | bytes 884744 | tf_op jit(solution)/shard_map/ppermute | solution.py:32
  37.3 6.2 %collective-permute-start.12 = (bf16[192,768]{1,0:T(8,128)(2,1)S(1)}, bf16[192,768]{1,0:T(8,128)(2,1)S(1)}, u32[]{:S(2)}, u32[]{:S(2)}) collective-permute-start(bf16[192,768]{1,0:T(8,128)(2,1)S(1)} %collective-permute-done.8.refs_3_), channel_id=1, source_target_pairs={{0,1},{1,0},{2,3},{3,2},{4,5},{5,4},{6,7},{7,6},{8,9},{9,8},{10,11... | collective-permute-start | bytes 884744 | tf_op jit(solution)/shard_map/ppermute | solution.py:32
  44.3 2.9 %collective-permute-start.14 = (bf16[192,768]{1,0:T(8,128)(2,1)S(1)}, bf16[192,768]{1,0:T(8,128)(2,1)S(1)}, u32[]{:S(2)}, u32[]{:S(2)}) collective-permute-start(bf16[192,768]{1,0:T(8,128)(2,1)S(1)} %collective-permute-done.10.refs_5_), channel_id=1, source_target_pairs={{0,1},{1,0},{2,3},{3,2},{4,5},{5,4},{6,7},{7,6},{8,9},{9,8},{10,11... | collective-permute-start | bytes 884744 | tf_op jit(solution)/shard_map/ppermute | solution.py:32
  50.8 1.0 copy-done.1
  55.3 36.0 %shard_map.93 = (bf16[12,128,768]{2,1,0:T(8,128)(2,1)}, bf16[12,128,768]{2,1,0:T(8,128)(2,1)}, f32[768,768]{1,0:T(8,128)S(1)}, f32[768,768]{1,0:T(8,128)}) custom-call(s32[3]{0:T(128)S(1)} %pad_add_fusion.refs_0_, s32[12]{0:T(128)S(1)} %bitcast.14, bf16[192,768]{1,0:T(8,128)(2,1)S(1)} %pad_maximum_fusion.refs_2_, ...), custom_call_target="tpu_custom_call" | custom-call | flops 14000000000 | bytes 20000000 | tf_op jit(solution)/shard_map/pallas_call | solution.py:229
  91.6 4.8 %collective-permute-done.15 = f32[768,768]{1,0:T(8,128)} collective-permute-done((f32[768,768]{1,0:T(8,128)}, f32[768,768]{1,0:T(8,128)}, u32[]{:S(2)}, u32[]{:S(2)}) %collective-permute-start.15) | collective-permute-done | bytes 2359328 | tf_op jit(solution)/shard_map/ppermute | solution.py:32
  96.4 2.0 %add.209 = f32[768,768]{1,0:T(8,128)S(1)} add(f32[768,768]{1,0:T(8,128)S(1)} %get-tuple-element.10, f32[768,768]{1,0:T(8,128)} %collective-permute-done.15) | non-fusion elementwise | flops 589824 | bytes 7077888 | tf_op jit(solution)/shard_map/add | solution.py:89
  98.4 1.4 copy-done.9
  99.9 2.7 %collective-permute-start.18 = (bf16[96,768]{1,0:T(8,128)(2,1)S(1)}, bf16[96,768]{1,0:T(8,128)(2,1)S(1)}, u32[]{:S(2)}, u32[]{:S(2)}) collective-permute-start(bf16[96,768]{1,0:T(8,128)(2,1)S(1)} %get-tuple-element.20), channel_id=1, source_target_pairs={{0,192},{16,208},{32,224},{48,240},{64,0},{80,16},{96,32},{112,48}... | collective-permute-start | bytes 442376 | tf_op jit(solution)/shard_map/ppermute | solution.py:24
  102.6 1.1 dynamic-slice_convert_fusion.2
  103.7 2.8 %collective-permute-done.16 = bf16[96,768]{1,0:T(8,128)(2,1)S(1)} collective-permute-done((bf16[96,768]{1,0:T(8,128)(2,1)S(1)}, bf16[96,768]{1,0:T(8,128)(2,1)S(1)}, u32[]{:S(2)}, u32[]{:S(2)}) %collective-permute-start.16) | collective-permute-done | bytes 147488 | tf_op jit(solution)/shard_map/ppermute | solution.py:24
  106.5 1.1 fusion.1
  107.6 2.4 %collective-permute-start.19 = (bf16[192,768]{1,0:T(8,128)(2,1)S(1)}, bf16[192,768]{1,0:T(8,128)(2,1)S(1)}, u32[]{:S(2)}, u32[]{:S(2)}) collective-permute-start(bf16[192,768]{1,0:T(8,128)(2,1)S(1)} %pad_maximum_fusion.2), channel_id=1, source_target_pairs={{0,192},{16,208},{32,224},{48,240},{64,0},{80,16},{96,32},{112,48}... | collective-permute-start | bytes 884744 | tf_op jit(solution)/shard_map/ppermute | solution.py:24
  110.2 5.0 %collective-permute-done.19 = bf16[192,768]{1,0:T(8,128)(2,1)S(1)} collective-permute-done((bf16[192,768]{1,0:T(8,128)(2,1)S(1)}, bf16[192,768]{1,0:T(8,128)(2,1)S(1)}, u32[]{:S(2)}, u32[]{:S(2)}) %collective-permute-start.19) | collective-permute-done | bytes 294944 | tf_op jit(solution)/shard_map/ppermute | solution.py:24
  115.2 3.1 %collective-permute-done.17 = bf16[192,768]{1,0:T(8,128)(2,1)S(1)} collective-permute-done((bf16[192,768]{1,0:T(8,128)(2,1)S(1)}, bf16[192,768]{1,0:T(8,128)(2,1)S(1)}, u32[]{:S(2)}, u32[]{:S(2)}) %collective-permute-start.17) | collective-permute-done | bytes 294944 | tf_op jit(solution)/shard_map/ppermute | solution.py:24
  118.3 1.1 convert_add_fusion
  119.5 2.4 %collective-permute-start.22 = (f32[48,768]{1,0:T(8,128)S(1)}, f32[48,768]{1,0:T(8,128)S(1)}, u32[]{:S(2)}, u32[]{:S(2)}) collective-permute-start(f32[48,768]{1,0:T(8,128)S(1)} %get-tuple-element.17), channel_id=1, source_target_pairs={{0,48},{16,0},{32,16},{48,32},{64,112},{80,64},{96,80},{112,96},{1... | collective-permute-start | bytes 442376 | tf_op jit(solution)/shard_map/ppermute | solution.py:20
  122.6 3.0 %collective-permute-done.22 = f32[48,768]{1,0:T(8,128)S(1)} collective-permute-done((f32[48,768]{1,0:T(8,128)S(1)}, f32[48,768]{1,0:T(8,128)S(1)}, u32[]{:S(2)}, u32[]{:S(2)}) %collective-permute-start.22) | collective-permute-done | bytes 147488 | tf_op jit(solution)/shard_map/ppermute | solution.py:20
  125.6 1.9 %collective-permute-done.21 = f32[48,768]{1,0:T(8,128)S(1)} collective-permute-done((f32[48,768]{1,0:T(8,128)S(1)}, f32[48,768]{1,0:T(8,128)S(1)}, u32[]{:S(2)}, u32[]{:S(2)}) %collective-permute-start.21) | collective-permute-done | bytes 147488 | tf_op jit(solution)/shard_map/ppermute | solution.py:20
  127.5 1.3 collective-permute-done.20
  128.9 19.9 %all_to_all.5 = f32[16,3,768]{2,1,0:T(4,128)S(1)} all-to-all(f32[16,3,768]{2,1,0:T(4,128)S(1)} %reshape.185), channel_id=1, replica_groups=mesh['il'=16,'xl'=16] {'xl'}, dimensions={0} | all-to-all | bytes 294912 | tf_op jit(solution)/shard_map/all_to_all | solution.py:96
  (64 shorter events, 15.8 us)
Async XLA Ops:
  2.1 4.2 %collective-permute-start = (bf16[3,768]{1,0:T(4,128)(2,1)S(1)}, bf16[3,768]{1,0:T(4,128)(2,1)S(1)}, u32[]{:S(2)}, u32[]{:S(2)}) collective-permute-start(bf16[3,768]{1,0:T(4,128)(2,1)S(1)} %get-tuple-element.23), channel_id=1, source_target_pairs={{0,1},{1,0},{2,3},{3,2},{4,5},{5,4},{6,7},{7,6},{8,9},{9,8},{10,11... | collective-permute-start | bytes 13832 | tf_op jit(solution)/shard_map/ppermute | solution.py:32
  6.2 2.6 %collective-permute-start.1 = (bf16[8,768]{1,0:T(8,128)(2,1)S(1)}, bf16[8,768]{1,0:T(8,128)(2,1)S(1)}, u32[]{:S(2)}, u32[]{:S(2)}) collective-permute-start(bf16[8,768]{1,0:T(8,128)(2,1)S(1)} %pad_maximum_fusion.5), channel_id=1, source_target_pairs={{0,2},{1,3},{2,0},{3,1},{4,6},{5,7},{6,4},{7,5},{8,10},{9,11},{10,... | collective-permute-start | bytes 36872 | tf_op jit(solution)/shard_map/ppermute | solution.py:58
  8.9 8.8 %collective-permute-start.2 = (bf16[16,768]{1,0:T(8,128)(2,1)S(1)}, bf16[16,768]{1,0:T(8,128)(2,1)S(1)}, u32[]{:S(2)}, u32[]{:S(2)}) collective-permute-start(bf16[16,768]{1,0:T(8,128)(2,1)S(1)} %pad_maximum_fusion.3), channel_id=1, source_target_pairs={{0,4},{1,5},{2,6},{3,7},{4,8},{5,9},{6,10},{7,11},{8,12},{9,13},{1... | collective-permute-start | bytes 73736 | tf_op jit(solution)/shard_map/ppermute | solution.py:28
  10.4 7.4 %collective-permute-start.3 = (bf16[16,768]{1,0:T(8,128)(2,1)S(1)}, bf16[16,768]{1,0:T(8,128)(2,1)S(1)}, u32[]{:S(2)}, u32[]{:S(2)}) collective-permute-start(bf16[16,768]{1,0:T(8,128)(2,1)S(1)} %pad_maximum_fusion.3), channel_id=1, source_target_pairs={{0,12},{1,13},{2,14},{3,15},{4,0},{5,1},{6,2},{7,3},{8,4},{9,5},{1... | collective-permute-start | bytes 73736 | tf_op jit(solution)/shard_map/ppermute | solution.py:28
  13.3 6.6 %collective-permute-start.4 = (bf16[16,768]{1,0:T(8,128)(2,1)S(1)}, bf16[16,768]{1,0:T(8,128)(2,1)S(1)}, u32[]{:S(2)}, u32[]{:S(2)}) collective-permute-start(bf16[16,768]{1,0:T(8,128)(2,1)S(1)} %pad_maximum_fusion.3), channel_id=1, source_target_pairs={{0,8},{1,9},{2,10},{3,11},{4,12},{5,13},{6,14},{7,15},{8,0},{9,1},... | collective-permute-start | bytes 73736 | tf_op jit(solution)/shard_map/ppermute | solution.py:28
  20.1 4.9 %collective-permute-start.7 = (bf16[48,768]{1,0:T(8,128)(2,1)S(1)}, bf16[48,768]{1,0:T(8,128)(2,1)S(1)}, u32[]{:S(2)}, u32[]{:S(2)}) collective-permute-start(bf16[48,768]{1,0:T(8,128)(2,1)S(1)} %convolution_convert_fusion), channel_id=1, source_target_pairs={{0,16},{16,32},{32,48},{48,0},{64,80},{80,96},{96,112},{112,64},{1... | collective-permute-start | bytes 221192 | tf_op jit(solution)/shard_map/ppermute | solution.py:20
  21.4 5.0 %collective-permute-start.6 = (bf16[48,768]{1,0:T(8,128)(2,1)S(1)}, bf16[48,768]{1,0:T(8,128)(2,1)S(1)}, u32[]{:S(2)}, u32[]{:S(2)}) collective-permute-start(bf16[48,768]{1,0:T(8,128)(2,1)S(1)} %convolution_convert_fusion), channel_id=1, source_target_pairs={{0,32},{16,48},{32,0},{48,16},{64,96},{80,112},{96,64},{112,80},{1... | collective-permute-start | bytes 221192 | tf_op jit(solution)/shard_map/ppermute | solution.py:20
  23.9 3.2 %collective-permute-start.5 = (bf16[48,768]{1,0:T(8,128)(2,1)S(1)}, bf16[48,768]{1,0:T(8,128)(2,1)S(1)}, u32[]{:S(2)}, u32[]{:S(2)}) collective-permute-start(bf16[48,768]{1,0:T(8,128)(2,1)S(1)} %convolution_convert_fusion), channel_id=1, source_target_pairs={{0,48},{16,0},{32,16},{48,32},{64,112},{80,64},{96,80},{112,96},{1... | collective-permute-start | bytes 221192 | tf_op jit(solution)/shard_map/ppermute | solution.py:20
  27.1 10.2 %collective-permute-start.8 = (bf16[192,768]{1,0:T(8,128)(2,1)S(1)}, bf16[192,768]{1,0:T(8,128)(2,1)S(1)}, u32[]{:S(2)}, u32[]{:S(2)}) collective-permute-start(bf16[192,768]{1,0:T(8,128)(2,1)S(1)} %pad_maximum_fusion.refs_2_), channel_id=1, source_target_pairs={{0,192},{16,208},{32,224},{48,240},{64,0},{80,16},{96,32},{112,48}... | collective-permute-start | bytes 884744 | tf_op jit(solution)/shard_map/ppermute | solution.py:24
  29.9 13.5 %collective-permute-start.9 = (bf16[192,768]{1,0:T(8,128)(2,1)S(1)}, bf16[192,768]{1,0:T(8,128)(2,1)S(1)}, u32[]{:S(2)}, u32[]{:S(2)}) collective-permute-start(bf16[192,768]{1,0:T(8,128)(2,1)S(1)} %pad_maximum_fusion.refs_2_), channel_id=1, source_target_pairs={{0,128},{16,144},{32,160},{48,176},{64,192},{80,208},{96,224},{112... | collective-permute-start | bytes 884744 | tf_op jit(solution)/shard_map/ppermute | solution.py:24
  30.3 14.0 %collective-permute-start.10 = (bf16[192,768]{1,0:T(8,128)(2,1)S(1)}, bf16[192,768]{1,0:T(8,128)(2,1)S(1)}, u32[]{:S(2)}, u32[]{:S(2)}) collective-permute-start(bf16[192,768]{1,0:T(8,128)(2,1)S(1)} %pad_maximum_fusion.refs_2_), channel_id=1, source_target_pairs={{0,64},{16,80},{32,96},{48,112},{64,128},{80,144},{96,160},{112,17... | collective-permute-start | bytes 884744 | tf_op jit(solution)/shard_map/ppermute | solution.py:24
  30.9 17.0 %collective-permute-start.11 = (bf16[192,768]{1,0:T(8,128)(2,1)S(1)}, bf16[192,768]{1,0:T(8,128)(2,1)S(1)}, u32[]{:S(2)}, u32[]{:S(2)}) collective-permute-start(bf16[192,768]{1,0:T(8,128)(2,1)S(1)} %pad_maximum_fusion.refs_2_), channel_id=1, source_target_pairs={{0,1},{1,0},{2,3},{3,2},{4,5},{5,4},{6,7},{7,6},{8,9},{9,8},{10,11... | collective-permute-start | bytes 884744 | tf_op jit(solution)/shard_map/ppermute | solution.py:32
  37.3 11.4 %collective-permute-start.12 = (bf16[192,768]{1,0:T(8,128)(2,1)S(1)}, bf16[192,768]{1,0:T(8,128)(2,1)S(1)}, u32[]{:S(2)}, u32[]{:S(2)}) collective-permute-start(bf16[192,768]{1,0:T(8,128)(2,1)S(1)} %collective-permute-done.8.refs_3_), channel_id=1, source_target_pairs={{0,1},{1,0},{2,3},{3,2},{4,5},{5,4},{6,7},{7,6},{8,9},{9,8},{10,11... | collective-permute-start | bytes 884744 | tf_op jit(solution)/shard_map/ppermute | solution.py:32
  43.4 5.9 %collective-permute-start.13 = (bf16[192,768]{1,0:T(8,128)(2,1)S(1)}, bf16[192,768]{1,0:T(8,128)(2,1)S(1)}, u32[]{:S(2)}, u32[]{:S(2)}) collective-permute-start(bf16[192,768]{1,0:T(8,128)(2,1)S(1)} %collective-permute-done.9.refs_4_), channel_id=1, source_target_pairs={{0,1},{1,0},{2,3},{3,2},{4,5},{5,4},{6,7},{7,6},{8,9},{9,8},{10,11... | collective-permute-start | bytes 884744 | tf_op jit(solution)/shard_map/ppermute | solution.py:32
  44.3 5.8 %collective-permute-start.14 = (bf16[192,768]{1,0:T(8,128)(2,1)S(1)}, bf16[192,768]{1,0:T(8,128)(2,1)S(1)}, u32[]{:S(2)}, u32[]{:S(2)}) collective-permute-start(bf16[192,768]{1,0:T(8,128)(2,1)S(1)} %collective-permute-done.10.refs_5_), channel_id=1, source_target_pairs={{0,1},{1,0},{2,3},{3,2},{4,5},{5,4},{6,7},{7,6},{8,9},{9,8},{10,11... | collective-permute-start | bytes 884744 | tf_op jit(solution)/shard_map/ppermute | solution.py:32
  47.9 0.7 copy-start
  48.6 0.7 copy-start.2
  49.4 0.7 copy-start.4
  50.1 0.7 copy-start.6
  50.8 1.0 copy-start.1
  51.7 1.0 copy-start.3
  52.7 1.0 copy-start.5
  53.7 1.0 copy-start.7
  91.2 5.2 %collective-permute-start.15 = (f32[768,768]{1,0:T(8,128)}, f32[768,768]{1,0:T(8,128)}, u32[]{:S(2)}, u32[]{:S(2)}) collective-permute-start(f32[768,768]{1,0:T(8,128)} %get-tuple-element.11), channel_id=1, source_target_pairs={{0,1},{1,0},{2,3},{3,2},{4,5},{5,4},{6,7},{7,6},{8,9},{9,8},{10,11... | collective-permute-start | bytes 7077896 | tf_op jit(solution)/shard_map/ppermute | solution.py:32
  98.4 1.4 copy-start.9
  99.9 6.6 %collective-permute-start.16 = (bf16[96,768]{1,0:T(8,128)(2,1)S(1)}, bf16[96,768]{1,0:T(8,128)(2,1)S(1)}, u32[]{:S(2)}, u32[]{:S(2)}) collective-permute-start(bf16[96,768]{1,0:T(8,128)(2,1)S(1)} %get-tuple-element.19), channel_id=1, source_target_pairs={{0,64},{16,80},{32,96},{48,112},{64,128},{80,144},{96,160},{112,17... | collective-permute-start | bytes 442376 | tf_op jit(solution)/shard_map/ppermute | solution.py:24
  99.9 6.5 %collective-permute-start.18 = (bf16[96,768]{1,0:T(8,128)(2,1)S(1)}, bf16[96,768]{1,0:T(8,128)(2,1)S(1)}, u32[]{:S(2)}, u32[]{:S(2)}) collective-permute-start(bf16[96,768]{1,0:T(8,128)(2,1)S(1)} %get-tuple-element.20), channel_id=1, source_target_pairs={{0,192},{16,208},{32,224},{48,240},{64,0},{80,16},{96,32},{112,48}... | collective-permute-start | bytes 442376 | tf_op jit(solution)/shard_map/ppermute | solution.py:24
  107.6 7.6 %collective-permute-start.19 = (bf16[192,768]{1,0:T(8,128)(2,1)S(1)}, bf16[192,768]{1,0:T(8,128)(2,1)S(1)}, u32[]{:S(2)}, u32[]{:S(2)}) collective-permute-start(bf16[192,768]{1,0:T(8,128)(2,1)S(1)} %pad_maximum_fusion.2), channel_id=1, source_target_pairs={{0,192},{16,208},{32,224},{48,240},{64,0},{80,16},{96,32},{112,48}... | collective-permute-start | bytes 884744 | tf_op jit(solution)/shard_map/ppermute | solution.py:24
  110.0 8.2 %collective-permute-start.17 = (bf16[192,768]{1,0:T(8,128)(2,1)S(1)}, bf16[192,768]{1,0:T(8,128)(2,1)S(1)}, u32[]{:S(2)}, u32[]{:S(2)}) collective-permute-start(bf16[192,768]{1,0:T(8,128)(2,1)S(1)} %pad_maximum_fusion.1), channel_id=1, source_target_pairs={{0,64},{16,80},{32,96},{48,112},{64,128},{80,144},{96,160},{112,17... | collective-permute-start | bytes 884744 | tf_op jit(solution)/shard_map/ppermute | solution.py:24
  119.5 6.1 %collective-permute-start.22 = (f32[48,768]{1,0:T(8,128)S(1)}, f32[48,768]{1,0:T(8,128)S(1)}, u32[]{:S(2)}, u32[]{:S(2)}) collective-permute-start(f32[48,768]{1,0:T(8,128)S(1)} %get-tuple-element.17), channel_id=1, source_target_pairs={{0,48},{16,0},{32,16},{48,32},{64,112},{80,64},{96,80},{112,96},{1... | collective-permute-start | bytes 442376 | tf_op jit(solution)/shard_map/ppermute | solution.py:20
  121.9 5.6 %collective-permute-start.21 = (f32[48,768]{1,0:T(8,128)S(1)}, f32[48,768]{1,0:T(8,128)S(1)}, u32[]{:S(2)}, u32[]{:S(2)}) collective-permute-start(f32[48,768]{1,0:T(8,128)S(1)} %get-tuple-element.18), channel_id=1, source_target_pairs={{0,32},{16,48},{32,0},{48,16},{64,96},{80,112},{96,64},{112,80},{1... | collective-permute-start | bytes 442376 | tf_op jit(solution)/shard_map/ppermute | solution.py:20
  122.0 6.8 %collective-permute-start.20 = (f32[48,768]{1,0:T(8,128)S(1)}, f32[48,768]{1,0:T(8,128)S(1)}, u32[]{:S(2)}, u32[]{:S(2)}) collective-permute-start(f32[48,768]{1,0:T(8,128)S(1)} %get-tuple-element.16), channel_id=1, source_target_pairs={{0,16},{16,32},{32,48},{48,0},{64,80},{80,96},{96,112},{112,64},{1... | collective-permute-start | bytes 442376 | tf_op jit(solution)/shard_map/ppermute | solution.py:20
  (1 other events, 0.7 us)

commit v3 on v2

v3 whole, which is shorter than its diff:
```python
import functools

import jax
import jax.numpy as jnp
from jax import lax
from jax.experimental import pallas as pl
from jax.experimental.pallas import tpu as pltpu
from jax.sharding import PartitionSpec as P

HEAD_DIM = 64
HEADS = 6
D = 768
HD = 384
VMAX = 128
BLOCKS = 12
GROUP = 4
ROWS = GROUP * VMAX
BF16 = jnp.bfloat16
F32 = jnp.float32


def hop_x(v, k):
    return lax.ppermute(v, "il", [(i, (i // 4) * 4 + (i + k) % 4) for i in range(16)])


def hop_y(v, k):
    return lax.ppermute(v, "il", [(i, (i + 4 * k) % 16) for i in range(16)])


def hop_z(v, k):
    return lax.ppermute(v, "xl", [(i, (i + 2 * k) % 16) for i in range(16)])


def hop_core(v):
    return lax.ppermute(v, "xl", [(i, i ^ 1) for i in range(16)])


def coords():
    il = lax.axis_index("il")
    xl = lax.axis_index("xl")
    return il // 4, il % 4, xl // 2, xl % 2


def gather4(v, hop, direct):
    r1 = hop(v, -1)
    r3 = hop(v, 1)
    if direct:
        r2 = hop(v, 2)
    else:
        h = v.shape[0] // 2
        r2 = jnp.concatenate([hop(r1[:h], -1), hop(r3[h:], 1)], axis=0)
    return [v, r1, r2, r3]


def gather_weights(w):
    y, x, z, c = coords()
    n = w.shape[1] // 2
    mine = lax.dynamic_slice(w, (0, c * n), (3, n))
    other = lax.dynamic_slice(w, (0, (1 - c) * n), (3, n))
    block = jnp.concatenate([mine, hop_core(other), jnp.zeros((2, n), w.dtype)], axis=0)
    block = jnp.concatenate([block, lax.ppermute(block, "xl", [(i, i ^ 2) for i in range(16)])], axis=0)
    stack = jnp.concatenate([block, hop_z(block, 2), hop_z(block, -2), hop_z(block, 4)], axis=0)
    r = jnp.arange(48)[:, None]
    s = jnp.arange(64)[None, :]
    slot = s // 16
    j = s % 8
    origin = (z + jnp.where(slot == 3, 4, jnp.where(slot == 2, 2, jnp.where(slot == 1, 6, 0)))) % 8
    row = (origin ^ ((s // 8) % 2)) * 6 + (c ^ (j // 3)) * 3 + j % 3
    order = ((row == r) & (j < 6)).astype(w.dtype)
    v = jnp.dot(order, stack, preferred_element_type=F32).astype(w.dtype)
    v = jnp.concatenate(gather4(v, hop_x, True), axis=0)
    mine = gather4(v, hop_y, True)
    return mine + [hop_core(u) for u in mine]


def scatter4(parts, hop):
    got = [hop(parts[k].astype(BF16), k) for k in (1, 2, 3)]
    return parts[0] + got[0].astype(F32) + got[1].astype(F32) + got[2].astype(F32)


def scatter_grads(at, keep, send):
    y, x, z, c = coords()
    n = keep.shape[1]
    v = scatter4(split_rows(at, keep, hop_core(send)), hop_y)
    rows = v.shape[0] // 4
    v = scatter4([lax.dynamic_slice(v, (((x + k) % 4) * rows, 0), (rows, n)) for k in range(4)], hop_x)
    got = lax.all_to_all(v.reshape(16, 3, n), "xl", split_axis=0, concat_axis=0, tiled=True)
    acc = jnp.sum(got.reshape(8, 2, 3, n), axis=0)
    return jnp.concatenate([acc[0], acc[1]], axis=1)


def mm(a, b):
    return jnp.dot(a, b, preferred_element_type=F32)


def mm_t(a, b):
    return lax.dot_general(a, b, (((1,), (1,)), ((), ())), preferred_element_type=F32)


def tmm(a, b):
    return lax.dot_general(a, b, (((0,), (0,)), ((), ())), preferred_element_type=F32)


def norm_rows(xf):
    centred = xf - jnp.mean(xf, axis=-1, keepdims=True)
    inv = lax.rsqrt(jnp.mean(centred * centred, axis=-1, keepdims=True) + 1e-6)
    return centred * inv, inv


def row_mask(counts_ref, first, group):
    row_id = lax.broadcasted_iota(jnp.int32, (VMAX, D), 0)
    return jnp.concatenate([row_id < counts_ref[first + b] for b in range(group)], axis=0)


def core_kernel(*refs):
    at_ref, counts_ref = refs[:2]
    pieces = refs[2:10]
    x_ref, cot_ref, gain_ref = refs[10:13]
    w_out, att_out, gp_out, keep_out, send_out = refs[13:18]
    w_ref, nb_ref, go_ref, att_ref, gp_ref, keep_ref, send_ref, w_sems, row_sems, dw_sems = refs[18:]
    step = pl.program_id(0)
    last = pl.num_programs(0) - 1
    factor = HEAD_DIM**-0.5
    core = at_ref[2]

    @pl.when(step == 0)
    def _():
        y, x = at_ref[0], at_ref[1]
        copies = []
        for rel in range(2):
            half = core ^ rel
            for ky in range(4):
                for kx in range(4):
                    row = pl.multiple_of(((y + ky) & 3) * 192 + ((x + kx) & 3) * 48, 16)
                    copies.append(
                        pltpu.make_async_copy(
                            pieces[rel * 4 + ky].at[pl.ds(kx * 48, 48), :],
                            w_ref.at[half, pl.ds(row, 48), :],
                            w_sems.at[len(copies)],
                        )
                    )
        for copy in copies:
            copy.start()
        for copy in copies:
            copy.wait()

    whole_w = pltpu.make_async_copy(w_ref, w_out, w_sems.at[32])

    @pl.when(step == 0)
    def _():
        whole_w.start()

    normed, _ = norm_rows(x_ref[...].reshape(ROWS, D).astype(F32))
    nb = (normed * gain_ref[...]).astype(BF16)
    mask = row_mask(counts_ref, step * GROUP, GROUP)
    go = jnp.where(mask, cot_ref[...].reshape(ROWS, D).astype(F32), 0.0).astype(BF16)
    at = pl.ds(pl.multiple_of(step * ROWS, ROWS), ROWS)
    nb_ref[at, :] = nb
    go_ref[at, :] = go

    qk = mm(nb, w_ref[0]).astype(BF16)
    vv = mm(nb, w_ref[1, :, :HD]).astype(BF16)
    ga = mm(go, w_ref[1, :, HD:]).astype(BF16)
    key_id = lax.broadcasted_iota(jnp.int32, (VMAX, 2 * VMAX), 0)
    lane = lax.broadcasted_iota(jnp.int32, (1, 2 * HEAD_DIM), 1)
    first = jnp.where(lane < HEAD_DIM, 1.0, 0.0)
    m0, m1 = first.astype(BF16), (1.0 - first).astype(BF16)
    f0, f1 = (first * factor).astype(BF16), ((1.0 - first) * factor).astype(BF16)
    pair = lambda a, u, w: jnp.concatenate([a * u, a * w], axis=0)
    stack = lambda a: jnp.concatenate([a[:, :VMAX], a[:, VMAX:]], axis=0)
    for b in range(GROUP):
        live = key_id < counts_ref[step * GROUP + b]
        rs = slice(b * VMAX, (b + 1) * VMAX)
        at_b = pl.ds(pl.multiple_of(step * ROWS + b * VMAX, VMAX), VMAX)
        for lo in range(0, HD, 2 * HEAD_DIM):
            hi = lo + 2 * HEAD_DIM
            k = qk[rs, HD + lo : HD + hi]
            v = vv[rs, lo:hi]
            q2 = pair(qk[rs, lo:hi], f0, f1)
            g2 = pair(ga[rs, lo:hi], m0, m1)
            s = jnp.where(live, mm_t(k, q2), -1e30)
            e = jnp.exp(s - jnp.max(s, axis=0, keepdims=True))
            p = e * (1.0 / jnp.sum(e, axis=0, keepdims=True))
            pb = p.astype(BF16)
            dp = mm_t(v, g2)
            ds = (p * (dp - jnp.sum(p * dp, axis=0, keepdims=True))).astype(BF16)
            att_ref[at_b, lo:hi] = tmm(stack(pb), pair(v, m0, m1)).astype(BF16)
            gp_ref[at_b, lo:hi] = tmm(stack(ds), pair(k, f0, f1)).astype(BF16)
            gp_ref[at_b, HD + lo : HD + hi] = mm(ds, q2).astype(BF16)
            gp_ref[at_b, D + lo : D + hi] = mm(pb, g2).astype(BF16)

    def row_copies(i):
        rows = pl.ds(pl.multiple_of(i * ROWS, ROWS), ROWS)
        return (
            pltpu.make_async_copy(att_ref.at[rows, :], att_out.at[rows, :], row_sems.at[0, i]),
            pltpu.make_async_copy(gp_ref.at[rows, :], gp_out.at[rows, :], row_sems.at[1, i]),
        )

    for copy in row_copies(step):
        copy.start()

    @pl.when(step == last)
    def _():
        copies = []
        for i in range(D // 256):
            rr = slice(i * 256, i * 256 + 256)
            gw = tmm(nb_ref[:, rr], gp_ref[...])
            for half, cols, val in (
                (0, slice(0, D), gw[:, :D]),
                (1, slice(0, HD), gw[:, D:]),
                (1, slice(HD, D), tmm(go_ref[:, rr], att_ref[...])),
            ):

                @pl.when(core == half)
                def _():
                    keep_ref[rr, cols] = val

                @pl.when(core != half)
                def _():
                    send_ref[rr, cols] = val.astype(send_ref.dtype)

            copies.append(pltpu.make_async_copy(keep_ref.at[rr, :], keep_out.at[rr, :], dw_sems.at[0, i]))
            copies.append(pltpu.make_async_copy(send_ref.at[rr, :], send_out.at[rr, :], dw_sems.at[1, i]))
            copies[-1].start()
            copies[-2].start()
        whole_w.wait()
        for i in range(BLOCKS // GROUP):
            for copy in row_copies(i):
                copy.wait()
        for copy in copies:
            copy.wait()


def grads_core(at, counts, pieces, tiles, cotan, gain):
    nblock = tiles.shape[0]
    rows = nblock * VMAX
    hbm = pl.BlockSpec(memory_space=pltpu.HBM)
    tile = pl.BlockSpec((GROUP, VMAX, D), lambda i, *_: (i, 0, 0))
    return pl.pallas_call(
        core_kernel,
        grid_spec=pltpu.PrefetchScalarGridSpec(
            num_scalar_prefetch=2,
            grid=(nblock // GROUP,),
            in_specs=[hbm] * 8 + [tile, tile, pl.BlockSpec((1, D), lambda i, *_: (0, 0))],
            out_specs=[hbm] * 5,
            scratch_shapes=[
                pltpu.VMEM((2, D, D), BF16),
                pltpu.VMEM((rows, D), BF16),
                pltpu.VMEM((rows, D), BF16),
                pltpu.VMEM((rows, HD), BF16),
                pltpu.VMEM((rows, 3 * HD), BF16),
                pltpu.VMEM((D, D), F32),
                pltpu.VMEM((D, D), BF16),
                pltpu.SemaphoreType.DMA((33,)),
                pltpu.SemaphoreType.DMA((2, nblock // GROUP)),
                pltpu.SemaphoreType.DMA((2, D // 256)),
            ],
        ),
        out_shape=[
            jax.ShapeDtypeStruct((2, D, D), BF16),
            jax.ShapeDtypeStruct((rows, HD), BF16),
            jax.ShapeDtypeStruct((rows, 3 * HD), BF16),
            jax.ShapeDtypeStruct((D, D), F32),
            jax.ShapeDtypeStruct((D, D), BF16),
        ],
        compiler_params=pltpu.CompilerParams(
            dimension_semantics=("arbitrary",), vmem_limit_bytes=56 * 1024 * 1024
        ),
        cost_estimate=pl.CostEstimate(flops=20_000_000_000, bytes_accessed=18_000_000, transcendentals=1_200_000),
    )(at, counts, *pieces, tiles, cotan, gain)


def rows_kernel(first, counts_ref, w_ref, att_ref, gp_ref, x_ref, cot_ref, gain_ref, *rest):
    enc_ref, gin_ref = rest[-2:]
    gain = gain_ref[...]
    xf = x_ref[...].reshape(ROWS, D).astype(F32)
    normed, inv = norm_rows(xf)
    mask = row_mask(counts_ref, (first + pl.program_id(0)) * GROUP, GROUP)
    enc = xf + mm_t(att_ref[...], w_ref[1, :, HD:])
    enc_ref[...] = jnp.where(mask, enc, 0.0).astype(BF16).reshape(GROUP, VMAX, D)
    gp = gp_ref[...]
    gn = (mm_t(gp[:, :D], w_ref[0]) + mm_t(gp[:, D:], w_ref[1, :, :HD])) * gain
    gl = inv * (
        gn - jnp.mean(gn, axis=-1, keepdims=True) - normed * jnp.mean(gn * normed, axis=-1, keepdims=True)
    )
    gin = cot_ref[...].reshape(ROWS, D).astype(F32) + gl
    gin_ref[...] = jnp.where(mask, gin, 0.0).astype(BF16).reshape(GROUP, VMAX, D)


def rows_part(first, count, counts, w, att, gp, tiles, cotan, gain, done):
    tile = pl.BlockSpec((GROUP, VMAX, D), lambda i, *_: (i + first, 0, 0))
    flat = lambda cols: pl.BlockSpec((ROWS, cols), lambda i, *_: (i + first, 0))
    return pl.pallas_call(
        functools.partial(rows_kernel, first),
        grid_spec=pltpu.PrefetchScalarGridSpec(
            num_scalar_prefetch=1,
            grid=(count,),
            in_specs=[
                pl.BlockSpec((2, D, D), lambda i, *_: (0, 0, 0), pipeline_mode=pl.Buffered(1)),
                flat(HD),
                flat(3 * HD),
                tile,
                tile,
                pl.BlockSpec((1, D), lambda i, *_: (0, 0)),
            ]
            + [pl.BlockSpec(memory_space=pltpu.HBM)] * len(done),
            out_specs=[tile, tile],
        ),
        out_shape=[jax.ShapeDtypeStruct(tiles.shape, BF16)] * 2,
        input_output_aliases={7 + i: i for i in range(len(done))},
        compiler_params=pltpu.CompilerParams(
            dimension_semantics=("arbitrary",), vmem_limit_bytes=40 * 1024 * 1024
        ),
        cost_estimate=pl.CostEstimate(
            flops=count * 1_300_000_000, bytes_accessed=count * 5_000_000, transcendentals=1000
        ),
    )(counts, w, att, gp, tiles, cotan, gain, *done)


def split_kernel(at_ref, keep_ref, got_ref, own_ref, *outs):
    step = pl.program_id(0)
    total = keep_ref[...] + got_ref[...].astype(F32)

    @pl.when(step == 0)
    def _():
        own_ref[...] = total

    for k in range(1, 4):

        @pl.when(step == k)
        def _():
            outs[k - 1][...] = total.astype(BF16)


def split_rows(at, keep, got):
    rows = keep.shape[0] // 4
    n = keep.shape[1]
    block = pl.BlockSpec((rows, n), lambda i, at: ((at[0] + i) % 4, 0))
    out = pl.BlockSpec((rows, n), lambda i, at: (0, 0))
    return pl.pallas_call(
        split_kernel,
        grid_spec=pltpu.PrefetchScalarGridSpec(
            num_scalar_prefetch=1, grid=(4,), in_specs=[block, block], out_specs=[out] * 4
        ),
        out_shape=[jax.ShapeDtypeStruct((rows, n), F32)] + [jax.ShapeDtypeStruct((rows, n), BF16)] * 3,
        compiler_params=pltpu.CompilerParams(dimension_semantics=("arbitrary",)),
        cost_estimate=pl.CostEstimate(flops=600_000, bytes_accessed=5_000_000, transcendentals=0),
    )(at, keep, got)


def shards(patches, out_cot, vis_count, w_qkv, w_out, ln_gain):
    y, x, z, c = coords()
    pieces = gather_weights(jnp.concatenate([w_qkv, w_out], axis=1))
    at = jnp.stack([y, x, c]).astype(jnp.int32)
    counts, tiles, cotan, gain = vis_count[0], patches[0], out_cot[0], ln_gain[None]
    w, att, gp, keep, send = grads_core(at, counts, pieces, tiles, cotan, gain)
    out = rows_part(0, 1, counts, w, att, gp, tiles, cotan, gain, ())
    enc, gin = rows_part(1, 2, counts, w, att, gp, tiles, cotan, gain, out)
    grads = scatter_grads(at, keep, send)
    n = w_qkv.shape[1]
    return enc[None], gin[None], grads[:, :n], grads[:, n:]


def solution(mesh):
    return jax.shard_map(
        shards,
        mesh=mesh,
        in_specs=(
            P("il", "xl", None, None),
            P("il", "xl", None, None),
            P("il", "xl"),
            P(("il", "xl"), None),
            P(("il", "xl"), None),
            P(),
        ),
        out_specs=(
            P("il", "xl", None, None),
            P("il", "xl", None, None),
            P(("il", "xl"), None),
            P(("il", "xl"), None),
        ),
        check_vma=False,
    )
```

time: 151 us -> 142 us (0.940)
  blocking collectives: 19.9 us -> 0 us
  starting transfers between devices: 44.9 us -> 51.1 us
  Pallas kernels: 36 us -> 41.6 us
  waiting for transfers between devices: 30.4 us -> 27.8 us
  local copies, waits for them, and re-layouts: 12.7 us -> 14.8 us
    all_to_all x1 -> x0, blocking collectives: 19.9 us -> none  [scatter_grads(): lax.all_to_all(v.reshape(16, 3, n), 'xl', split_axis=0, concat_axis=0, ti...]
    all_to_all x0 -> x1, starting transfers between devices: none -> 8.54 us  [scatter_grads(): lax.all_to_all(v.reshape(16, 3, n), 'xl', split_axis=0, concat_axis=0, ti...]
    pallas_call x1 -> x4, Pallas kernels: 36 us -> 41.6 us  [the longest x1 27.7 us: grads_core(): pl.pallas_call(core_kernel, grid_spec=pltpu.PrefetchScalarGridSpec(num_sc...]
    add x1 -> x2, other arithmetic: 0.03 us -> 3.16 us  [scatter4(): parts[0] + got[0].astype(F32) + got[1].astype(F32) + got[2].astype(F32)]
    add x2 -> x0, other arithmetic: 3.1 us -> none  [the longest x1 1.96 us: scatter_grads(): total = keep + hop_core(send).astype(F32)]
    ppermute x6, waiting for transfers between devices: 5.67 us -> 3.67 us  [hop_core(): return lax.ppermute(v, 'xl', [(i, i ^ 1) for i in range(16)])]
    ppermute x6, starting transfers between devices: 18.9 us -> 17.1 us  [hop_core(): return lax.ppermute(v, 'xl', [(i, i ^ 1) for i in range(16)])]
    reshape x1, local copies, waits for them, and re-layouts: 0.06 us -> 1.67 us  [scatter_grads(): v.reshape(16, 3, n)]
  transfers between devices with their start and end apart: 23 -> 23, of which waited for: 14 -> 12; matrix products, arithmetic and copies ran while one was open for 1% -> 1% of each run, Pallas kernels for 0% -> 7%
where the time goes in v3:
time: 142 us
  starting transfers between devices  51.1 us (36%)
  Pallas kernels  41.6 us (29%)
  waiting for transfers between devices  27.8 us (20%)
  local copies, waits for them, and re-layouts  14.8 us (10%)
  other arithmetic  5.43 us (4%)
    pallas_call x1, Pallas kernels, grads_core(): pl.pallas_call(core_kernel, grid_spec=pltpu.PrefetchScalarGridSpec(num_sc...  27.7 us
    ppermute x6, starting transfers between devices, hop_core(): return lax.ppermute(v, 'xl', [(i, i ^ 1) for i in range(16)])  17.1 us
    ppermute x6, waiting for transfers between devices, hop_y(): return lax.ppermute(v, 'il', [(i, (i + 4 * k) % 16) for i in range(16)])  12.4 us
    unnamed x35, local copies, waits for them, and re-layouts  9.88 us
    pallas_call x2, Pallas kernels, rows_part(): pl.pallas_call(functools.partial(rows_kernel, first), grid_spec=pltpu.Pre...  9.32 us
    ppermute x6, starting transfers between devices, hop_y(): return lax.ppermute(v, 'il', [(i, (i + 4 * k) % 16) for i in range(16)])  9.27 us
    all_to_all x1, starting transfers between devices, scatter_grads(): lax.all_to_all(v.reshape(16, 3, n), 'xl', split_axis=0, concat_axis=0, ti...  8.54 us
    ppermute x6, starting transfers between devices, hop_x(): lax.ppermute(v, 'il', [(i, i // 4 * 4 + (i + k) % 4) for i in range(16)])  8.45 us
  transfers between devices with their start and end apart: 23, of which 12 were waited for; matrix products, arithmetic and copies ran while one was open for 1% of the time, Pallas kernels for 7%

profile of v3, /device:TPU:1, one launch (start us, length us, event | category | flops | bytes accessed | tf_op | source)
XLA Modules:
  0.0 141.8 jit_solution(6355428241210423967)
XLA Ops:
  2.1 3.3 %collective-permute-start = (bf16[3,768]{1,0:T(4,128)(2,1)S(1)}, bf16[3,768]{1,0:T(4,128)(2,1)S(1)}, u32[]{:S(2)}, u32[]{:S(2)}) collective-permute-start(bf16[3,768]{1,0:T(4,128)(2,1)S(1)} %get-tuple-element.35), channel_id=1, source_target_pairs={{0,1},{1,0},{2,3},{3,2},{4,5},{5,4},{6,7},{7,6},{8,9},{9,8},{10,11... | collective-permute-start | bytes 13832 | tf_op jit(solution)/shard_map/ppermute | solution.py:35
  6.4 2.5 %collective-permute-done.1 = bf16[8,768]{1,0:T(8,128)(2,1)S(1)} collective-permute-done((bf16[8,768]{1,0:T(8,128)(2,1)S(1)}, bf16[8,768]{1,0:T(8,128)(2,1)S(1)}, u32[]{:S(2)}, u32[]{:S(2)}) %collective-permute-start.1) | collective-permute-done | bytes 12320 | tf_op jit(solution)/shard_map/ppermute | solution.py:61
  8.9 5.3 %collective-permute-start.4 = (bf16[16,768]{1,0:T(8,128)(2,1)S(1)}, bf16[16,768]{1,0:T(8,128)(2,1)S(1)}, u32[]{:S(2)}, u32[]{:S(2)}) collective-permute-start(bf16[16,768]{1,0:T(8,128)(2,1)S(1)} %pad_maximum_fusion.1), channel_id=1, source_target_pairs={{0,8},{1,9},{2,10},{3,11},{4,12},{5,13},{6,14},{7,15},{8,0},{9,1},... | collective-permute-start | bytes 73736 | tf_op jit(solution)/shard_map/ppermute | solution.py:31
  14.2 2.4 %collective-permute-start.2 = (bf16[16,768]{1,0:T(8,128)(2,1)S(1)}, bf16[16,768]{1,0:T(8,128)(2,1)S(1)}, u32[]{:S(2)}, u32[]{:S(2)}) collective-permute-start(bf16[16,768]{1,0:T(8,128)(2,1)S(1)} %pad_maximum_fusion.1), channel_id=1, source_target_pairs={{0,4},{1,5},{2,6},{3,7},{4,8},{5,9},{6,10},{7,11},{8,12},{9,13},{1... | collective-permute-start | bytes 73736 | tf_op jit(solution)/shard_map/ppermute | solution.py:31
  19.2 1.3 collective-permute-start.7
  20.5 2.5 %collective-permute-start.6 = (bf16[48,768]{1,0:T(8,128)(2,1)S(1)}, bf16[48,768]{1,0:T(8,128)(2,1)S(1)}, u32[]{:S(2)}, u32[]{:S(2)}) collective-permute-start(bf16[48,768]{1,0:T(8,128)(2,1)S(1)} %convolution_convert_fusion), channel_id=1, source_target_pairs={{0,32},{16,48},{32,0},{48,16},{64,96},{80,112},{96,64},{112,80},{1... | collective-permute-start | bytes 221192 | tf_op jit(solution)/shard_map/ppermute | solution.py:23
  24.1 1.4 collective-permute-done.6
  26.2 1.4 collective-permute-start.10
  27.6 2.6 %collective-permute-start.9 = (bf16[192,768]{1,0:T(8,128)(2,1)S(1)}, bf16[192,768]{1,0:T(8,128)(2,1)S(1)}, u32[]{:S(2)}, u32[]{:S(2)}) collective-permute-start(bf16[192,768]{1,0:T(8,128)(2,1)S(1)} %pad_maximum_fusion.refs_2_), channel_id=1, source_target_pairs={{0,128},{16,144},{32,160},{48,176},{64,192},{80,208},{96,224},{112... | collective-permute-start | bytes 884744 | tf_op jit(solution)/shard_map/ppermute | solution.py:27
  31.3 5.4 %collective-permute-start.11 = (bf16[192,768]{1,0:T(8,128)(2,1)S(1)}, bf16[192,768]{1,0:T(8,128)(2,1)S(1)}, u32[]{:S(2)}, u32[]{:S(2)}) collective-permute-start(bf16[192,768]{1,0:T(8,128)(2,1)S(1)} %pad_maximum_fusion.refs_2_), channel_id=1, source_target_pairs={{0,1},{1,0},{2,3},{3,2},{4,5},{5,4},{6,7},{7,6},{8,9},{9,8},{10,11... | collective-permute-start | bytes 884744 | tf_op jit(solution)/shard_map/ppermute | solution.py:35
  36.7 4.6 %collective-permute-start.14 = (bf16[192,768]{1,0:T(8,128)(2,1)S(1)}, bf16[192,768]{1,0:T(8,128)(2,1)S(1)}, u32[]{:S(2)}, u32[]{:S(2)}) collective-permute-start(bf16[192,768]{1,0:T(8,128)(2,1)S(1)} %collective-permute-done.10.refs_5_), channel_id=1, source_target_pairs={{0,1},{1,0},{2,3},{3,2},{4,5},{5,4},{6,7},{7,6},{8,9},{9,8},{10,11... | collective-permute-start | bytes 884744 | tf_op jit(solution)/shard_map/ppermute | solution.py:35
  41.3 3.2 %collective-permute-start.13 = (bf16[192,768]{1,0:T(8,128)(2,1)S(1)}, bf16[192,768]{1,0:T(8,128)(2,1)S(1)}, u32[]{:S(2)}, u32[]{:S(2)}) collective-permute-start(bf16[192,768]{1,0:T(8,128)(2,1)S(1)} %collective-permute-done.9.refs_4_), channel_id=1, source_target_pairs={{0,1},{1,0},{2,3},{3,2},{4,5},{5,4},{6,7},{7,6},{8,9},{9,8},{10,11... | collective-permute-start | bytes 884744 | tf_op jit(solution)/shard_map/ppermute | solution.py:35
  44.7 1.3 broadcast_in_dim.25.refs_12_.gain_ref
  47.7 27.7 %shard_map.93 = (bf16[2,768,768]{2,1,0:T(8,128)(2,1)}, bf16[1536,384]{1,0:T(8,128)(2,1)}, bf16[1536,1152]{1,0:T(8,128)(2,1)}, f32[768,768]{1,0:T(8,128)}, bf16[768,768]{1,0:T(8,128)(2,1)}) custom-call(s32[3]{0:T(128)} %pad_add_fusion.refs_0_.at_ref, s32[12]{0:T(128)} %bitcast.20, bf16[192,768]{1,0:T(8,128)(2,1)} %copy-done.9, bf16[192,768]{1,0:T(8,128)(2,1)} %copy-done.12, ...), custom_call_target="tpu_custom_call" | custom-call | flops 20000000000 | bytes 18000000 | tf_op jit(solution)/shard_map/pallas_call | solution.py:239
  75.7 2.8 %collective-permute-done.15.got_ref = bf16[768,768]{1,0:T(8,128)(2,1)S(1)} collective-permute-done((bf16[768,768]{1,0:T(8,128)(2,1)}, bf16[768,768]{1,0:T(8,128)(2,1)S(1)}, u32[]{:S(2)}, u32[]{:S(2)}) %collective-permute-start.15) | collective-permute-done | bytes 1179680 | tf_op jit(solution)/shard_map/ppermute | solution.py:35
  79.6 4.6 %shard_map.96 = (f32[192,768]{1,0:T(8,128)}, bf16[192,768]{1,0:T(8,128)(2,1)}, bf16[192,768]{1,0:T(8,128)(2,1)}, bf16[192,768]{1,0:T(8,128)(2,1)}) custom-call(s32[3]{0:T(128)} %pad_add_fusion.refs_0_.at_ref, f32[768,768]{1,0:T(8,128)} %get-tuple-element.24.keep_ref, bf16[768,768]{1,0:T(8,128)(2,1)} %copy-done.8), custom_call_target="tpu_custom_call" | custom-call | flops 600000 | bytes 5000000 | tf_op jit(solution)/shard_map/pallas_call | solution.py:340
  85.0 2.1 %collective-permute-start.17 = (bf16[192,768]{1,0:T(8,128)(2,1)}, bf16[192,768]{1,0:T(8,128)(2,1)}, u32[]{:S(2)}, u32[]{:S(2)}) collective-permute-start(bf16[192,768]{1,0:T(8,128)(2,1)} %get-tuple-element.28), channel_id=1, source_target_pairs={{0,128},{16,144},{32,160},{48,176},{64,192},{80,208},{96,224},{112... | collective-permute-start | bytes 884744 | tf_op jit(solution)/shard_map/ppermute | solution.py:27
  87.1 1.3 collective-permute-start.18
  88.5 5.8 %collective-permute-done.16 = bf16[192,768]{1,0:T(8,128)(2,1)} collective-permute-done((bf16[192,768]{1,0:T(8,128)(2,1)}, bf16[192,768]{1,0:T(8,128)(2,1)}, u32[]{:S(2)}, u32[]{:S(2)}) %collective-permute-start.16) | collective-permute-done | bytes 294944 | tf_op jit(solution)/shard_map/ppermute | solution.py:27
  94.2 6.5 %collective-permute-done.17 = bf16[192,768]{1,0:T(8,128)(2,1)} collective-permute-done((bf16[192,768]{1,0:T(8,128)(2,1)}, bf16[192,768]{1,0:T(8,128)(2,1)}, u32[]{:S(2)}, u32[]{:S(2)}) %collective-permute-start.17) | collective-permute-done | bytes 294944 | tf_op jit(solution)/shard_map/ppermute | solution.py:27
  100.9 1.4 %convert_add_fusion = f32[192,768]{1,0:T(8,128)S(1)} fusion(bf16[192,768]{1,0:T(8,128)(2,1)} %collective-permute-done.18, bf16[192,768]{1,0:T(8,128)(2,1)} %collective-permute-done.17, f32[192,768]{1,0:T(8,128)} %get-tuple-element.26, bf16[192,768]{1,0:T(8,128)(2,1)} %collective-permute-done.16), kind=kLoop, calls=%fused_computation.1 | loop fusion | flops 884736 | bytes 2064384 | tf_op jit(solution)/shard_map/add | solution.py:78
  104.5 2.0 %collective-permute-start.21 = (bf16[48,768]{1,0:T(8,128)(2,1)}, bf16[48,768]{1,0:T(8,128)(2,1)}, u32[]{:S(2)}, u32[]{:S(2)}) collective-permute-start(bf16[48,768]{1,0:T(8,128)(2,1)} %get-tuple-element.31), channel_id=1, source_target_pairs={{0,48},{16,0},{32,16},{48,32},{64,112},{80,64},{96,80},{112,96},{1... | collective-permute-start | bytes 221192 | tf_op jit(solution)/shard_map/ppermute | solution.py:23
  108.6 3.5 %collective-permute-done.20 = bf16[48,768]{1,0:T(8,128)(2,1)} collective-permute-done((bf16[48,768]{1,0:T(8,128)(2,1)}, bf16[48,768]{1,0:T(8,128)(2,1)}, u32[]{:S(2)}, u32[]{:S(2)}) %collective-permute-start.20) | collective-permute-done | bytes 73760 | tf_op jit(solution)/shard_map/ppermute | solution.py:23
  112.0 1.7 %convert_add_fusion.1 = f32[48,768]{1,0:T(8,128)} fusion(bf16[48,768]{1,0:T(8,128)(2,1)} %collective-permute-done.21, bf16[48,768]{1,0:T(8,128)(2,1)} %collective-permute-done.20, bf16[48,768]{1,0:T(8,128)(2,1)} %collective-permute-done.19, f32[192,768]{1,0:T(8,128)} %copy-done.7, s32[]{:T(128)S(6)} %select_n.170), kind=kLoop, calls=%fused_computation.3 | loop fusion | flops 221184 | bytes 516100 | tf_op jit(solution)/shard_map/add | solution.py:78
  113.7 1.7 %reshape.185 = f32[16,3,768]{2,1,0:T(4,128)} reshape(f32[48,768]{1,0:T(8,128)} %convert_add_fusion.1) | data formatting | bytes 294912 | tf_op jit(solution)/shard_map/reshape | solution.py:87
  115.4 8.5 %all-to-all-start = ((f32[16,3,768]{2,1,0:T(4,128)}), f32[16,3,768]{2,1,0:T(4,128)}, u32[]{:S(2)}, u32[]{:S(2)}) async-start(f32[16,3,768]{2,1,0:T(4,128)} %reshape.185), calls=%async_computation | async-start | bytes 393216 | tf_op jit(solution)/shard_map/all_to_all | solution.py:87
  124.0 1.7 %copy-done.1 = bf16[1,12,128,768]{3,2,1,0:T(8,128)(2,1)S(1)} copy-done((bf16[1,12,128,768]{3,2,1,0:T(8,128)(2,1)S(1)}, bf16[1,12,128,768]{3,2,1,0:T(8,128)(2,1)}, u32[]{:S(2)}) %copy-start.1) | copy-done | bytes 2359320
  125.7 1.7 %copy-done.2 = bf16[1,12,128,768]{3,2,1,0:T(8,128)(2,1)S(1)} copy-done((bf16[1,12,128,768]{3,2,1,0:T(8,128)(2,1)S(1)}, bf16[1,12,128,768]{3,2,1,0:T(8,128)(2,1)}, u32[]{:S(2)}) %copy-start.2) | copy-done | bytes 2359320
  127.3 1.7 %copy-done.3 = bf16[2,768,768]{2,1,0:T(8,128)(2,1)S(1)} copy-done((bf16[2,768,768]{2,1,0:T(8,128)(2,1)S(1)}, bf16[2,768,768]{2,1,0:T(8,128)(2,1)}, u32[]{:S(2)}) %copy-start.3) | copy-done | bytes 2359320
  129.0 1.3 copy-done.4
  130.3 3.6 %shard_map.94 = (bf16[12,128,768]{2,1,0:T(8,128)(2,1)}, bf16[12,128,768]{2,1,0:T(8,128)(2,1)}) custom-call(s32[12]{0:T(128)S(1)} %bitcast.21, bf16[2,768,768]{2,1,0:T(8,128)(2,1)S(1)} %copy-done.3, bf16[1536,384]{1,0:T(8,128)(2,1)S(1)} %copy-done.4, bf16[1536,1152]{1,0:T(8,128)(2,1)S(1)} %copy-done, bf16[12,128,768]{2,1,0:T(8,128)(2,1)S(1)} %bitcast.15, ...), custom_call_target="tpu_custom_call" | custom-call | flops 1300000000 | bytes 5000000 | tf_op jit(solution)/shard_map/pallas_call | solution.py:293
  133.8 5.7 %shard_map.95 = (bf16[12,128,768]{2,1,0:T(8,128)(2,1)}, bf16[12,128,768]{2,1,0:T(8,128)(2,1)}) custom-call(s32[12]{0:T(128)S(1)} %bitcast.22, bf16[2,768,768]{2,1,0:T(8,128)(2,1)S(1)} %copy-done.3, bf16[1536,384]{1,0:T(8,128)(2,1)S(1)} %copy-done.4, bf16[1536,1152]{1,0:T(8,128)(2,1)S(1)} %copy-done, ...), custom_call_target="tpu_custom_call", output_to_operand_aliasing={{0}: (7, {}), {1}: (8, {})} | custom-call | flops 2600000000 | bytes 10000000 | tf_op jit(solution)/shard_map/pallas_call | solution.py:293
  (73 shorter events, 18.6 us)
Async XLA Ops:
  2.1 4.2 %collective-permute-start = (bf16[3,768]{1,0:T(4,128)(2,1)S(1)}, bf16[3,768]{1,0:T(4,128)(2,1)S(1)}, u32[]{:S(2)}, u32[]{:S(2)}) collective-permute-start(bf16[3,768]{1,0:T(4,128)(2,1)S(1)} %get-tuple-element.35), channel_id=1, source_target_pairs={{0,1},{1,0},{2,3},{3,2},{4,5},{5,4},{6,7},{7,6},{8,9},{9,8},{10,11... | collective-permute-start | bytes 13832 | tf_op jit(solution)/shard_map/ppermute | solution.py:35
  6.2 2.6 %collective-permute-start.1 = (bf16[8,768]{1,0:T(8,128)(2,1)S(1)}, bf16[8,768]{1,0:T(8,128)(2,1)S(1)}, u32[]{:S(2)}, u32[]{:S(2)}) collective-permute-start(bf16[8,768]{1,0:T(8,128)(2,1)S(1)} %pad_maximum_fusion.3), channel_id=1, source_target_pairs={{0,2},{1,3},{2,0},{3,1},{4,6},{5,7},{6,4},{7,5},{8,10},{9,11},{10,... | collective-permute-start | bytes 36872 | tf_op jit(solution)/shard_map/ppermute | solution.py:61
  8.9 7.6 %collective-permute-start.4 = (bf16[16,768]{1,0:T(8,128)(2,1)S(1)}, bf16[16,768]{1,0:T(8,128)(2,1)S(1)}, u32[]{:S(2)}, u32[]{:S(2)}) collective-permute-start(bf16[16,768]{1,0:T(8,128)(2,1)S(1)} %pad_maximum_fusion.1), channel_id=1, source_target_pairs={{0,8},{1,9},{2,10},{3,11},{4,12},{5,13},{6,14},{7,15},{8,0},{9,1},... | collective-permute-start | bytes 73736 | tf_op jit(solution)/shard_map/ppermute | solution.py:31
  14.2 3.7 %collective-permute-start.3 = (bf16[16,768]{1,0:T(8,128)(2,1)S(1)}, bf16[16,768]{1,0:T(8,128)(2,1)S(1)}, u32[]{:S(2)}, u32[]{:S(2)}) collective-permute-start(bf16[16,768]{1,0:T(8,128)(2,1)S(1)} %pad_maximum_fusion.1), channel_id=1, source_target_pairs={{0,12},{1,13},{2,14},{3,15},{4,0},{5,1},{6,2},{7,3},{8,4},{9,5},{1... | collective-permute-start | bytes 73736 | tf_op jit(solution)/shard_map/ppermute | solution.py:31
  14.2 4.9 %collective-permute-start.2 = (bf16[16,768]{1,0:T(8,128)(2,1)S(1)}, bf16[16,768]{1,0:T(8,128)(2,1)S(1)}, u32[]{:S(2)}, u32[]{:S(2)}) collective-permute-start(bf16[16,768]{1,0:T(8,128)(2,1)S(1)} %pad_maximum_fusion.1), channel_id=1, source_target_pairs={{0,4},{1,5},{2,6},{3,7},{4,8},{5,9},{6,10},{7,11},{8,12},{9,13},{1... | collective-permute-start | bytes 73736 | tf_op jit(solution)/shard_map/ppermute | solution.py:31
  19.2 4.9 %collective-permute-start.7 = (bf16[48,768]{1,0:T(8,128)(2,1)S(1)}, bf16[48,768]{1,0:T(8,128)(2,1)S(1)}, u32[]{:S(2)}, u32[]{:S(2)}) collective-permute-start(bf16[48,768]{1,0:T(8,128)(2,1)S(1)} %convolution_convert_fusion), channel_id=1, source_target_pairs={{0,16},{16,32},{32,48},{48,0},{64,80},{80,96},{96,112},{112,64},{1... | collective-permute-start | bytes 221192 | tf_op jit(solution)/shard_map/ppermute | solution.py:23
  20.5 5.0 %collective-permute-start.6 = (bf16[48,768]{1,0:T(8,128)(2,1)S(1)}, bf16[48,768]{1,0:T(8,128)(2,1)S(1)}, u32[]{:S(2)}, u32[]{:S(2)}) collective-permute-start(bf16[48,768]{1,0:T(8,128)(2,1)S(1)} %convolution_convert_fusion), channel_id=1, source_target_pairs={{0,32},{16,48},{32,0},{48,16},{64,96},{80,112},{96,64},{112,80},{1... | collective-permute-start | bytes 221192 | tf_op jit(solution)/shard_map/ppermute | solution.py:23
  22.9 3.2 %collective-permute-start.5 = (bf16[48,768]{1,0:T(8,128)(2,1)S(1)}, bf16[48,768]{1,0:T(8,128)(2,1)S(1)}, u32[]{:S(2)}, u32[]{:S(2)}) collective-permute-start(bf16[48,768]{1,0:T(8,128)(2,1)S(1)} %convolution_convert_fusion), channel_id=1, source_target_pairs={{0,48},{16,0},{32,16},{48,32},{64,112},{80,64},{96,80},{112,96},{1... | collective-permute-start | bytes 221192 | tf_op jit(solution)/shard_map/ppermute | solution.py:23
  26.2 20.5 %copy-start.9 = (bf16[192,768]{1,0:T(8,128)(2,1)}, bf16[192,768]{1,0:T(8,128)(2,1)S(1)}, u32[]{:S(2)}) copy-start(bf16[192,768]{1,0:T(8,128)(2,1)S(1)} %pad_maximum_fusion.refs_2_) | copy-start | bytes 884740
  26.2 10.5 %collective-permute-start.10 = (bf16[192,768]{1,0:T(8,128)(2,1)S(1)}, bf16[192,768]{1,0:T(8,128)(2,1)S(1)}, u32[]{:S(2)}, u32[]{:S(2)}) collective-permute-start(bf16[192,768]{1,0:T(8,128)(2,1)S(1)} %pad_maximum_fusion.refs_2_), channel_id=1, source_target_pairs={{0,64},{16,80},{32,96},{48,112},{64,128},{80,144},{96,160},{112,17... | collective-permute-start | bytes 884744 | tf_op jit(solution)/shard_map/ppermute | solution.py:27
  27.6 13.7 %collective-permute-start.9 = (bf16[192,768]{1,0:T(8,128)(2,1)S(1)}, bf16[192,768]{1,0:T(8,128)(2,1)S(1)}, u32[]{:S(2)}, u32[]{:S(2)}) collective-permute-start(bf16[192,768]{1,0:T(8,128)(2,1)S(1)} %pad_maximum_fusion.refs_2_), channel_id=1, source_target_pairs={{0,128},{16,144},{32,160},{48,176},{64,192},{80,208},{96,224},{112... | collective-permute-start | bytes 884744 | tf_op jit(solution)/shard_map/ppermute | solution.py:27
  30.2 14.3 %collective-permute-start.8 = (bf16[192,768]{1,0:T(8,128)(2,1)S(1)}, bf16[192,768]{1,0:T(8,128)(2,1)S(1)}, u32[]{:S(2)}, u32[]{:S(2)}) collective-permute-start(bf16[192,768]{1,0:T(8,128)(2,1)S(1)} %pad_maximum_fusion.refs_2_), channel_id=1, source_target_pairs={{0,192},{16,208},{32,224},{48,240},{64,0},{80,16},{96,32},{112,48}... | collective-permute-start | bytes 884744 | tf_op jit(solution)/shard_map/ppermute | solution.py:27
  31.3 15.4 %collective-permute-start.11 = (bf16[192,768]{1,0:T(8,128)(2,1)S(1)}, bf16[192,768]{1,0:T(8,128)(2,1)S(1)}, u32[]{:S(2)}, u32[]{:S(2)}) collective-permute-start(bf16[192,768]{1,0:T(8,128)(2,1)S(1)} %pad_maximum_fusion.refs_2_), channel_id=1, source_target_pairs={{0,1},{1,0},{2,3},{3,2},{4,5},{5,4},{6,7},{7,6},{8,9},{9,8},{10,11... | collective-permute-start | bytes 884744 | tf_op jit(solution)/shard_map/ppermute | solution.py:35
  36.7 10.0 %copy-start.10 = (bf16[192,768]{1,0:T(8,128)(2,1)}, bf16[192,768]{1,0:T(8,128)(2,1)S(1)}, u32[]{:S(2)}) copy-start(bf16[192,768]{1,0:T(8,128)(2,1)S(1)} %collective-permute-done.10.refs_5_) | copy-start | bytes 884740
  36.7 10.0 %collective-permute-start.14 = (bf16[192,768]{1,0:T(8,128)(2,1)S(1)}, bf16[192,768]{1,0:T(8,128)(2,1)S(1)}, u32[]{:S(2)}, u32[]{:S(2)}) collective-permute-start(bf16[192,768]{1,0:T(8,128)(2,1)S(1)} %collective-permute-done.10.refs_5_), channel_id=1, source_target_pairs={{0,1},{1,0},{2,3},{3,2},{4,5},{5,4},{6,7},{7,6},{8,9},{9,8},{10,11... | collective-permute-start | bytes 884744 | tf_op jit(solution)/shard_map/ppermute | solution.py:35
  41.3 5.4 %copy-start.11 = (bf16[192,768]{1,0:T(8,128)(2,1)}, bf16[192,768]{1,0:T(8,128)(2,1)S(1)}, u32[]{:S(2)}) copy-start(bf16[192,768]{1,0:T(8,128)(2,1)S(1)} %collective-permute-done.9.refs_4_) | copy-start | bytes 884740
  41.3 5.3 %collective-permute-start.13 = (bf16[192,768]{1,0:T(8,128)(2,1)S(1)}, bf16[192,768]{1,0:T(8,128)(2,1)S(1)}, u32[]{:S(2)}, u32[]{:S(2)}) collective-permute-start(bf16[192,768]{1,0:T(8,128)(2,1)S(1)} %collective-permute-done.9.refs_4_), channel_id=1, source_target_pairs={{0,1},{1,0},{2,3},{3,2},{4,5},{5,4},{6,7},{7,6},{8,9},{9,8},{10,11... | collective-permute-start | bytes 884744 | tf_op jit(solution)/shard_map/ppermute | solution.py:35
  44.5 2.3 %copy-start.12 = (bf16[192,768]{1,0:T(8,128)(2,1)}, bf16[192,768]{1,0:T(8,128)(2,1)S(1)}, u32[]{:S(2)}) copy-start(bf16[192,768]{1,0:T(8,128)(2,1)S(1)} %collective-permute-done.8.refs_3_) | copy-start | bytes 884740
  44.5 2.2 %collective-permute-start.12 = (bf16[192,768]{1,0:T(8,128)(2,1)S(1)}, bf16[192,768]{1,0:T(8,128)(2,1)S(1)}, u32[]{:S(2)}, u32[]{:S(2)}) collective-permute-start(bf16[192,768]{1,0:T(8,128)(2,1)S(1)} %collective-permute-done.8.refs_3_), channel_id=1, source_target_pairs={{0,1},{1,0},{2,3},{3,2},{4,5},{5,4},{6,7},{7,6},{8,9},{9,8},{10,11... | collective-permute-start | bytes 884744 | tf_op jit(solution)/shard_map/ppermute | solution.py:35
  75.4 3.1 %collective-permute-start.15 = (bf16[768,768]{1,0:T(8,128)(2,1)}, bf16[768,768]{1,0:T(8,128)(2,1)S(1)}, u32[]{:S(2)}, u32[]{:S(2)}) collective-permute-start(bf16[768,768]{1,0:T(8,128)(2,1)} %get-tuple-element.25), channel_id=1, source_target_pairs={{0,1},{1,0},{2,3},{3,2},{4,5},{5,4},{6,7},{7,6},{8,9},{9,8},{10,11... | collective-permute-start | bytes 3538952 | tf_op jit(solution)/shard_map/ppermute | solution.py:35
  84.2 39.7 %copy-start = (bf16[1536,1152]{1,0:T(8,128)(2,1)S(1)}, bf16[1536,1152]{1,0:T(8,128)(2,1)}, u32[]{:S(2)}) copy-start(bf16[1536,1152]{1,0:T(8,128)(2,1)} %get-tuple-element.19.gp_ref) | copy-start | bytes 10616836
  84.2 39.7 %copy-start.5 = (f32[1,768]{1,0:T(1,128)S(1)}, f32[1,768]{1,0:T(1,128)}, u32[]{:S(2)}) copy-start(f32[1,768]{1,0:T(1,128)} %broadcast_in_dim.25.refs_12_.gain_ref) | copy-start | bytes 9220
  84.2 39.7 %copy-start.6 = (s32[1,12]{1,0:T(1,128)S(1)}, s32[1,12]{1,0:T(1,128)}, u32[]{:S(2)}) copy-start(s32[1,12]{1,0:T(1,128)} %param.8) | copy-start | bytes 148
  84.2 10.0 %collective-permute-start.16 = (bf16[192,768]{1,0:T(8,128)(2,1)}, bf16[192,768]{1,0:T(8,128)(2,1)}, u32[]{:S(2)}, u32[]{:S(2)}) collective-permute-start(bf16[192,768]{1,0:T(8,128)(2,1)} %get-tuple-element.27), channel_id=1, source_target_pairs={{0,64},{16,80},{32,96},{48,112},{64,128},{80,144},{96,160},{112,17... | collective-permute-start | bytes 884744 | tf_op jit(solution)/shard_map/ppermute | solution.py:27
  85.0 15.8 %collective-permute-start.17 = (bf16[192,768]{1,0:T(8,128)(2,1)}, bf16[192,768]{1,0:T(8,128)(2,1)}, u32[]{:S(2)}, u32[]{:S(2)}) collective-permute-start(bf16[192,768]{1,0:T(8,128)(2,1)} %get-tuple-element.28), channel_id=1, source_target_pairs={{0,128},{16,144},{32,160},{48,176},{64,192},{80,208},{96,224},{112... | collective-permute-start | bytes 884744 | tf_op jit(solution)/shard_map/ppermute | solution.py:27
  87.1 13.8 %collective-permute-start.18 = (bf16[192,768]{1,0:T(8,128)(2,1)}, bf16[192,768]{1,0:T(8,128)(2,1)}, u32[]{:S(2)}, u32[]{:S(2)}) collective-permute-start(bf16[192,768]{1,0:T(8,128)(2,1)} %get-tuple-element.29), channel_id=1, source_target_pairs={{0,192},{16,208},{32,224},{48,240},{64,0},{80,16},{96,32},{112,48}... | collective-permute-start | bytes 884744 | tf_op jit(solution)/shard_map/ppermute | solution.py:27
  103.8 4.7 %collective-permute-start.19 = (bf16[48,768]{1,0:T(8,128)(2,1)}, bf16[48,768]{1,0:T(8,128)(2,1)}, u32[]{:S(2)}, u32[]{:S(2)}) collective-permute-start(bf16[48,768]{1,0:T(8,128)(2,1)} %get-tuple-element.30), channel_id=1, source_target_pairs={{0,16},{16,32},{32,48},{48,0},{64,80},{80,96},{96,112},{112,64},{1... | collective-permute-start | bytes 221192 | tf_op jit(solution)/shard_map/ppermute | solution.py:23
  104.5 4.1 %collective-permute-start.21 = (bf16[48,768]{1,0:T(8,128)(2,1)}, bf16[48,768]{1,0:T(8,128)(2,1)}, u32[]{:S(2)}, u32[]{:S(2)}) collective-permute-start(bf16[48,768]{1,0:T(8,128)(2,1)} %get-tuple-element.31), channel_id=1, source_target_pairs={{0,48},{16,0},{32,16},{48,32},{64,112},{80,64},{96,80},{112,96},{1... | collective-permute-start | bytes 221192 | tf_op jit(solution)/shard_map/ppermute | solution.py:23
  106.5 5.5 %collective-permute-start.20 = (bf16[48,768]{1,0:T(8,128)(2,1)}, bf16[48,768]{1,0:T(8,128)(2,1)}, u32[]{:S(2)}, u32[]{:S(2)}) collective-permute-start(bf16[48,768]{1,0:T(8,128)(2,1)} %get-tuple-element.32), channel_id=1, source_target_pairs={{0,32},{16,48},{32,0},{48,16},{64,96},{80,112},{96,64},{112,80},{1... | collective-permute-start | bytes 221192 | tf_op jit(solution)/shard_map/ppermute | solution.py:23
  115.4 24.2 %all-to-all-start = ((f32[16,3,768]{2,1,0:T(4,128)}), f32[16,3,768]{2,1,0:T(4,128)}, u32[]{:S(2)}, u32[]{:S(2)}) async-start(f32[16,3,768]{2,1,0:T(4,128)} %reshape.185), calls=%async_computation | async-start | bytes 393216 | tf_op jit(solution)/shard_map/all_to_all | solution.py:87
  124.0 1.7 %copy-start.1 = (bf16[1,12,128,768]{3,2,1,0:T(8,128)(2,1)S(1)}, bf16[1,12,128,768]{3,2,1,0:T(8,128)(2,1)}, u32[]{:S(2)}) copy-start(bf16[1,12,128,768]{3,2,1,0:T(8,128)(2,1)} %param.6) | copy-start | bytes 7077892
  125.7 1.7 %copy-start.2 = (bf16[1,12,128,768]{3,2,1,0:T(8,128)(2,1)S(1)}, bf16[1,12,128,768]{3,2,1,0:T(8,128)(2,1)}, u32[]{:S(2)}) copy-start(bf16[1,12,128,768]{3,2,1,0:T(8,128)(2,1)} %param.7) | copy-start | bytes 7077892
  (8 other events, 8.4 us)

commit v4 on v3

--- a/solution.py
+++ b/solution.py
@@ -71,22 +71,6 @@
     v = jnp.concatenate(gather4(v, hop_x, True), axis=0)
     mine = gather4(v, hop_y, True)
     return mine + [hop_core(u) for u in mine]
-
-
-def scatter4(parts, hop):
-    got = [hop(parts[k].astype(BF16), k) for k in (1, 2, 3)]
-    return parts[0] + got[0].astype(F32) + got[1].astype(F32) + got[2].astype(F32)
-
-
-def scatter_grads(at, keep, send):
-    y, x, z, c = coords()
-    n = keep.shape[1]
-    v = scatter4(split_rows(at, keep, hop_core(send)), hop_y)
-    rows = v.shape[0] // 4
-    v = scatter4([lax.dynamic_slice(v, (((x + k) % 4) * rows, 0), (rows, n)) for k in range(4)], hop_x)
-    got = lax.all_to_all(v.reshape(16, 3, n), "xl", split_axis=0, concat_axis=0, tiled=True)
-    acc = jnp.sum(got.reshape(8, 2, 3, n), axis=0)
-    return jnp.concatenate([acc[0], acc[1]], axis=1)
 
 
 def mm(a, b):
@@ -242,7 +226,7 @@
             num_scalar_prefetch=2,
             grid=(nblock // GROUP,),
             in_specs=[hbm] * 8 + [tile, tile, pl.BlockSpec((1, D), lambda i, *_: (0, 0))],
-            out_specs=[hbm] * 5,
+            out_specs=[hbm] * 3 + [pl.BlockSpec(memory_space=pl.ANY)] * 2,
             scratch_shapes=[
                 pltpu.VMEM((2, D, D), BF16),
                 pltpu.VMEM((rows, D), BF16),
@@ -264,7 +248,7 @@
             jax.ShapeDtypeStruct((D, D), BF16),
         ],
         compiler_params=pltpu.CompilerParams(
-            dimension_semantics=("arbitrary",), vmem_limit_bytes=56 * 1024 * 1024
+            dimension_semantics=("arbitrary",), vmem_limit_bytes=28 * 1024 * 1024
         ),
         cost_estimate=pl.CostEstimate(flops=20_000_000_000, bytes_accessed=18_000_000, transcendentals=1_200_000),
     )(at, counts, *pieces, tiles, cotan, gain)
@@ -303,13 +287,13 @@
                 tile,
                 pl.BlockSpec((1, D), lambda i, *_: (0, 0)),
             ]
-            + [pl.BlockSpec(memory_space=pltpu.HBM)] * len(done),
+            + [pl.BlockSpec(memory_space=pl.ANY)] * len(done),
             out_specs=[tile, tile],
         ),
         out_shape=[jax.ShapeDtypeStruct(tiles.shape, BF16)] * 2,
         input_output_aliases={7 + i: i for i in range(len(done))},
         compiler_params=pltpu.CompilerParams(
-            dimension_semantics=("arbitrary",), vmem_limit_bytes=40 * 1024 * 1024
+            dimension_semantics=("arbitrary",), vmem_limit_bytes=60 * 1024 * 1024
         ),
         cost_estimate=pl.CostEstimate(
             flops=count * 1_300_000_000, bytes_accessed=count * 5_000_000, transcendentals=1000
@@ -317,35 +301,63 @@
     )(counts, w, att, gp, tiles, cotan, gain, *done)
 
 
-def split_kernel(at_ref, keep_ref, got_ref, own_ref, *outs):
-    step = pl.program_id(0)
-    total = keep_ref[...] + got_ref[...].astype(F32)
-
-    @pl.when(step == 0)
-    def _():
-        own_ref[...] = total
-
-    for k in range(1, 4):
-
-        @pl.when(step == k)
-        def _():
-            outs[k - 1][...] = total.astype(BF16)
-
-
-def split_rows(at, keep, got):
-    rows = keep.shape[0] // 4
+def small_call(kernel, at, args, outs):
+    smem = [] if at is None else [pl.BlockSpec(memory_space=pltpu.SMEM)]
+    vmem = pl.BlockSpec(memory_space=pltpu.VMEM)
+    size = sum(a.size * a.dtype.itemsize for a in args)
+    return pl.pallas_call(
+        kernel,
+        in_specs=smem + [vmem] * len(args),
+        out_specs=[vmem] * len(outs),
+        out_shape=[jax.ShapeDtypeStruct(shape, dtype) for shape, dtype in outs],
+        compiler_params=pltpu.CompilerParams(vmem_limit_bytes=12 * 1024 * 1024),
+        cost_estimate=pl.CostEstimate(flops=size, bytes_accessed=2 * size, transcendentals=0),
+    )(*([] if at is None else [at]), *args)
+
+
+def cut_kernel(axis, at_ref, own_ref, *refs):
+    got, outs = refs[:-4], refs[-4:]
+    rows = outs[0].shape[0]
+    for k in range(4):
+        at = pl.ds(pl.multiple_of(((at_ref[axis] + k) & 3) * rows, rows), rows)
+        total = own_ref[at, :]
+        for ref in got:
+            total = total + ref[at, :].astype(F32)
+        outs[k][...] = total.astype(outs[k].dtype)
+
+
+def cut(at, axis, own, *got):
+    rows, n = own.shape[0] // 4, own.shape[1]
+    outs = [((rows, n), F32)] + [((rows, n), BF16)] * 3
+    return small_call(functools.partial(cut_kernel, axis), at, [own, *got], outs)
+
+
+def triples_kernel(own_ref, *refs):
+    total = own_ref[...]
+    for ref in refs[:-1]:
+        total = total + ref[...].astype(F32)
+    for i in range(16):
+        refs[-1][i] = total[3 * i : 3 * i + 3, :]
+
+
+def finish_kernel(got_ref, qkv_ref, out_ref):
+    lo, hi = got_ref[0], got_ref[1]
+    for z in range(1, 8):
+        lo = lo + got_ref[2 * z]
+        hi = hi + got_ref[2 * z + 1]
+    qkv_ref[:, :D] = lo
+    qkv_ref[:, D:] = hi[:, :HD]
+    out_ref[...] = hi[:, HD:]
+
+
+def scatter_grads(at, keep, send):
+    own, *out = cut(at, 0, keep, hop_core(send))
+    own, *out = cut(at, 1, own, *[hop_y(v, k + 1) for k, v in enumerate(out)])
+    parts = [own] + [hop_x(v, k + 1) for k, v in enumerate(out)]
     n = keep.shape[1]
-    block = pl.BlockSpec((rows, n), lambda i, at: ((at[0] + i) % 4, 0))
-    out = pl.BlockSpec((rows, n), lambda i, at: (0, 0))
-    return pl.pallas_call(
-        split_kernel,
-        grid_spec=pltpu.PrefetchScalarGridSpec(
-            num_scalar_prefetch=1, grid=(4,), in_specs=[block, block], out_specs=[out] * 4
-        ),
-        out_shape=[jax.ShapeDtypeStruct((rows, n), F32)] + [jax.ShapeDtypeStruct((rows, n), BF16)] * 3,
-        compiler_params=pltpu.CompilerParams(dimension_semantics=("arbitrary",)),
-        cost_estimate=pl.CostEstimate(flops=600_000, bytes_accessed=5_000_000, transcendentals=0),
-    )(at, keep, got)
+    (v,) = small_call(triples_kernel, None, parts, [((16, 3, n), F32)])
+    got = lax.all_to_all(v, "xl", split_axis=0, concat_axis=0, tiled=True)
+    return small_call(finish_kernel, None, [got], [((3, n + n // 2), F32), ((3, n // 2), F32)])
 
 
 def shards(patches, out_cot, vis_count, w_qkv, w_out, ln_gain):
@@ -356,9 +368,8 @@
     w, att, gp, keep, send = grads_core(at, counts, pieces, tiles, cotan, gain)
     out = rows_part(0, 1, counts, w, att, gp, tiles, cotan, gain, ())
     enc, gin = rows_part(1, 2, counts, w, att, gp, tiles, cotan, gain, out)
-    grads = scatter_grads(at, keep, send)
-    n = w_qkv.shape[1]
-    return enc[None], gin[None], grads[:, :n], grads[:, n:]
+    grad_qkv, grad_out = scatter_grads(at, keep, send)
+    return enc[None], gin[None], grad_qkv, grad_out
 
 
 def solution(mesh):

time: 142 us -> 134 us (0.944)
  local copies, waits for them, and re-layouts: 14.8 us -> 7.53 us
  Pallas kernels: 41.6 us -> 47.4 us
  other arithmetic: 5.43 us -> 0.16 us
    pallas_call x2, Pallas kernels: 9.32 us -> 15.2 us  [rows_part(): pl.pallas_call(functools.partial(rows_kernel, first), grid_spec=pltpu.Pre...]
    unnamed x35 -> x15, local copies, waits for them, and re-layouts: 9.88 us -> 6.11 us
    add x2 -> x0, other arithmetic: 3.16 us -> none  [scatter4(): parts[0] + got[0].astype(F32) + got[1].astype(F32) + got[2].astype(F32)]
    pallas_call x1 -> x4, Pallas kernels: 4.63 us -> 2.85 us  [small_call(): pl.pallas_call(kernel, in_specs=smem + [vmem] * len(args), out_specs=[vme...]
    pallas_call x1, Pallas kernels: 27.7 us -> 29.4 us  [grads_core(): pl.pallas_call(core_kernel, grid_spec=pltpu.PrefetchScalarGridSpec(num_sc...]
    reshape x1 -> x0, local copies, waits for them, and re-layouts: 1.67 us -> none  [scatter_grads(): v.reshape(16, 3, n)]
  transfers between devices with their start and end apart: 23 -> 23, of which waited for: 12 -> 15; matrix products, arithmetic and copies ran while one was open for 1% -> 1% of each run, Pallas kernels for 7% -> 11%
where the time goes in v4:
time: 134 us
  starting transfers between devices  51.3 us (38%)
  Pallas kernels  47.4 us (35%)
  waiting for transfers between devices  26.7 us (20%)
  local copies, waits for them, and re-layouts  7.53 us (6%)
    pallas_call x1, Pallas kernels, grads_core(): pl.pallas_call(core_kernel, grid_spec=pltpu.PrefetchScalarGridSpec(num_sc...  29.4 us
    ppermute x6, starting transfers between devices, hop_core(): return lax.ppermute(v, 'xl', [(i, i ^ 1) for i in range(16)])  16.9 us
    pallas_call x2, Pallas kernels, rows_part(): pl.pallas_call(functools.partial(rows_kernel, first), grid_spec=pltpu.Pre...  15.2 us
    ppermute x6, waiting for transfers between devices, hop_y(): return lax.ppermute(v, 'il', [(i, (i + 4 * k) % 16) for i in range(16)])  12.1 us
    ppermute x6, starting transfers between devices, hop_y(): return lax.ppermute(v, 'il', [(i, (i + 4 * k) % 16) for i in range(16)])  9.13 us
    ppermute x6, starting transfers between devices, hop_x(): lax.ppermute(v, 'il', [(i, i // 4 * 4 + (i + k) % 4) for i in range(16)])  8.99 us
    all_to_all x1, starting transfers between devices, scatter_grads(): got = lax.all_to_all(v, 'xl', split_axis=0, concat_axis=0, tiled=True)  8.56 us
    ppermute x3, starting transfers between devices, hop_z(): return lax.ppermute(v, 'xl', [(i, (i + 2 * k) % 16) for i in range(16)])  7.63 us
  transfers between devices with their start and end apart: 23, of which 15 were waited for; matrix products, arithmetic and copies ran while one was open for 1% of the time, Pallas kernels for 11%

profile of v4, /device:TPU:1, one launch (start us, length us, event | category | flops | bytes accessed | tf_op | source)
XLA Modules:
  0.0 134.0 jit_solution(6418427548653294658)
XLA Ops:
  2.1 3.3 %collective-permute-start = (bf16[3,768]{1,0:T(4,128)(2,1)S(1)}, bf16[3,768]{1,0:T(4,128)(2,1)S(1)}, u32[]{:S(2)}, u32[]{:S(2)}) collective-permute-start(bf16[3,768]{1,0:T(4,128)(2,1)S(1)} %get-tuple-element.42), channel_id=1, source_target_pairs={{0,1},{1,0},{2,3},{3,2},{4,5},{5,4},{6,7},{7,6},{8,9},{9,8},{10,11... | collective-permute-start | bytes 13832 | tf_op jit(solution)/shard_map/ppermute | solution.py:35
  5.4 0.8 collective-permute-done
  6.4 2.5 %collective-permute-done.1 = bf16[8,768]{1,0:T(8,128)(2,1)S(1)} collective-permute-done((bf16[8,768]{1,0:T(8,128)(2,1)S(1)}, bf16[8,768]{1,0:T(8,128)(2,1)S(1)}, u32[]{:S(2)}, u32[]{:S(2)}) %collective-permute-start.1) | collective-permute-done | bytes 12320 | tf_op jit(solution)/shard_map/ppermute | solution.py:61
  8.9 5.3 %collective-permute-start.4 = (bf16[16,768]{1,0:T(8,128)(2,1)S(1)}, bf16[16,768]{1,0:T(8,128)(2,1)S(1)}, u32[]{:S(2)}, u32[]{:S(2)}) collective-permute-start(bf16[16,768]{1,0:T(8,128)(2,1)S(1)} %pad_maximum_fusion.1), channel_id=1, source_target_pairs={{0,8},{1,9},{2,10},{3,11},{4,12},{5,13},{6,14},{7,15},{8,0},{9,1},... | collective-permute-start | bytes 73736 | tf_op jit(solution)/shard_map/ppermute | solution.py:31
  14.2 2.4 %collective-permute-start.2 = (bf16[16,768]{1,0:T(8,128)(2,1)S(1)}, bf16[16,768]{1,0:T(8,128)(2,1)S(1)}, u32[]{:S(2)}, u32[]{:S(2)}) collective-permute-start(bf16[16,768]{1,0:T(8,128)(2,1)S(1)} %pad_maximum_fusion.1), channel_id=1, source_target_pairs={{0,4},{1,5},{2,6},{3,7},{4,8},{5,9},{6,10},{7,11},{8,12},{9,13},{1... | collective-permute-start | bytes 73736 | tf_op jit(solution)/shard_map/ppermute | solution.py:31
  16.6 1.3 collective-permute-done.3
  17.8 1.2 collective-permute-done.2
  19.2 1.3 collective-permute-start.7
  20.5 2.5 %collective-permute-start.6 = (bf16[48,768]{1,0:T(8,128)(2,1)S(1)}, bf16[48,768]{1,0:T(8,128)(2,1)S(1)}, u32[]{:S(2)}, u32[]{:S(2)}) collective-permute-start(bf16[48,768]{1,0:T(8,128)(2,1)S(1)} %convolution_convert_fusion), channel_id=1, source_target_pairs={{0,32},{16,48},{32,0},{48,16},{64,96},{80,112},{96,64},{112,80},{1... | collective-permute-start | bytes 221192 | tf_op jit(solution)/shard_map/ppermute | solution.py:23
  22.9 1.2 collective-permute-start.5
  24.1 1.4 %collective-permute-done.6 = bf16[48,768]{1,0:T(8,128)(2,1)S(1)} collective-permute-done((bf16[48,768]{1,0:T(8,128)(2,1)S(1)}, bf16[48,768]{1,0:T(8,128)(2,1)S(1)}, u32[]{:S(2)}, u32[]{:S(2)}) %collective-permute-start.6) | collective-permute-done | bytes 73760 | tf_op jit(solution)/shard_map/ppermute | solution.py:23
  26.2 1.4 %collective-permute-start.10 = (bf16[192,768]{1,0:T(8,128)(2,1)S(1)}, bf16[192,768]{1,0:T(8,128)(2,1)S(1)}, u32[]{:S(2)}, u32[]{:S(2)}) collective-permute-start(bf16[192,768]{1,0:T(8,128)(2,1)S(1)} %pad_maximum_fusion.refs_2_), channel_id=1, source_target_pairs={{0,64},{16,80},{32,96},{48,112},{64,128},{80,144},{96,160},{112,17... | collective-permute-start | bytes 884744 | tf_op jit(solution)/shard_map/ppermute | solution.py:27
  27.6 2.6 %collective-permute-start.9 = (bf16[192,768]{1,0:T(8,128)(2,1)S(1)}, bf16[192,768]{1,0:T(8,128)(2,1)S(1)}, u32[]{:S(2)}, u32[]{:S(2)}) collective-permute-start(bf16[192,768]{1,0:T(8,128)(2,1)S(1)} %pad_maximum_fusion.refs_2_), channel_id=1, source_target_pairs={{0,128},{16,144},{32,160},{48,176},{64,192},{80,208},{96,224},{112... | collective-permute-start | bytes 884744 | tf_op jit(solution)/shard_map/ppermute | solution.py:27
  30.2 1.1 collective-permute-start.8
  31.2 5.4 %collective-permute-start.11 = (bf16[192,768]{1,0:T(8,128)(2,1)S(1)}, bf16[192,768]{1,0:T(8,128)(2,1)S(1)}, u32[]{:S(2)}, u32[]{:S(2)}) collective-permute-start(bf16[192,768]{1,0:T(8,128)(2,1)S(1)} %pad_maximum_fusion.refs_2_), channel_id=1, source_target_pairs={{0,1},{1,0},{2,3},{3,2},{4,5},{5,4},{6,7},{7,6},{8,9},{9,8},{10,11... | collective-permute-start | bytes 884744 | tf_op jit(solution)/shard_map/ppermute | solution.py:35
  36.6 4.6 %collective-permute-start.14 = (bf16[192,768]{1,0:T(8,128)(2,1)S(1)}, bf16[192,768]{1,0:T(8,128)(2,1)S(1)}, u32[]{:S(2)}, u32[]{:S(2)}) collective-permute-start(bf16[192,768]{1,0:T(8,128)(2,1)S(1)} %collective-permute-done.10.refs_5_), channel_id=1, source_target_pairs={{0,1},{1,0},{2,3},{3,2},{4,5},{5,4},{6,7},{7,6},{8,9},{9,8},{10,11... | collective-permute-start | bytes 884744 | tf_op jit(solution)/shard_map/ppermute | solution.py:35
  41.3 3.2 %collective-permute-start.13 = (bf16[192,768]{1,0:T(8,128)(2,1)S(1)}, bf16[192,768]{1,0:T(8,128)(2,1)S(1)}, u32[]{:S(2)}, u32[]{:S(2)}) collective-permute-start(bf16[192,768]{1,0:T(8,128)(2,1)S(1)} %collective-permute-done.9.refs_4_), channel_id=1, source_target_pairs={{0,1},{1,0},{2,3},{3,2},{4,5},{5,4},{6,7},{7,6},{8,9},{9,8},{10,11... | collective-permute-start | bytes 884744 | tf_op jit(solution)/shard_map/ppermute | solution.py:35
  46.1 1.7 %copy-done.1 = bf16[1,12,128,768]{3,2,1,0:T(8,128)(2,1)S(1)} copy-done((bf16[1,12,128,768]{3,2,1,0:T(8,128)(2,1)S(1)}, bf16[1,12,128,768]{3,2,1,0:T(8,128)(2,1)}, u32[]{:S(2)}) %copy-start.1) | copy-done | bytes 2359320
  47.8 1.7 %copy-done.2 = bf16[1,12,128,768]{3,2,1,0:T(8,128)(2,1)S(1)} copy-done((bf16[1,12,128,768]{3,2,1,0:T(8,128)(2,1)S(1)}, bf16[1,12,128,768]{3,2,1,0:T(8,128)(2,1)}, u32[]{:S(2)}) %copy-start.2) | copy-done | bytes 2359320
  50.1 29.4 %shard_map.93 = (bf16[2,768,768]{2,1,0:T(8,128)(2,1)S(1)}, bf16[1536,384]{1,0:T(8,128)(2,1)S(1)}, bf16[1536,1152]{1,0:T(8,128)(2,1)S(1)}, f32[768,768]{1,0:T(8,128)S(1)}, bf16[768,768]{1,0:T(8,128)(2,1)S(1)}) custom-call(s32[3]{0:T(128)S(1)} %pad_add_fusion.refs_0_.at_ref, s32[12]{0:T(128)S(1)} %bitcast.17, bf16[192,768]{1,0:T(8,128)(2,1)S(1)} %pad_maximum_fusion.refs_2_, ...), custom_call_target="tpu_custom_call" | custom-call | flops 20000000000 | bytes 18000000 | tf_op jit(solution)/shard_map/pallas_call | solution.py:223
  79.5 1.4 %copy-done.3 = bf16[2,768,768]{2,1,0:T(8,128)(2,1)} copy-done((bf16[2,768,768]{2,1,0:T(8,128)(2,1)}, bf16[2,768,768]{2,1,0:T(8,128)(2,1)S(1)}, u32[]{:S(2)}) %copy-start.3) | copy-done | bytes 2359320
  81.3 2.5 %collective-permute-done.15.refs_0_ = bf16[768,768]{1,0:T(8,128)(2,1)S(1)} collective-permute-done((bf16[768,768]{1,0:T(8,128)(2,1)S(1)}, bf16[768,768]{1,0:T(8,128)(2,1)S(1)}, u32[]{:S(2)}, u32[]{:S(2)}) %collective-permute-start.15) | collective-permute-done | bytes 1179680 | tf_op jit(solution)/shard_map/ppermute | solution.py:35
  85.2 2.1 %collective-permute-start.17 = (bf16[192,768]{1,0:T(8,128)(2,1)S(1)}, bf16[192,768]{1,0:T(8,128)(2,1)S(1)}, u32[]{:S(2)}, u32[]{:S(2)}) collective-permute-start(bf16[192,768]{1,0:T(8,128)(2,1)S(1)} %get-tuple-element.34), channel_id=1, source_target_pairs={{0,128},{16,144},{32,160},{48,176},{64,192},{80,208},{96,224},{112... | collective-permute-start | bytes 884744 | tf_op jit(solution)/shard_map/ppermute | solution.py:27
  87.3 1.3 %collective-permute-start.18 = (bf16[192,768]{1,0:T(8,128)(2,1)S(1)}, bf16[192,768]{1,0:T(8,128)(2,1)S(1)}, u32[]{:S(2)}, u32[]{:S(2)}) collective-permute-start(bf16[192,768]{1,0:T(8,128)(2,1)S(1)} %get-tuple-element.35), channel_id=1, source_target_pairs={{0,192},{16,208},{32,224},{48,240},{64,0},{80,16},{96,32},{112,48}... | collective-permute-start | bytes 884744 | tf_op jit(solution)/shard_map/ppermute | solution.py:27
  88.6 5.5 %collective-permute-done.16.refs_0_ = bf16[192,768]{1,0:T(8,128)(2,1)S(1)} collective-permute-done((bf16[192,768]{1,0:T(8,128)(2,1)S(1)}, bf16[192,768]{1,0:T(8,128)(2,1)S(1)}, u32[]{:S(2)}, u32[]{:S(2)}) %collective-permute-start.16) | collective-permute-done | bytes 294944 | tf_op jit(solution)/shard_map/ppermute | solution.py:27
  94.1 6.3 %collective-permute-done.17.refs_1_ = bf16[192,768]{1,0:T(8,128)(2,1)S(1)} collective-permute-done((bf16[192,768]{1,0:T(8,128)(2,1)S(1)}, bf16[192,768]{1,0:T(8,128)(2,1)S(1)}, u32[]{:S(2)}, u32[]{:S(2)}) %collective-permute-start.17) | collective-permute-done | bytes 294944 | tf_op jit(solution)/shard_map/ppermute | solution.py:27
  102.2 2.9 %collective-permute-start.20 = (bf16[48,768]{1,0:T(8,128)(2,1)S(1)}, bf16[48,768]{1,0:T(8,128)(2,1)S(1)}, u32[]{:S(2)}, u32[]{:S(2)}) collective-permute-start(bf16[48,768]{1,0:T(8,128)(2,1)S(1)} %get-tuple-element.38), channel_id=1, source_target_pairs={{0,32},{16,48},{32,0},{48,16},{64,96},{80,112},{96,64},{112,80},{1... | collective-permute-start | bytes 221192 | tf_op jit(solution)/shard_map/ppermute | solution.py:23
  105.9 1.7 %collective-permute-done.20.refs_1_ = bf16[48,768]{1,0:T(8,128)(2,1)S(1)} collective-permute-done((bf16[48,768]{1,0:T(8,128)(2,1)S(1)}, bf16[48,768]{1,0:T(8,128)(2,1)S(1)}, u32[]{:S(2)}, u32[]{:S(2)}) %collective-permute-start.20) | collective-permute-done | bytes 73760 | tf_op jit(solution)/shard_map/ppermute | solution.py:23
  107.6 1.3 collective-permute-done.21.refs_2_
  109.6 8.6 %all-to-all-start = ((f32[16,3,768]{2,1,0:T(4,128)}), f32[16,3,768]{2,1,0:T(4,128)S(1)}, u32[]{:S(2)}, u32[]{:S(2)}) async-start(f32[16,3,768]{2,1,0:T(4,128)} %shard_map.98), calls=%async_computation | async-start | bytes 393216 | tf_op jit(solution)/shard_map/all_to_all | solution.py:359
  118.2 6.3 %shard_map.94 = (bf16[12,128,768]{2,1,0:T(8,128)(2,1)}, bf16[12,128,768]{2,1,0:T(8,128)(2,1)}) custom-call(s32[12]{0:T(128)} %bitcast.15, bf16[2,768,768]{2,1,0:T(8,128)(2,1)} %copy-done.3, bf16[1536,384]{1,0:T(8,128)(2,1)} %copy-done.4, bf16[1536,1152]{1,0:T(8,128)(2,1)} %copy-done, bf16[12,128,768]{2,1,0:T(8,128)(2,1)} %bitcast.9, ...), custom_call_target="tpu_custom_call" | custom-call | flops 1300000000 | bytes 5000000 | tf_op jit(solution)/shard_map/pallas_call | solution.py:277
  124.4 8.9 %shard_map.95 = (bf16[12,128,768]{2,1,0:T(8,128)(2,1)}, bf16[12,128,768]{2,1,0:T(8,128)(2,1)}) custom-call(s32[12]{0:T(128)} %bitcast.16, bf16[2,768,768]{2,1,0:T(8,128)(2,1)} %copy-done.3, bf16[1536,384]{1,0:T(8,128)(2,1)} %copy-done.4, bf16[1536,1152]{1,0:T(8,128)(2,1)} %copy-done, ...), custom_call_target="tpu_custom_call", output_to_operand_aliasing={{0}: (7, {}), {1}: (8, {})} | custom-call | flops 2600000000 | bytes 10000000 | tf_op jit(solution)/shard_map/pallas_call | solution.py:277
  (48 shorter events, 10.6 us)
Async XLA Ops:
  2.1 4.2 %collective-permute-start = (bf16[3,768]{1,0:T(4,128)(2,1)S(1)}, bf16[3,768]{1,0:T(4,128)(2,1)S(1)}, u32[]{:S(2)}, u32[]{:S(2)}) collective-permute-start(bf16[3,768]{1,0:T(4,128)(2,1)S(1)} %get-tuple-element.42), channel_id=1, source_target_pairs={{0,1},{1,0},{2,3},{3,2},{4,5},{5,4},{6,7},{7,6},{8,9},{9,8},{10,11... | collective-permute-start | bytes 13832 | tf_op jit(solution)/shard_map/ppermute | solution.py:35
  6.2 2.6 %collective-permute-start.1 = (bf16[8,768]{1,0:T(8,128)(2,1)S(1)}, bf16[8,768]{1,0:T(8,128)(2,1)S(1)}, u32[]{:S(2)}, u32[]{:S(2)}) collective-permute-start(bf16[8,768]{1,0:T(8,128)(2,1)S(1)} %pad_maximum_fusion.2), channel_id=1, source_target_pairs={{0,2},{1,3},{2,0},{3,1},{4,6},{5,7},{6,4},{7,5},{8,10},{9,11},{10,... | collective-permute-start | bytes 36872 | tf_op jit(solution)/shard_map/ppermute | solution.py:61
  8.9 7.6 %collective-permute-start.4 = (bf16[16,768]{1,0:T(8,128)(2,1)S(1)}, bf16[16,768]{1,0:T(8,128)(2,1)S(1)}, u32[]{:S(2)}, u32[]{:S(2)}) collective-permute-start(bf16[16,768]{1,0:T(8,128)(2,1)S(1)} %pad_maximum_fusion.1), channel_id=1, source_target_pairs={{0,8},{1,9},{2,10},{3,11},{4,12},{5,13},{6,14},{7,15},{8,0},{9,1},... | collective-permute-start | bytes 73736 | tf_op jit(solution)/shard_map/ppermute | solution.py:31
  14.2 3.7 %collective-permute-start.3 = (bf16[16,768]{1,0:T(8,128)(2,1)S(1)}, bf16[16,768]{1,0:T(8,128)(2,1)S(1)}, u32[]{:S(2)}, u32[]{:S(2)}) collective-permute-start(bf16[16,768]{1,0:T(8,128)(2,1)S(1)} %pad_maximum_fusion.1), channel_id=1, source_target_pairs={{0,12},{1,13},{2,14},{3,15},{4,0},{5,1},{6,2},{7,3},{8,4},{9,5},{1... | collective-permute-start | bytes 73736 | tf_op jit(solution)/shard_map/ppermute | solution.py:31
  14.2 4.9 %collective-permute-start.2 = (bf16[16,768]{1,0:T(8,128)(2,1)S(1)}, bf16[16,768]{1,0:T(8,128)(2,1)S(1)}, u32[]{:S(2)}, u32[]{:S(2)}) collective-permute-start(bf16[16,768]{1,0:T(8,128)(2,1)S(1)} %pad_maximum_fusion.1), channel_id=1, source_target_pairs={{0,4},{1,5},{2,6},{3,7},{4,8},{5,9},{6,10},{7,11},{8,12},{9,13},{1... | collective-permute-start | bytes 73736 | tf_op jit(solution)/shard_map/ppermute | solution.py:31
  19.2 4.9 %collective-permute-start.7 = (bf16[48,768]{1,0:T(8,128)(2,1)S(1)}, bf16[48,768]{1,0:T(8,128)(2,1)S(1)}, u32[]{:S(2)}, u32[]{:S(2)}) collective-permute-start(bf16[48,768]{1,0:T(8,128)(2,1)S(1)} %convolution_convert_fusion), channel_id=1, source_target_pairs={{0,16},{16,32},{32,48},{48,0},{64,80},{80,96},{96,112},{112,64},{1... | collective-permute-start | bytes 221192 | tf_op jit(solution)/shard_map/ppermute | solution.py:23
  20.5 5.0 %collective-permute-start.6 = (bf16[48,768]{1,0:T(8,128)(2,1)S(1)}, bf16[48,768]{1,0:T(8,128)(2,1)S(1)}, u32[]{:S(2)}, u32[]{:S(2)}) collective-permute-start(bf16[48,768]{1,0:T(8,128)(2,1)S(1)} %convolution_convert_fusion), channel_id=1, source_target_pairs={{0,32},{16,48},{32,0},{48,16},{64,96},{80,112},{96,64},{112,80},{1... | collective-permute-start | bytes 221192 | tf_op jit(solution)/shard_map/ppermute | solution.py:23
  22.9 3.2 %collective-permute-start.5 = (bf16[48,768]{1,0:T(8,128)(2,1)S(1)}, bf16[48,768]{1,0:T(8,128)(2,1)S(1)}, u32[]{:S(2)}, u32[]{:S(2)}) collective-permute-start(bf16[48,768]{1,0:T(8,128)(2,1)S(1)} %convolution_convert_fusion), channel_id=1, source_target_pairs={{0,48},{16,0},{32,16},{48,32},{64,112},{80,64},{96,80},{112,96},{1... | collective-permute-start | bytes 221192 | tf_op jit(solution)/shard_map/ppermute | solution.py:23
  26.2 10.5 %collective-permute-start.10 = (bf16[192,768]{1,0:T(8,128)(2,1)S(1)}, bf16[192,768]{1,0:T(8,128)(2,1)S(1)}, u32[]{:S(2)}, u32[]{:S(2)}) collective-permute-start(bf16[192,768]{1,0:T(8,128)(2,1)S(1)} %pad_maximum_fusion.refs_2_), channel_id=1, source_target_pairs={{0,64},{16,80},{32,96},{48,112},{64,128},{80,144},{96,160},{112,17... | collective-permute-start | bytes 884744 | tf_op jit(solution)/shard_map/ppermute | solution.py:27
  27.6 13.7 %collective-permute-start.9 = (bf16[192,768]{1,0:T(8,128)(2,1)S(1)}, bf16[192,768]{1,0:T(8,128)(2,1)S(1)}, u32[]{:S(2)}, u32[]{:S(2)}) collective-permute-start(bf16[192,768]{1,0:T(8,128)(2,1)S(1)} %pad_maximum_fusion.refs_2_), channel_id=1, source_target_pairs={{0,128},{16,144},{32,160},{48,176},{64,192},{80,208},{96,224},{112... | collective-permute-start | bytes 884744 | tf_op jit(solution)/shard_map/ppermute | solution.py:27
  30.2 14.3 %collective-permute-start.8 = (bf16[192,768]{1,0:T(8,128)(2,1)S(1)}, bf16[192,768]{1,0:T(8,128)(2,1)S(1)}, u32[]{:S(2)}, u32[]{:S(2)}) collective-permute-start(bf16[192,768]{1,0:T(8,128)(2,1)S(1)} %pad_maximum_fusion.refs_2_), channel_id=1, source_target_pairs={{0,192},{16,208},{32,224},{48,240},{64,0},{80,16},{96,32},{112,48}... | collective-permute-start | bytes 884744 | tf_op jit(solution)/shard_map/ppermute | solution.py:27
  31.2 14.0 %collective-permute-start.11 = (bf16[192,768]{1,0:T(8,128)(2,1)S(1)}, bf16[192,768]{1,0:T(8,128)(2,1)S(1)}, u32[]{:S(2)}, u32[]{:S(2)}) collective-permute-start(bf16[192,768]{1,0:T(8,128)(2,1)S(1)} %pad_maximum_fusion.refs_2_), channel_id=1, source_target_pairs={{0,1},{1,0},{2,3},{3,2},{4,5},{5,4},{6,7},{7,6},{8,9},{9,8},{10,11... | collective-permute-start | bytes 884744 | tf_op jit(solution)/shard_map/ppermute | solution.py:35
  36.6 8.6 %collective-permute-start.14 = (bf16[192,768]{1,0:T(8,128)(2,1)S(1)}, bf16[192,768]{1,0:T(8,128)(2,1)S(1)}, u32[]{:S(2)}, u32[]{:S(2)}) collective-permute-start(bf16[192,768]{1,0:T(8,128)(2,1)S(1)} %collective-permute-done.10.refs_5_), channel_id=1, source_target_pairs={{0,1},{1,0},{2,3},{3,2},{4,5},{5,4},{6,7},{7,6},{8,9},{9,8},{10,11... | collective-permute-start | bytes 884744 | tf_op jit(solution)/shard_map/ppermute | solution.py:35
  41.3 4.4 %collective-permute-start.13 = (bf16[192,768]{1,0:T(8,128)(2,1)S(1)}, bf16[192,768]{1,0:T(8,128)(2,1)S(1)}, u32[]{:S(2)}, u32[]{:S(2)}) collective-permute-start(bf16[192,768]{1,0:T(8,128)(2,1)S(1)} %collective-permute-done.9.refs_4_), channel_id=1, source_target_pairs={{0,1},{1,0},{2,3},{3,2},{4,5},{5,4},{6,7},{7,6},{8,9},{9,8},{10,11... | collective-permute-start | bytes 884744 | tf_op jit(solution)/shard_map/ppermute | solution.py:35
  44.5 1.6 %collective-permute-start.12 = (bf16[192,768]{1,0:T(8,128)(2,1)S(1)}, bf16[192,768]{1,0:T(8,128)(2,1)S(1)}, u32[]{:S(2)}, u32[]{:S(2)}) collective-permute-start(bf16[192,768]{1,0:T(8,128)(2,1)S(1)} %collective-permute-done.8.refs_3_), channel_id=1, source_target_pairs={{0,1},{1,0},{2,3},{3,2},{4,5},{5,4},{6,7},{7,6},{8,9},{9,8},{10,11... | collective-permute-start | bytes 884744 | tf_op jit(solution)/shard_map/ppermute | solution.py:35
  45.1 34.3 %copy-start.5 = (f32[1,768]{1,0:T(1,128)}, f32[1,768]{1,0:T(1,128)S(1)}, u32[]{:S(2)}) copy-start(f32[1,768]{1,0:T(1,128)S(1)} %broadcast_in_dim.25.refs_12_.gain_ref) | copy-start | bytes 9220
  46.1 1.7 %copy-start.1 = (bf16[1,12,128,768]{3,2,1,0:T(8,128)(2,1)S(1)}, bf16[1,12,128,768]{3,2,1,0:T(8,128)(2,1)}, u32[]{:S(2)}) copy-start(bf16[1,12,128,768]{3,2,1,0:T(8,128)(2,1)} %param.6) | copy-start | bytes 7077892
  47.7 1.7 %copy-start.2 = (bf16[1,12,128,768]{3,2,1,0:T(8,128)(2,1)S(1)}, bf16[1,12,128,768]{3,2,1,0:T(8,128)(2,1)}, u32[]{:S(2)}) copy-start(bf16[1,12,128,768]{3,2,1,0:T(8,128)(2,1)} %param.7) | copy-start | bytes 7077892
  49.4 0.7 copy-start.6
  79.5 1.4 %copy-start.3 = (bf16[2,768,768]{2,1,0:T(8,128)(2,1)}, bf16[2,768,768]{2,1,0:T(8,128)(2,1)S(1)}, u32[]{:S(2)}) copy-start(bf16[2,768,768]{2,1,0:T(8,128)(2,1)S(1)} %get-tuple-element.23.w_ref) | copy-start | bytes 7077892
  80.9 20.5 %copy-start = (bf16[1536,1152]{1,0:T(8,128)(2,1)}, bf16[1536,1152]{1,0:T(8,128)(2,1)S(1)}, u32[]{:S(2)}) copy-start(bf16[1536,1152]{1,0:T(8,128)(2,1)S(1)} %get-tuple-element.25.gp_ref) | copy-start | bytes 10616836
  80.9 20.5 %copy-start.4 = (bf16[1536,384]{1,0:T(8,128)(2,1)}, bf16[1536,384]{1,0:T(8,128)(2,1)S(1)}, u32[]{:S(2)}) copy-start(bf16[1536,384]{1,0:T(8,128)(2,1)S(1)} %get-tuple-element.24.att_ref) | copy-start | bytes 3538948
  80.9 2.8 %collective-permute-start.15 = (bf16[768,768]{1,0:T(8,128)(2,1)S(1)}, bf16[768,768]{1,0:T(8,128)(2,1)S(1)}, u32[]{:S(2)}, u32[]{:S(2)}) collective-permute-start(bf16[768,768]{1,0:T(8,128)(2,1)S(1)} %get-tuple-element.31), channel_id=1, source_target_pairs={{0,1},{1,0},{2,3},{3,2},{4,5},{5,4},{6,7},{7,6},{8,9},{9,8},{10,11... | collective-permute-start | bytes 3538952 | tf_op jit(solution)/shard_map/ppermute | solution.py:35
  84.6 9.5 %collective-permute-start.16 = (bf16[192,768]{1,0:T(8,128)(2,1)S(1)}, bf16[192,768]{1,0:T(8,128)(2,1)S(1)}, u32[]{:S(2)}, u32[]{:S(2)}) collective-permute-start(bf16[192,768]{1,0:T(8,128)(2,1)S(1)} %get-tuple-element.33), channel_id=1, source_target_pairs={{0,64},{16,80},{32,96},{48,112},{64,128},{80,144},{96,160},{112,17... | collective-permute-start | bytes 884744 | tf_op jit(solution)/shard_map/ppermute | solution.py:27
  85.2 15.2 %collective-permute-start.17 = (bf16[192,768]{1,0:T(8,128)(2,1)S(1)}, bf16[192,768]{1,0:T(8,128)(2,1)S(1)}, u32[]{:S(2)}, u32[]{:S(2)}) collective-permute-start(bf16[192,768]{1,0:T(8,128)(2,1)S(1)} %get-tuple-element.34), channel_id=1, source_target_pairs={{0,128},{16,144},{32,160},{48,176},{64,192},{80,208},{96,224},{112... | collective-permute-start | bytes 884744 | tf_op jit(solution)/shard_map/ppermute | solution.py:27
  87.3 13.4 %collective-permute-start.18 = (bf16[192,768]{1,0:T(8,128)(2,1)S(1)}, bf16[192,768]{1,0:T(8,128)(2,1)S(1)}, u32[]{:S(2)}, u32[]{:S(2)}) collective-permute-start(bf16[192,768]{1,0:T(8,128)(2,1)S(1)} %get-tuple-element.35), channel_id=1, source_target_pairs={{0,192},{16,208},{32,224},{48,240},{64,0},{80,16},{96,32},{112,48}... | collective-permute-start | bytes 884744 | tf_op jit(solution)/shard_map/ppermute | solution.py:27
  101.4 4.5 %collective-permute-start.19 = (bf16[48,768]{1,0:T(8,128)(2,1)S(1)}, bf16[48,768]{1,0:T(8,128)(2,1)S(1)}, u32[]{:S(2)}, u32[]{:S(2)}) collective-permute-start(bf16[48,768]{1,0:T(8,128)(2,1)S(1)} %get-tuple-element.37), channel_id=1, source_target_pairs={{0,16},{16,32},{32,48},{48,0},{64,80},{80,96},{96,112},{112,64},{1... | collective-permute-start | bytes 221192 | tf_op jit(solution)/shard_map/ppermute | solution.py:23
  102.2 5.4 %collective-permute-start.20 = (bf16[48,768]{1,0:T(8,128)(2,1)S(1)}, bf16[48,768]{1,0:T(8,128)(2,1)S(1)}, u32[]{:S(2)}, u32[]{:S(2)}) collective-permute-start(bf16[48,768]{1,0:T(8,128)(2,1)S(1)} %get-tuple-element.38), channel_id=1, source_target_pairs={{0,32},{16,48},{32,0},{48,16},{64,96},{80,112},{96,64},{112,80},{1... | collective-permute-start | bytes 221192 | tf_op jit(solution)/shard_map/ppermute | solution.py:23
  105.0 3.9 %collective-permute-start.21 = (bf16[48,768]{1,0:T(8,128)(2,1)S(1)}, bf16[48,768]{1,0:T(8,128)(2,1)S(1)}, u32[]{:S(2)}, u32[]{:S(2)}) collective-permute-start(bf16[48,768]{1,0:T(8,128)(2,1)S(1)} %get-tuple-element.39), channel_id=1, source_target_pairs={{0,48},{16,0},{32,16},{48,32},{64,112},{80,64},{96,80},{112,96},{1... | collective-permute-start | bytes 221192 | tf_op jit(solution)/shard_map/ppermute | solution.py:23
  109.6 23.7 %all-to-all-start = ((f32[16,3,768]{2,1,0:T(4,128)}), f32[16,3,768]{2,1,0:T(4,128)S(1)}, u32[]{:S(2)}, u32[]{:S(2)}) async-start(f32[16,3,768]{2,1,0:T(4,128)} %shard_map.98), calls=%async_computation | async-start | bytes 393216 | tf_op jit(solution)/shard_map/all_to_all | solution.py:359

commit v5 on v4

--- a/solution.py
+++ b/solution.py
@@ -15,6 +15,11 @@
 BLOCKS = 12
 GROUP = 4
 ROWS = GROUP * VMAX
+PRE = 2
+TAIL = 2
+NORM_MIB = 60
+CORE_MIB = 44
+TAIL_MIB = 60
 BF16 = jnp.bfloat16
 F32 = jnp.float32
 
@@ -52,7 +57,7 @@
     return [v, r1, r2, r3]
 
 
-def gather_weights(w):
+def gather_weights(w, during):
     y, x, z, c = coords()
     n = w.shape[1] // 2
     mine = lax.dynamic_slice(w, (0, c * n), (3, n))
@@ -70,7 +75,9 @@
     v = jnp.dot(order, stack, preferred_element_type=F32).astype(w.dtype)
     v = jnp.concatenate(gather4(v, hop_x, True), axis=0)
     mine = gather4(v, hop_y, True)
-    return mine + [hop_core(u) for u in mine]
+    extra = during(v)
+    mine[1], extra = lax.optimization_barrier((mine[1], extra))
+    return mine + [hop_core(u) for u in mine], extra
 
 
 def mm(a, b):
@@ -96,12 +103,40 @@
     return jnp.concatenate([row_id < counts_ref[first + b] for b in range(group)], axis=0)
 
 
+def norm_kernel(counts_ref, x_ref, cot_ref, gain_ref, nb_ref, go_ref):
+    rows = PRE * VMAX
+    normed, _ = norm_rows(x_ref[...].reshape(rows, D).astype(F32))
+    nb_ref[...] = (normed * gain_ref[...]).astype(BF16)
+    mask = row_mask(counts_ref, pl.program_id(0) * PRE, PRE)
+    go_ref[...] = jnp.where(mask, cot_ref[...].reshape(rows, D).astype(F32), 0.0).astype(BF16)
+
+
+def norm_part(counts, tiles, cotan, gain):
+    nblock = tiles.shape[0]
+    tile = pl.BlockSpec((PRE, VMAX, D), lambda i, *_: (i, 0, 0))
+    flat = pl.BlockSpec((PRE * VMAX, D), lambda i, *_: (i, 0))
+    return pl.pallas_call(
+        norm_kernel,
+        grid_spec=pltpu.PrefetchScalarGridSpec(
+            num_scalar_prefetch=1,
+            grid=(nblock // PRE,),
+            in_specs=[tile, tile, pl.BlockSpec((1, D), lambda i, *_: (0, 0))],
+            out_specs=[flat, flat],
+        ),
+        out_shape=[jax.ShapeDtypeStruct((nblock * VMAX, D), BF16)] * 2,
+        compiler_params=pltpu.CompilerParams(
+            dimension_semantics=("arbitrary",), vmem_limit_bytes=NORM_MIB * 1024 * 1024
+        ),
+        cost_estimate=pl.CostEstimate(flops=20_000_000, bytes_accessed=9_500_000, transcendentals=2000),
+    )(counts, tiles, cotan, gain)
+
+
 def core_kernel(*refs):
     at_ref, counts_ref = refs[:2]
     pieces = refs[2:10]
-    x_ref, cot_ref, gain_ref = refs[10:13]
-    w_out, att_out, gp_out, keep_out, send_out = refs[13:18]
-    w_ref, nb_ref, go_ref, att_ref, gp_ref, keep_ref, send_ref, w_sems, row_sems, dw_sems = refs[18:]
+    nb_in, go_in = refs[10:12]
+    w_out, att_out, gp_out, keep_out, send_out = refs[12:17]
+    w_ref, nb_ref, go_ref, att_ref, gp_ref, keep_ref, send_ref, w_sems, row_sems, dw_sems = refs[17:]
     step = pl.program_id(0)
     last = pl.num_programs(0) - 1
     factor = HEAD_DIM**-0.5
@@ -134,10 +169,7 @@
     def _():
         whole_w.start()
 
-    normed, _ = norm_rows(x_ref[...].reshape(ROWS, D).astype(F32))
-    nb = (normed * gain_ref[...]).astype(BF16)
-    mask = row_mask(counts_ref, step * GROUP, GROUP)
-    go = jnp.where(mask, cot_ref[...].reshape(ROWS, D).astype(F32), 0.0).astype(BF16)
+    nb, go = nb_in[...], go_in[...]
     at = pl.ds(pl.multiple_of(step * ROWS, ROWS), ROWS)
     nb_ref[at, :] = nb
     go_ref[at, :] = go
@@ -215,17 +247,17 @@
             copy.wait()
 
 
-def grads_core(at, counts, pieces, tiles, cotan, gain):
-    nblock = tiles.shape[0]
-    rows = nblock * VMAX
+def grads_core(at, counts, pieces, nb, go):
+    rows = nb.shape[0]
+    nblock = rows // VMAX
     hbm = pl.BlockSpec(memory_space=pltpu.HBM)
-    tile = pl.BlockSpec((GROUP, VMAX, D), lambda i, *_: (i, 0, 0))
+    tile = pl.BlockSpec((ROWS, D), lambda i, *_: (i, 0))
     return pl.pallas_call(
         core_kernel,
         grid_spec=pltpu.PrefetchScalarGridSpec(
             num_scalar_prefetch=2,
             grid=(nblock // GROUP,),
-            in_specs=[hbm] * 8 + [tile, tile, pl.BlockSpec((1, D), lambda i, *_: (0, 0))],
+            in_specs=[hbm] * 8 + [tile, tile],
             out_specs=[hbm] * 3 + [pl.BlockSpec(memory_space=pl.ANY)] * 2,
             scratch_shapes=[
                 pltpu.VMEM((2, D, D), BF16),
@@ -248,37 +280,37 @@
             jax.ShapeDtypeStruct((D, D), BF16),
         ],
         compiler_params=pltpu.CompilerParams(
-            dimension_semantics=("arbitrary",), vmem_limit_bytes=28 * 1024 * 1024
+            dimension_semantics=("arbitrary",), vmem_limit_bytes=CORE_MIB * 1024 * 1024
         ),
         cost_estimate=pl.CostEstimate(flops=20_000_000_000, bytes_accessed=18_000_000, transcendentals=1_200_000),
-    )(at, counts, *pieces, tiles, cotan, gain)
-
-
-def rows_kernel(first, counts_ref, w_ref, att_ref, gp_ref, x_ref, cot_ref, gain_ref, *rest):
-    enc_ref, gin_ref = rest[-2:]
+    )(at, counts, *pieces, nb, go)
+
+
+def rows_kernel(counts_ref, w_ref, att_ref, gp_ref, x_ref, cot_ref, gain_ref, enc_ref, gin_ref):
     gain = gain_ref[...]
-    xf = x_ref[...].reshape(ROWS, D).astype(F32)
+    xf = x_ref[...].reshape(TAIL * VMAX, D).astype(F32)
     normed, inv = norm_rows(xf)
-    mask = row_mask(counts_ref, (first + pl.program_id(0)) * GROUP, GROUP)
+    mask = row_mask(counts_ref, pl.program_id(0) * TAIL, TAIL)
     enc = xf + mm_t(att_ref[...], w_ref[1, :, HD:])
-    enc_ref[...] = jnp.where(mask, enc, 0.0).astype(BF16).reshape(GROUP, VMAX, D)
+    enc_ref[...] = jnp.where(mask, enc, 0.0).astype(BF16).reshape(TAIL, VMAX, D)
     gp = gp_ref[...]
     gn = (mm_t(gp[:, :D], w_ref[0]) + mm_t(gp[:, D:], w_ref[1, :, :HD])) * gain
     gl = inv * (
         gn - jnp.mean(gn, axis=-1, keepdims=True) - normed * jnp.mean(gn * normed, axis=-1, keepdims=True)
     )
-    gin = cot_ref[...].reshape(ROWS, D).astype(F32) + gl
-    gin_ref[...] = jnp.where(mask, gin, 0.0).astype(BF16).reshape(GROUP, VMAX, D)
-
-
-def rows_part(first, count, counts, w, att, gp, tiles, cotan, gain, done):
-    tile = pl.BlockSpec((GROUP, VMAX, D), lambda i, *_: (i + first, 0, 0))
-    flat = lambda cols: pl.BlockSpec((ROWS, cols), lambda i, *_: (i + first, 0))
+    gin = cot_ref[...].reshape(TAIL * VMAX, D).astype(F32) + gl
+    gin_ref[...] = jnp.where(mask, gin, 0.0).astype(BF16).reshape(TAIL, VMAX, D)
+
+
+def rows_part(counts, w, att, gp, tiles, cotan, gain):
+    nblock = tiles.shape[0]
+    tile = pl.BlockSpec((TAIL, VMAX, D), lambda i, *_: (i, 0, 0))
+    flat = lambda cols: pl.BlockSpec((TAIL * VMAX, cols), lambda i, *_: (i, 0))
     return pl.pallas_call(
-        functools.partial(rows_kernel, first),
+        rows_kernel,
         grid_spec=pltpu.PrefetchScalarGridSpec(
             num_scalar_prefetch=1,
-            grid=(count,),
+            grid=(nblock // TAIL,),
             in_specs=[
                 pl.BlockSpec((2, D, D), lambda i, *_: (0, 0, 0), pipeline_mode=pl.Buffered(1)),
                 flat(HD),
@@ -286,19 +318,15 @@
                 tile,
                 tile,
                 pl.BlockSpec((1, D), lambda i, *_: (0, 0)),
-            ]
-            + [pl.BlockSpec(memory_space=pl.ANY)] * len(done),
+            ],
             out_specs=[tile, tile],
         ),
         out_shape=[jax.ShapeDtypeStruct(tiles.shape, BF16)] * 2,
-        input_output_aliases={7 + i: i for i in range(len(done))},
         compiler_params=pltpu.CompilerParams(
-            dimension_semantics=("arbitrary",), vmem_limit_bytes=60 * 1024 * 1024
-        ),
-        cost_estimate=pl.CostEstimate(
-            flops=count * 1_300_000_000, bytes_accessed=count * 5_000_000, transcendentals=1000
-        ),
-    )(counts, w, att, gp, tiles, cotan, gain, *done)
+            dimension_semantics=("arbitrary",), vmem_limit_bytes=TAIL_MIB * 1024 * 1024
+        ),
+        cost_estimate=pl.CostEstimate(flops=4_000_000_000, bytes_accessed=16_000_000, transcendentals=3000),
+    )(counts, w, att, gp, tiles, cotan, gain)
 
 
 def small_call(kernel, at, args, outs):
@@ -315,29 +343,34 @@
     )(*([] if at is None else [at]), *args)
 
 
-def cut_kernel(axis, at_ref, own_ref, *refs):
-    got, outs = refs[:-4], refs[-4:]
-    rows = outs[0].shape[0]
+def first_cut_kernel(at_ref, keep_ref, got_ref, *outs):
     for k in range(4):
-        at = pl.ds(pl.multiple_of(((at_ref[axis] + k) & 3) * rows, rows), rows)
-        total = own_ref[at, :]
-        for ref in got:
-            total = total + ref[at, :].astype(F32)
-        outs[k][...] = total.astype(outs[k].dtype)
-
-
-def cut(at, axis, own, *got):
-    rows, n = own.shape[0] // 4, own.shape[1]
-    outs = [((rows, n), F32)] + [((rows, n), BF16)] * 3
-    return small_call(functools.partial(cut_kernel, axis), at, [own, *got], outs)
-
-
-def triples_kernel(own_ref, *refs):
-    total = own_ref[...]
-    for ref in refs[:-1]:
-        total = total + ref[...].astype(F32)
-    for i in range(16):
-        refs[-1][i] = total[3 * i : 3 * i + 3, :]
+        at = pl.ds(pl.multiple_of(((at_ref[0] + k) & 3) * 192, 192), 192)
+        outs[k][...] = (keep_ref[at, :HD] + got_ref[at, :HD].astype(F32)).astype(outs[k].dtype)
+        for j in range(4):
+            at = pl.ds(pl.multiple_of(j * 192 + ((at_ref[1] + k) & 3) * 48, 48), 48)
+            part = keep_ref[at, HD:] + got_ref[at, HD:].astype(F32)
+            outs[4 + k][j * 48 : j * 48 + 48, :] = part.astype(outs[4 + k].dtype)
+
+
+def next_cut_kernel(at_ref, *refs):
+    ins, outs = refs[:8], refs[8:]
+    for side in range(2):
+        for k in range(4):
+            at = pl.ds(pl.multiple_of(((at_ref[1 - side] + k) & 3) * 48, 48), 48)
+            total = ins[4 * side][at, :]
+            for ref in ins[4 * side + 1 : 4 * side + 4]:
+                total = total + ref[at, :].astype(F32)
+            outs[4 * side + k][...] = total.astype(outs[4 * side + k].dtype)
+
+
+def triples_kernel(*refs):
+    for side in range(2):
+        total = refs[4 * side][...]
+        for ref in refs[4 * side + 1 : 4 * side + 4]:
+            total = total + ref[...].astype(F32)
+        for i in range(16):
+            refs[-1][i, :, side * HD : side * HD + HD] = total[3 * i : 3 * i + 3, :]
 
 
 def finish_kernel(got_ref, qkv_ref, out_ref):
@@ -351,23 +384,31 @@
 
 
 def scatter_grads(at, keep, send):
-    own, *out = cut(at, 0, keep, hop_core(send))
-    own, *out = cut(at, 1, own, *[hop_y(v, k + 1) for k, v in enumerate(out)])
-    parts = [own] + [hop_x(v, k + 1) for k, v in enumerate(out)]
     n = keep.shape[1]
-    (v,) = small_call(triples_kernel, None, parts, [((16, 3, n), F32)])
+    slots = lambda rows: ([((rows, HD), F32)] + [((rows, HD), BF16)] * 3) * 2
+    v = small_call(first_cut_kernel, at, [keep, hop_core(send)], slots(192))
+    left = [v[0]] + [hop_y(v[k], k) for k in (1, 3, 2)]
+    right = [v[4]] + [hop_x(v[4 + k], k) for k in (1, 3, 2)]
+    v = small_call(next_cut_kernel, at, left + right, slots(48))
+    left = [v[0]] + [hop_x(v[k], k) for k in (1, 3, 2)]
+    right = [v[4]] + [hop_y(v[4 + k], k) for k in (1, 3, 2)]
+    (v,) = small_call(triples_kernel, None, left + right, [((16, 3, n), F32)])
     got = lax.all_to_all(v, "xl", split_axis=0, concat_axis=0, tiled=True)
     return small_call(finish_kernel, None, [got], [((3, n + n // 2), F32), ((3, n // 2), F32)])
 
 
 def shards(patches, out_cot, vis_count, w_qkv, w_out, ln_gain):
     y, x, z, c = coords()
-    pieces = gather_weights(jnp.concatenate([w_qkv, w_out], axis=1))
     at = jnp.stack([y, x, c]).astype(jnp.int32)
     counts, tiles, cotan, gain = vis_count[0], patches[0], out_cot[0], ln_gain[None]
-    w, att, gp, keep, send = grads_core(at, counts, pieces, tiles, cotan, gain)
-    out = rows_part(0, 1, counts, w, att, gp, tiles, cotan, gain, ())
-    enc, gin = rows_part(1, 2, counts, w, att, gp, tiles, cotan, gain, out)
+
+    def during(v):
+        late, _ = lax.optimization_barrier((counts, v))
+        return norm_part(late, tiles, cotan, gain)
+
+    pieces, (nb, go) = gather_weights(jnp.concatenate([w_qkv, w_out], axis=1), during)
+    w, att, gp, keep, send = grads_core(at, counts, pieces, nb, go)
+    enc, gin = rows_part(counts, w, att, gp, tiles, cotan, gain)
     grad_qkv, grad_out = scatter_grads(at, keep, send)
     return enc[None], gin[None], grad_qkv, grad_out
 

time: 134 us -> 132 us (0.985)
  waiting for transfers between devices: 26.7 us -> 19.1 us
  starting transfers between devices: 51.3 us -> 57.3 us
  local copies, waits for them, and re-layouts: 7.53 us -> 2.72 us
  Pallas kernels: 47.4 us -> 50.9 us
    ppermute x6 -> x9, waiting for transfers between devices: 12.1 us -> 4.08 us  [hop_y(): return lax.ppermute(v, 'il', [(i, (i + 4 * k) % 16) for i in range(16)])]
    ppermute x6, starting transfers between devices: 16.9 us -> 11 us  [hop_core(): return lax.ppermute(v, 'xl', [(i, i ^ 1) for i in range(16)])]
    unnamed x15 -> x7, local copies, waits for them, and re-layouts: 6.11 us -> 0.72 us
    all_to_all x1, starting transfers between devices: 8.56 us -> 13.9 us  [scatter_grads(): got = lax.all_to_all(v, 'xl', split_axis=0, concat_axis=0, tiled=True)]
    ppermute x6 -> x9, starting transfers between devices: 8.99 us -> 13 us  [hop_x(): lax.ppermute(v, 'il', [(i, i // 4 * 4 + (i + k) % 4) for i in range(16)])]
    pallas_call x2, Pallas kernels: 15.2 us -> 19 us  [the longest x1 11.7 us: rows_part(): pl.pallas_call(rows_kernel, grid_spec=pltpu.PrefetchScalarGridSpec(num_sc...]
    ppermute x6 -> x9, starting transfers between devices: 9.13 us -> 11.6 us  [hop_y(): return lax.ppermute(v, 'il', [(i, (i + 4 * k) % 16) for i in range(16)])]
    ppermute x6 -> x9, waiting for transfers between devices: 5.42 us -> 5.27 us  [hop_x(): lax.ppermute(v, 'il', [(i, i // 4 * 4 + (i + k) % 4) for i in range(16)])]
  transfers between devices with their start and end apart: 23 -> 29, of which waited for: 15 -> 14; matrix products, arithmetic and copies ran while one was open for 1% -> 1% of each run, Pallas kernels for 11% -> 15%
where the time goes in v5:
time: 132 us; the launch traced here: 131 us
  starting transfers between devices  57.3 us (43%)
  Pallas kernels  50.9 us (39%)
  waiting for transfers between devices  19.1 us (14%)
  local copies, waits for them, and re-layouts  2.72 us (2%)
    pallas_call x1, Pallas kernels, grads_core(): pl.pallas_call(core_kernel, grid_spec=pltpu.PrefetchScalarGridSpec(num_sc...  29 us
    all_to_all x1, starting transfers between devices, scatter_grads(): got = lax.all_to_all(v, 'xl', split_axis=0, concat_axis=0, tiled=True)  13.9 us
    ppermute x9, starting transfers between devices, hop_x(): lax.ppermute(v, 'il', [(i, i // 4 * 4 + (i + k) % 4) for i in range(16)])  13 us
    pallas_call x1, Pallas kernels, rows_part(): pl.pallas_call(rows_kernel, grid_spec=pltpu.PrefetchScalarGridSpec(num_sc...  11.7 us
    ppermute x9, starting transfers between devices, hop_y(): return lax.ppermute(v, 'il', [(i, (i + 4 * k) % 16) for i in range(16)])  11.6 us
    ppermute x6, starting transfers between devices, hop_core(): return lax.ppermute(v, 'xl', [(i, i ^ 1) for i in range(16)])  11 us
    ppermute x3, starting transfers between devices, hop_z(): return lax.ppermute(v, 'xl', [(i, (i + 2 * k) % 16) for i in range(16)])  7.63 us
    pallas_call x1, Pallas kernels, norm_part(): pl.pallas_call(norm_kernel, grid_spec=pltpu.PrefetchScalarGridSpec(num_sc...  7.32 us
  transfers between devices with their start and end apart: 29, of which 14 were waited for; matrix products, arithmetic and copies ran while one was open for 1% of the time, Pallas kernels for 15%

profile of v5, /device:TPU:1, one launch (start us, length us, event | category | flops | bytes accessed | tf_op | source)
XLA Modules:
  0.0 131.1 jit_solution(17610795952648370596)
XLA Ops:
  2.1 3.3 %collective-permute-start = (bf16[3,768]{1,0:T(4,128)(2,1)S(1)}, bf16[3,768]{1,0:T(4,128)(2,1)S(1)}, u32[]{:S(2)}, u32[]{:S(2)}) collective-permute-start(bf16[3,768]{1,0:T(4,128)(2,1)S(1)} %get-tuple-element.66), channel_id=1, source_target_pairs={{0,1},{1,0},{2,3},{3,2},{4,5},{5,4},{6,7},{7,6},{8,9},{9,8},{10,11... | collective-permute-start | bytes 13832 | tf_op jit(solution)/shard_map/ppermute | solution.py:40
  5.4 0.8 collective-permute-done
  6.4 2.5 %collective-permute-done.1 = bf16[8,768]{1,0:T(8,128)(2,1)S(1)} collective-permute-done((bf16[8,768]{1,0:T(8,128)(2,1)S(1)}, bf16[8,768]{1,0:T(8,128)(2,1)S(1)}, u32[]{:S(2)}, u32[]{:S(2)}) %collective-permute-start.1) | collective-permute-done | bytes 12320 | tf_op jit(solution)/shard_map/ppermute | solution.py:66
  8.9 5.3 %collective-permute-start.4 = (bf16[16,768]{1,0:T(8,128)(2,1)S(1)}, bf16[16,768]{1,0:T(8,128)(2,1)S(1)}, u32[]{:S(2)}, u32[]{:S(2)}) collective-permute-start(bf16[16,768]{1,0:T(8,128)(2,1)S(1)} %pad_maximum_fusion.1), channel_id=1, source_target_pairs={{0,8},{1,9},{2,10},{3,11},{4,12},{5,13},{6,14},{7,15},{8,0},{9,1},... | collective-permute-start | bytes 73736 | tf_op jit(solution)/shard_map/ppermute | solution.py:36
  14.2 2.4 %collective-permute-start.2 = (bf16[16,768]{1,0:T(8,128)(2,1)S(1)}, bf16[16,768]{1,0:T(8,128)(2,1)S(1)}, u32[]{:S(2)}, u32[]{:S(2)}) collective-permute-start(bf16[16,768]{1,0:T(8,128)(2,1)S(1)} %pad_maximum_fusion.1), channel_id=1, source_target_pairs={{0,4},{1,5},{2,6},{3,7},{4,8},{5,9},{6,10},{7,11},{8,12},{9,13},{1... | collective-permute-start | bytes 73736 | tf_op jit(solution)/shard_map/ppermute | solution.py:36
  16.6 1.3 collective-permute-done.3
  17.8 1.2 collective-permute-done.2
  19.2 1.3 collective-permute-start.7
  20.5 2.5 %collective-permute-start.6 = (bf16[48,768]{1,0:T(8,128)(2,1)S(1)}, bf16[48,768]{1,0:T(8,128)(2,1)S(1)}, u32[]{:S(2)}, u32[]{:S(2)}) collective-permute-start(bf16[48,768]{1,0:T(8,128)(2,1)S(1)} %convolution_convert_fusion), channel_id=1, source_target_pairs={{0,32},{16,48},{32,0},{48,16},{64,96},{80,112},{96,64},{112,80},{1... | collective-permute-start | bytes 221192 | tf_op jit(solution)/shard_map/ppermute | solution.py:28
  22.9 1.2 collective-permute-start.5
  24.1 1.4 %collective-permute-done.6 = bf16[48,768]{1,0:T(8,128)(2,1)S(1)} collective-permute-done((bf16[48,768]{1,0:T(8,128)(2,1)S(1)}, bf16[48,768]{1,0:T(8,128)(2,1)S(1)}, u32[]{:S(2)}, u32[]{:S(2)}) %collective-permute-start.6) | collective-permute-done | bytes 73760 | tf_op jit(solution)/shard_map/ppermute | solution.py:28
  26.2 2.8 %collective-permute-start.8 = (bf16[192,768]{1,0:T(8,128)(2,1)S(1)}, bf16[192,768]{1,0:T(8,128)(2,1)S(1)}, u32[]{:S(2)}, u32[]{:S(2)}) collective-permute-start(bf16[192,768]{1,0:T(8,128)(2,1)S(1)} %pad_maximum_fusion.refs_2_), channel_id=1, source_target_pairs={{0,192},{16,208},{32,224},{48,240},{64,0},{80,16},{96,32},{112,48}... | collective-permute-start | bytes 884744 | tf_op jit(solution)/shard_map/ppermute | solution.py:32
  29.0 1.6 %collective-permute-start.9 = (bf16[192,768]{1,0:T(8,128)(2,1)S(1)}, bf16[192,768]{1,0:T(8,128)(2,1)S(1)}, u32[]{:S(2)}, u32[]{:S(2)}) collective-permute-start(bf16[192,768]{1,0:T(8,128)(2,1)S(1)} %pad_maximum_fusion.refs_2_), channel_id=1, source_target_pairs={{0,128},{16,144},{32,160},{48,176},{64,192},{80,208},{96,224},{112... | collective-permute-start | bytes 884744 | tf_op jit(solution)/shard_map/ppermute | solution.py:32
  30.6 1.3 broadcast_in_dim.25.gain_ref
  31.9 5.4 %collective-permute-start.11 = (bf16[192,768]{1,0:T(8,128)(2,1)S(1)}, bf16[192,768]{1,0:T(8,128)(2,1)S(1)}, u32[]{:S(2)}, u32[]{:S(2)}) collective-permute-start(bf16[192,768]{1,0:T(8,128)(2,1)S(1)} %pad_maximum_fusion.refs_2_), channel_id=1, source_target_pairs={{0,1},{1,0},{2,3},{3,2},{4,5},{5,4},{6,7},{7,6},{8,9},{9,8},{10,11... | collective-permute-start | bytes 884744 | tf_op jit(solution)/shard_map/ppermute | solution.py:40
  37.3 7.3 %shard_map.93 = (bf16[1536,768]{1,0:T(8,128)(2,1)}, bf16[1536,768]{1,0:T(8,128)(2,1)}) custom-call(s32[12]{0:T(128)} %bitcast.9, bf16[12,128,768]{2,1,0:T(8,128)(2,1)} %bitcast.12, bf16[12,128,768]{2,1,0:T(8,128)(2,1)} %bitcast.14, f32[1,768]{1,0:T(1,128)} %broadcast_in_dim.25.gain_ref), custom_call_target="tpu_custom_call" | custom-call | flops 20000000 | bytes 9500000 | tf_op jit(solution)/shard_map/pallas_call | solution.py:118
  44.6 1.3 collective-permute-start.14
  48.0 29.0 %shard_map.94 = (bf16[2,768,768]{2,1,0:T(8,128)(2,1)S(1)}, bf16[1536,384]{1,0:T(8,128)(2,1)S(1)}, bf16[1536,1152]{1,0:T(8,128)(2,1)}, f32[768,768]{1,0:T(8,128)S(1)}, bf16[768,768]{1,0:T(8,128)(2,1)S(1)}) custom-call(s32[3]{0:T(128)S(1)} %pad_add_fusion.refs_0_.at_ref, s32[12]{0:T(128)S(1)} %bitcast.11, bf16[192,768]{1,0:T(8,128)(2,1)S(1)} %pad_maximum_fusion.refs_2_, ...), custom_call_target="tpu_custom_call" | custom-call | flops 20000000000 | bytes 18000000 | tf_op jit(solution)/shard_map/pallas_call | solution.py:255
  77.5 2.5 %collective-permute-done.15.got_ref = bf16[768,768]{1,0:T(8,128)(2,1)S(1)} collective-permute-done((bf16[768,768]{1,0:T(8,128)(2,1)S(1)}, bf16[768,768]{1,0:T(8,128)(2,1)S(1)}, u32[]{:S(2)}, u32[]{:S(2)}) %collective-permute-start.15) | collective-permute-done | bytes 1179680 | tf_op jit(solution)/shard_map/ppermute | solution.py:40
  80.7 0.8 collective-permute-start.16
  81.6 1.9 %collective-permute-start.17 = (bf16[192,384]{1,0:T(8,128)(2,1)S(1)}, bf16[192,384]{1,0:T(8,128)(2,1)S(1)}, u32[]{:S(2)}, u32[]{:S(2)}) collective-permute-start(bf16[192,384]{1,0:T(8,128)(2,1)S(1)} %get-tuple-element.50), channel_id=1, source_target_pairs={{0,192},{16,208},{32,224},{48,240},{64,0},{80,16},{96,32},{112,48}... | collective-permute-start | bytes 442376 | tf_op jit(solution)/shard_map/ppermute | solution.py:32
  84.2 2.0 %collective-permute-start.20 = (bf16[192,384]{1,0:T(8,128)(2,1)S(1)}, bf16[192,384]{1,0:T(8,128)(2,1)S(1)}, u32[]{:S(2)}, u32[]{:S(2)}) collective-permute-start(bf16[192,384]{1,0:T(8,128)(2,1)S(1)} %get-tuple-element.54), channel_id=1, source_target_pairs={{0,48},{16,0},{32,16},{48,32},{64,112},{80,64},{96,80},{112,96},{1... | collective-permute-start | bytes 442376 | tf_op jit(solution)/shard_map/ppermute | solution.py:28
  86.2 0.9 collective-permute-done.16.refs_1_
  87.1 1.9 %collective-permute-start.21 = (bf16[192,384]{1,0:T(8,128)(2,1)S(1)}, bf16[192,384]{1,0:T(8,128)(2,1)S(1)}, u32[]{:S(2)}, u32[]{:S(2)}) collective-permute-start(bf16[192,384]{1,0:T(8,128)(2,1)S(1)} %get-tuple-element.55), channel_id=1, source_target_pairs={{0,32},{16,48},{32,0},{48,16},{64,96},{80,112},{96,64},{112,80},{1... | collective-permute-start | bytes 442376 | tf_op jit(solution)/shard_map/ppermute | solution.py:28
  89.5 3.2 %collective-permute-done.21.refs_7_ = bf16[192,384]{1,0:T(8,128)(2,1)S(1)} collective-permute-done((bf16[192,384]{1,0:T(8,128)(2,1)S(1)}, bf16[192,384]{1,0:T(8,128)(2,1)S(1)}, u32[]{:S(2)}, u32[]{:S(2)}) %collective-permute-start.21) | collective-permute-done | bytes 147488 | tf_op jit(solution)/shard_map/ppermute | solution.py:28
  93.5 1.0 collective-permute-start.22
  94.5 1.7 %collective-permute-start.23 = (bf16[48,384]{1,0:T(8,128)(2,1)S(1)}, bf16[48,384]{1,0:T(8,128)(2,1)S(1)}, u32[]{:S(2)}, u32[]{:S(2)}) collective-permute-start(bf16[48,384]{1,0:T(8,128)(2,1)S(1)} %get-tuple-element.58), channel_id=1, source_target_pairs={{0,48},{16,0},{32,16},{48,32},{64,112},{80,64},{96,80},{112,96},{1... | collective-permute-start | bytes 110600 | tf_op jit(solution)/shard_map/ppermute | solution.py:28
  97.6 2.1 %collective-permute-start.26 = (bf16[48,384]{1,0:T(8,128)(2,1)S(1)}, bf16[48,384]{1,0:T(8,128)(2,1)S(1)}, u32[]{:S(2)}, u32[]{:S(2)}) collective-permute-start(bf16[48,384]{1,0:T(8,128)(2,1)S(1)} %get-tuple-element.62), channel_id=1, source_target_pairs={{0,192},{16,208},{32,224},{48,240},{64,0},{80,16},{96,32},{112,48}... | collective-permute-start | bytes 110600 | tf_op jit(solution)/shard_map/ppermute | solution.py:32
  99.6 1.8 %collective-permute-start.27 = (bf16[48,384]{1,0:T(8,128)(2,1)S(1)}, bf16[48,384]{1,0:T(8,128)(2,1)S(1)}, u32[]{:S(2)}, u32[]{:S(2)}) collective-permute-start(bf16[48,384]{1,0:T(8,128)(2,1)S(1)} %get-tuple-element.63), channel_id=1, source_target_pairs={{0,128},{16,144},{32,160},{48,176},{64,192},{80,208},{96,224},{112... | collective-permute-start | bytes 110600 | tf_op jit(solution)/shard_map/ppermute | solution.py:32
  101.4 2.7 %collective-permute-done.27.refs_7_ = bf16[48,384]{1,0:T(8,128)(2,1)S(1)} collective-permute-done((bf16[48,384]{1,0:T(8,128)(2,1)S(1)}, bf16[48,384]{1,0:T(8,128)(2,1)S(1)}, u32[]{:S(2)}, u32[]{:S(2)}) %collective-permute-start.27) | collective-permute-done | bytes 36896 | tf_op jit(solution)/shard_map/ppermute | solution.py:32
  104.8 13.9 %all-to-all-start = ((f32[16,3,768]{2,1,0:T(4,128)}), f32[16,3,768]{2,1,0:T(4,128)S(1)}, u32[]{:S(2)}, u32[]{:S(2)}) async-start(f32[16,3,768]{2,1,0:T(4,128)} %shard_map.98), calls=%async_computation | async-start | bytes 393216 | tf_op jit(solution)/shard_map/all_to_all | solution.py:396
  118.7 11.7 %shard_map.95 = (bf16[12,128,768]{2,1,0:T(8,128)(2,1)}, bf16[12,128,768]{2,1,0:T(8,128)(2,1)}) custom-call(s32[12]{0:T(128)} %bitcast.10, bf16[2,768,768]{2,1,0:T(8,128)(2,1)} %copy-done.1, bf16[1536,384]{1,0:T(8,128)(2,1)} %copy-done.2, bf16[1536,1152]{1,0:T(8,128)(2,1)} %get-tuple-element.43.gp_ref, bf16[12,128,768]{2,1,0:T(8,128)(2,1)} %bitcast.13, ...), custom_call_target="tpu_custom_call" | custom-call | flops 4000000000 | bytes 16000000 | tf_op jit(solution)/shard_map/pallas_call | solution.py:309
  (52 shorter events, 10.3 us)
Async XLA Ops:
  2.1 4.2 %collective-permute-start = (bf16[3,768]{1,0:T(4,128)(2,1)S(1)}, bf16[3,768]{1,0:T(4,128)(2,1)S(1)}, u32[]{:S(2)}, u32[]{:S(2)}) collective-permute-start(bf16[3,768]{1,0:T(4,128)(2,1)S(1)} %get-tuple-element.66), channel_id=1, source_target_pairs={{0,1},{1,0},{2,3},{3,2},{4,5},{5,4},{6,7},{7,6},{8,9},{9,8},{10,11... | collective-permute-start | bytes 13832 | tf_op jit(solution)/shard_map/ppermute | solution.py:40
  6.2 2.6 %collective-permute-start.1 = (bf16[8,768]{1,0:T(8,128)(2,1)S(1)}, bf16[8,768]{1,0:T(8,128)(2,1)S(1)}, u32[]{:S(2)}, u32[]{:S(2)}) collective-permute-start(bf16[8,768]{1,0:T(8,128)(2,1)S(1)} %pad_maximum_fusion.2), channel_id=1, source_target_pairs={{0,2},{1,3},{2,0},{3,1},{4,6},{5,7},{6,4},{7,5},{8,10},{9,11},{10,... | collective-permute-start | bytes 36872 | tf_op jit(solution)/shard_map/ppermute | solution.py:66
  8.9 7.6 %collective-permute-start.4 = (bf16[16,768]{1,0:T(8,128)(2,1)S(1)}, bf16[16,768]{1,0:T(8,128)(2,1)S(1)}, u32[]{:S(2)}, u32[]{:S(2)}) collective-permute-start(bf16[16,768]{1,0:T(8,128)(2,1)S(1)} %pad_maximum_fusion.1), channel_id=1, source_target_pairs={{0,8},{1,9},{2,10},{3,11},{4,12},{5,13},{6,14},{7,15},{8,0},{9,1},... | collective-permute-start | bytes 73736 | tf_op jit(solution)/shard_map/ppermute | solution.py:36
  14.2 3.7 %collective-permute-start.3 = (bf16[16,768]{1,0:T(8,128)(2,1)S(1)}, bf16[16,768]{1,0:T(8,128)(2,1)S(1)}, u32[]{:S(2)}, u32[]{:S(2)}) collective-permute-start(bf16[16,768]{1,0:T(8,128)(2,1)S(1)} %pad_maximum_fusion.1), channel_id=1, source_target_pairs={{0,12},{1,13},{2,14},{3,15},{4,0},{5,1},{6,2},{7,3},{8,4},{9,5},{1... | collective-permute-start | bytes 73736 | tf_op jit(solution)/shard_map/ppermute | solution.py:36
  14.2 4.9 %collective-permute-start.2 = (bf16[16,768]{1,0:T(8,128)(2,1)S(1)}, bf16[16,768]{1,0:T(8,128)(2,1)S(1)}, u32[]{:S(2)}, u32[]{:S(2)}) collective-permute-start(bf16[16,768]{1,0:T(8,128)(2,1)S(1)} %pad_maximum_fusion.1), channel_id=1, source_target_pairs={{0,4},{1,5},{2,6},{3,7},{4,8},{5,9},{6,10},{7,11},{8,12},{9,13},{1... | collective-permute-start | bytes 73736 | tf_op jit(solution)/shard_map/ppermute | solution.py:36
  19.2 4.9 %collective-permute-start.7 = (bf16[48,768]{1,0:T(8,128)(2,1)S(1)}, bf16[48,768]{1,0:T(8,128)(2,1)S(1)}, u32[]{:S(2)}, u32[]{:S(2)}) collective-permute-start(bf16[48,768]{1,0:T(8,128)(2,1)S(1)} %convolution_convert_fusion), channel_id=1, source_target_pairs={{0,16},{16,32},{32,48},{48,0},{64,80},{80,96},{96,112},{112,64},{1... | collective-permute-start | bytes 221192 | tf_op jit(solution)/shard_map/ppermute | solution.py:28
  20.5 5.0 %collective-permute-start.6 = (bf16[48,768]{1,0:T(8,128)(2,1)S(1)}, bf16[48,768]{1,0:T(8,128)(2,1)S(1)}, u32[]{:S(2)}, u32[]{:S(2)}) collective-permute-start(bf16[48,768]{1,0:T(8,128)(2,1)S(1)} %convolution_convert_fusion), channel_id=1, source_target_pairs={{0,32},{16,48},{32,0},{48,16},{64,96},{80,112},{96,64},{112,80},{1... | collective-permute-start | bytes 221192 | tf_op jit(solution)/shard_map/ppermute | solution.py:28
  22.9 3.2 %collective-permute-start.5 = (bf16[48,768]{1,0:T(8,128)(2,1)S(1)}, bf16[48,768]{1,0:T(8,128)(2,1)S(1)}, u32[]{:S(2)}, u32[]{:S(2)}) collective-permute-start(bf16[48,768]{1,0:T(8,128)(2,1)S(1)} %convolution_convert_fusion), channel_id=1, source_target_pairs={{0,48},{16,0},{32,16},{48,32},{64,112},{80,64},{96,80},{112,96},{1... | collective-permute-start | bytes 221192 | tf_op jit(solution)/shard_map/ppermute | solution.py:28
  26.2 18.5 %collective-permute-start.8 = (bf16[192,768]{1,0:T(8,128)(2,1)S(1)}, bf16[192,768]{1,0:T(8,128)(2,1)S(1)}, u32[]{:S(2)}, u32[]{:S(2)}) collective-permute-start(bf16[192,768]{1,0:T(8,128)(2,1)S(1)} %pad_maximum_fusion.refs_2_), channel_id=1, source_target_pairs={{0,192},{16,208},{32,224},{48,240},{64,0},{80,16},{96,32},{112,48}... | collective-permute-start | bytes 884744 | tf_op jit(solution)/shard_map/ppermute | solution.py:32
  29.0 15.6 %collective-permute-start.10 = (bf16[192,768]{1,0:T(8,128)(2,1)S(1)}, bf16[192,768]{1,0:T(8,128)(2,1)S(1)}, u32[]{:S(2)}, u32[]{:S(2)}) collective-permute-start(bf16[192,768]{1,0:T(8,128)(2,1)S(1)} %pad_maximum_fusion.refs_2_), channel_id=1, source_target_pairs={{0,64},{16,80},{32,96},{48,112},{64,128},{80,144},{96,160},{112,17... | collective-permute-start | bytes 884744 | tf_op jit(solution)/shard_map/ppermute | solution.py:32
  29.0 17.0 %collective-permute-start.9 = (bf16[192,768]{1,0:T(8,128)(2,1)S(1)}, bf16[192,768]{1,0:T(8,128)(2,1)S(1)}, u32[]{:S(2)}, u32[]{:S(2)}) collective-permute-start(bf16[192,768]{1,0:T(8,128)(2,1)S(1)} %pad_maximum_fusion.refs_2_), channel_id=1, source_target_pairs={{0,128},{16,144},{32,160},{48,176},{64,192},{80,208},{96,224},{112... | collective-permute-start | bytes 884744 | tf_op jit(solution)/shard_map/ppermute | solution.py:32
  31.9 14.6 %collective-permute-start.11 = (bf16[192,768]{1,0:T(8,128)(2,1)S(1)}, bf16[192,768]{1,0:T(8,128)(2,1)S(1)}, u32[]{:S(2)}, u32[]{:S(2)}) collective-permute-start(bf16[192,768]{1,0:T(8,128)(2,1)S(1)} %pad_maximum_fusion.refs_2_), channel_id=1, source_target_pairs={{0,1},{1,0},{2,3},{3,2},{4,5},{5,4},{6,7},{7,6},{8,9},{9,8},{10,11... | collective-permute-start | bytes 884744 | tf_op jit(solution)/shard_map/ppermute | solution.py:40
  37.3 10.7 %copy-start = (s32[1,12]{1,0:T(1,128)S(1)}, s32[1,12]{1,0:T(1,128)}, u32[]{:S(2)}) copy-start(s32[1,12]{1,0:T(1,128)} %param.8) | copy-start | bytes 148
  44.6 2.5 %collective-permute-start.14 = (bf16[192,768]{1,0:T(8,128)(2,1)S(1)}, bf16[192,768]{1,0:T(8,128)(2,1)S(1)}, u32[]{:S(2)}, u32[]{:S(2)}) collective-permute-start(bf16[192,768]{1,0:T(8,128)(2,1)S(1)} %collective-permute-done.10.refs_5_), channel_id=1, source_target_pairs={{0,1},{1,0},{2,3},{3,2},{4,5},{5,4},{6,7},{7,6},{8,9},{9,8},{10,11... | collective-permute-start | bytes 884744 | tf_op jit(solution)/shard_map/ppermute | solution.py:40
  45.9 1.6 %collective-permute-start.13 = (bf16[192,768]{1,0:T(8,128)(2,1)S(1)}, bf16[192,768]{1,0:T(8,128)(2,1)S(1)}, u32[]{:S(2)}, u32[]{:S(2)}) collective-permute-start(bf16[192,768]{1,0:T(8,128)(2,1)S(1)} %collective-permute-done.9.refs_4_), channel_id=1, source_target_pairs={{0,1},{1,0},{2,3},{3,2},{4,5},{5,4},{6,7},{7,6},{8,9},{9,8},{10,11... | collective-permute-start | bytes 884744 | tf_op jit(solution)/shard_map/ppermute | solution.py:40
  46.0 2.0 %collective-permute-start.12 = (bf16[192,768]{1,0:T(8,128)(2,1)S(1)}, bf16[192,768]{1,0:T(8,128)(2,1)S(1)}, u32[]{:S(2)}, u32[]{:S(2)}) collective-permute-start(bf16[192,768]{1,0:T(8,128)(2,1)S(1)} %collective-permute-done.8.refs_3_), channel_id=1, source_target_pairs={{0,1},{1,0},{2,3},{3,2},{4,5},{5,4},{6,7},{7,6},{8,9},{9,8},{10,11... | collective-permute-start | bytes 884744 | tf_op jit(solution)/shard_map/ppermute | solution.py:40
  77.0 16.4 %copy-start.1 = (bf16[2,768,768]{2,1,0:T(8,128)(2,1)}, bf16[2,768,768]{2,1,0:T(8,128)(2,1)S(1)}, u32[]{:S(2)}) copy-start(bf16[2,768,768]{2,1,0:T(8,128)(2,1)S(1)} %get-tuple-element.41.w_ref) | copy-start | bytes 7077892
  77.0 16.4 %copy-start.2 = (bf16[1536,384]{1,0:T(8,128)(2,1)}, bf16[1536,384]{1,0:T(8,128)(2,1)S(1)}, u32[]{:S(2)}) copy-start(bf16[1536,384]{1,0:T(8,128)(2,1)S(1)} %get-tuple-element.42.att_ref) | copy-start | bytes 3538948
  77.0 2.9 %collective-permute-start.15 = (bf16[768,768]{1,0:T(8,128)(2,1)S(1)}, bf16[768,768]{1,0:T(8,128)(2,1)S(1)}, u32[]{:S(2)}, u32[]{:S(2)}) collective-permute-start(bf16[768,768]{1,0:T(8,128)(2,1)S(1)} %get-tuple-element.47), channel_id=1, source_target_pairs={{0,1},{1,0},{2,3},{3,2},{4,5},{5,4},{6,7},{7,6},{8,9},{9,8},{10,11... | collective-permute-start | bytes 3538952 | tf_op jit(solution)/shard_map/ppermute | solution.py:40
  80.7 6.4 %collective-permute-start.16 = (bf16[192,384]{1,0:T(8,128)(2,1)S(1)}, bf16[192,384]{1,0:T(8,128)(2,1)S(1)}, u32[]{:S(2)}, u32[]{:S(2)}) collective-permute-start(bf16[192,384]{1,0:T(8,128)(2,1)S(1)} %get-tuple-element.49), channel_id=1, source_target_pairs={{0,64},{16,80},{32,96},{48,112},{64,128},{80,144},{96,160},{112,17... | collective-permute-start | bytes 442376 | tf_op jit(solution)/shard_map/ppermute | solution.py:32
  81.6 7.5 %collective-permute-start.17 = (bf16[192,384]{1,0:T(8,128)(2,1)S(1)}, bf16[192,384]{1,0:T(8,128)(2,1)S(1)}, u32[]{:S(2)}, u32[]{:S(2)}) collective-permute-start(bf16[192,384]{1,0:T(8,128)(2,1)S(1)} %get-tuple-element.50), channel_id=1, source_target_pairs={{0,192},{16,208},{32,224},{48,240},{64,0},{80,16},{96,32},{112,48}... | collective-permute-start | bytes 442376 | tf_op jit(solution)/shard_map/ppermute | solution.py:32
  83.5 6.0 %collective-permute-start.18 = (bf16[192,384]{1,0:T(8,128)(2,1)S(1)}, bf16[192,384]{1,0:T(8,128)(2,1)S(1)}, u32[]{:S(2)}, u32[]{:S(2)}) collective-permute-start(bf16[192,384]{1,0:T(8,128)(2,1)S(1)} %get-tuple-element.51), channel_id=1, source_target_pairs={{0,128},{16,144},{32,160},{48,176},{64,192},{80,208},{96,224},{112... | collective-permute-start | bytes 442376 | tf_op jit(solution)/shard_map/ppermute | solution.py:32
  83.5 6.0 %collective-permute-start.19 = (bf16[192,384]{1,0:T(8,128)(2,1)S(1)}, bf16[192,384]{1,0:T(8,128)(2,1)S(1)}, u32[]{:S(2)}, u32[]{:S(2)}) collective-permute-start(bf16[192,384]{1,0:T(8,128)(2,1)S(1)} %get-tuple-element.53), channel_id=1, source_target_pairs={{0,16},{16,32},{32,48},{48,0},{64,80},{80,96},{96,112},{112,64},{1... | collective-permute-start | bytes 442376 | tf_op jit(solution)/shard_map/ppermute | solution.py:28
  84.2 5.4 %collective-permute-start.20 = (bf16[192,384]{1,0:T(8,128)(2,1)S(1)}, bf16[192,384]{1,0:T(8,128)(2,1)S(1)}, u32[]{:S(2)}, u32[]{:S(2)}) collective-permute-start(bf16[192,384]{1,0:T(8,128)(2,1)S(1)} %get-tuple-element.54), channel_id=1, source_target_pairs={{0,48},{16,0},{32,16},{48,32},{64,112},{80,64},{96,80},{112,96},{1... | collective-permute-start | bytes 442376 | tf_op jit(solution)/shard_map/ppermute | solution.py:28
  87.1 5.6 %collective-permute-start.21 = (bf16[192,384]{1,0:T(8,128)(2,1)S(1)}, bf16[192,384]{1,0:T(8,128)(2,1)S(1)}, u32[]{:S(2)}, u32[]{:S(2)}) collective-permute-start(bf16[192,384]{1,0:T(8,128)(2,1)S(1)} %get-tuple-element.55), channel_id=1, source_target_pairs={{0,32},{16,48},{32,0},{48,16},{64,96},{80,112},{96,64},{112,80},{1... | collective-permute-start | bytes 442376 | tf_op jit(solution)/shard_map/ppermute | solution.py:28
  93.5 6.2 %collective-permute-start.22 = (bf16[48,384]{1,0:T(8,128)(2,1)S(1)}, bf16[48,384]{1,0:T(8,128)(2,1)S(1)}, u32[]{:S(2)}, u32[]{:S(2)}) collective-permute-start(bf16[48,384]{1,0:T(8,128)(2,1)S(1)} %get-tuple-element.57), channel_id=1, source_target_pairs={{0,16},{16,32},{32,48},{48,0},{64,80},{80,96},{96,112},{112,64},{1... | collective-permute-start | bytes 110600 | tf_op jit(solution)/shard_map/ppermute | solution.py:28
  94.5 6.9 %collective-permute-start.23 = (bf16[48,384]{1,0:T(8,128)(2,1)S(1)}, bf16[48,384]{1,0:T(8,128)(2,1)S(1)}, u32[]{:S(2)}, u32[]{:S(2)}) collective-permute-start(bf16[48,384]{1,0:T(8,128)(2,1)S(1)} %get-tuple-element.58), channel_id=1, source_target_pairs={{0,48},{16,0},{32,16},{48,32},{64,112},{80,64},{96,80},{112,96},{1... | collective-permute-start | bytes 110600 | tf_op jit(solution)/shard_map/ppermute | solution.py:28
  96.2 5.2 %collective-permute-start.24 = (bf16[48,384]{1,0:T(8,128)(2,1)S(1)}, bf16[48,384]{1,0:T(8,128)(2,1)S(1)}, u32[]{:S(2)}, u32[]{:S(2)}) collective-permute-start(bf16[48,384]{1,0:T(8,128)(2,1)S(1)} %get-tuple-element.59), channel_id=1, source_target_pairs={{0,32},{16,48},{32,0},{48,16},{64,96},{80,112},{96,64},{112,80},{1... | collective-permute-start | bytes 110600 | tf_op jit(solution)/shard_map/ppermute | solution.py:28
  96.9 4.4 %collective-permute-start.25 = (bf16[48,384]{1,0:T(8,128)(2,1)S(1)}, bf16[48,384]{1,0:T(8,128)(2,1)S(1)}, u32[]{:S(2)}, u32[]{:S(2)}) collective-permute-start(bf16[48,384]{1,0:T(8,128)(2,1)S(1)} %get-tuple-element.61), channel_id=1, source_target_pairs={{0,64},{16,80},{32,96},{48,112},{64,128},{80,144},{96,160},{112,17... | collective-permute-start | bytes 110600 | tf_op jit(solution)/shard_map/ppermute | solution.py:32
  97.6 3.8 %collective-permute-start.26 = (bf16[48,384]{1,0:T(8,128)(2,1)S(1)}, bf16[48,384]{1,0:T(8,128)(2,1)S(1)}, u32[]{:S(2)}, u32[]{:S(2)}) collective-permute-start(bf16[48,384]{1,0:T(8,128)(2,1)S(1)} %get-tuple-element.62), channel_id=1, source_target_pairs={{0,192},{16,208},{32,224},{48,240},{64,0},{80,16},{96,32},{112,48}... | collective-permute-start | bytes 110600 | tf_op jit(solution)/shard_map/ppermute | solution.py:32
  99.6 4.5 %collective-permute-start.27 = (bf16[48,384]{1,0:T(8,128)(2,1)S(1)}, bf16[48,384]{1,0:T(8,128)(2,1)S(1)}, u32[]{:S(2)}, u32[]{:S(2)}) collective-permute-start(bf16[48,384]{1,0:T(8,128)(2,1)S(1)} %get-tuple-element.63), channel_id=1, source_target_pairs={{0,128},{16,144},{32,160},{48,176},{64,192},{80,208},{96,224},{112... | collective-permute-start | bytes 110600 | tf_op jit(solution)/shard_map/ppermute | solution.py:32
  104.8 25.6 %all-to-all-start = ((f32[16,3,768]{2,1,0:T(4,128)}), f32[16,3,768]{2,1,0:T(4,128)S(1)}, u32[]{:S(2)}, u32[]{:S(2)}) async-start(f32[16,3,768]{2,1,0:T(4,128)} %shard_map.98), calls=%async_computation | async-start | bytes 393216 | tf_op jit(solution)/shard_map/all_to_all | solution.py:396

commit v6 on v4

--- a/solution.py
+++ b/solution.py
@@ -15,6 +15,11 @@
 BLOCKS = 12
 GROUP = 4
 ROWS = GROUP * VMAX
+TAIL = 2
+HEAD = 3
+NORM_MIB = 0
+CORE_MIB = 51
+TAIL_MIB = 60
 BF16 = jnp.bfloat16
 F32 = jnp.float32
 
@@ -248,7 +253,7 @@
             jax.ShapeDtypeStruct((D, D), BF16),
         ],
         compiler_params=pltpu.CompilerParams(
-            dimension_semantics=("arbitrary",), vmem_limit_bytes=28 * 1024 * 1024
+            dimension_semantics=("arbitrary",), vmem_limit_bytes=CORE_MIB * 1024 * 1024
         ),
         cost_estimate=pl.CostEstimate(flops=20_000_000_000, bytes_accessed=18_000_000, transcendentals=1_200_000),
     )(at, counts, *pieces, tiles, cotan, gain)
@@ -257,23 +262,23 @@
 def rows_kernel(first, counts_ref, w_ref, att_ref, gp_ref, x_ref, cot_ref, gain_ref, *rest):
     enc_ref, gin_ref = rest[-2:]
     gain = gain_ref[...]
-    xf = x_ref[...].reshape(ROWS, D).astype(F32)
+    xf = x_ref[...].reshape(TAIL * VMAX, D).astype(F32)
     normed, inv = norm_rows(xf)
-    mask = row_mask(counts_ref, (first + pl.program_id(0)) * GROUP, GROUP)
+    mask = row_mask(counts_ref, (first + pl.program_id(0)) * TAIL, TAIL)
     enc = xf + mm_t(att_ref[...], w_ref[1, :, HD:])
-    enc_ref[...] = jnp.where(mask, enc, 0.0).astype(BF16).reshape(GROUP, VMAX, D)
+    enc_ref[...] = jnp.where(mask, enc, 0.0).astype(BF16).reshape(TAIL, VMAX, D)
     gp = gp_ref[...]
     gn = (mm_t(gp[:, :D], w_ref[0]) + mm_t(gp[:, D:], w_ref[1, :, :HD])) * gain
     gl = inv * (
         gn - jnp.mean(gn, axis=-1, keepdims=True) - normed * jnp.mean(gn * normed, axis=-1, keepdims=True)
     )
-    gin = cot_ref[...].reshape(ROWS, D).astype(F32) + gl
-    gin_ref[...] = jnp.where(mask, gin, 0.0).astype(BF16).reshape(GROUP, VMAX, D)
+    gin = cot_ref[...].reshape(TAIL * VMAX, D).astype(F32) + gl
+    gin_ref[...] = jnp.where(mask, gin, 0.0).astype(BF16).reshape(TAIL, VMAX, D)
 
 
 def rows_part(first, count, counts, w, att, gp, tiles, cotan, gain, done):
-    tile = pl.BlockSpec((GROUP, VMAX, D), lambda i, *_: (i + first, 0, 0))
-    flat = lambda cols: pl.BlockSpec((ROWS, cols), lambda i, *_: (i + first, 0))
+    tile = pl.BlockSpec((TAIL, VMAX, D), lambda i, *_: (i + first, 0, 0))
+    flat = lambda cols: pl.BlockSpec((TAIL * VMAX, cols), lambda i, *_: (i + first, 0))
     return pl.pallas_call(
         functools.partial(rows_kernel, first),
         grid_spec=pltpu.PrefetchScalarGridSpec(
@@ -293,10 +298,10 @@
         out_shape=[jax.ShapeDtypeStruct(tiles.shape, BF16)] * 2,
         input_output_aliases={7 + i: i for i in range(len(done))},
         compiler_params=pltpu.CompilerParams(
-            dimension_semantics=("arbitrary",), vmem_limit_bytes=60 * 1024 * 1024
+            dimension_semantics=("arbitrary",), vmem_limit_bytes=TAIL_MIB * 1024 * 1024
         ),
         cost_estimate=pl.CostEstimate(
-            flops=count * 1_300_000_000, bytes_accessed=count * 5_000_000, transcendentals=1000
+            flops=count * 650_000_000, bytes_accessed=count * 2_500_000, transcendentals=1000
         ),
     )(counts, w, att, gp, tiles, cotan, gain, *done)
 
@@ -350,14 +355,17 @@
     out_ref[...] = hi[:, HD:]
 
 
-def scatter_grads(at, keep, send):
+def scatter_grads(at, keep, send, during):
     own, *out = cut(at, 0, keep, hop_core(send))
-    own, *out = cut(at, 1, own, *[hop_y(v, k + 1) for k, v in enumerate(out)])
+    got = [hop_y(v, k + 1) for k, v in enumerate(out)]
+    extra = during(own)
+    got[0], extra = lax.optimization_barrier((got[0], extra))
+    own, *out = cut(at, 1, own, *got)
     parts = [own] + [hop_x(v, k + 1) for k, v in enumerate(out)]
     n = keep.shape[1]
     (v,) = small_call(triples_kernel, None, parts, [((16, 3, n), F32)])
     got = lax.all_to_all(v, "xl", split_axis=0, concat_axis=0, tiled=True)
-    return small_call(finish_kernel, None, [got], [((3, n + n // 2), F32), ((3, n // 2), F32)])
+    return small_call(finish_kernel, None, [got], [((3, n + n // 2), F32), ((3, n // 2), F32)]), extra
 
 
 def shards(patches, out_cot, vis_count, w_qkv, w_out, ln_gain):
@@ -366,9 +374,13 @@
     at = jnp.stack([y, x, c]).astype(jnp.int32)
     counts, tiles, cotan, gain = vis_count[0], patches[0], out_cot[0], ln_gain[None]
     w, att, gp, keep, send = grads_core(at, counts, pieces, tiles, cotan, gain)
-    out = rows_part(0, 1, counts, w, att, gp, tiles, cotan, gain, ())
-    enc, gin = rows_part(1, 2, counts, w, att, gp, tiles, cotan, gain, out)
-    grad_qkv, grad_out = scatter_grads(at, keep, send)
+
+    def during(own):
+        late, _ = lax.optimization_barrier((counts, own))
+        return rows_part(0, HEAD, late, w, att, gp, tiles, cotan, gain, ())
+
+    (grad_qkv, grad_out), out = scatter_grads(at, keep, send, during)
+    enc, gin = rows_part(HEAD, BLOCKS // TAIL - HEAD, counts, w, att, gp, tiles, cotan, gain, out)
     return enc[None], gin[None], grad_qkv, grad_out
 
 

time: 134 us -> 129 us (0.963)
  local copies, waits for them, and re-layouts: 7.53 us -> 4.45 us
  starting transfers between devices: 51.3 us -> 49.2 us
    ppermute x6, waiting for transfers between devices: 12.1 us -> 7.25 us  [hop_y(): return lax.ppermute(v, 'il', [(i, (i + 4 * k) % 16) for i in range(16)])]
    unnamed x15 -> x7, local copies, waits for them, and re-layouts: 6.11 us -> 3.03 us
    all_to_all x1, waiting for transfers between devices: 0.01 us -> 2.59 us  [scatter_grads(): got = lax.all_to_all(v, 'xl', split_axis=0, concat_axis=0, tiled=True)]
    ppermute x6, starting transfers between devices: 9.13 us -> 6.6 us  [hop_y(): return lax.ppermute(v, 'il', [(i, (i + 4 * k) % 16) for i in range(16)])]
    ppermute x6, starting transfers between devices: 8.99 us -> 6.79 us  [hop_x(): lax.ppermute(v, 'il', [(i, i // 4 * 4 + (i + k) % 4) for i in range(16)])]
    ppermute x6, waiting for transfers between devices: 5.42 us -> 7.4 us  [hop_x(): lax.ppermute(v, 'il', [(i, i // 4 * 4 + (i + k) % 4) for i in range(16)])]
    ppermute x6, starting transfers between devices: 16.9 us -> 18.4 us  [hop_core(): return lax.ppermute(v, 'xl', [(i, i ^ 1) for i in range(16)])]
  transfers between devices with their start and end apart: 23 -> 23, of which waited for: 15 -> 16; matrix products, arithmetic and copies ran while one was open for 1% -> 1% of each run, Pallas kernels for 11% -> 12%
where the time goes in v6:
time: 129 us; the launch traced here: 128 us
  starting transfers between devices  49.2 us (38%)
  Pallas kernels  47.6 us (37%)
  waiting for transfers between devices  25.9 us (20%)
  local copies, waits for them, and re-layouts  4.45 us (3%)
    pallas_call x1, Pallas kernels, grads_core(): pl.pallas_call(core_kernel, grid_spec=pltpu.PrefetchScalarGridSpec(num_sc...  29.4 us
    ppermute x6, starting transfers between devices, hop_core(): return lax.ppermute(v, 'xl', [(i, i ^ 1) for i in range(16)])  18.4 us
    pallas_call x2, Pallas kernels, rows_part(): pl.pallas_call(functools.partial(rows_kernel, first), grid_spec=pltpu.Pre...  15.5 us
    ppermute x3, starting transfers between devices, hop_z(): return lax.ppermute(v, 'xl', [(i, (i + 2 * k) % 16) for i in range(16)])  8.83 us
    all_to_all x1, starting transfers between devices, scatter_grads(): got = lax.all_to_all(v, 'xl', split_axis=0, concat_axis=0, tiled=True)  8.51 us
    ppermute x6, waiting for transfers between devices, hop_x(): lax.ppermute(v, 'il', [(i, i // 4 * 4 + (i + k) % 4) for i in range(16)])  7.4 us
    ppermute x6, waiting for transfers between devices, hop_y(): return lax.ppermute(v, 'il', [(i, (i + 4 * k) % 16) for i in range(16)])  7.25 us
    ppermute x6, starting transfers between devices, hop_x(): lax.ppermute(v, 'il', [(i, i // 4 * 4 + (i + k) % 4) for i in range(16)])  6.79 us
  transfers between devices with their start and end apart: 23, of which 16 were waited for; matrix products, arithmetic and copies ran while one was open for 1% of the time, Pallas kernels for 12%

profile of v6, /device:TPU:1, one launch (start us, length us, event | category | flops | bytes accessed | tf_op | source)
XLA Modules:
  0.0 128.3 jit_solution(11230528643166477447)
XLA Ops:
  0.7 0.7 constant_dynamic-update-slice_fusion.1
  2.1 3.3 %collective-permute-start = (bf16[3,768]{1,0:T(4,128)(2,1)S(1)}, bf16[3,768]{1,0:T(4,128)(2,1)S(1)}, u32[]{:S(2)}, u32[]{:S(2)}) collective-permute-start(bf16[3,768]{1,0:T(4,128)(2,1)S(1)} %get-tuple-element.50), channel_id=1, source_target_pairs={{0,1},{1,0},{2,3},{3,2},{4,5},{5,4},{6,7},{7,6},{8,9},{9,8},{10,11... | collective-permute-start | bytes 13832 | tf_op jit(solution)/shard_map/ppermute | solution.py:40
  5.4 0.8 collective-permute-done
  6.4 2.5 %collective-permute-done.1 = bf16[8,768]{1,0:T(8,128)(2,1)S(1)} collective-permute-done((bf16[8,768]{1,0:T(8,128)(2,1)S(1)}, bf16[8,768]{1,0:T(8,128)(2,1)S(1)}, u32[]{:S(2)}, u32[]{:S(2)}) %collective-permute-start.1) | collective-permute-done | bytes 12320 | tf_op jit(solution)/shard_map/ppermute | solution.py:66
  8.9 1.5 %collective-permute-start.2 = (bf16[16,768]{1,0:T(8,128)(2,1)S(1)}, bf16[16,768]{1,0:T(8,128)(2,1)S(1)}, u32[]{:S(2)}, u32[]{:S(2)}) collective-permute-start(bf16[16,768]{1,0:T(8,128)(2,1)S(1)} %pad_maximum_fusion.1), channel_id=1, source_target_pairs={{0,4},{1,5},{2,6},{3,7},{4,8},{5,9},{6,10},{7,11},{8,12},{9,13},{1... | collective-permute-start | bytes 73736 | tf_op jit(solution)/shard_map/ppermute | solution.py:36
  10.4 2.9 %collective-permute-start.3 = (bf16[16,768]{1,0:T(8,128)(2,1)S(1)}, bf16[16,768]{1,0:T(8,128)(2,1)S(1)}, u32[]{:S(2)}, u32[]{:S(2)}) collective-permute-start(bf16[16,768]{1,0:T(8,128)(2,1)S(1)} %pad_maximum_fusion.1), channel_id=1, source_target_pairs={{0,12},{1,13},{2,14},{3,15},{4,0},{5,1},{6,2},{7,3},{8,4},{9,5},{1... | collective-permute-start | bytes 73736 | tf_op jit(solution)/shard_map/ppermute | solution.py:36
  13.3 4.4 %collective-permute-start.4 = (bf16[16,768]{1,0:T(8,128)(2,1)S(1)}, bf16[16,768]{1,0:T(8,128)(2,1)S(1)}, u32[]{:S(2)}, u32[]{:S(2)}) collective-permute-start(bf16[16,768]{1,0:T(8,128)(2,1)S(1)} %pad_maximum_fusion.1), channel_id=1, source_target_pairs={{0,8},{1,9},{2,10},{3,11},{4,12},{5,13},{6,14},{7,15},{8,0},{9,1},... | collective-permute-start | bytes 73736 | tf_op jit(solution)/shard_map/ppermute | solution.py:36
  17.8 2.2 %collective-permute-done.4 = bf16[16,768]{1,0:T(8,128)(2,1)S(1)} collective-permute-done((bf16[16,768]{1,0:T(8,128)(2,1)S(1)}, bf16[16,768]{1,0:T(8,128)(2,1)S(1)}, u32[]{:S(2)}, u32[]{:S(2)}) %collective-permute-start.4) | collective-permute-done | bytes 24608 | tf_op jit(solution)/shard_map/ppermute | solution.py:36
  20.1 2.6 %collective-permute-start.5 = (bf16[48,768]{1,0:T(8,128)(2,1)S(1)}, bf16[48,768]{1,0:T(8,128)(2,1)S(1)}, u32[]{:S(2)}, u32[]{:S(2)}) collective-permute-start(bf16[48,768]{1,0:T(8,128)(2,1)S(1)} %convolution_convert_fusion), channel_id=1, source_target_pairs={{0,48},{16,0},{32,16},{48,32},{64,112},{80,64},{96,80},{112,96},{1... | collective-permute-start | bytes 221192 | tf_op jit(solution)/shard_map/ppermute | solution.py:28
  24.1 3.4 %collective-permute-done.6 = bf16[48,768]{1,0:T(8,128)(2,1)S(1)} collective-permute-done((bf16[48,768]{1,0:T(8,128)(2,1)S(1)}, bf16[48,768]{1,0:T(8,128)(2,1)S(1)}, u32[]{:S(2)}, u32[]{:S(2)}) %collective-permute-start.6) | collective-permute-done | bytes 73760 | tf_op jit(solution)/shard_map/ppermute | solution.py:28
  27.4 0.7 collective-permute-done.7
  28.2 2.8 %collective-permute-start.8 = (bf16[192,768]{1,0:T(8,128)(2,1)S(1)}, bf16[192,768]{1,0:T(8,128)(2,1)S(1)}, u32[]{:S(2)}, u32[]{:S(2)}) collective-permute-start(bf16[192,768]{1,0:T(8,128)(2,1)S(1)} %pad_maximum_fusion.refs_2_), channel_id=1, source_target_pairs={{0,192},{16,208},{32,224},{48,240},{64,0},{80,16},{96,32},{112,48}... | collective-permute-start | bytes 884744 | tf_op jit(solution)/shard_map/ppermute | solution.py:32
  32.1 5.2 %collective-permute-start.11 = (bf16[192,768]{1,0:T(8,128)(2,1)S(1)}, bf16[192,768]{1,0:T(8,128)(2,1)S(1)}, u32[]{:S(2)}, u32[]{:S(2)}) collective-permute-start(bf16[192,768]{1,0:T(8,128)(2,1)S(1)} %pad_maximum_fusion.refs_2_), channel_id=1, source_target_pairs={{0,1},{1,0},{2,3},{3,2},{4,5},{5,4},{6,7},{7,6},{8,9},{9,8},{10,11... | collective-permute-start | bytes 884744 | tf_op jit(solution)/shard_map/ppermute | solution.py:40
  37.3 1.1 collective-permute-done.8.refs_3_
  38.4 6.2 %collective-permute-start.12 = (bf16[192,768]{1,0:T(8,128)(2,1)S(1)}, bf16[192,768]{1,0:T(8,128)(2,1)S(1)}, u32[]{:S(2)}, u32[]{:S(2)}) collective-permute-start(bf16[192,768]{1,0:T(8,128)(2,1)S(1)} %collective-permute-done.8.refs_3_), channel_id=1, source_target_pairs={{0,1},{1,0},{2,3},{3,2},{4,5},{5,4},{6,7},{7,6},{8,9},{9,8},{10,11... | collective-permute-start | bytes 884744 | tf_op jit(solution)/shard_map/ppermute | solution.py:40
  45.7 2.6 %collective-permute-start.14 = (bf16[192,768]{1,0:T(8,128)(2,1)S(1)}, bf16[192,768]{1,0:T(8,128)(2,1)S(1)}, u32[]{:S(2)}, u32[]{:S(2)}) collective-permute-start(bf16[192,768]{1,0:T(8,128)(2,1)S(1)} %collective-permute-done.10.refs_5_), channel_id=1, source_target_pairs={{0,1},{1,0},{2,3},{3,2},{4,5},{5,4},{6,7},{7,6},{8,9},{9,8},{10,11... | collective-permute-start | bytes 884744 | tf_op jit(solution)/shard_map/ppermute | solution.py:40
  50.1 29.4 %shard_map.93 = (bf16[2,768,768]{2,1,0:T(8,128)(2,1)}, bf16[1536,384]{1,0:T(8,128)(2,1)}, bf16[1536,1152]{1,0:T(8,128)(2,1)}, f32[768,768]{1,0:T(8,128)}, bf16[768,768]{1,0:T(8,128)(2,1)}) custom-call(s32[3]{0:T(128)S(1)} %pad_add_fusion.refs_0_.at_ref, s32[12]{0:T(128)S(1)} %bitcast.11, bf16[192,768]{1,0:T(8,128)(2,1)S(1)} %pad_maximum_fusion.refs_2_, ...), custom_call_target="tpu_custom_call" | custom-call | flops 20000000000 | bytes 18000000 | tf_op jit(solution)/shard_map/pallas_call | solution.py:228
  80.0 2.7 %collective-permute-done.15.refs_0_ = bf16[768,768]{1,0:T(8,128)(2,1)S(1)} collective-permute-done((bf16[768,768]{1,0:T(8,128)(2,1)}, bf16[768,768]{1,0:T(8,128)(2,1)S(1)}, u32[]{:S(2)}, u32[]{:S(2)}) %collective-permute-start.15) | collective-permute-done | bytes 1179680 | tf_op jit(solution)/shard_map/ppermute | solution.py:40
  82.7 1.7 %copy-done = f32[768,768]{1,0:T(8,128)S(1)} copy-done((f32[768,768]{1,0:T(8,128)S(1)}, f32[768,768]{1,0:T(8,128)}, u32[]{:S(2)}) %copy-start) | copy-done | bytes 2359320
  84.4 0.7 shard_map.94
  85.2 1.7 %collective-permute-start.17 = (bf16[192,768]{1,0:T(8,128)(2,1)S(1)}, bf16[192,768]{1,0:T(8,128)(2,1)S(1)}, u32[]{:S(2)}, u32[]{:S(2)}) collective-permute-start(bf16[192,768]{1,0:T(8,128)(2,1)S(1)} %get-tuple-element.42), channel_id=1, source_target_pairs={{0,128},{16,144},{32,160},{48,176},{64,192},{80,208},{96,224},{112... | collective-permute-start | bytes 884744 | tf_op jit(solution)/shard_map/ppermute | solution.py:32
  86.9 1.0 collective-permute-start.18
  87.9 7.7 %shard_map.95 = (bf16[12,128,768]{2,1,0:T(8,128)(2,1)}, bf16[12,128,768]{2,1,0:T(8,128)(2,1)}) custom-call(s32[12]{0:T(128)} %bitcast.9, bf16[2,768,768]{2,1,0:T(8,128)(2,1)} %get-tuple-element.27.w_ref, bf16[1536,384]{1,0:T(8,128)(2,1)} %get-tuple-element.28.att_ref, bf16[1536,1152]{1,0:T(8,128)(2,1)} %get-tuple-element.29.gp_ref, ...), custom_call_target="tpu_custom_call" | custom-call | flops 1950000000 | bytes 7500000 | tf_op jit(solution)/shard_map/pallas_call | solution.py:282
  95.6 5.4 %collective-permute-done.16.refs_0_ = bf16[192,768]{1,0:T(8,128)(2,1)S(1)} collective-permute-done((bf16[192,768]{1,0:T(8,128)(2,1)S(1)}, bf16[192,768]{1,0:T(8,128)(2,1)S(1)}, u32[]{:S(2)}, u32[]{:S(2)}) %collective-permute-start.16) | collective-permute-done | bytes 294944 | tf_op jit(solution)/shard_map/ppermute | solution.py:32
  102.1 1.4 %collective-permute-start.20 = (bf16[48,768]{1,0:T(8,128)(2,1)S(1)}, bf16[48,768]{1,0:T(8,128)(2,1)S(1)}, u32[]{:S(2)}, u32[]{:S(2)}) collective-permute-start(bf16[48,768]{1,0:T(8,128)(2,1)S(1)} %get-tuple-element.46), channel_id=1, source_target_pairs={{0,32},{16,48},{32,0},{48,16},{64,96},{80,112},{96,64},{112,80},{1... | collective-permute-start | bytes 221192 | tf_op jit(solution)/shard_map/ppermute | solution.py:28
  103.5 1.6 %collective-permute-start.21 = (bf16[48,768]{1,0:T(8,128)(2,1)S(1)}, bf16[48,768]{1,0:T(8,128)(2,1)S(1)}, u32[]{:S(2)}, u32[]{:S(2)}) collective-permute-start(bf16[48,768]{1,0:T(8,128)(2,1)S(1)} %get-tuple-element.47), channel_id=1, source_target_pairs={{0,48},{16,0},{32,16},{48,32},{64,112},{80,64},{96,80},{112,96},{1... | collective-permute-start | bytes 221192 | tf_op jit(solution)/shard_map/ppermute | solution.py:28
  105.1 2.1 %collective-permute-done.19.refs_0_ = bf16[48,768]{1,0:T(8,128)(2,1)S(1)} collective-permute-done((bf16[48,768]{1,0:T(8,128)(2,1)S(1)}, bf16[48,768]{1,0:T(8,128)(2,1)S(1)}, u32[]{:S(2)}, u32[]{:S(2)}) %collective-permute-start.19) | collective-permute-done | bytes 73760 | tf_op jit(solution)/shard_map/ppermute | solution.py:28
  107.4 0.8 collective-permute-done.21.refs_2_
  108.2 0.7 shard_map.98
  108.9 8.5 %all-to-all-start = ((f32[16,3,768]{2,1,0:T(4,128)}), f32[16,3,768]{2,1,0:T(4,128)S(1)}, u32[]{:S(2)}, u32[]{:S(2)}) async-start(f32[16,3,768]{2,1,0:T(4,128)} %shard_map.98), calls=%async_computation | async-start | bytes 393216 | tf_op jit(solution)/shard_map/all_to_all | solution.py:367
  117.4 7.7 %shard_map.96 = (bf16[12,128,768]{2,1,0:T(8,128)(2,1)}, bf16[12,128,768]{2,1,0:T(8,128)(2,1)}) custom-call(s32[12]{0:T(128)} %bitcast.10, bf16[2,768,768]{2,1,0:T(8,128)(2,1)} %get-tuple-element.27.w_ref, bf16[1536,384]{1,0:T(8,128)(2,1)} %get-tuple-element.28.att_ref, ...), custom_call_target="tpu_custom_call", output_to_operand_aliasing={{0}: (7, {}), {1}: (8, {})} | custom-call | flops 1950000000 | bytes 7500000 | tf_op jit(solution)/shard_map/pallas_call | solution.py:282
  125.1 2.6 %all-to-all-done.got_ref = f32[16,3,768]{2,1,0:T(4,128)S(1)} async-done(((f32[16,3,768]{2,1,0:T(4,128)}), f32[16,3,768]{2,1,0:T(4,128)S(1)}, u32[]{:S(2)}, u32[]{:S(2)}) %all-to-all-start) | async-done | bytes 147488 | tf_op jit(solution)/shard_map/all_to_all | solution.py:367
  (40 shorter events, 8.9 us)
Async XLA Ops:
  2.1 4.2 %collective-permute-start = (bf16[3,768]{1,0:T(4,128)(2,1)S(1)}, bf16[3,768]{1,0:T(4,128)(2,1)S(1)}, u32[]{:S(2)}, u32[]{:S(2)}) collective-permute-start(bf16[3,768]{1,0:T(4,128)(2,1)S(1)} %get-tuple-element.50), channel_id=1, source_target_pairs={{0,1},{1,0},{2,3},{3,2},{4,5},{5,4},{6,7},{7,6},{8,9},{9,8},{10,11... | collective-permute-start | bytes 13832 | tf_op jit(solution)/shard_map/ppermute | solution.py:40
  6.2 2.6 %collective-permute-start.1 = (bf16[8,768]{1,0:T(8,128)(2,1)S(1)}, bf16[8,768]{1,0:T(8,128)(2,1)S(1)}, u32[]{:S(2)}, u32[]{:S(2)}) collective-permute-start(bf16[8,768]{1,0:T(8,128)(2,1)S(1)} %pad_maximum_fusion.2), channel_id=1, source_target_pairs={{0,2},{1,3},{2,0},{3,1},{4,6},{5,7},{6,4},{7,5},{8,10},{9,11},{10,... | collective-permute-start | bytes 36872 | tf_op jit(solution)/shard_map/ppermute | solution.py:66
  8.9 8.8 %collective-permute-start.2 = (bf16[16,768]{1,0:T(8,128)(2,1)S(1)}, bf16[16,768]{1,0:T(8,128)(2,1)S(1)}, u32[]{:S(2)}, u32[]{:S(2)}) collective-permute-start(bf16[16,768]{1,0:T(8,128)(2,1)S(1)} %pad_maximum_fusion.1), channel_id=1, source_target_pairs={{0,4},{1,5},{2,6},{3,7},{4,8},{5,9},{6,10},{7,11},{8,12},{9,13},{1... | collective-permute-start | bytes 73736 | tf_op jit(solution)/shard_map/ppermute | solution.py:36
  10.4 7.4 %collective-permute-start.3 = (bf16[16,768]{1,0:T(8,128)(2,1)S(1)}, bf16[16,768]{1,0:T(8,128)(2,1)S(1)}, u32[]{:S(2)}, u32[]{:S(2)}) collective-permute-start(bf16[16,768]{1,0:T(8,128)(2,1)S(1)} %pad_maximum_fusion.1), channel_id=1, source_target_pairs={{0,12},{1,13},{2,14},{3,15},{4,0},{5,1},{6,2},{7,3},{8,4},{9,5},{1... | collective-permute-start | bytes 73736 | tf_op jit(solution)/shard_map/ppermute | solution.py:36
  13.3 6.6 %collective-permute-start.4 = (bf16[16,768]{1,0:T(8,128)(2,1)S(1)}, bf16[16,768]{1,0:T(8,128)(2,1)S(1)}, u32[]{:S(2)}, u32[]{:S(2)}) collective-permute-start(bf16[16,768]{1,0:T(8,128)(2,1)S(1)} %pad_maximum_fusion.1), channel_id=1, source_target_pairs={{0,8},{1,9},{2,10},{3,11},{4,12},{5,13},{6,14},{7,15},{8,0},{9,1},... | collective-permute-start | bytes 73736 | tf_op jit(solution)/shard_map/ppermute | solution.py:36
  20.1 4.0 %collective-permute-start.5 = (bf16[48,768]{1,0:T(8,128)(2,1)S(1)}, bf16[48,768]{1,0:T(8,128)(2,1)S(1)}, u32[]{:S(2)}, u32[]{:S(2)}) collective-permute-start(bf16[48,768]{1,0:T(8,128)(2,1)S(1)} %convolution_convert_fusion), channel_id=1, source_target_pairs={{0,48},{16,0},{32,16},{48,32},{64,112},{80,64},{96,80},{112,96},{1... | collective-permute-start | bytes 221192 | tf_op jit(solution)/shard_map/ppermute | solution.py:28
  22.7 4.8 %collective-permute-start.6 = (bf16[48,768]{1,0:T(8,128)(2,1)S(1)}, bf16[48,768]{1,0:T(8,128)(2,1)S(1)}, u32[]{:S(2)}, u32[]{:S(2)}) collective-permute-start(bf16[48,768]{1,0:T(8,128)(2,1)S(1)} %convolution_convert_fusion), channel_id=1, source_target_pairs={{0,32},{16,48},{32,0},{48,16},{64,96},{80,112},{96,64},{112,80},{1... | collective-permute-start | bytes 221192 | tf_op jit(solution)/shard_map/ppermute | solution.py:28
  23.2 5.0 %collective-permute-start.7 = (bf16[48,768]{1,0:T(8,128)(2,1)S(1)}, bf16[48,768]{1,0:T(8,128)(2,1)S(1)}, u32[]{:S(2)}, u32[]{:S(2)}) collective-permute-start(bf16[48,768]{1,0:T(8,128)(2,1)S(1)} %convolution_convert_fusion), channel_id=1, source_target_pairs={{0,16},{16,32},{32,48},{48,0},{64,80},{80,96},{96,112},{112,64},{1... | collective-permute-start | bytes 221192 | tf_op jit(solution)/shard_map/ppermute | solution.py:28
  28.2 10.2 %collective-permute-start.8 = (bf16[192,768]{1,0:T(8,128)(2,1)S(1)}, bf16[192,768]{1,0:T(8,128)(2,1)S(1)}, u32[]{:S(2)}, u32[]{:S(2)}) collective-permute-start(bf16[192,768]{1,0:T(8,128)(2,1)S(1)} %pad_maximum_fusion.refs_2_), channel_id=1, source_target_pairs={{0,192},{16,208},{32,224},{48,240},{64,0},{80,16},{96,32},{112,48}... | collective-permute-start | bytes 884744 | tf_op jit(solution)/shard_map/ppermute | solution.py:32
  31.0 13.5 %collective-permute-start.9 = (bf16[192,768]{1,0:T(8,128)(2,1)S(1)}, bf16[192,768]{1,0:T(8,128)(2,1)S(1)}, u32[]{:S(2)}, u32[]{:S(2)}) collective-permute-start(bf16[192,768]{1,0:T(8,128)(2,1)S(1)} %pad_maximum_fusion.refs_2_), channel_id=1, source_target_pairs={{0,128},{16,144},{32,160},{48,176},{64,192},{80,208},{96,224},{112... | collective-permute-start | bytes 884744 | tf_op jit(solution)/shard_map/ppermute | solution.py:32
  31.4 14.3 %collective-permute-start.10 = (bf16[192,768]{1,0:T(8,128)(2,1)S(1)}, bf16[192,768]{1,0:T(8,128)(2,1)S(1)}, u32[]{:S(2)}, u32[]{:S(2)}) collective-permute-start(bf16[192,768]{1,0:T(8,128)(2,1)S(1)} %pad_maximum_fusion.refs_2_), channel_id=1, source_target_pairs={{0,64},{16,80},{32,96},{48,112},{64,128},{80,144},{96,160},{112,17... | collective-permute-start | bytes 884744 | tf_op jit(solution)/shard_map/ppermute | solution.py:32
  32.1 17.0 %collective-permute-start.11 = (bf16[192,768]{1,0:T(8,128)(2,1)S(1)}, bf16[192,768]{1,0:T(8,128)(2,1)S(1)}, u32[]{:S(2)}, u32[]{:S(2)}) collective-permute-start(bf16[192,768]{1,0:T(8,128)(2,1)S(1)} %pad_maximum_fusion.refs_2_), channel_id=1, source_target_pairs={{0,1},{1,0},{2,3},{3,2},{4,5},{5,4},{6,7},{7,6},{8,9},{9,8},{10,11... | collective-permute-start | bytes 884744 | tf_op jit(solution)/shard_map/ppermute | solution.py:40
  38.4 10.6 %collective-permute-start.12 = (bf16[192,768]{1,0:T(8,128)(2,1)S(1)}, bf16[192,768]{1,0:T(8,128)(2,1)S(1)}, u32[]{:S(2)}, u32[]{:S(2)}) collective-permute-start(bf16[192,768]{1,0:T(8,128)(2,1)S(1)} %collective-permute-done.8.refs_3_), channel_id=1, source_target_pairs={{0,1},{1,0},{2,3},{3,2},{4,5},{5,4},{6,7},{7,6},{8,9},{9,8},{10,11... | collective-permute-start | bytes 884744 | tf_op jit(solution)/shard_map/ppermute | solution.py:40
  44.6 4.5 %collective-permute-start.13 = (bf16[192,768]{1,0:T(8,128)(2,1)S(1)}, bf16[192,768]{1,0:T(8,128)(2,1)S(1)}, u32[]{:S(2)}, u32[]{:S(2)}) collective-permute-start(bf16[192,768]{1,0:T(8,128)(2,1)S(1)} %collective-permute-done.9.refs_4_), channel_id=1, source_target_pairs={{0,1},{1,0},{2,3},{3,2},{4,5},{5,4},{6,7},{7,6},{8,9},{9,8},{10,11... | collective-permute-start | bytes 884744 | tf_op jit(solution)/shard_map/ppermute | solution.py:40
  45.7 3.8 %collective-permute-start.14 = (bf16[192,768]{1,0:T(8,128)(2,1)S(1)}, bf16[192,768]{1,0:T(8,128)(2,1)S(1)}, u32[]{:S(2)}, u32[]{:S(2)}) collective-permute-start(bf16[192,768]{1,0:T(8,128)(2,1)S(1)} %collective-permute-done.10.refs_5_), channel_id=1, source_target_pairs={{0,1},{1,0},{2,3},{3,2},{4,5},{5,4},{6,7},{7,6},{8,9},{9,8},{10,11... | collective-permute-start | bytes 884744 | tf_op jit(solution)/shard_map/ppermute | solution.py:40
  49.0 30.6 %copy-start.1 = (f32[1,768]{1,0:T(1,128)}, f32[1,768]{1,0:T(1,128)S(1)}, u32[]{:S(2)}) copy-start(f32[1,768]{1,0:T(1,128)S(1)} %broadcast_in_dim.25.refs_12_.gain_ref) | copy-start | bytes 9220
  49.5 0.7 copy-start.2
  79.6 3.1 %collective-permute-start.15 = (bf16[768,768]{1,0:T(8,128)(2,1)}, bf16[768,768]{1,0:T(8,128)(2,1)S(1)}, u32[]{:S(2)}, u32[]{:S(2)}) collective-permute-start(bf16[768,768]{1,0:T(8,128)(2,1)} %get-tuple-element.31), channel_id=1, source_target_pairs={{0,1},{1,0},{2,3},{3,2},{4,5},{5,4},{6,7},{7,6},{8,9},{9,8},{10,11... | collective-permute-start | bytes 3538952 | tf_op jit(solution)/shard_map/ppermute | solution.py:40
  82.7 1.7 %copy-start = (f32[768,768]{1,0:T(8,128)S(1)}, f32[768,768]{1,0:T(8,128)}, u32[]{:S(2)}) copy-start(f32[768,768]{1,0:T(8,128)} %get-tuple-element.30.own_ref) | copy-start | bytes 7077892
  85.1 15.9 %collective-permute-start.16 = (bf16[192,768]{1,0:T(8,128)(2,1)S(1)}, bf16[192,768]{1,0:T(8,128)(2,1)S(1)}, u32[]{:S(2)}, u32[]{:S(2)}) collective-permute-start(bf16[192,768]{1,0:T(8,128)(2,1)S(1)} %get-tuple-element.32), channel_id=1, source_target_pairs={{0,64},{16,80},{32,96},{48,112},{64,128},{80,144},{96,160},{112,17... | collective-permute-start | bytes 884744 | tf_op jit(solution)/shard_map/ppermute | solution.py:32
  85.2 15.8 %collective-permute-start.17 = (bf16[192,768]{1,0:T(8,128)(2,1)S(1)}, bf16[192,768]{1,0:T(8,128)(2,1)S(1)}, u32[]{:S(2)}, u32[]{:S(2)}) collective-permute-start(bf16[192,768]{1,0:T(8,128)(2,1)S(1)} %get-tuple-element.42), channel_id=1, source_target_pairs={{0,128},{16,144},{32,160},{48,176},{64,192},{80,208},{96,224},{112... | collective-permute-start | bytes 884744 | tf_op jit(solution)/shard_map/ppermute | solution.py:32
  86.9 14.4 %collective-permute-start.18 = (bf16[192,768]{1,0:T(8,128)(2,1)S(1)}, bf16[192,768]{1,0:T(8,128)(2,1)S(1)}, u32[]{:S(2)}, u32[]{:S(2)}) collective-permute-start(bf16[192,768]{1,0:T(8,128)(2,1)S(1)} %get-tuple-element.43), channel_id=1, source_target_pairs={{0,192},{16,208},{32,224},{48,240},{64,0},{80,16},{96,32},{112,48}... | collective-permute-start | bytes 884744 | tf_op jit(solution)/shard_map/ppermute | solution.py:32
  102.0 5.2 %collective-permute-start.19 = (bf16[48,768]{1,0:T(8,128)(2,1)S(1)}, bf16[48,768]{1,0:T(8,128)(2,1)S(1)}, u32[]{:S(2)}, u32[]{:S(2)}) collective-permute-start(bf16[48,768]{1,0:T(8,128)(2,1)S(1)} %get-tuple-element.45), channel_id=1, source_target_pairs={{0,16},{16,32},{32,48},{48,0},{64,80},{80,96},{96,112},{112,64},{1... | collective-permute-start | bytes 221192 | tf_op jit(solution)/shard_map/ppermute | solution.py:28
  102.1 5.3 %collective-permute-start.20 = (bf16[48,768]{1,0:T(8,128)(2,1)S(1)}, bf16[48,768]{1,0:T(8,128)(2,1)S(1)}, u32[]{:S(2)}, u32[]{:S(2)}) collective-permute-start(bf16[48,768]{1,0:T(8,128)(2,1)S(1)} %get-tuple-element.46), channel_id=1, source_target_pairs={{0,32},{16,48},{32,0},{48,16},{64,96},{80,112},{96,64},{112,80},{1... | collective-permute-start | bytes 221192 | tf_op jit(solution)/shard_map/ppermute | solution.py:28
  103.5 4.6 %collective-permute-start.21 = (bf16[48,768]{1,0:T(8,128)(2,1)S(1)}, bf16[48,768]{1,0:T(8,128)(2,1)S(1)}, u32[]{:S(2)}, u32[]{:S(2)}) collective-permute-start(bf16[48,768]{1,0:T(8,128)(2,1)S(1)} %get-tuple-element.47), channel_id=1, source_target_pairs={{0,48},{16,0},{32,16},{48,32},{64,112},{80,64},{96,80},{112,96},{1... | collective-permute-start | bytes 221192 | tf_op jit(solution)/shard_map/ppermute | solution.py:28
  108.9 18.8 %all-to-all-start = ((f32[16,3,768]{2,1,0:T(4,128)}), f32[16,3,768]{2,1,0:T(4,128)S(1)}, u32[]{:S(2)}, u32[]{:S(2)}) async-start(f32[16,3,768]{2,1,0:T(4,128)} %shard_map.98), calls=%async_computation | async-start | bytes 393216 | tf_op jit(solution)/shard_map/all_to_all | solution.py:367

commit v7 on v6

--- a/solution.py
+++ b/solution.py
@@ -13,12 +13,13 @@
 HD = 384
 VMAX = 128
 BLOCKS = 12
+STEPS = (0, 2, 1, 3)
 GROUP = 4
 ROWS = GROUP * VMAX
 TAIL = 2
 HEAD = 3
 NORM_MIB = 0
-CORE_MIB = 51
+CORE_MIB = 48
 TAIL_MIB = 60
 BF16 = jnp.bfloat16
 F32 = jnp.float32
@@ -46,15 +47,8 @@
     return il // 4, il % 4, xl // 2, xl % 2
 
 
-def gather4(v, hop, direct):
-    r1 = hop(v, -1)
-    r3 = hop(v, 1)
-    if direct:
-        r2 = hop(v, 2)
-    else:
-        h = v.shape[0] // 2
-        r2 = jnp.concatenate([hop(r1[:h], -1), hop(r3[h:], 1)], axis=0)
-    return [v, r1, r2, r3]
+def gather4(v, hop):
+    return [v, hop(v, 2), hop(v, -1), hop(v, 1)]
 
 
 def gather_weights(w):
@@ -64,17 +58,17 @@
     other = lax.dynamic_slice(w, (0, (1 - c) * n), (3, n))
     block = jnp.concatenate([mine, hop_core(other), jnp.zeros((2, n), w.dtype)], axis=0)
     block = jnp.concatenate([block, lax.ppermute(block, "xl", [(i, i ^ 2) for i in range(16)])], axis=0)
-    stack = jnp.concatenate([block, hop_z(block, 2), hop_z(block, -2), hop_z(block, 4)], axis=0)
+    stack = jnp.concatenate([block, hop_z(block, 4), hop_z(block, 2), hop_z(block, -2)], axis=0)
     r = jnp.arange(48)[:, None]
     s = jnp.arange(64)[None, :]
     slot = s // 16
     j = s % 8
-    origin = (z + jnp.where(slot == 3, 4, jnp.where(slot == 2, 2, jnp.where(slot == 1, 6, 0)))) % 8
+    origin = (z + jnp.where(slot == 1, 4, jnp.where(slot == 2, 6, jnp.where(slot == 3, 2, 0)))) % 8
     row = (origin ^ ((s // 8) % 2)) * 6 + (c ^ (j // 3)) * 3 + j % 3
     order = ((row == r) & (j < 6)).astype(w.dtype)
     v = jnp.dot(order, stack, preferred_element_type=F32).astype(w.dtype)
-    v = jnp.concatenate(gather4(v, hop_x, True), axis=0)
-    mine = gather4(v, hop_y, True)
+    v = jnp.concatenate(gather4(v, hop_x), axis=0)
+    mine = gather4(v, hop_y)
     return mine + [hop_core(u) for u in mine]
 
 
@@ -120,7 +114,7 @@
             half = core ^ rel
             for ky in range(4):
                 for kx in range(4):
-                    row = pl.multiple_of(((y + ky) & 3) * 192 + ((x + kx) & 3) * 48, 16)
+                    row = pl.multiple_of(((y + STEPS[ky]) & 3) * 192 + ((x + STEPS[kx]) & 3) * 48, 16)
                     copies.append(
                         pltpu.make_async_copy(
                             pieces[rel * 4 + ky].at[pl.ds(kx * 48, 48), :],
@@ -246,9 +240,9 @@
             ],
         ),
         out_shape=[
-            jax.ShapeDtypeStruct((2, D, D), BF16),
-            jax.ShapeDtypeStruct((rows, HD), BF16),
-            jax.ShapeDtypeStruct((rows, 3 * HD), BF16),
+            pltpu.HBM((2, D, D), BF16),
+            pltpu.HBM((rows, HD), BF16),
+            pltpu.HBM((rows, 3 * HD), BF16),
             jax.ShapeDtypeStruct((D, D), F32),
             jax.ShapeDtypeStruct((D, D), BF16),
         ],
@@ -357,11 +351,11 @@
 
 def scatter_grads(at, keep, send, during):
     own, *out = cut(at, 0, keep, hop_core(send))
-    got = [hop_y(v, k + 1) for k, v in enumerate(out)]
+    got = [hop_y(out[k - 1], k) for k in (2, 1, 3)]
     extra = during(own)
     got[0], extra = lax.optimization_barrier((got[0], extra))
     own, *out = cut(at, 1, own, *got)
-    parts = [own] + [hop_x(v, k + 1) for k, v in enumerate(out)]
+    parts = [own] + [hop_x(out[k - 1], k) for k in (2, 1, 3)]
     n = keep.shape[1]
     (v,) = small_call(triples_kernel, None, parts, [((16, 3, n), F32)])
     got = lax.all_to_all(v, "xl", split_axis=0, concat_axis=0, tiled=True)

time: 129 us -> 124 us (0.961)
  waiting for transfers between devices: 25.9 us -> 24.1 us
  local copies, waits for them, and re-layouts: 4.45 us -> 2.79 us
  starting transfers between devices: 49.2 us -> 47.7 us
    all_to_all x1, starting transfers between devices: 8.51 us -> 5.64 us  [scatter_grads(): got = lax.all_to_all(v, 'xl', split_axis=0, concat_axis=0, tiled=True)]
    ppermute x6, starting transfers between devices: 6.6 us -> 9.33 us  [hop_y(): return lax.ppermute(v, 'il', [(i, (i + 4 * k) % 16) for i in range(16)])]
    ppermute x6, waiting for transfers between devices: 7.25 us -> 4.6 us  [hop_y(): return lax.ppermute(v, 'il', [(i, (i + 4 * k) % 16) for i in range(16)])]
    ppermute x6, starting transfers between devices: 18.4 us -> 16.7 us  [hop_core(): return lax.ppermute(v, 'xl', [(i, i ^ 1) for i in range(16)])]
    unnamed x7 -> x5, local copies, waits for them, and re-layouts: 3.03 us -> 1.36 us
  transfers between devices with their start and end apart: 23 -> 23, of which waited for: 16 -> 15; matrix products, arithmetic and copies ran while one was open for 1% -> 1% of each run, Pallas kernels for 12% -> 13%
where the time goes in v7:
time: 124 us; the launch traced here: 123 us
  starting transfers between devices  47.7 us (38%)
  Pallas kernels  47.5 us (38%)
  waiting for transfers between devices  24.1 us (19%)
  local copies, waits for them, and re-layouts  2.79 us (2%)
    pallas_call x1, Pallas kernels, grads_core(): pl.pallas_call(core_kernel, grid_spec=pltpu.PrefetchScalarGridSpec(num_sc...  29.2 us
    ppermute x6, starting transfers between devices, hop_core(): return lax.ppermute(v, 'xl', [(i, i ^ 1) for i in range(16)])  16.7 us
    pallas_call x2, Pallas kernels, rows_part(): pl.pallas_call(functools.partial(rows_kernel, first), grid_spec=pltpu.Pre...  15.4 us
    ppermute x6, starting transfers between devices, hop_y(): return lax.ppermute(v, 'il', [(i, (i + 4 * k) % 16) for i in range(16)])  9.33 us
    ppermute x3, starting transfers between devices, hop_z(): return lax.ppermute(v, 'xl', [(i, (i + 2 * k) % 16) for i in range(16)])  8.84 us
    ppermute x6, waiting for transfers between devices, hop_x(): lax.ppermute(v, 'il', [(i, i // 4 * 4 + (i + k) % 4) for i in range(16)])  8.52 us
    ppermute x6, starting transfers between devices, hop_x(): lax.ppermute(v, 'il', [(i, i // 4 * 4 + (i + k) % 4) for i in range(16)])  7.14 us
    all_to_all x1, starting transfers between devices, scatter_grads(): got = lax.all_to_all(v, 'xl', split_axis=0, concat_axis=0, tiled=True)  5.64 us
  transfers between devices with their start and end apart: 23, of which 15 were waited for; matrix products, arithmetic and copies ran while one was open for 1% of the time, Pallas kernels for 13%

profile of v7, /device:TPU:1, one launch (start us, length us, event | category | flops | bytes accessed | tf_op | source)
XLA Modules:
  0.0 123.2 jit_solution(6216197026589075991)
XLA Ops:
  0.7 0.7 constant_dynamic-update-slice_fusion.1
  2.1 3.3 %collective-permute-start = (bf16[3,768]{1,0:T(4,128)(2,1)S(1)}, bf16[3,768]{1,0:T(4,128)(2,1)S(1)}, u32[]{:S(2)}, u32[]{:S(2)}) collective-permute-start(bf16[3,768]{1,0:T(4,128)(2,1)S(1)} %get-tuple-element.50), channel_id=1, source_target_pairs={{0,1},{1,0},{2,3},{3,2},{4,5},{5,4},{6,7},{7,6},{8,9},{9,8},{10,11... | collective-permute-start | bytes 13832 | tf_op jit(solution)/shard_map/ppermute | solution.py:41
  5.4 0.8 collective-permute-done
  6.4 2.5 %collective-permute-done.1 = bf16[8,768]{1,0:T(8,128)(2,1)S(1)} collective-permute-done((bf16[8,768]{1,0:T(8,128)(2,1)S(1)}, bf16[8,768]{1,0:T(8,128)(2,1)S(1)}, u32[]{:S(2)}, u32[]{:S(2)}) %collective-permute-start.1) | collective-permute-done | bytes 12320 | tf_op jit(solution)/shard_map/ppermute | solution.py:60
  8.9 5.3 %collective-permute-start.2 = (bf16[16,768]{1,0:T(8,128)(2,1)S(1)}, bf16[16,768]{1,0:T(8,128)(2,1)S(1)}, u32[]{:S(2)}, u32[]{:S(2)}) collective-permute-start(bf16[16,768]{1,0:T(8,128)(2,1)S(1)} %pad_maximum_fusion.1), channel_id=1, source_target_pairs={{0,8},{1,9},{2,10},{3,11},{4,12},{5,13},{6,14},{7,15},{8,0},{9,1},... | collective-permute-start | bytes 73736 | tf_op jit(solution)/shard_map/ppermute | solution.py:37
  14.2 1.2 collective-permute-start.3
  15.3 2.4 %collective-permute-start.4 = (bf16[16,768]{1,0:T(8,128)(2,1)S(1)}, bf16[16,768]{1,0:T(8,128)(2,1)S(1)}, u32[]{:S(2)}, u32[]{:S(2)}) collective-permute-start(bf16[16,768]{1,0:T(8,128)(2,1)S(1)} %pad_maximum_fusion.1), channel_id=1, source_target_pairs={{0,12},{1,13},{2,14},{3,15},{4,0},{5,1},{6,2},{7,3},{8,4},{9,5},{1... | collective-permute-start | bytes 73736 | tf_op jit(solution)/shard_map/ppermute | solution.py:37
  17.8 1.2 collective-permute-done.3
  19.6 2.8 %collective-permute-start.5 = (bf16[48,768]{1,0:T(8,128)(2,1)S(1)}, bf16[48,768]{1,0:T(8,128)(2,1)S(1)}, u32[]{:S(2)}, u32[]{:S(2)}) collective-permute-start(bf16[48,768]{1,0:T(8,128)(2,1)S(1)} %convolution_convert_fusion), channel_id=1, source_target_pairs={{0,32},{16,48},{32,0},{48,16},{64,96},{80,112},{96,64},{112,80},{1... | collective-permute-start | bytes 221192 | tf_op jit(solution)/shard_map/ppermute | solution.py:29
  22.5 0.9 collective-permute-start.6
  24.4 1.2 %collective-permute-done.6 = bf16[48,768]{1,0:T(8,128)(2,1)S(1)} collective-permute-done((bf16[48,768]{1,0:T(8,128)(2,1)S(1)}, bf16[48,768]{1,0:T(8,128)(2,1)S(1)}, u32[]{:S(2)}, u32[]{:S(2)}) %collective-permute-start.6) | collective-permute-done | bytes 73760 | tf_op jit(solution)/shard_map/ppermute | solution.py:29
  25.7 2.7 %collective-permute-done.7 = bf16[48,768]{1,0:T(8,128)(2,1)S(1)} collective-permute-done((bf16[48,768]{1,0:T(8,128)(2,1)S(1)}, bf16[48,768]{1,0:T(8,128)(2,1)S(1)}, u32[]{:S(2)}, u32[]{:S(2)}) %collective-permute-start.7) | collective-permute-done | bytes 73760 | tf_op jit(solution)/shard_map/ppermute | solution.py:29
  28.4 3.0 %collective-permute-start.8 = (bf16[192,768]{1,0:T(8,128)(2,1)S(1)}, bf16[192,768]{1,0:T(8,128)(2,1)S(1)}, u32[]{:S(2)}, u32[]{:S(2)}) collective-permute-start(bf16[192,768]{1,0:T(8,128)(2,1)S(1)} %pad_maximum_fusion.refs_2_), channel_id=1, source_target_pairs={{0,128},{16,144},{32,160},{48,176},{64,192},{80,208},{96,224},{112... | collective-permute-start | bytes 884744 | tf_op jit(solution)/shard_map/ppermute | solution.py:33
  31.4 0.8 collective-permute-start.9
  32.8 4.6 %collective-permute-start.11 = (bf16[192,768]{1,0:T(8,128)(2,1)S(1)}, bf16[192,768]{1,0:T(8,128)(2,1)S(1)}, u32[]{:S(2)}, u32[]{:S(2)}) collective-permute-start(bf16[192,768]{1,0:T(8,128)(2,1)S(1)} %pad_maximum_fusion.refs_2_), channel_id=1, source_target_pairs={{0,1},{1,0},{2,3},{3,2},{4,5},{5,4},{6,7},{7,6},{8,9},{9,8},{10,11... | collective-permute-start | bytes 884744 | tf_op jit(solution)/shard_map/ppermute | solution.py:41
  37.5 5.2 %collective-permute-start.12 = (bf16[192,768]{1,0:T(8,128)(2,1)S(1)}, bf16[192,768]{1,0:T(8,128)(2,1)S(1)}, u32[]{:S(2)}, u32[]{:S(2)}) collective-permute-start(bf16[192,768]{1,0:T(8,128)(2,1)S(1)} %collective-permute-done.8.refs_3_), channel_id=1, source_target_pairs={{0,1},{1,0},{2,3},{3,2},{4,5},{5,4},{6,7},{7,6},{8,9},{9,8},{10,11... | collective-permute-start | bytes 884744 | tf_op jit(solution)/shard_map/ppermute | solution.py:41
  43.0 3.1 %collective-permute-start.13 = (bf16[192,768]{1,0:T(8,128)(2,1)S(1)}, bf16[192,768]{1,0:T(8,128)(2,1)S(1)}, u32[]{:S(2)}, u32[]{:S(2)}) collective-permute-start(bf16[192,768]{1,0:T(8,128)(2,1)S(1)} %collective-permute-done.9.refs_4_), channel_id=1, source_target_pairs={{0,1},{1,0},{2,3},{3,2},{4,5},{5,4},{6,7},{7,6},{8,9},{9,8},{10,11... | collective-permute-start | bytes 884744 | tf_op jit(solution)/shard_map/ppermute | solution.py:41
  48.4 29.2 %shard_map.93 = (bf16[2,768,768]{2,1,0:T(8,128)(2,1)}, bf16[1536,384]{1,0:T(8,128)(2,1)}, bf16[1536,1152]{1,0:T(8,128)(2,1)}, f32[768,768]{1,0:T(8,128)S(1)}, bf16[768,768]{1,0:T(8,128)(2,1)S(1)}) custom-call(s32[3]{0:T(128)S(1)} %pad_add_fusion.refs_0_.at_ref, s32[12]{0:T(128)S(1)} %bitcast.11, bf16[192,768]{1,0:T(8,128)(2,1)S(1)} %pad_maximum_fusion.refs_2_, ...), custom_call_target="tpu_custom_call" | custom-call | flops 20000000000 | bytes 18000000 | tf_op jit(solution)/shard_map/pallas_call | solution.py:222
  78.1 2.5 %collective-permute-done.15.refs_0_ = bf16[768,768]{1,0:T(8,128)(2,1)S(1)} collective-permute-done((bf16[768,768]{1,0:T(8,128)(2,1)S(1)}, bf16[768,768]{1,0:T(8,128)(2,1)S(1)}, u32[]{:S(2)}, u32[]{:S(2)}) %collective-permute-start.15) | collective-permute-done | bytes 1179680 | tf_op jit(solution)/shard_map/ppermute | solution.py:41
  80.6 0.8 shard_map.94
  81.4 2.2 %collective-permute-start.16 = (bf16[192,768]{1,0:T(8,128)(2,1)S(1)}, bf16[192,768]{1,0:T(8,128)(2,1)S(1)}, u32[]{:S(2)}, u32[]{:S(2)}) collective-permute-start(bf16[192,768]{1,0:T(8,128)(2,1)S(1)} %get-tuple-element.32), channel_id=1, source_target_pairs={{0,128},{16,144},{32,160},{48,176},{64,192},{80,208},{96,224},{112... | collective-permute-start | bytes 884744 | tf_op jit(solution)/shard_map/ppermute | solution.py:33
  83.6 0.8 collective-permute-start.17
  84.4 1.9 %collective-permute-start.18 = (bf16[192,768]{1,0:T(8,128)(2,1)S(1)}, bf16[192,768]{1,0:T(8,128)(2,1)S(1)}, u32[]{:S(2)}, u32[]{:S(2)}) collective-permute-start(bf16[192,768]{1,0:T(8,128)(2,1)S(1)} %get-tuple-element.43), channel_id=1, source_target_pairs={{0,192},{16,208},{32,224},{48,240},{64,0},{80,16},{96,32},{112,48}... | collective-permute-start | bytes 884744 | tf_op jit(solution)/shard_map/ppermute | solution.py:33
  86.3 7.7 %shard_map.95 = (bf16[12,128,768]{2,1,0:T(8,128)(2,1)}, bf16[12,128,768]{2,1,0:T(8,128)(2,1)}) custom-call(s32[12]{0:T(128)} %bitcast.9, bf16[2,768,768]{2,1,0:T(8,128)(2,1)} %get-tuple-element.27.w_ref, bf16[1536,384]{1,0:T(8,128)(2,1)} %get-tuple-element.28.att_ref, bf16[1536,1152]{1,0:T(8,128)(2,1)} %get-tuple-element.29.gp_ref, ...), custom_call_target="tpu_custom_call" | custom-call | flops 1950000000 | bytes 7500000 | tf_op jit(solution)/shard_map/pallas_call | solution.py:276
  94.0 4.2 %collective-permute-done.17.refs_1_ = bf16[192,768]{1,0:T(8,128)(2,1)S(1)} collective-permute-done((bf16[192,768]{1,0:T(8,128)(2,1)S(1)}, bf16[192,768]{1,0:T(8,128)(2,1)S(1)}, u32[]{:S(2)}, u32[]{:S(2)}) %collective-permute-start.17) | collective-permute-done | bytes 294944 | tf_op jit(solution)/shard_map/ppermute | solution.py:33
  99.2 2.6 %collective-permute-start.21 = (bf16[48,768]{1,0:T(8,128)(2,1)S(1)}, bf16[48,768]{1,0:T(8,128)(2,1)S(1)}, u32[]{:S(2)}, u32[]{:S(2)}) collective-permute-start(bf16[48,768]{1,0:T(8,128)(2,1)S(1)} %get-tuple-element.47), channel_id=1, source_target_pairs={{0,48},{16,0},{32,16},{48,32},{64,112},{80,64},{96,80},{112,96},{1... | collective-permute-start | bytes 221192 | tf_op jit(solution)/shard_map/ppermute | solution.py:29
  101.8 2.0 %collective-permute-done.19.refs_0_ = bf16[48,768]{1,0:T(8,128)(2,1)S(1)} collective-permute-done((bf16[48,768]{1,0:T(8,128)(2,1)S(1)}, bf16[48,768]{1,0:T(8,128)(2,1)S(1)}, u32[]{:S(2)}, u32[]{:S(2)}) %collective-permute-start.19) | collective-permute-done | bytes 73760 | tf_op jit(solution)/shard_map/ppermute | solution.py:29
  103.8 2.1 %collective-permute-done.20.refs_1_ = bf16[48,768]{1,0:T(8,128)(2,1)S(1)} collective-permute-done((bf16[48,768]{1,0:T(8,128)(2,1)S(1)}, bf16[48,768]{1,0:T(8,128)(2,1)S(1)}, u32[]{:S(2)}, u32[]{:S(2)}) %collective-permute-start.20) | collective-permute-done | bytes 73760 | tf_op jit(solution)/shard_map/ppermute | solution.py:29
  105.9 0.7 shard_map.98
  106.6 5.6 %all-to-all-start = ((f32[16,3,768]{2,1,0:T(4,128)}), f32[16,3,768]{2,1,0:T(4,128)S(1)}, u32[]{:S(2)}, u32[]{:S(2)}) async-start(f32[16,3,768]{2,1,0:T(4,128)} %shard_map.98), calls=%async_computation | async-start | bytes 393216 | tf_op jit(solution)/shard_map/all_to_all | solution.py:361
  112.3 7.7 %shard_map.96 = (bf16[12,128,768]{2,1,0:T(8,128)(2,1)}, bf16[12,128,768]{2,1,0:T(8,128)(2,1)}) custom-call(s32[12]{0:T(128)} %bitcast.10, bf16[2,768,768]{2,1,0:T(8,128)(2,1)} %get-tuple-element.27.w_ref, bf16[1536,384]{1,0:T(8,128)(2,1)} %get-tuple-element.28.att_ref, ...), custom_call_target="tpu_custom_call", output_to_operand_aliasing={{0}: (7, {}), {1}: (8, {})} | custom-call | flops 1950000000 | bytes 7500000 | tf_op jit(solution)/shard_map/pallas_call | solution.py:276
  120.0 2.6 %all-to-all-done.got_ref = f32[16,3,768]{2,1,0:T(4,128)S(1)} async-done(((f32[16,3,768]{2,1,0:T(4,128)}), f32[16,3,768]{2,1,0:T(4,128)S(1)}, u32[]{:S(2)}, u32[]{:S(2)}) %all-to-all-start) | async-done | bytes 147488 | tf_op jit(solution)/shard_map/all_to_all | solution.py:361
  (38 shorter events, 8.0 us)
Async XLA Ops:
  2.1 4.2 %collective-permute-start = (bf16[3,768]{1,0:T(4,128)(2,1)S(1)}, bf16[3,768]{1,0:T(4,128)(2,1)S(1)}, u32[]{:S(2)}, u32[]{:S(2)}) collective-permute-start(bf16[3,768]{1,0:T(4,128)(2,1)S(1)} %get-tuple-element.50), channel_id=1, source_target_pairs={{0,1},{1,0},{2,3},{3,2},{4,5},{5,4},{6,7},{7,6},{8,9},{9,8},{10,11... | collective-permute-start | bytes 13832 | tf_op jit(solution)/shard_map/ppermute | solution.py:41
  6.2 2.6 %collective-permute-start.1 = (bf16[8,768]{1,0:T(8,128)(2,1)S(1)}, bf16[8,768]{1,0:T(8,128)(2,1)S(1)}, u32[]{:S(2)}, u32[]{:S(2)}) collective-permute-start(bf16[8,768]{1,0:T(8,128)(2,1)S(1)} %pad_maximum_fusion.2), channel_id=1, source_target_pairs={{0,2},{1,3},{2,0},{3,1},{4,6},{5,7},{6,4},{7,5},{8,10},{9,11},{10,... | collective-permute-start | bytes 36872 | tf_op jit(solution)/shard_map/ppermute | solution.py:60
  8.9 8.9 %collective-permute-start.2 = (bf16[16,768]{1,0:T(8,128)(2,1)S(1)}, bf16[16,768]{1,0:T(8,128)(2,1)S(1)}, u32[]{:S(2)}, u32[]{:S(2)}) collective-permute-start(bf16[16,768]{1,0:T(8,128)(2,1)S(1)} %pad_maximum_fusion.1), channel_id=1, source_target_pairs={{0,8},{1,9},{2,10},{3,11},{4,12},{5,13},{6,14},{7,15},{8,0},{9,1},... | collective-permute-start | bytes 73736 | tf_op jit(solution)/shard_map/ppermute | solution.py:37
  14.2 4.8 %collective-permute-start.3 = (bf16[16,768]{1,0:T(8,128)(2,1)S(1)}, bf16[16,768]{1,0:T(8,128)(2,1)S(1)}, u32[]{:S(2)}, u32[]{:S(2)}) collective-permute-start(bf16[16,768]{1,0:T(8,128)(2,1)S(1)} %pad_maximum_fusion.1), channel_id=1, source_target_pairs={{0,4},{1,5},{2,6},{3,7},{4,8},{5,9},{6,10},{7,11},{8,12},{9,13},{1... | collective-permute-start | bytes 73736 | tf_op jit(solution)/shard_map/ppermute | solution.py:37
  15.3 4.1 %collective-permute-start.4 = (bf16[16,768]{1,0:T(8,128)(2,1)S(1)}, bf16[16,768]{1,0:T(8,128)(2,1)S(1)}, u32[]{:S(2)}, u32[]{:S(2)}) collective-permute-start(bf16[16,768]{1,0:T(8,128)(2,1)S(1)} %pad_maximum_fusion.1), channel_id=1, source_target_pairs={{0,12},{1,13},{2,14},{3,15},{4,0},{5,1},{6,2},{7,3},{8,4},{9,5},{1... | collective-permute-start | bytes 73736 | tf_op jit(solution)/shard_map/ppermute | solution.py:37
  19.6 4.8 %collective-permute-start.5 = (bf16[48,768]{1,0:T(8,128)(2,1)S(1)}, bf16[48,768]{1,0:T(8,128)(2,1)S(1)}, u32[]{:S(2)}, u32[]{:S(2)}) collective-permute-start(bf16[48,768]{1,0:T(8,128)(2,1)S(1)} %convolution_convert_fusion), channel_id=1, source_target_pairs={{0,32},{16,48},{32,0},{48,16},{64,96},{80,112},{96,64},{112,80},{1... | collective-permute-start | bytes 221192 | tf_op jit(solution)/shard_map/ppermute | solution.py:29
  22.5 3.2 %collective-permute-start.6 = (bf16[48,768]{1,0:T(8,128)(2,1)S(1)}, bf16[48,768]{1,0:T(8,128)(2,1)S(1)}, u32[]{:S(2)}, u32[]{:S(2)}) collective-permute-start(bf16[48,768]{1,0:T(8,128)(2,1)S(1)} %convolution_convert_fusion), channel_id=1, source_target_pairs={{0,48},{16,0},{32,16},{48,32},{64,112},{80,64},{96,80},{112,96},{1... | collective-permute-start | bytes 221192 | tf_op jit(solution)/shard_map/ppermute | solution.py:29
  23.3 5.0 %collective-permute-start.7 = (bf16[48,768]{1,0:T(8,128)(2,1)S(1)}, bf16[48,768]{1,0:T(8,128)(2,1)S(1)}, u32[]{:S(2)}, u32[]{:S(2)}) collective-permute-start(bf16[48,768]{1,0:T(8,128)(2,1)S(1)} %convolution_convert_fusion), channel_id=1, source_target_pairs={{0,16},{16,32},{32,48},{48,0},{64,80},{80,96},{96,112},{112,64},{1... | collective-permute-start | bytes 221192 | tf_op jit(solution)/shard_map/ppermute | solution.py:29
  28.4 9.1 %collective-permute-start.8 = (bf16[192,768]{1,0:T(8,128)(2,1)S(1)}, bf16[192,768]{1,0:T(8,128)(2,1)S(1)}, u32[]{:S(2)}, u32[]{:S(2)}) collective-permute-start(bf16[192,768]{1,0:T(8,128)(2,1)S(1)} %pad_maximum_fusion.refs_2_), channel_id=1, source_target_pairs={{0,128},{16,144},{32,160},{48,176},{64,192},{80,208},{96,224},{112... | collective-permute-start | bytes 884744 | tf_op jit(solution)/shard_map/ppermute | solution.py:33
  31.4 11.6 %collective-permute-start.9 = (bf16[192,768]{1,0:T(8,128)(2,1)S(1)}, bf16[192,768]{1,0:T(8,128)(2,1)S(1)}, u32[]{:S(2)}, u32[]{:S(2)}) collective-permute-start(bf16[192,768]{1,0:T(8,128)(2,1)S(1)} %pad_maximum_fusion.refs_2_), channel_id=1, source_target_pairs={{0,192},{16,208},{32,224},{48,240},{64,0},{80,16},{96,32},{112,48}... | collective-permute-start | bytes 884744 | tf_op jit(solution)/shard_map/ppermute | solution.py:33
  32.2 13.9 %collective-permute-start.10 = (bf16[192,768]{1,0:T(8,128)(2,1)S(1)}, bf16[192,768]{1,0:T(8,128)(2,1)S(1)}, u32[]{:S(2)}, u32[]{:S(2)}) collective-permute-start(bf16[192,768]{1,0:T(8,128)(2,1)S(1)} %pad_maximum_fusion.refs_2_), channel_id=1, source_target_pairs={{0,64},{16,80},{32,96},{48,112},{64,128},{80,144},{96,160},{112,17... | collective-permute-start | bytes 884744 | tf_op jit(solution)/shard_map/ppermute | solution.py:33
  32.8 14.0 %collective-permute-start.11 = (bf16[192,768]{1,0:T(8,128)(2,1)S(1)}, bf16[192,768]{1,0:T(8,128)(2,1)S(1)}, u32[]{:S(2)}, u32[]{:S(2)}) collective-permute-start(bf16[192,768]{1,0:T(8,128)(2,1)S(1)} %pad_maximum_fusion.refs_2_), channel_id=1, source_target_pairs={{0,1},{1,0},{2,3},{3,2},{4,5},{5,4},{6,7},{7,6},{8,9},{9,8},{10,11... | collective-permute-start | bytes 884744 | tf_op jit(solution)/shard_map/ppermute | solution.py:41
  37.5 9.4 %collective-permute-start.12 = (bf16[192,768]{1,0:T(8,128)(2,1)S(1)}, bf16[192,768]{1,0:T(8,128)(2,1)S(1)}, u32[]{:S(2)}, u32[]{:S(2)}) collective-permute-start(bf16[192,768]{1,0:T(8,128)(2,1)S(1)} %collective-permute-done.8.refs_3_), channel_id=1, source_target_pairs={{0,1},{1,0},{2,3},{3,2},{4,5},{5,4},{6,7},{7,6},{8,9},{9,8},{10,11... | collective-permute-start | bytes 884744 | tf_op jit(solution)/shard_map/ppermute | solution.py:41
  43.0 4.3 %collective-permute-start.13 = (bf16[192,768]{1,0:T(8,128)(2,1)S(1)}, bf16[192,768]{1,0:T(8,128)(2,1)S(1)}, u32[]{:S(2)}, u32[]{:S(2)}) collective-permute-start(bf16[192,768]{1,0:T(8,128)(2,1)S(1)} %collective-permute-done.9.refs_4_), channel_id=1, source_target_pairs={{0,1},{1,0},{2,3},{3,2},{4,5},{5,4},{6,7},{7,6},{8,9},{9,8},{10,11... | collective-permute-start | bytes 884744 | tf_op jit(solution)/shard_map/ppermute | solution.py:41
  46.1 1.6 %collective-permute-start.14 = (bf16[192,768]{1,0:T(8,128)(2,1)S(1)}, bf16[192,768]{1,0:T(8,128)(2,1)S(1)}, u32[]{:S(2)}, u32[]{:S(2)}) collective-permute-start(bf16[192,768]{1,0:T(8,128)(2,1)S(1)} %collective-permute-done.10.refs_5_), channel_id=1, source_target_pairs={{0,1},{1,0},{2,3},{3,2},{4,5},{5,4},{6,7},{7,6},{8,9},{9,8},{10,11... | collective-permute-start | bytes 884744 | tf_op jit(solution)/shard_map/ppermute | solution.py:41
  46.8 30.8 %copy-start = (f32[1,768]{1,0:T(1,128)}, f32[1,768]{1,0:T(1,128)S(1)}, u32[]{:S(2)}) copy-start(f32[1,768]{1,0:T(1,128)S(1)} %broadcast_in_dim.25.refs_12_.gain_ref) | copy-start | bytes 9220
  47.7 0.7 copy-start.1
  77.6 2.9 %collective-permute-start.15 = (bf16[768,768]{1,0:T(8,128)(2,1)S(1)}, bf16[768,768]{1,0:T(8,128)(2,1)S(1)}, u32[]{:S(2)}, u32[]{:S(2)}) collective-permute-start(bf16[768,768]{1,0:T(8,128)(2,1)S(1)} %get-tuple-element.31), channel_id=1, source_target_pairs={{0,1},{1,0},{2,3},{3,2},{4,5},{5,4},{6,7},{7,6},{8,9},{9,8},{10,11... | collective-permute-start | bytes 3538952 | tf_op jit(solution)/shard_map/ppermute | solution.py:41
  81.4 12.6 %collective-permute-start.16 = (bf16[192,768]{1,0:T(8,128)(2,1)S(1)}, bf16[192,768]{1,0:T(8,128)(2,1)S(1)}, u32[]{:S(2)}, u32[]{:S(2)}) collective-permute-start(bf16[192,768]{1,0:T(8,128)(2,1)S(1)} %get-tuple-element.32), channel_id=1, source_target_pairs={{0,128},{16,144},{32,160},{48,176},{64,192},{80,208},{96,224},{112... | collective-permute-start | bytes 884744 | tf_op jit(solution)/shard_map/ppermute | solution.py:33
  83.6 14.7 %collective-permute-start.17 = (bf16[192,768]{1,0:T(8,128)(2,1)S(1)}, bf16[192,768]{1,0:T(8,128)(2,1)S(1)}, u32[]{:S(2)}, u32[]{:S(2)}) collective-permute-start(bf16[192,768]{1,0:T(8,128)(2,1)S(1)} %get-tuple-element.42), channel_id=1, source_target_pairs={{0,64},{16,80},{32,96},{48,112},{64,128},{80,144},{96,160},{112,17... | collective-permute-start | bytes 884744 | tf_op jit(solution)/shard_map/ppermute | solution.py:33
  84.4 13.8 %collective-permute-start.18 = (bf16[192,768]{1,0:T(8,128)(2,1)S(1)}, bf16[192,768]{1,0:T(8,128)(2,1)S(1)}, u32[]{:S(2)}, u32[]{:S(2)}) collective-permute-start(bf16[192,768]{1,0:T(8,128)(2,1)S(1)} %get-tuple-element.43), channel_id=1, source_target_pairs={{0,192},{16,208},{32,224},{48,240},{64,0},{80,16},{96,32},{112,48}... | collective-permute-start | bytes 884744 | tf_op jit(solution)/shard_map/ppermute | solution.py:33
  98.9 4.9 %collective-permute-start.19 = (bf16[48,768]{1,0:T(8,128)(2,1)S(1)}, bf16[48,768]{1,0:T(8,128)(2,1)S(1)}, u32[]{:S(2)}, u32[]{:S(2)}) collective-permute-start(bf16[48,768]{1,0:T(8,128)(2,1)S(1)} %get-tuple-element.45), channel_id=1, source_target_pairs={{0,32},{16,48},{32,0},{48,16},{64,96},{80,112},{96,64},{112,80},{1... | collective-permute-start | bytes 221192 | tf_op jit(solution)/shard_map/ppermute | solution.py:29
  99.0 6.9 %collective-permute-start.20 = (bf16[48,768]{1,0:T(8,128)(2,1)S(1)}, bf16[48,768]{1,0:T(8,128)(2,1)S(1)}, u32[]{:S(2)}, u32[]{:S(2)}) collective-permute-start(bf16[48,768]{1,0:T(8,128)(2,1)S(1)} %get-tuple-element.46), channel_id=1, source_target_pairs={{0,16},{16,32},{32,48},{48,0},{64,80},{80,96},{96,112},{112,64},{1... | collective-permute-start | bytes 221192 | tf_op jit(solution)/shard_map/ppermute | solution.py:29
  99.2 6.7 %collective-permute-start.21 = (bf16[48,768]{1,0:T(8,128)(2,1)S(1)}, bf16[48,768]{1,0:T(8,128)(2,1)S(1)}, u32[]{:S(2)}, u32[]{:S(2)}) collective-permute-start(bf16[48,768]{1,0:T(8,128)(2,1)S(1)} %get-tuple-element.47), channel_id=1, source_target_pairs={{0,48},{16,0},{32,16},{48,32},{64,112},{80,64},{96,80},{112,96},{1... | collective-permute-start | bytes 221192 | tf_op jit(solution)/shard_map/ppermute | solution.py:29
  106.6 16.0 %all-to-all-start = ((f32[16,3,768]{2,1,0:T(4,128)}), f32[16,3,768]{2,1,0:T(4,128)S(1)}, u32[]{:S(2)}, u32[]{:S(2)}) async-start(f32[16,3,768]{2,1,0:T(4,128)} %shard_map.98), calls=%async_computation | async-start | bytes 393216 | tf_op jit(solution)/shard_map/all_to_all | solution.py:361

commit v8 on v7

--- a/solution.py
+++ b/solution.py
@@ -51,12 +51,14 @@
     return [v, hop(v, 2), hop(v, -1), hop(v, 1)]
 
 
-def gather_weights(w):
+def gather_weights(w_qkv, w_out):
     y, x, z, c = coords()
-    n = w.shape[1] // 2
-    mine = lax.dynamic_slice(w, (0, c * n), (3, n))
-    other = lax.dynamic_slice(w, (0, (1 - c) * n), (3, n))
-    block = jnp.concatenate([mine, hop_core(other), jnp.zeros((2, n), w.dtype)], axis=0)
+    n = D
+    left = w_qkv[:, :n]
+    right = jnp.concatenate([w_qkv[:, n:], w_out], axis=1)
+    mine = jnp.where(c == 0, left, right)
+    other = jnp.where(c == 0, right, left)
+    block = jnp.concatenate([mine, hop_core(other), jnp.zeros((2, n), BF16)], axis=0)
     block = jnp.concatenate([block, lax.ppermute(block, "xl", [(i, i ^ 2) for i in range(16)])], axis=0)
     stack = jnp.concatenate([block, hop_z(block, 4), hop_z(block, 2), hop_z(block, -2)], axis=0)
     r = jnp.arange(48)[:, None]
@@ -65,8 +67,8 @@
     j = s % 8
     origin = (z + jnp.where(slot == 1, 4, jnp.where(slot == 2, 6, jnp.where(slot == 3, 2, 0)))) % 8
     row = (origin ^ ((s // 8) % 2)) * 6 + (c ^ (j // 3)) * 3 + j % 3
-    order = ((row == r) & (j < 6)).astype(w.dtype)
-    v = jnp.dot(order, stack, preferred_element_type=F32).astype(w.dtype)
+    order = ((row == r) & (j < 6)).astype(BF16)
+    v = jnp.dot(order, stack, preferred_element_type=F32).astype(BF16)
     v = jnp.concatenate(gather4(v, hop_x), axis=0)
     mine = gather4(v, hop_y)
     return mine + [hop_core(u) for u in mine]
@@ -90,24 +92,23 @@
     return centred * inv, inv
 
 
-def row_mask(counts_ref, first, group):
+def row_mask(at_ref, first, group):
     row_id = lax.broadcasted_iota(jnp.int32, (VMAX, D), 0)
-    return jnp.concatenate([row_id < counts_ref[first + b] for b in range(group)], axis=0)
+    return jnp.concatenate([row_id < at_ref[3 + first + b] for b in range(group)], axis=0)
 
 
 def core_kernel(*refs):
-    at_ref, counts_ref = refs[:2]
-    pieces = refs[2:10]
-    x_ref, cot_ref, gain_ref = refs[10:13]
-    w_out, att_out, gp_out, keep_out, send_out = refs[13:18]
-    w_ref, nb_ref, go_ref, att_ref, gp_ref, keep_ref, send_ref, w_sems, row_sems, dw_sems = refs[18:]
+    at_ref = refs[0]
+    pieces = refs[1:9]
+    x_ref, cot_ref, gain_ref = refs[9:12]
+    w_out, att_out, gp_out, keep_out, send_out = refs[12:17]
+    w_ref, nb_ref, go_ref, att_ref, gp_ref, keep_ref, send_ref, w_sems, row_sems, dw_sems = refs[17:]
     step = pl.program_id(0)
     last = pl.num_programs(0) - 1
     factor = HEAD_DIM**-0.5
     core = at_ref[2]
 
-    @pl.when(step == 0)
-    def _():
+    def weight_copies():
         y, x = at_ref[0], at_ref[1]
         copies = []
         for rel in range(2):
@@ -122,24 +123,28 @@
                             w_sems.at[len(copies)],
                         )
                     )
-        for copy in copies:
-            copy.start()
-        for copy in copies:
-            copy.wait()
-
-    whole_w = pltpu.make_async_copy(w_ref, w_out, w_sems.at[32])
+        return copies
 
     @pl.when(step == 0)
     def _():
-        whole_w.start()
+        for copy in weight_copies():
+            copy.start()
+
+    whole_w = pltpu.make_async_copy(w_ref, w_out, w_sems.at[32])
 
     normed, _ = norm_rows(x_ref[...].reshape(ROWS, D).astype(F32))
     nb = (normed * gain_ref[...]).astype(BF16)
-    mask = row_mask(counts_ref, step * GROUP, GROUP)
+    mask = row_mask(at_ref, step * GROUP, GROUP)
     go = jnp.where(mask, cot_ref[...].reshape(ROWS, D).astype(F32), 0.0).astype(BF16)
     at = pl.ds(pl.multiple_of(step * ROWS, ROWS), ROWS)
     nb_ref[at, :] = nb
     go_ref[at, :] = go
+
+    @pl.when(step == 0)
+    def _():
+        for copy in weight_copies():
+            copy.wait()
+        whole_w.start()
 
     qk = mm(nb, w_ref[0]).astype(BF16)
     vv = mm(nb, w_ref[1, :, :HD]).astype(BF16)
@@ -152,7 +157,7 @@
     pair = lambda a, u, w: jnp.concatenate([a * u, a * w], axis=0)
     stack = lambda a: jnp.concatenate([a[:, :VMAX], a[:, VMAX:]], axis=0)
     for b in range(GROUP):
-        live = key_id < counts_ref[step * GROUP + b]
+        live = key_id < at_ref[3 + step * GROUP + b]
         rs = slice(b * VMAX, (b + 1) * VMAX)
         at_b = pl.ds(pl.multiple_of(step * ROWS + b * VMAX, VMAX), VMAX)
         for lo in range(0, HD, 2 * HEAD_DIM):
@@ -214,7 +219,7 @@
             copy.wait()
 
 
-def grads_core(at, counts, pieces, tiles, cotan, gain):
+def grads_core(at, pieces, tiles, cotan, gain):
     nblock = tiles.shape[0]
     rows = nblock * VMAX
     hbm = pl.BlockSpec(memory_space=pltpu.HBM)
@@ -222,7 +227,7 @@
     return pl.pallas_call(
         core_kernel,
         grid_spec=pltpu.PrefetchScalarGridSpec(
-            num_scalar_prefetch=2,
+            num_scalar_prefetch=1,
             grid=(nblock // GROUP,),
             in_specs=[hbm] * 8 + [tile, tile, pl.BlockSpec((1, D), lambda i, *_: (0, 0))],
             out_specs=[hbm] * 3 + [pl.BlockSpec(memory_space=pl.ANY)] * 2,
@@ -250,15 +255,15 @@
             dimension_semantics=("arbitrary",), vmem_limit_bytes=CORE_MIB * 1024 * 1024
         ),
         cost_estimate=pl.CostEstimate(flops=20_000_000_000, bytes_accessed=18_000_000, transcendentals=1_200_000),
-    )(at, counts, *pieces, tiles, cotan, gain)
-
-
-def rows_kernel(first, counts_ref, w_ref, att_ref, gp_ref, x_ref, cot_ref, gain_ref, *rest):
+    )(at, *pieces, tiles, cotan, gain)
+
+
+def rows_kernel(first, at_ref, w_ref, att_ref, gp_ref, x_ref, cot_ref, gain_ref, *rest):
     enc_ref, gin_ref = rest[-2:]
     gain = gain_ref[...]
     xf = x_ref[...].reshape(TAIL * VMAX, D).astype(F32)
     normed, inv = norm_rows(xf)
-    mask = row_mask(counts_ref, (first + pl.program_id(0)) * TAIL, TAIL)
+    mask = row_mask(at_ref, (first + pl.program_id(0)) * TAIL, TAIL)
     enc = xf + mm_t(att_ref[...], w_ref[1, :, HD:])
     enc_ref[...] = jnp.where(mask, enc, 0.0).astype(BF16).reshape(TAIL, VMAX, D)
     gp = gp_ref[...]
@@ -270,7 +275,7 @@
     gin_ref[...] = jnp.where(mask, gin, 0.0).astype(BF16).reshape(TAIL, VMAX, D)
 
 
-def rows_part(first, count, counts, w, att, gp, tiles, cotan, gain, done):
+def rows_part(first, count, at, w, att, gp, tiles, cotan, gain, done):
     tile = pl.BlockSpec((TAIL, VMAX, D), lambda i, *_: (i + first, 0, 0))
     flat = lambda cols: pl.BlockSpec((TAIL * VMAX, cols), lambda i, *_: (i + first, 0))
     return pl.pallas_call(
@@ -297,7 +302,7 @@
         cost_estimate=pl.CostEstimate(
             flops=count * 650_000_000, bytes_accessed=count * 2_500_000, transcendentals=1000
         ),
-    )(counts, w, att, gp, tiles, cotan, gain, *done)
+    )(at, w, att, gp, tiles, cotan, gain, *done)
 
 
 def small_call(kernel, at, args, outs):
@@ -364,17 +369,17 @@
 
 def shards(patches, out_cot, vis_count, w_qkv, w_out, ln_gain):
     y, x, z, c = coords()
-    pieces = gather_weights(jnp.concatenate([w_qkv, w_out], axis=1))
-    at = jnp.stack([y, x, c]).astype(jnp.int32)
-    counts, tiles, cotan, gain = vis_count[0], patches[0], out_cot[0], ln_gain[None]
-    w, att, gp, keep, send = grads_core(at, counts, pieces, tiles, cotan, gain)
+    pieces = gather_weights(w_qkv, w_out)
+    at = jnp.concatenate([jnp.stack([y, x, c]).astype(jnp.int32), vis_count[0]])
+    tiles, cotan, gain = patches[0], out_cot[0], ln_gain[None]
+    w, att, gp, keep, send = grads_core(at, pieces, tiles, cotan, gain)
 
     def during(own):
-        late, _ = lax.optimization_barrier((counts, own))
+        late, _ = lax.optimization_barrier((at, own))
         return rows_part(0, HEAD, late, w, att, gp, tiles, cotan, gain, ())
 
     (grad_qkv, grad_out), out = scatter_grads(at, keep, send, during)
-    enc, gin = rows_part(HEAD, BLOCKS // TAIL - HEAD, counts, w, att, gp, tiles, cotan, gain, out)
+    enc, gin = rows_part(HEAD, BLOCKS // TAIL - HEAD, at, w, att, gp, tiles, cotan, gain, out)
     return enc[None], gin[None], grad_qkv, grad_out
 
 

time: 124 us -> 124 us (level)
  Pallas kernels: 47.5 us -> 49.1 us
  other arithmetic: 0.16 us -> 1.53 us
  local copies, waits for them, and re-layouts: 2.79 us -> 1.42 us
    pallas_call x1, Pallas kernels: 29.2 us -> 30.8 us  [grads_core(): pl.pallas_call(core_kernel, grid_spec=pltpu.PrefetchScalarGridSpec(num_sc...]
    unnamed x5 -> x6, local copies, waits for them, and re-layouts: 1.36 us -> 0.01 us
  transfers between devices with their start and end apart: 23 -> 23, of which waited for: 15 -> 14; matrix products, arithmetic and copies ran while one was open for 1% -> 1% of each run, Pallas kernels for 13% -> 12%
where the time goes in v8:
time: 124 us
  Pallas kernels  49.1 us (40%)
  starting transfers between devices  48 us (39%)
  waiting for transfers between devices  23.1 us (19%)
  other arithmetic  1.53 us (1%)
  local copies, waits for them, and re-layouts  1.42 us (1%)
    pallas_call x1, Pallas kernels, grads_core(): pl.pallas_call(core_kernel, grid_spec=pltpu.PrefetchScalarGridSpec(num_sc...  30.8 us
    ppermute x6, starting transfers between devices, hop_core(): return lax.ppermute(v, 'xl', [(i, i ^ 1) for i in range(16)])  16.7 us
    pallas_call x2, Pallas kernels, rows_part(): pl.pallas_call(functools.partial(rows_kernel, first), grid_spec=pltpu.Pre...  15.5 us
    ppermute x6, starting transfers between devices, hop_y(): return lax.ppermute(v, 'il', [(i, (i + 4 * k) % 16) for i in range(16)])  9.6 us
    ppermute x3, starting transfers between devices, hop_z(): return lax.ppermute(v, 'xl', [(i, (i + 2 * k) % 16) for i in range(16)])  8.84 us
    ppermute x6, waiting for transfers between devices, hop_x(): lax.ppermute(v, 'il', [(i, i // 4 * 4 + (i + k) % 4) for i in range(16)])  8.52 us
    ppermute x6, starting transfers between devices, hop_x(): lax.ppermute(v, 'il', [(i, i // 4 * 4 + (i + k) % 4) for i in range(16)])  7.14 us
    all_to_all x1, starting transfers between devices, scatter_grads(): got = lax.all_to_all(v, 'xl', split_axis=0, concat_axis=0, tiled=True)  5.65 us
  transfers between devices with their start and end apart: 23, of which 14 were waited for; matrix products, arithmetic and copies ran while one was open for 1% of the time, Pallas kernels for 12%

profile of v8, /device:TPU:1, one launch (start us, length us, event | category | flops | bytes accessed | tf_op | source)
XLA Modules:
  0.0 124.1 jit_solution(6352225668063949330)
XLA Ops:
  1.3 0.7 broadcast_select_fusion
  2.1 3.3 %collective-permute-start = (bf16[3,768]{1,0:T(4,128)(2,1)S(1)}, bf16[3,768]{1,0:T(4,128)(2,1)S(1)}, u32[]{:S(2)}, u32[]{:S(2)}) collective-permute-start(bf16[3,768]{1,0:T(4,128)(2,1)S(1)} %get-tuple-element.50), channel_id=1, source_target_pairs={{0,1},{1,0},{2,3},{3,2},{4,5},{5,4},{6,7},{7,6},{8,9},{9,8},{10,11... | collective-permute-start | bytes 13832 | tf_op jit(solution)/shard_map/ppermute | solution.py:41
  5.4 0.8 collective-permute-done
  6.4 2.5 %collective-permute-done.1 = bf16[8,768]{1,0:T(8,128)(2,1)S(1)} collective-permute-done((bf16[8,768]{1,0:T(8,128)(2,1)S(1)}, bf16[8,768]{1,0:T(8,128)(2,1)S(1)}, u32[]{:S(2)}, u32[]{:S(2)}) %collective-permute-start.1) | collective-permute-done | bytes 12320 | tf_op jit(solution)/shard_map/ppermute | solution.py:62
  8.9 5.3 %collective-permute-start.2 = (bf16[16,768]{1,0:T(8,128)(2,1)S(1)}, bf16[16,768]{1,0:T(8,128)(2,1)S(1)}, u32[]{:S(2)}, u32[]{:S(2)}) collective-permute-start(bf16[16,768]{1,0:T(8,128)(2,1)S(1)} %pad_maximum_fusion.1), channel_id=1, source_target_pairs={{0,8},{1,9},{2,10},{3,11},{4,12},{5,13},{6,14},{7,15},{8,0},{9,1},... | collective-permute-start | bytes 73736 | tf_op jit(solution)/shard_map/ppermute | solution.py:37
  14.1 1.2 collective-permute-start.3
  15.3 2.4 %collective-permute-start.4 = (bf16[16,768]{1,0:T(8,128)(2,1)S(1)}, bf16[16,768]{1,0:T(8,128)(2,1)S(1)}, u32[]{:S(2)}, u32[]{:S(2)}) collective-permute-start(bf16[16,768]{1,0:T(8,128)(2,1)S(1)} %pad_maximum_fusion.1), channel_id=1, source_target_pairs={{0,12},{1,13},{2,14},{3,15},{4,0},{5,1},{6,2},{7,3},{8,4},{9,5},{1... | collective-permute-start | bytes 73736 | tf_op jit(solution)/shard_map/ppermute | solution.py:37
  17.8 1.2 collective-permute-done.3
  19.6 2.8 %collective-permute-start.5 = (bf16[48,768]{1,0:T(8,128)(2,1)S(1)}, bf16[48,768]{1,0:T(8,128)(2,1)S(1)}, u32[]{:S(2)}, u32[]{:S(2)}) collective-permute-start(bf16[48,768]{1,0:T(8,128)(2,1)S(1)} %convolution_convert_fusion), channel_id=1, source_target_pairs={{0,32},{16,48},{32,0},{48,16},{64,96},{80,112},{96,64},{112,80},{1... | collective-permute-start | bytes 221192 | tf_op jit(solution)/shard_map/ppermute | solution.py:29
  22.5 0.9 collective-permute-start.6
  24.4 1.2 collective-permute-done.6
  25.7 2.7 %collective-permute-done.7 = bf16[48,768]{1,0:T(8,128)(2,1)S(1)} collective-permute-done((bf16[48,768]{1,0:T(8,128)(2,1)S(1)}, bf16[48,768]{1,0:T(8,128)(2,1)S(1)}, u32[]{:S(2)}, u32[]{:S(2)}) %collective-permute-start.7) | collective-permute-done | bytes 73760 | tf_op jit(solution)/shard_map/ppermute | solution.py:29
  28.4 3.0 %collective-permute-start.8 = (bf16[192,768]{1,0:T(8,128)(2,1)S(1)}, bf16[192,768]{1,0:T(8,128)(2,1)S(1)}, u32[]{:S(2)}, u32[]{:S(2)}) collective-permute-start(bf16[192,768]{1,0:T(8,128)(2,1)S(1)} %pad_maximum_fusion.refs_1_), channel_id=1, source_target_pairs={{0,128},{16,144},{32,160},{48,176},{64,192},{80,208},{96,224},{112... | collective-permute-start | bytes 884744 | tf_op jit(solution)/shard_map/ppermute | solution.py:33
  31.4 0.8 collective-permute-start.9
  32.8 4.6 %collective-permute-start.11 = (bf16[192,768]{1,0:T(8,128)(2,1)S(1)}, bf16[192,768]{1,0:T(8,128)(2,1)S(1)}, u32[]{:S(2)}, u32[]{:S(2)}) collective-permute-start(bf16[192,768]{1,0:T(8,128)(2,1)S(1)} %pad_maximum_fusion.refs_1_), channel_id=1, source_target_pairs={{0,1},{1,0},{2,3},{3,2},{4,5},{5,4},{6,7},{7,6},{8,9},{9,8},{10,11... | collective-permute-start | bytes 884744 | tf_op jit(solution)/shard_map/ppermute | solution.py:41
  37.5 5.2 %collective-permute-start.12 = (bf16[192,768]{1,0:T(8,128)(2,1)S(1)}, bf16[192,768]{1,0:T(8,128)(2,1)S(1)}, u32[]{:S(2)}, u32[]{:S(2)}) collective-permute-start(bf16[192,768]{1,0:T(8,128)(2,1)S(1)} %collective-permute-done.8.refs_2_), channel_id=1, source_target_pairs={{0,1},{1,0},{2,3},{3,2},{4,5},{5,4},{6,7},{7,6},{8,9},{9,8},{10,11... | collective-permute-start | bytes 884744 | tf_op jit(solution)/shard_map/ppermute | solution.py:41
  43.0 3.1 %collective-permute-start.13 = (bf16[192,768]{1,0:T(8,128)(2,1)S(1)}, bf16[192,768]{1,0:T(8,128)(2,1)S(1)}, u32[]{:S(2)}, u32[]{:S(2)}) collective-permute-start(bf16[192,768]{1,0:T(8,128)(2,1)S(1)} %collective-permute-done.9.refs_3_), channel_id=1, source_target_pairs={{0,1},{1,0},{2,3},{3,2},{4,5},{5,4},{6,7},{7,6},{8,9},{9,8},{10,11... | collective-permute-start | bytes 884744 | tf_op jit(solution)/shard_map/ppermute | solution.py:41
  46.8 0.7 pad_add_fusion.refs_0_.at_ref
  47.7 30.8 %shard_map.93 = (bf16[2,768,768]{2,1,0:T(8,128)(2,1)}, bf16[1536,384]{1,0:T(8,128)(2,1)}, bf16[1536,1152]{1,0:T(8,128)(2,1)}, f32[768,768]{1,0:T(8,128)S(1)}, bf16[768,768]{1,0:T(8,128)(2,1)S(1)}) custom-call(s32[15]{0:T(128)S(1)} %pad_add_fusion.refs_0_.at_ref, bf16[192,768]{1,0:T(8,128)(2,1)S(1)} %pad_maximum_fusion.refs_1_, ...), custom_call_target="tpu_custom_call" | custom-call | flops 20000000000 | bytes 18000000 | tf_op jit(solution)/shard_map/pallas_call | solution.py:227
  78.9 2.5 %collective-permute-done.15.refs_0_ = bf16[768,768]{1,0:T(8,128)(2,1)S(1)} collective-permute-done((bf16[768,768]{1,0:T(8,128)(2,1)S(1)}, bf16[768,768]{1,0:T(8,128)(2,1)S(1)}, u32[]{:S(2)}, u32[]{:S(2)}) %collective-permute-start.15) | collective-permute-done | bytes 1179680 | tf_op jit(solution)/shard_map/ppermute | solution.py:41
  81.4 0.8 shard_map.94
  82.3 2.5 %collective-permute-start.16 = (bf16[192,768]{1,0:T(8,128)(2,1)S(1)}, bf16[192,768]{1,0:T(8,128)(2,1)S(1)}, u32[]{:S(2)}, u32[]{:S(2)}) collective-permute-start(bf16[192,768]{1,0:T(8,128)(2,1)S(1)} %get-tuple-element.32), channel_id=1, source_target_pairs={{0,128},{16,144},{32,160},{48,176},{64,192},{80,208},{96,224},{112... | collective-permute-start | bytes 884744 | tf_op jit(solution)/shard_map/ppermute | solution.py:33
  85.3 2.1 %collective-permute-start.18 = (bf16[192,768]{1,0:T(8,128)(2,1)S(1)}, bf16[192,768]{1,0:T(8,128)(2,1)S(1)}, u32[]{:S(2)}, u32[]{:S(2)}) collective-permute-start(bf16[192,768]{1,0:T(8,128)(2,1)S(1)} %get-tuple-element.43), channel_id=1, source_target_pairs={{0,192},{16,208},{32,224},{48,240},{64,0},{80,16},{96,32},{112,48}... | collective-permute-start | bytes 884744 | tf_op jit(solution)/shard_map/ppermute | solution.py:33
  87.4 7.9 %shard_map.95 = (bf16[12,128,768]{2,1,0:T(8,128)(2,1)}, bf16[12,128,768]{2,1,0:T(8,128)(2,1)}) custom-call(s32[15]{0:T(128)} %copy-done.1, bf16[2,768,768]{2,1,0:T(8,128)(2,1)} %get-tuple-element.27.w_ref, bf16[1536,384]{1,0:T(8,128)(2,1)} %get-tuple-element.28.att_ref, bf16[1536,1152]{1,0:T(8,128)(2,1)} %get-tuple-element.29.gp_ref, ...), custom_call_target="tpu_custom_call" | custom-call | flops 1950000000 | bytes 7500000 | tf_op jit(solution)/shard_map/pallas_call | solution.py:281
  95.3 3.8 %collective-permute-done.17.refs_1_ = bf16[192,768]{1,0:T(8,128)(2,1)S(1)} collective-permute-done((bf16[192,768]{1,0:T(8,128)(2,1)S(1)}, bf16[192,768]{1,0:T(8,128)(2,1)S(1)}, u32[]{:S(2)}, u32[]{:S(2)}) %collective-permute-start.17) | collective-permute-done | bytes 294944 | tf_op jit(solution)/shard_map/ppermute | solution.py:33
  100.1 2.6 %collective-permute-start.21 = (bf16[48,768]{1,0:T(8,128)(2,1)S(1)}, bf16[48,768]{1,0:T(8,128)(2,1)S(1)}, u32[]{:S(2)}, u32[]{:S(2)}) collective-permute-start(bf16[48,768]{1,0:T(8,128)(2,1)S(1)} %get-tuple-element.47), channel_id=1, source_target_pairs={{0,48},{16,0},{32,16},{48,32},{64,112},{80,64},{96,80},{112,96},{1... | collective-permute-start | bytes 221192 | tf_op jit(solution)/shard_map/ppermute | solution.py:29
  102.7 2.0 %collective-permute-done.19.refs_0_ = bf16[48,768]{1,0:T(8,128)(2,1)S(1)} collective-permute-done((bf16[48,768]{1,0:T(8,128)(2,1)S(1)}, bf16[48,768]{1,0:T(8,128)(2,1)S(1)}, u32[]{:S(2)}, u32[]{:S(2)}) %collective-permute-start.19) | collective-permute-done | bytes 73760 | tf_op jit(solution)/shard_map/ppermute | solution.py:29
  104.7 2.1 %collective-permute-done.20.refs_1_ = bf16[48,768]{1,0:T(8,128)(2,1)S(1)} collective-permute-done((bf16[48,768]{1,0:T(8,128)(2,1)S(1)}, bf16[48,768]{1,0:T(8,128)(2,1)S(1)}, u32[]{:S(2)}, u32[]{:S(2)}) %collective-permute-start.20) | collective-permute-done | bytes 73760 | tf_op jit(solution)/shard_map/ppermute | solution.py:29
  106.8 0.7 shard_map.98
  107.5 5.7 %all-to-all-start = ((f32[16,3,768]{2,1,0:T(4,128)}), f32[16,3,768]{2,1,0:T(4,128)S(1)}, u32[]{:S(2)}, u32[]{:S(2)}) async-start(f32[16,3,768]{2,1,0:T(4,128)} %shard_map.98), calls=%async_computation | async-start | bytes 393216 | tf_op jit(solution)/shard_map/all_to_all | solution.py:366
  113.1 7.6 %shard_map.96 = (bf16[12,128,768]{2,1,0:T(8,128)(2,1)}, bf16[12,128,768]{2,1,0:T(8,128)(2,1)}) custom-call(s32[15]{0:T(128)} %copy-done.1, bf16[2,768,768]{2,1,0:T(8,128)(2,1)} %get-tuple-element.27.w_ref, bf16[1536,384]{1,0:T(8,128)(2,1)} %get-tuple-element.28.att_ref, ...), custom_call_target="tpu_custom_call", output_to_operand_aliasing={{0}: (7, {}), {1}: (8, {})} | custom-call | flops 1950000000 | bytes 7500000 | tf_op jit(solution)/shard_map/pallas_call | solution.py:281
  120.8 2.7 %all-to-all-done.got_ref = f32[16,3,768]{2,1,0:T(4,128)S(1)} async-done(((f32[16,3,768]{2,1,0:T(4,128)}), f32[16,3,768]{2,1,0:T(4,128)S(1)}, u32[]{:S(2)}, u32[]{:S(2)}) %all-to-all-start) | async-done | bytes 147488 | tf_op jit(solution)/shard_map/all_to_all | solution.py:366
  (39 shorter events, 7.2 us)
Async XLA Ops:
  2.1 4.2 %collective-permute-start = (bf16[3,768]{1,0:T(4,128)(2,1)S(1)}, bf16[3,768]{1,0:T(4,128)(2,1)S(1)}, u32[]{:S(2)}, u32[]{:S(2)}) collective-permute-start(bf16[3,768]{1,0:T(4,128)(2,1)S(1)} %get-tuple-element.50), channel_id=1, source_target_pairs={{0,1},{1,0},{2,3},{3,2},{4,5},{5,4},{6,7},{7,6},{8,9},{9,8},{10,11... | collective-permute-start | bytes 13832 | tf_op jit(solution)/shard_map/ppermute | solution.py:41
  6.2 2.6 %collective-permute-start.1 = (bf16[8,768]{1,0:T(8,128)(2,1)S(1)}, bf16[8,768]{1,0:T(8,128)(2,1)S(1)}, u32[]{:S(2)}, u32[]{:S(2)}) collective-permute-start(bf16[8,768]{1,0:T(8,128)(2,1)S(1)} %pad_maximum_fusion.2), channel_id=1, source_target_pairs={{0,2},{1,3},{2,0},{3,1},{4,6},{5,7},{6,4},{7,5},{8,10},{9,11},{10,... | collective-permute-start | bytes 36872 | tf_op jit(solution)/shard_map/ppermute | solution.py:62
  8.9 8.9 %collective-permute-start.2 = (bf16[16,768]{1,0:T(8,128)(2,1)S(1)}, bf16[16,768]{1,0:T(8,128)(2,1)S(1)}, u32[]{:S(2)}, u32[]{:S(2)}) collective-permute-start(bf16[16,768]{1,0:T(8,128)(2,1)S(1)} %pad_maximum_fusion.1), channel_id=1, source_target_pairs={{0,8},{1,9},{2,10},{3,11},{4,12},{5,13},{6,14},{7,15},{8,0},{9,1},... | collective-permute-start | bytes 73736 | tf_op jit(solution)/shard_map/ppermute | solution.py:37
  14.1 4.8 %collective-permute-start.3 = (bf16[16,768]{1,0:T(8,128)(2,1)S(1)}, bf16[16,768]{1,0:T(8,128)(2,1)S(1)}, u32[]{:S(2)}, u32[]{:S(2)}) collective-permute-start(bf16[16,768]{1,0:T(8,128)(2,1)S(1)} %pad_maximum_fusion.1), channel_id=1, source_target_pairs={{0,4},{1,5},{2,6},{3,7},{4,8},{5,9},{6,10},{7,11},{8,12},{9,13},{1... | collective-permute-start | bytes 73736 | tf_op jit(solution)/shard_map/ppermute | solution.py:37
  15.3 4.1 %collective-permute-start.4 = (bf16[16,768]{1,0:T(8,128)(2,1)S(1)}, bf16[16,768]{1,0:T(8,128)(2,1)S(1)}, u32[]{:S(2)}, u32[]{:S(2)}) collective-permute-start(bf16[16,768]{1,0:T(8,128)(2,1)S(1)} %pad_maximum_fusion.1), channel_id=1, source_target_pairs={{0,12},{1,13},{2,14},{3,15},{4,0},{5,1},{6,2},{7,3},{8,4},{9,5},{1... | collective-permute-start | bytes 73736 | tf_op jit(solution)/shard_map/ppermute | solution.py:37
  19.6 4.8 %collective-permute-start.5 = (bf16[48,768]{1,0:T(8,128)(2,1)S(1)}, bf16[48,768]{1,0:T(8,128)(2,1)S(1)}, u32[]{:S(2)}, u32[]{:S(2)}) collective-permute-start(bf16[48,768]{1,0:T(8,128)(2,1)S(1)} %convolution_convert_fusion), channel_id=1, source_target_pairs={{0,32},{16,48},{32,0},{48,16},{64,96},{80,112},{96,64},{112,80},{1... | collective-permute-start | bytes 221192 | tf_op jit(solution)/shard_map/ppermute | solution.py:29
  22.5 3.2 %collective-permute-start.6 = (bf16[48,768]{1,0:T(8,128)(2,1)S(1)}, bf16[48,768]{1,0:T(8,128)(2,1)S(1)}, u32[]{:S(2)}, u32[]{:S(2)}) collective-permute-start(bf16[48,768]{1,0:T(8,128)(2,1)S(1)} %convolution_convert_fusion), channel_id=1, source_target_pairs={{0,48},{16,0},{32,16},{48,32},{64,112},{80,64},{96,80},{112,96},{1... | collective-permute-start | bytes 221192 | tf_op jit(solution)/shard_map/ppermute | solution.py:29
  23.3 5.0 %collective-permute-start.7 = (bf16[48,768]{1,0:T(8,128)(2,1)S(1)}, bf16[48,768]{1,0:T(8,128)(2,1)S(1)}, u32[]{:S(2)}, u32[]{:S(2)}) collective-permute-start(bf16[48,768]{1,0:T(8,128)(2,1)S(1)} %convolution_convert_fusion), channel_id=1, source_target_pairs={{0,16},{16,32},{32,48},{48,0},{64,80},{80,96},{96,112},{112,64},{1... | collective-permute-start | bytes 221192 | tf_op jit(solution)/shard_map/ppermute | solution.py:29
  28.4 9.1 %collective-permute-start.8 = (bf16[192,768]{1,0:T(8,128)(2,1)S(1)}, bf16[192,768]{1,0:T(8,128)(2,1)S(1)}, u32[]{:S(2)}, u32[]{:S(2)}) collective-permute-start(bf16[192,768]{1,0:T(8,128)(2,1)S(1)} %pad_maximum_fusion.refs_1_), channel_id=1, source_target_pairs={{0,128},{16,144},{32,160},{48,176},{64,192},{80,208},{96,224},{112... | collective-permute-start | bytes 884744 | tf_op jit(solution)/shard_map/ppermute | solution.py:33
  31.4 11.6 %collective-permute-start.9 = (bf16[192,768]{1,0:T(8,128)(2,1)S(1)}, bf16[192,768]{1,0:T(8,128)(2,1)S(1)}, u32[]{:S(2)}, u32[]{:S(2)}) collective-permute-start(bf16[192,768]{1,0:T(8,128)(2,1)S(1)} %pad_maximum_fusion.refs_1_), channel_id=1, source_target_pairs={{0,192},{16,208},{32,224},{48,240},{64,0},{80,16},{96,32},{112,48}... | collective-permute-start | bytes 884744 | tf_op jit(solution)/shard_map/ppermute | solution.py:33
  32.1 13.9 %collective-permute-start.10 = (bf16[192,768]{1,0:T(8,128)(2,1)S(1)}, bf16[192,768]{1,0:T(8,128)(2,1)S(1)}, u32[]{:S(2)}, u32[]{:S(2)}) collective-permute-start(bf16[192,768]{1,0:T(8,128)(2,1)S(1)} %pad_maximum_fusion.refs_1_), channel_id=1, source_target_pairs={{0,64},{16,80},{32,96},{48,112},{64,128},{80,144},{96,160},{112,17... | collective-permute-start | bytes 884744 | tf_op jit(solution)/shard_map/ppermute | solution.py:33
  32.8 14.7 %collective-permute-start.11 = (bf16[192,768]{1,0:T(8,128)(2,1)S(1)}, bf16[192,768]{1,0:T(8,128)(2,1)S(1)}, u32[]{:S(2)}, u32[]{:S(2)}) collective-permute-start(bf16[192,768]{1,0:T(8,128)(2,1)S(1)} %pad_maximum_fusion.refs_1_), channel_id=1, source_target_pairs={{0,1},{1,0},{2,3},{3,2},{4,5},{5,4},{6,7},{7,6},{8,9},{9,8},{10,11... | collective-permute-start | bytes 884744 | tf_op jit(solution)/shard_map/ppermute | solution.py:41
  37.5 10.1 %collective-permute-start.12 = (bf16[192,768]{1,0:T(8,128)(2,1)S(1)}, bf16[192,768]{1,0:T(8,128)(2,1)S(1)}, u32[]{:S(2)}, u32[]{:S(2)}) collective-permute-start(bf16[192,768]{1,0:T(8,128)(2,1)S(1)} %collective-permute-done.8.refs_2_), channel_id=1, source_target_pairs={{0,1},{1,0},{2,3},{3,2},{4,5},{5,4},{6,7},{7,6},{8,9},{9,8},{10,11... | collective-permute-start | bytes 884744 | tf_op jit(solution)/shard_map/ppermute | solution.py:41
  43.0 4.5 %collective-permute-start.13 = (bf16[192,768]{1,0:T(8,128)(2,1)S(1)}, bf16[192,768]{1,0:T(8,128)(2,1)S(1)}, u32[]{:S(2)}, u32[]{:S(2)}) collective-permute-start(bf16[192,768]{1,0:T(8,128)(2,1)S(1)} %collective-permute-done.9.refs_3_), channel_id=1, source_target_pairs={{0,1},{1,0},{2,3},{3,2},{4,5},{5,4},{6,7},{7,6},{8,9},{9,8},{10,11... | collective-permute-start | bytes 884744 | tf_op jit(solution)/shard_map/ppermute | solution.py:41
  46.1 1.6 %collective-permute-start.14 = (bf16[192,768]{1,0:T(8,128)(2,1)S(1)}, bf16[192,768]{1,0:T(8,128)(2,1)S(1)}, u32[]{:S(2)}, u32[]{:S(2)}) collective-permute-start(bf16[192,768]{1,0:T(8,128)(2,1)S(1)} %collective-permute-done.10.refs_4_), channel_id=1, source_target_pairs={{0,1},{1,0},{2,3},{3,2},{4,5},{5,4},{6,7},{7,6},{8,9},{9,8},{10,11... | collective-permute-start | bytes 884744 | tf_op jit(solution)/shard_map/ppermute | solution.py:41
  46.8 31.7 %copy-start = (f32[1,768]{1,0:T(1,128)}, f32[1,768]{1,0:T(1,128)S(1)}, u32[]{:S(2)}) copy-start(f32[1,768]{1,0:T(1,128)S(1)} %broadcast_in_dim.25.refs_11_.gain_ref) | copy-start | bytes 9220
  47.5 33.9 %copy-start.1 = (s32[15]{0:T(128)}, s32[15]{0:T(128)S(1)}, u32[]{:S(2)}) copy-start(s32[15]{0:T(128)S(1)} %pad_add_fusion.refs_0_.at_ref) | copy-start | bytes 184
  78.5 2.9 %collective-permute-start.15 = (bf16[768,768]{1,0:T(8,128)(2,1)S(1)}, bf16[768,768]{1,0:T(8,128)(2,1)S(1)}, u32[]{:S(2)}, u32[]{:S(2)}) collective-permute-start(bf16[768,768]{1,0:T(8,128)(2,1)S(1)} %get-tuple-element.31), channel_id=1, source_target_pairs={{0,1},{1,0},{2,3},{3,2},{4,5},{5,4},{6,7},{7,6},{8,9},{9,8},{10,11... | collective-permute-start | bytes 3538952 | tf_op jit(solution)/shard_map/ppermute | solution.py:41
  82.3 13.0 %collective-permute-start.16 = (bf16[192,768]{1,0:T(8,128)(2,1)S(1)}, bf16[192,768]{1,0:T(8,128)(2,1)S(1)}, u32[]{:S(2)}, u32[]{:S(2)}) collective-permute-start(bf16[192,768]{1,0:T(8,128)(2,1)S(1)} %get-tuple-element.32), channel_id=1, source_target_pairs={{0,128},{16,144},{32,160},{48,176},{64,192},{80,208},{96,224},{112... | collective-permute-start | bytes 884744 | tf_op jit(solution)/shard_map/ppermute | solution.py:33
  84.7 14.4 %collective-permute-start.17 = (bf16[192,768]{1,0:T(8,128)(2,1)S(1)}, bf16[192,768]{1,0:T(8,128)(2,1)S(1)}, u32[]{:S(2)}, u32[]{:S(2)}) collective-permute-start(bf16[192,768]{1,0:T(8,128)(2,1)S(1)} %get-tuple-element.42), channel_id=1, source_target_pairs={{0,64},{16,80},{32,96},{48,112},{64,128},{80,144},{96,160},{112,17... | collective-permute-start | bytes 884744 | tf_op jit(solution)/shard_map/ppermute | solution.py:33
  85.3 13.8 %collective-permute-start.18 = (bf16[192,768]{1,0:T(8,128)(2,1)S(1)}, bf16[192,768]{1,0:T(8,128)(2,1)S(1)}, u32[]{:S(2)}, u32[]{:S(2)}) collective-permute-start(bf16[192,768]{1,0:T(8,128)(2,1)S(1)} %get-tuple-element.43), channel_id=1, source_target_pairs={{0,192},{16,208},{32,224},{48,240},{64,0},{80,16},{96,32},{112,48}... | collective-permute-start | bytes 884744 | tf_op jit(solution)/shard_map/ppermute | solution.py:33
  87.4 11.7 %copy-start.2 = (s32[15]{0:T(128)S(1)}, s32[15]{0:T(128)}, u32[]{:S(2)}) copy-start(s32[15]{0:T(128)} %copy-done.1) | copy-start | bytes 184
  99.8 4.9 %collective-permute-start.19 = (bf16[48,768]{1,0:T(8,128)(2,1)S(1)}, bf16[48,768]{1,0:T(8,128)(2,1)S(1)}, u32[]{:S(2)}, u32[]{:S(2)}) collective-permute-start(bf16[48,768]{1,0:T(8,128)(2,1)S(1)} %get-tuple-element.45), channel_id=1, source_target_pairs={{0,32},{16,48},{32,0},{48,16},{64,96},{80,112},{96,64},{112,80},{1... | collective-permute-start | bytes 221192 | tf_op jit(solution)/shard_map/ppermute | solution.py:29
  99.9 6.9 %collective-permute-start.20 = (bf16[48,768]{1,0:T(8,128)(2,1)S(1)}, bf16[48,768]{1,0:T(8,128)(2,1)S(1)}, u32[]{:S(2)}, u32[]{:S(2)}) collective-permute-start(bf16[48,768]{1,0:T(8,128)(2,1)S(1)} %get-tuple-element.46), channel_id=1, source_target_pairs={{0,16},{16,32},{32,48},{48,0},{64,80},{80,96},{96,112},{112,64},{1... | collective-permute-start | bytes 221192 | tf_op jit(solution)/shard_map/ppermute | solution.py:29
  100.1 6.7 %collective-permute-start.21 = (bf16[48,768]{1,0:T(8,128)(2,1)S(1)}, bf16[48,768]{1,0:T(8,128)(2,1)S(1)}, u32[]{:S(2)}, u32[]{:S(2)}) collective-permute-start(bf16[48,768]{1,0:T(8,128)(2,1)S(1)} %get-tuple-element.47), channel_id=1, source_target_pairs={{0,48},{16,0},{32,16},{48,32},{64,112},{80,64},{96,80},{112,96},{1... | collective-permute-start | bytes 221192 | tf_op jit(solution)/shard_map/ppermute | solution.py:29
  107.5 16.0 %all-to-all-start = ((f32[16,3,768]{2,1,0:T(4,128)}), f32[16,3,768]{2,1,0:T(4,128)S(1)}, u32[]{:S(2)}, u32[]{:S(2)}) async-start(f32[16,3,768]{2,1,0:T(4,128)} %shard_map.98), calls=%async_computation | async-start | bytes 393216 | tf_op jit(solution)/shard_map/all_to_all | solution.py:366

commit v9 on v8

--- a/solution.py
+++ b/solution.py
@@ -125,12 +125,16 @@
                     )
         return copies
 
+    whole_w = pltpu.make_async_copy(w_ref, w_out, w_sems.at[32])
+
     @pl.when(step == 0)
     def _():
-        for copy in weight_copies():
+        copies = weight_copies()
+        for copy in copies:
             copy.start()
-
-    whole_w = pltpu.make_async_copy(w_ref, w_out, w_sems.at[32])
+        for copy in copies:
+            copy.wait()
+        whole_w.start()
 
     normed, _ = norm_rows(x_ref[...].reshape(ROWS, D).astype(F32))
     nb = (normed * gain_ref[...]).astype(BF16)
@@ -139,12 +143,6 @@
     at = pl.ds(pl.multiple_of(step * ROWS, ROWS), ROWS)
     nb_ref[at, :] = nb
     go_ref[at, :] = go
-
-    @pl.when(step == 0)
-    def _():
-        for copy in weight_copies():
-            copy.wait()
-        whole_w.start()
 
     qk = mm(nb, w_ref[0]).astype(BF16)
     vv = mm(nb, w_ref[1, :, :HD]).astype(BF16)

time: 124 us -> 123 us (level)
  Pallas kernels: 49.1 us -> 47.6 us
    pallas_call x1, Pallas kernels: 30.8 us -> 29.2 us  [grads_core(): pl.pallas_call(core_kernel, grid_spec=pltpu.PrefetchScalarGridSpec(num_sc...]
  transfers between devices with their start and end apart: 23 -> 23, of which waited for: 14 -> 14; matrix products, arithmetic and copies ran while one was open for 1% -> 1% of each run, Pallas kernels for 12% -> 13%
where the time goes in v9:
time: 123 us
  starting transfers between devices  48 us (39%)
  Pallas kernels  47.6 us (39%)
  waiting for transfers between devices  23.1 us (19%)
  other arithmetic  1.53 us (1%)
  local copies, waits for them, and re-layouts  1.42 us (1%)
    pallas_call x1, Pallas kernels, grads_core(): pl.pallas_call(core_kernel, grid_spec=pltpu.PrefetchScalarGridSpec(num_sc...  29.2 us
    ppermute x6, starting transfers between devices, hop_core(): return lax.ppermute(v, 'xl', [(i, i ^ 1) for i in range(16)])  16.7 us
    pallas_call x2, Pallas kernels, rows_part(): pl.pallas_call(functools.partial(rows_kernel, first), grid_spec=pltpu.Pre...  15.5 us
    ppermute x6, starting transfers between devices, hop_y(): return lax.ppermute(v, 'il', [(i, (i + 4 * k) % 16) for i in range(16)])  9.6 us
    ppermute x3, starting transfers between devices, hop_z(): return lax.ppermute(v, 'xl', [(i, (i + 2 * k) % 16) for i in range(16)])  8.84 us
    ppermute x6, waiting for transfers between devices, hop_x(): lax.ppermute(v, 'il', [(i, i // 4 * 4 + (i + k) % 4) for i in range(16)])  8.52 us
    ppermute x6, starting transfers between devices, hop_x(): lax.ppermute(v, 'il', [(i, i // 4 * 4 + (i + k) % 4) for i in range(16)])  7.14 us
    all_to_all x1, starting transfers between devices, scatter_grads(): got = lax.all_to_all(v, 'xl', split_axis=0, concat_axis=0, tiled=True)  5.66 us
  transfers between devices with their start and end apart: 23, of which 14 were waited for; matrix products, arithmetic and copies ran while one was open for 1% of the time, Pallas kernels for 13%

profile of v9, /device:TPU:1, one launch (start us, length us, event | category | flops | bytes accessed | tf_op | source)
XLA Modules:
  0.0 122.6 jit_solution(15848679643169591389)
XLA Ops:
  1.3 0.7 broadcast_select_fusion
  2.1 3.3 %collective-permute-start = (bf16[3,768]{1,0:T(4,128)(2,1)S(1)}, bf16[3,768]{1,0:T(4,128)(2,1)S(1)}, u32[]{:S(2)}, u32[]{:S(2)}) collective-permute-start(bf16[3,768]{1,0:T(4,128)(2,1)S(1)} %get-tuple-element.50), channel_id=1, source_target_pairs={{0,1},{1,0},{2,3},{3,2},{4,5},{5,4},{6,7},{7,6},{8,9},{9,8},{10,11... | collective-permute-start | bytes 13832 | tf_op jit(solution)/shard_map/ppermute | solution.py:41
  5.4 0.8 collective-permute-done
  6.4 2.5 %collective-permute-done.1 = bf16[8,768]{1,0:T(8,128)(2,1)S(1)} collective-permute-done((bf16[8,768]{1,0:T(8,128)(2,1)S(1)}, bf16[8,768]{1,0:T(8,128)(2,1)S(1)}, u32[]{:S(2)}, u32[]{:S(2)}) %collective-permute-start.1) | collective-permute-done | bytes 12320 | tf_op jit(solution)/shard_map/ppermute | solution.py:62
  8.9 5.3 %collective-permute-start.2 = (bf16[16,768]{1,0:T(8,128)(2,1)S(1)}, bf16[16,768]{1,0:T(8,128)(2,1)S(1)}, u32[]{:S(2)}, u32[]{:S(2)}) collective-permute-start(bf16[16,768]{1,0:T(8,128)(2,1)S(1)} %pad_maximum_fusion.1), channel_id=1, source_target_pairs={{0,8},{1,9},{2,10},{3,11},{4,12},{5,13},{6,14},{7,15},{8,0},{9,1},... | collective-permute-start | bytes 73736 | tf_op jit(solution)/shard_map/ppermute | solution.py:37
  14.1 1.2 collective-permute-start.3
  15.3 2.4 %collective-permute-start.4 = (bf16[16,768]{1,0:T(8,128)(2,1)S(1)}, bf16[16,768]{1,0:T(8,128)(2,1)S(1)}, u32[]{:S(2)}, u32[]{:S(2)}) collective-permute-start(bf16[16,768]{1,0:T(8,128)(2,1)S(1)} %pad_maximum_fusion.1), channel_id=1, source_target_pairs={{0,12},{1,13},{2,14},{3,15},{4,0},{5,1},{6,2},{7,3},{8,4},{9,5},{1... | collective-permute-start | bytes 73736 | tf_op jit(solution)/shard_map/ppermute | solution.py:37
  17.8 1.2 collective-permute-done.3
  19.6 2.8 %collective-permute-start.5 = (bf16[48,768]{1,0:T(8,128)(2,1)S(1)}, bf16[48,768]{1,0:T(8,128)(2,1)S(1)}, u32[]{:S(2)}, u32[]{:S(2)}) collective-permute-start(bf16[48,768]{1,0:T(8,128)(2,1)S(1)} %convolution_convert_fusion), channel_id=1, source_target_pairs={{0,32},{16,48},{32,0},{48,16},{64,96},{80,112},{96,64},{112,80},{1... | collective-permute-start | bytes 221192 | tf_op jit(solution)/shard_map/ppermute | solution.py:29
  22.5 0.9 collective-permute-start.6
  24.4 1.2 %collective-permute-done.6 = bf16[48,768]{1,0:T(8,128)(2,1)S(1)} collective-permute-done((bf16[48,768]{1,0:T(8,128)(2,1)S(1)}, bf16[48,768]{1,0:T(8,128)(2,1)S(1)}, u32[]{:S(2)}, u32[]{:S(2)}) %collective-permute-start.6) | collective-permute-done | bytes 73760 | tf_op jit(solution)/shard_map/ppermute | solution.py:29
  25.7 2.7 %collective-permute-done.7 = bf16[48,768]{1,0:T(8,128)(2,1)S(1)} collective-permute-done((bf16[48,768]{1,0:T(8,128)(2,1)S(1)}, bf16[48,768]{1,0:T(8,128)(2,1)S(1)}, u32[]{:S(2)}, u32[]{:S(2)}) %collective-permute-start.7) | collective-permute-done | bytes 73760 | tf_op jit(solution)/shard_map/ppermute | solution.py:29
  28.4 3.0 %collective-permute-start.8 = (bf16[192,768]{1,0:T(8,128)(2,1)S(1)}, bf16[192,768]{1,0:T(8,128)(2,1)S(1)}, u32[]{:S(2)}, u32[]{:S(2)}) collective-permute-start(bf16[192,768]{1,0:T(8,128)(2,1)S(1)} %pad_maximum_fusion.refs_1_), channel_id=1, source_target_pairs={{0,128},{16,144},{32,160},{48,176},{64,192},{80,208},{96,224},{112... | collective-permute-start | bytes 884744 | tf_op jit(solution)/shard_map/ppermute | solution.py:33
  31.4 0.8 collective-permute-start.9
  32.8 4.6 %collective-permute-start.11 = (bf16[192,768]{1,0:T(8,128)(2,1)S(1)}, bf16[192,768]{1,0:T(8,128)(2,1)S(1)}, u32[]{:S(2)}, u32[]{:S(2)}) collective-permute-start(bf16[192,768]{1,0:T(8,128)(2,1)S(1)} %pad_maximum_fusion.refs_1_), channel_id=1, source_target_pairs={{0,1},{1,0},{2,3},{3,2},{4,5},{5,4},{6,7},{7,6},{8,9},{9,8},{10,11... | collective-permute-start | bytes 884744 | tf_op jit(solution)/shard_map/ppermute | solution.py:41
  37.5 5.2 %collective-permute-start.12 = (bf16[192,768]{1,0:T(8,128)(2,1)S(1)}, bf16[192,768]{1,0:T(8,128)(2,1)S(1)}, u32[]{:S(2)}, u32[]{:S(2)}) collective-permute-start(bf16[192,768]{1,0:T(8,128)(2,1)S(1)} %collective-permute-done.8.refs_2_), channel_id=1, source_target_pairs={{0,1},{1,0},{2,3},{3,2},{4,5},{5,4},{6,7},{7,6},{8,9},{9,8},{10,11... | collective-permute-start | bytes 884744 | tf_op jit(solution)/shard_map/ppermute | solution.py:41
  43.0 3.1 %collective-permute-start.13 = (bf16[192,768]{1,0:T(8,128)(2,1)S(1)}, bf16[192,768]{1,0:T(8,128)(2,1)S(1)}, u32[]{:S(2)}, u32[]{:S(2)}) collective-permute-start(bf16[192,768]{1,0:T(8,128)(2,1)S(1)} %collective-permute-done.9.refs_3_), channel_id=1, source_target_pairs={{0,1},{1,0},{2,3},{3,2},{4,5},{5,4},{6,7},{7,6},{8,9},{9,8},{10,11... | collective-permute-start | bytes 884744 | tf_op jit(solution)/shard_map/ppermute | solution.py:41
  46.8 0.7 pad_add_fusion.refs_0_.at_ref
  47.7 29.2 %shard_map.93 = (bf16[2,768,768]{2,1,0:T(8,128)(2,1)}, bf16[1536,384]{1,0:T(8,128)(2,1)}, bf16[1536,1152]{1,0:T(8,128)(2,1)}, f32[768,768]{1,0:T(8,128)S(1)}, bf16[768,768]{1,0:T(8,128)(2,1)S(1)}) custom-call(s32[15]{0:T(128)S(1)} %pad_add_fusion.refs_0_.at_ref, bf16[192,768]{1,0:T(8,128)(2,1)S(1)} %pad_maximum_fusion.refs_1_, ...), custom_call_target="tpu_custom_call" | custom-call | flops 20000000000 | bytes 18000000 | tf_op jit(solution)/shard_map/pallas_call | solution.py:225
  77.4 2.5 %collective-permute-done.15.refs_0_ = bf16[768,768]{1,0:T(8,128)(2,1)S(1)} collective-permute-done((bf16[768,768]{1,0:T(8,128)(2,1)S(1)}, bf16[768,768]{1,0:T(8,128)(2,1)S(1)}, u32[]{:S(2)}, u32[]{:S(2)}) %collective-permute-start.15) | collective-permute-done | bytes 1179680 | tf_op jit(solution)/shard_map/ppermute | solution.py:41
  79.9 0.8 shard_map.94
  80.7 2.5 %collective-permute-start.16 = (bf16[192,768]{1,0:T(8,128)(2,1)S(1)}, bf16[192,768]{1,0:T(8,128)(2,1)S(1)}, u32[]{:S(2)}, u32[]{:S(2)}) collective-permute-start(bf16[192,768]{1,0:T(8,128)(2,1)S(1)} %get-tuple-element.32), channel_id=1, source_target_pairs={{0,128},{16,144},{32,160},{48,176},{64,192},{80,208},{96,224},{112... | collective-permute-start | bytes 884744 | tf_op jit(solution)/shard_map/ppermute | solution.py:33
  83.8 2.1 %collective-permute-start.18 = (bf16[192,768]{1,0:T(8,128)(2,1)S(1)}, bf16[192,768]{1,0:T(8,128)(2,1)S(1)}, u32[]{:S(2)}, u32[]{:S(2)}) collective-permute-start(bf16[192,768]{1,0:T(8,128)(2,1)S(1)} %get-tuple-element.43), channel_id=1, source_target_pairs={{0,192},{16,208},{32,224},{48,240},{64,0},{80,16},{96,32},{112,48}... | collective-permute-start | bytes 884744 | tf_op jit(solution)/shard_map/ppermute | solution.py:33
  85.9 7.9 %shard_map.95 = (bf16[12,128,768]{2,1,0:T(8,128)(2,1)}, bf16[12,128,768]{2,1,0:T(8,128)(2,1)}) custom-call(s32[15]{0:T(128)} %copy-done.1, bf16[2,768,768]{2,1,0:T(8,128)(2,1)} %get-tuple-element.27.w_ref, bf16[1536,384]{1,0:T(8,128)(2,1)} %get-tuple-element.28.att_ref, bf16[1536,1152]{1,0:T(8,128)(2,1)} %get-tuple-element.29.gp_ref, ...), custom_call_target="tpu_custom_call" | custom-call | flops 1950000000 | bytes 7500000 | tf_op jit(solution)/shard_map/pallas_call | solution.py:279
  93.7 3.8 %collective-permute-done.17.refs_1_ = bf16[192,768]{1,0:T(8,128)(2,1)S(1)} collective-permute-done((bf16[192,768]{1,0:T(8,128)(2,1)S(1)}, bf16[192,768]{1,0:T(8,128)(2,1)S(1)}, u32[]{:S(2)}, u32[]{:S(2)}) %collective-permute-start.17) | collective-permute-done | bytes 294944 | tf_op jit(solution)/shard_map/ppermute | solution.py:33
  98.5 2.6 %collective-permute-start.21 = (bf16[48,768]{1,0:T(8,128)(2,1)S(1)}, bf16[48,768]{1,0:T(8,128)(2,1)S(1)}, u32[]{:S(2)}, u32[]{:S(2)}) collective-permute-start(bf16[48,768]{1,0:T(8,128)(2,1)S(1)} %get-tuple-element.47), channel_id=1, source_target_pairs={{0,48},{16,0},{32,16},{48,32},{64,112},{80,64},{96,80},{112,96},{1... | collective-permute-start | bytes 221192 | tf_op jit(solution)/shard_map/ppermute | solution.py:29
  101.1 2.0 %collective-permute-done.19.refs_0_ = bf16[48,768]{1,0:T(8,128)(2,1)S(1)} collective-permute-done((bf16[48,768]{1,0:T(8,128)(2,1)S(1)}, bf16[48,768]{1,0:T(8,128)(2,1)S(1)}, u32[]{:S(2)}, u32[]{:S(2)}) %collective-permute-start.19) | collective-permute-done | bytes 73760 | tf_op jit(solution)/shard_map/ppermute | solution.py:29
  103.2 2.1 %collective-permute-done.20.refs_1_ = bf16[48,768]{1,0:T(8,128)(2,1)S(1)} collective-permute-done((bf16[48,768]{1,0:T(8,128)(2,1)S(1)}, bf16[48,768]{1,0:T(8,128)(2,1)S(1)}, u32[]{:S(2)}, u32[]{:S(2)}) %collective-permute-start.20) | collective-permute-done | bytes 73760 | tf_op jit(solution)/shard_map/ppermute | solution.py:29
  105.2 0.7 shard_map.98
  106.0 5.7 %all-to-all-start = ((f32[16,3,768]{2,1,0:T(4,128)}), f32[16,3,768]{2,1,0:T(4,128)S(1)}, u32[]{:S(2)}, u32[]{:S(2)}) async-start(f32[16,3,768]{2,1,0:T(4,128)} %shard_map.98), calls=%async_computation | async-start | bytes 393216 | tf_op jit(solution)/shard_map/all_to_all | solution.py:364
  111.6 7.6 %shard_map.96 = (bf16[12,128,768]{2,1,0:T(8,128)(2,1)}, bf16[12,128,768]{2,1,0:T(8,128)(2,1)}) custom-call(s32[15]{0:T(128)} %copy-done.1, bf16[2,768,768]{2,1,0:T(8,128)(2,1)} %get-tuple-element.27.w_ref, bf16[1536,384]{1,0:T(8,128)(2,1)} %get-tuple-element.28.att_ref, ...), custom_call_target="tpu_custom_call", output_to_operand_aliasing={{0}: (7, {}), {1}: (8, {})} | custom-call | flops 1950000000 | bytes 7500000 | tf_op jit(solution)/shard_map/pallas_call | solution.py:279
  119.3 2.7 %all-to-all-done.got_ref = f32[16,3,768]{2,1,0:T(4,128)S(1)} async-done(((f32[16,3,768]{2,1,0:T(4,128)}), f32[16,3,768]{2,1,0:T(4,128)S(1)}, u32[]{:S(2)}, u32[]{:S(2)}) %all-to-all-start) | async-done | bytes 147488 | tf_op jit(solution)/shard_map/all_to_all | solution.py:364
  (39 shorter events, 7.2 us)
Async XLA Ops:
  2.1 4.2 %collective-permute-start = (bf16[3,768]{1,0:T(4,128)(2,1)S(1)}, bf16[3,768]{1,0:T(4,128)(2,1)S(1)}, u32[]{:S(2)}, u32[]{:S(2)}) collective-permute-start(bf16[3,768]{1,0:T(4,128)(2,1)S(1)} %get-tuple-element.50), channel_id=1, source_target_pairs={{0,1},{1,0},{2,3},{3,2},{4,5},{5,4},{6,7},{7,6},{8,9},{9,8},{10,11... | collective-permute-start | bytes 13832 | tf_op jit(solution)/shard_map/ppermute | solution.py:41
  6.2 2.6 %collective-permute-start.1 = (bf16[8,768]{1,0:T(8,128)(2,1)S(1)}, bf16[8,768]{1,0:T(8,128)(2,1)S(1)}, u32[]{:S(2)}, u32[]{:S(2)}) collective-permute-start(bf16[8,768]{1,0:T(8,128)(2,1)S(1)} %pad_maximum_fusion.2), channel_id=1, source_target_pairs={{0,2},{1,3},{2,0},{3,1},{4,6},{5,7},{6,4},{7,5},{8,10},{9,11},{10,... | collective-permute-start | bytes 36872 | tf_op jit(solution)/shard_map/ppermute | solution.py:62
  8.9 8.9 %collective-permute-start.2 = (bf16[16,768]{1,0:T(8,128)(2,1)S(1)}, bf16[16,768]{1,0:T(8,128)(2,1)S(1)}, u32[]{:S(2)}, u32[]{:S(2)}) collective-permute-start(bf16[16,768]{1,0:T(8,128)(2,1)S(1)} %pad_maximum_fusion.1), channel_id=1, source_target_pairs={{0,8},{1,9},{2,10},{3,11},{4,12},{5,13},{6,14},{7,15},{8,0},{9,1},... | collective-permute-start | bytes 73736 | tf_op jit(solution)/shard_map/ppermute | solution.py:37
  14.1 4.8 %collective-permute-start.3 = (bf16[16,768]{1,0:T(8,128)(2,1)S(1)}, bf16[16,768]{1,0:T(8,128)(2,1)S(1)}, u32[]{:S(2)}, u32[]{:S(2)}) collective-permute-start(bf16[16,768]{1,0:T(8,128)(2,1)S(1)} %pad_maximum_fusion.1), channel_id=1, source_target_pairs={{0,4},{1,5},{2,6},{3,7},{4,8},{5,9},{6,10},{7,11},{8,12},{9,13},{1... | collective-permute-start | bytes 73736 | tf_op jit(solution)/shard_map/ppermute | solution.py:37
  15.3 4.1 %collective-permute-start.4 = (bf16[16,768]{1,0:T(8,128)(2,1)S(1)}, bf16[16,768]{1,0:T(8,128)(2,1)S(1)}, u32[]{:S(2)}, u32[]{:S(2)}) collective-permute-start(bf16[16,768]{1,0:T(8,128)(2,1)S(1)} %pad_maximum_fusion.1), channel_id=1, source_target_pairs={{0,12},{1,13},{2,14},{3,15},{4,0},{5,1},{6,2},{7,3},{8,4},{9,5},{1... | collective-permute-start | bytes 73736 | tf_op jit(solution)/shard_map/ppermute | solution.py:37
  19.6 4.8 %collective-permute-start.5 = (bf16[48,768]{1,0:T(8,128)(2,1)S(1)}, bf16[48,768]{1,0:T(8,128)(2,1)S(1)}, u32[]{:S(2)}, u32[]{:S(2)}) collective-permute-start(bf16[48,768]{1,0:T(8,128)(2,1)S(1)} %convolution_convert_fusion), channel_id=1, source_target_pairs={{0,32},{16,48},{32,0},{48,16},{64,96},{80,112},{96,64},{112,80},{1... | collective-permute-start | bytes 221192 | tf_op jit(solution)/shard_map/ppermute | solution.py:29
  22.5 3.2 %collective-permute-start.6 = (bf16[48,768]{1,0:T(8,128)(2,1)S(1)}, bf16[48,768]{1,0:T(8,128)(2,1)S(1)}, u32[]{:S(2)}, u32[]{:S(2)}) collective-permute-start(bf16[48,768]{1,0:T(8,128)(2,1)S(1)} %convolution_convert_fusion), channel_id=1, source_target_pairs={{0,48},{16,0},{32,16},{48,32},{64,112},{80,64},{96,80},{112,96},{1... | collective-permute-start | bytes 221192 | tf_op jit(solution)/shard_map/ppermute | solution.py:29
  23.3 5.0 %collective-permute-start.7 = (bf16[48,768]{1,0:T(8,128)(2,1)S(1)}, bf16[48,768]{1,0:T(8,128)(2,1)S(1)}, u32[]{:S(2)}, u32[]{:S(2)}) collective-permute-start(bf16[48,768]{1,0:T(8,128)(2,1)S(1)} %convolution_convert_fusion), channel_id=1, source_target_pairs={{0,16},{16,32},{32,48},{48,0},{64,80},{80,96},{96,112},{112,64},{1... | collective-permute-start | bytes 221192 | tf_op jit(solution)/shard_map/ppermute | solution.py:29
  28.4 9.1 %collective-permute-start.8 = (bf16[192,768]{1,0:T(8,128)(2,1)S(1)}, bf16[192,768]{1,0:T(8,128)(2,1)S(1)}, u32[]{:S(2)}, u32[]{:S(2)}) collective-permute-start(bf16[192,768]{1,0:T(8,128)(2,1)S(1)} %pad_maximum_fusion.refs_1_), channel_id=1, source_target_pairs={{0,128},{16,144},{32,160},{48,176},{64,192},{80,208},{96,224},{112... | collective-permute-start | bytes 884744 | tf_op jit(solution)/shard_map/ppermute | solution.py:33
  31.4 11.6 %collective-permute-start.9 = (bf16[192,768]{1,0:T(8,128)(2,1)S(1)}, bf16[192,768]{1,0:T(8,128)(2,1)S(1)}, u32[]{:S(2)}, u32[]{:S(2)}) collective-permute-start(bf16[192,768]{1,0:T(8,128)(2,1)S(1)} %pad_maximum_fusion.refs_1_), channel_id=1, source_target_pairs={{0,192},{16,208},{32,224},{48,240},{64,0},{80,16},{96,32},{112,48}... | collective-permute-start | bytes 884744 | tf_op jit(solution)/shard_map/ppermute | solution.py:33
  32.1 13.9 %collective-permute-start.10 = (bf16[192,768]{1,0:T(8,128)(2,1)S(1)}, bf16[192,768]{1,0:T(8,128)(2,1)S(1)}, u32[]{:S(2)}, u32[]{:S(2)}) collective-permute-start(bf16[192,768]{1,0:T(8,128)(2,1)S(1)} %pad_maximum_fusion.refs_1_), channel_id=1, source_target_pairs={{0,64},{16,80},{32,96},{48,112},{64,128},{80,144},{96,160},{112,17... | collective-permute-start | bytes 884744 | tf_op jit(solution)/shard_map/ppermute | solution.py:33
  32.8 14.7 %collective-permute-start.11 = (bf16[192,768]{1,0:T(8,128)(2,1)S(1)}, bf16[192,768]{1,0:T(8,128)(2,1)S(1)}, u32[]{:S(2)}, u32[]{:S(2)}) collective-permute-start(bf16[192,768]{1,0:T(8,128)(2,1)S(1)} %pad_maximum_fusion.refs_1_), channel_id=1, source_target_pairs={{0,1},{1,0},{2,3},{3,2},{4,5},{5,4},{6,7},{7,6},{8,9},{9,8},{10,11... | collective-permute-start | bytes 884744 | tf_op jit(solution)/shard_map/ppermute | solution.py:41
  37.5 10.1 %collective-permute-start.12 = (bf16[192,768]{1,0:T(8,128)(2,1)S(1)}, bf16[192,768]{1,0:T(8,128)(2,1)S(1)}, u32[]{:S(2)}, u32[]{:S(2)}) collective-permute-start(bf16[192,768]{1,0:T(8,128)(2,1)S(1)} %collective-permute-done.8.refs_2_), channel_id=1, source_target_pairs={{0,1},{1,0},{2,3},{3,2},{4,5},{5,4},{6,7},{7,6},{8,9},{9,8},{10,11... | collective-permute-start | bytes 884744 | tf_op jit(solution)/shard_map/ppermute | solution.py:41
  43.0 4.5 %collective-permute-start.13 = (bf16[192,768]{1,0:T(8,128)(2,1)S(1)}, bf16[192,768]{1,0:T(8,128)(2,1)S(1)}, u32[]{:S(2)}, u32[]{:S(2)}) collective-permute-start(bf16[192,768]{1,0:T(8,128)(2,1)S(1)} %collective-permute-done.9.refs_3_), channel_id=1, source_target_pairs={{0,1},{1,0},{2,3},{3,2},{4,5},{5,4},{6,7},{7,6},{8,9},{9,8},{10,11... | collective-permute-start | bytes 884744 | tf_op jit(solution)/shard_map/ppermute | solution.py:41
  46.1 1.6 %collective-permute-start.14 = (bf16[192,768]{1,0:T(8,128)(2,1)S(1)}, bf16[192,768]{1,0:T(8,128)(2,1)S(1)}, u32[]{:S(2)}, u32[]{:S(2)}) collective-permute-start(bf16[192,768]{1,0:T(8,128)(2,1)S(1)} %collective-permute-done.10.refs_4_), channel_id=1, source_target_pairs={{0,1},{1,0},{2,3},{3,2},{4,5},{5,4},{6,7},{7,6},{8,9},{9,8},{10,11... | collective-permute-start | bytes 884744 | tf_op jit(solution)/shard_map/ppermute | solution.py:41
  46.8 30.2 %copy-start = (f32[1,768]{1,0:T(1,128)}, f32[1,768]{1,0:T(1,128)S(1)}, u32[]{:S(2)}) copy-start(f32[1,768]{1,0:T(1,128)S(1)} %broadcast_in_dim.25.refs_11_.gain_ref) | copy-start | bytes 9220
  47.5 32.4 %copy-start.1 = (s32[15]{0:T(128)}, s32[15]{0:T(128)S(1)}, u32[]{:S(2)}) copy-start(s32[15]{0:T(128)S(1)} %pad_add_fusion.refs_0_.at_ref) | copy-start | bytes 184
  77.0 2.9 %collective-permute-start.15 = (bf16[768,768]{1,0:T(8,128)(2,1)S(1)}, bf16[768,768]{1,0:T(8,128)(2,1)S(1)}, u32[]{:S(2)}, u32[]{:S(2)}) collective-permute-start(bf16[768,768]{1,0:T(8,128)(2,1)S(1)} %get-tuple-element.31), channel_id=1, source_target_pairs={{0,1},{1,0},{2,3},{3,2},{4,5},{5,4},{6,7},{7,6},{8,9},{9,8},{10,11... | collective-permute-start | bytes 3538952 | tf_op jit(solution)/shard_map/ppermute | solution.py:41
  80.7 13.0 %collective-permute-start.16 = (bf16[192,768]{1,0:T(8,128)(2,1)S(1)}, bf16[192,768]{1,0:T(8,128)(2,1)S(1)}, u32[]{:S(2)}, u32[]{:S(2)}) collective-permute-start(bf16[192,768]{1,0:T(8,128)(2,1)S(1)} %get-tuple-element.32), channel_id=1, source_target_pairs={{0,128},{16,144},{32,160},{48,176},{64,192},{80,208},{96,224},{112... | collective-permute-start | bytes 884744 | tf_op jit(solution)/shard_map/ppermute | solution.py:33
  83.2 14.4 %collective-permute-start.17 = (bf16[192,768]{1,0:T(8,128)(2,1)S(1)}, bf16[192,768]{1,0:T(8,128)(2,1)S(1)}, u32[]{:S(2)}, u32[]{:S(2)}) collective-permute-start(bf16[192,768]{1,0:T(8,128)(2,1)S(1)} %get-tuple-element.42), channel_id=1, source_target_pairs={{0,64},{16,80},{32,96},{48,112},{64,128},{80,144},{96,160},{112,17... | collective-permute-start | bytes 884744 | tf_op jit(solution)/shard_map/ppermute | solution.py:33
  83.8 13.8 %collective-permute-start.18 = (bf16[192,768]{1,0:T(8,128)(2,1)S(1)}, bf16[192,768]{1,0:T(8,128)(2,1)S(1)}, u32[]{:S(2)}, u32[]{:S(2)}) collective-permute-start(bf16[192,768]{1,0:T(8,128)(2,1)S(1)} %get-tuple-element.43), channel_id=1, source_target_pairs={{0,192},{16,208},{32,224},{48,240},{64,0},{80,16},{96,32},{112,48}... | collective-permute-start | bytes 884744 | tf_op jit(solution)/shard_map/ppermute | solution.py:33
  85.9 11.7 %copy-start.2 = (s32[15]{0:T(128)S(1)}, s32[15]{0:T(128)}, u32[]{:S(2)}) copy-start(s32[15]{0:T(128)} %copy-done.1) | copy-start | bytes 184
  98.3 4.9 %collective-permute-start.19 = (bf16[48,768]{1,0:T(8,128)(2,1)S(1)}, bf16[48,768]{1,0:T(8,128)(2,1)S(1)}, u32[]{:S(2)}, u32[]{:S(2)}) collective-permute-start(bf16[48,768]{1,0:T(8,128)(2,1)S(1)} %get-tuple-element.45), channel_id=1, source_target_pairs={{0,32},{16,48},{32,0},{48,16},{64,96},{80,112},{96,64},{112,80},{1... | collective-permute-start | bytes 221192 | tf_op jit(solution)/shard_map/ppermute | solution.py:29
  98.4 6.9 %collective-permute-start.20 = (bf16[48,768]{1,0:T(8,128)(2,1)S(1)}, bf16[48,768]{1,0:T(8,128)(2,1)S(1)}, u32[]{:S(2)}, u32[]{:S(2)}) collective-permute-start(bf16[48,768]{1,0:T(8,128)(2,1)S(1)} %get-tuple-element.46), channel_id=1, source_target_pairs={{0,16},{16,32},{32,48},{48,0},{64,80},{80,96},{96,112},{112,64},{1... | collective-permute-start | bytes 221192 | tf_op jit(solution)/shard_map/ppermute | solution.py:29
  98.5 6.7 %collective-permute-start.21 = (bf16[48,768]{1,0:T(8,128)(2,1)S(1)}, bf16[48,768]{1,0:T(8,128)(2,1)S(1)}, u32[]{:S(2)}, u32[]{:S(2)}) collective-permute-start(bf16[48,768]{1,0:T(8,128)(2,1)S(1)} %get-tuple-element.47), channel_id=1, source_target_pairs={{0,48},{16,0},{32,16},{48,32},{64,112},{80,64},{96,80},{112,96},{1... | collective-permute-start | bytes 221192 | tf_op jit(solution)/shard_map/ppermute | solution.py:29
  106.0 16.0 %all-to-all-start = ((f32[16,3,768]{2,1,0:T(4,128)}), f32[16,3,768]{2,1,0:T(4,128)S(1)}, u32[]{:S(2)}, u32[]{:S(2)}) async-start(f32[16,3,768]{2,1,0:T(4,128)} %shard_map.98), calls=%async_computation | async-start | bytes 393216 | tf_op jit(solution)/shard_map/all_to_all | solution.py:364
